TPU v7x, 32 devices: a whole 2x2x4 slice. The times are simulated.
32 devices in a mesh: dp: 4 (over y, x), expert: 8 (over z, core).
Axes of the slice: x: 2, y: 2, z: 4, core: 2. Of those that a mesh axis runs over, the one named last changes fastest.
Arguments:
- layer_input: bfloat16 [6144, 2048], P(('dp', 'expert')), may hold values from -6 to 6
- out_cotangent: bfloat16 [6144, 2048], P(('dp', 'expert')), may hold values from -6 to 6
- segments: int32 [32, 192], P(('dp', 'expert')), may hold values from 0 to 2, never falling along the last dimension, each value on 1 to 96 neighbouring positions
- routes: int32 [6144, 8], P(('dp', 'expert')), may hold values from 0 to 23, all different within a row; in each aligned block of 192 rows (0 to 191, 192 to 383, ...) at most 72 rows name the same one
- w_qkv: bfloat16 [2048, 6144], P(('dp', 'expert')), may hold values from -0.125 to 0.125
- w_out: bfloat16 [2048, 2048], P(('dp', 'expert')), may hold values from -0.5 to 0.5
- w_router: bfloat16 [2048, 24], P(('dp', 'expert')), may hold values from -0.0625 to 0.0625
- attn_gain: bfloat16 [2048], P(('dp', 'expert')), may hold values from 0.5 to 1.5
- mlp_gain: bfloat16 [2048], P(('dp', 'expert')), may hold values from 0.5 to 1.5
- query_gain: bfloat16 [2048], P(('dp', 'expert')), may hold values from 0.099609375 to 1.8984375
- key_gain: bfloat16 [2048], P(('dp', 'expert')), may hold values from 0.099609375 to 1.8984375
- w_gate_up: bfloat16 [24, 2048, 2048], P('expert'), may hold values from -0.125 to 0.125
- w_down: bfloat16 [24, 1024, 2048], P('expert'), may hold values from -0.75 to 0.75
Outputs:
- out: bfloat16 [6144, 2048], P(('dp', 'expert'))
- grad_input: float32 [6144, 2048], P(('dp', 'expert'))
- grad_qkv: float32 [2048, 3, 2048], P('dp', None, 'expert')
- grad_out: float32 [2048, 2048], P('expert', 'dp')
- grad_router: float32 [2048, 24], P(('dp', 'expert'))
- grad_attn_gain: float32 [2048], P(('dp', 'expert'))
- grad_mlp_gain: float32 [2048], P(('dp', 'expert'))
- grad_query_gain: float32 [2048], P('expert')
- grad_key_gain: float32 [2048], P('expert')
- grad_gate_up: float32 [24, 2048, 2048], P('expert', 'dp')
- grad_down: float32 [24, 1024, 2048], P('expert', 'dp')
Inputs may be any that keep to these rules, and one draw needn't show every extreme that they name: `routes`: each row names 8 different experts. Among the rows of one device no expert is named more than 72 times, a bound that some block reaches. `segments`: within a sequence the numbers never fall; a document has at most 96 tokens and one has exactly that many.
All inputs are finite; a program needn't handle non-finite values.
Results may differ from a plain program's by a relative error of at most 0.02.
Values may be sent and summed in bfloat16 or wider, within the bound.
A program may use at most 320 MiB of HBM per device.

v0:
```python
import math

import jax
import jax.numpy as jnp
from jax import lax
from jax.sharding import PartitionSpec as P

HEADS = 16


NORM_EPS = 1e-05


def rms_scale(values):
    return lax.rsqrt(jnp.mean(values * values, axis=-1, keepdims=True) + NORM_EPS)


def rotary(values, direction):
    length = values.shape[-3]
    half_size = values.shape[-1] // 2
    index_half = jnp.arange(half_size, dtype=jnp.float32)
    frequency = jnp.exp(index_half * (-2.0 * math.log(10000.0) / values.shape[-1]))
    angles = jnp.arange(length, dtype=jnp.float32)[:, None] * frequency[None, :]
    cosine = jnp.cos(angles)[:, None, :]
    sine_table = direction * jnp.sin(angles)[:, None, :]
    first_half = values[..., :half_size]
    second = values[..., half_size:]
    return jnp.concatenate(
        [first_half * cosine - second * sine_table, second * cosine + first_half * sine_table],
        axis=-1,
    )


def norm_back(grad_normed, normed, scale_rows):
    return scale_rows * (
        grad_normed - normed * jnp.mean(grad_normed * normed, axis=-1, keepdims=True)
    )


def contract_rows(left_side, right_side):
    return lax.dot_general(
        left_side, right_side, (((0,), (0,)), ((), ())), preferred_element_type=jnp.float32
    )


def contract_cols(left_side, right_side):
    return lax.dot_general(
        left_side, right_side, (((1,), (1,)), ((), ())), preferred_element_type=jnp.float32
    )


def masked_scores(query_rot, key_rot, allowed, scaling):
    raw_scores = (
        jnp.einsum("gqhd,gkhd->ghqk", query_rot, key_rot, preferred_element_type=jnp.float32)
        * scaling
    )
    return jnp.where(allowed[:, None], raw_scores, -1e30)


def on_device(
    layer_input,
    out_cotangent,
    segments,
    routes,
    w_qkv,
    w_out,
    w_router,
    attn_gain,
    mlp_gain,
    query_gain,
    key_gain,
    w_gate_up,
    w_down,
):
    row_count, model_dim = layer_input.shape
    top_count = routes.shape[1]
    expert_count = w_router.shape[1]
    head_size = model_dim // HEADS
    capacity = (row_count * top_count * 9 // 8 + expert_count - 1) // expert_count
    slot_count = expert_count * capacity
    scaling = 1.0 / math.sqrt(head_size)
    dp_count = lax.axis_size("dp")
    dense = (w_qkv, w_out, w_router, attn_gain, mlp_gain, query_gain, key_gain)
    qkv_full, out_full, router_full, gain_attn, gain_mlp, gain_query, gain_key = (
        lax.all_gather(dense[0], ("dp", "expert"), axis=0, tiled=True),
        lax.all_gather(dense[1], ("dp", "expert"), axis=0, tiled=True),
        lax.all_gather(dense[2], ("dp", "expert"), axis=0, tiled=True),
        lax.all_gather(dense[3], ("dp", "expert"), axis=0, tiled=True),
        lax.all_gather(dense[4], ("dp", "expert"), axis=0, tiled=True),
        lax.all_gather(dense[5], ("dp", "expert"), axis=0, tiled=True),
        lax.all_gather(dense[6], ("dp", "expert"), axis=0, tiled=True),
    )
    gain_attn = gain_attn.astype(jnp.float32)
    gain_mlp = gain_mlp.astype(jnp.float32)
    gain_query = gain_query.astype(jnp.float32)
    gain_key = gain_key.astype(jnp.float32)
    inputs = layer_input.astype(jnp.float32)
    scale_attn = rms_scale(inputs)
    normed_attn = inputs * scale_attn
    hidden_one = (normed_attn * gain_attn).astype(jnp.bfloat16)
    group_count = segments.shape[0]
    heads_here = model_dim // head_size
    projected = jnp.dot(hidden_one, qkv_full, preferred_element_type=jnp.float32)
    query_rows = projected[:, :model_dim]
    key_rows = projected[:, model_dim : 2 * model_dim]
    value_rows = projected[:, 2 * model_dim :]
    square_query = jnp.sum(query_rows * query_rows, axis=-1, keepdims=True)
    square_key = jnp.sum(key_rows * key_rows, axis=-1, keepdims=True)
    scale_query = lax.rsqrt(square_query / model_dim + NORM_EPS)
    scale_key = lax.rsqrt(square_key / model_dim + NORM_EPS)
    normed_query = query_rows * scale_query
    normed_key = key_rows * scale_key
    head_shape = (group_count, row_count, heads_here, head_size)
    query_rot = rotary((normed_query * gain_query).reshape(head_shape), 1.0).astype(jnp.bfloat16)
    key_rot = rotary((normed_key * gain_key).reshape(head_shape), 1.0).astype(jnp.bfloat16)
    value_low = value_rows.reshape(head_shape).astype(jnp.bfloat16)
    position = jnp.arange(row_count)
    allowed = (position[:, None] >= position[None, :])[None] & (
        segments[:, :, None] == segments[:, None, :]
    )
    scores = masked_scores(query_rot, key_rot, allowed, scaling)
    row_top = jnp.max(scores, axis=-1, keepdims=True)
    expanded = jnp.exp(scores - row_top)
    row_total = jnp.sum(expanded, axis=-1, keepdims=True)
    log_total = row_top + jnp.log(row_total)
    attn_low = (expanded / row_total).astype(jnp.bfloat16)
    attended = jnp.einsum(
        "ghqk,gkhd->gqhd", attn_low, value_low, preferred_element_type=jnp.float32
    )
    attended = attended.reshape(group_count * row_count, model_dim).astype(jnp.bfloat16)
    attn_proj = jnp.dot(attended, out_full, preferred_element_type=jnp.float32)
    residual = inputs + attn_proj
    scale_mlp = rms_scale(residual)
    normed_mlp = residual * scale_mlp
    hidden_two = (normed_mlp * gain_mlp).astype(jnp.bfloat16)
    logits = jnp.dot(hidden_two, router_full, preferred_element_type=jnp.float32)
    chooser = (routes[:, :, None] == jnp.arange(expert_count)[None, None, :]).astype(jnp.float32)
    chosen = jnp.sum(chooser * logits[:, None, :], axis=-1)
    gate_values = jax.nn.softmax(chosen, axis=-1)
    used_table = jnp.sum(chooser, axis=1).astype(jnp.bfloat16)
    lower_tri = (position[:, None] > position[None, :]).astype(jnp.bfloat16)
    earlier = jnp.dot(lower_tri, used_table, preferred_element_type=jnp.float32)
    rank_in = jnp.sum(chooser * earlier[:, None, :], axis=-1).astype(jnp.int32)
    slot_index = routes * capacity + rank_in
    slot_flat = slot_index.reshape(-1)
    dispatch_table = jnp.any(
        slot_index[None, :, :] == jnp.arange(slot_count)[:, None, None], axis=-1
    ).astype(jnp.bfloat16)
    send_rows = jnp.dot(dispatch_table, hidden_two, preferred_element_type=jnp.float32).astype(
        jnp.bfloat16
    )
    send_rows = send_rows.reshape(expert_count, capacity, model_dim)
    expert_rows = lax.all_to_all(send_rows, "expert", split_axis=0, concat_axis=1, tiled=True)
    hidden = jnp.einsum("erd,edf->erf", expert_rows, w_gate_up, preferred_element_type=jnp.float32)
    hidden_size = hidden.shape[2] // 2
    gate_part = hidden[..., :hidden_size]
    up_part = hidden[..., hidden_size:]
    sigmoid_gate = jax.nn.sigmoid(gate_part)
    silu_gate = gate_part * sigmoid_gate
    activated = (silu_gate * up_part).astype(jnp.bfloat16)
    expert_out = jnp.einsum(
        "erf,efd->erd", activated, w_down, preferred_element_type=jnp.float32
    ).astype(jnp.bfloat16)
    returned = lax.all_to_all(
        expert_out, "expert", split_axis=1, concat_axis=0, tiled=True
    ).reshape(slot_count, model_dim)
    picked = (
        jnp.take(returned, slot_flat, axis=0)
        .reshape(row_count, top_count, model_dim)
        .astype(jnp.float32)
    )
    mixture = jnp.sum(gate_values[:, :, None] * picked, axis=1)
    output = (residual + mixture).astype(jnp.bfloat16)
    grad_out_rows = out_cotangent.astype(jnp.float32)
    grad_gates = jnp.sum(picked * grad_out_rows[:, None, :], axis=-1)
    grad_slots = (
        (gate_values[:, :, None] * grad_out_rows[:, None, :])
        .astype(jnp.bfloat16)
        .reshape(row_count * top_count, model_dim)
    )
    back_send = jnp.zeros((slot_count, model_dim), jnp.bfloat16).at[slot_flat].set(grad_slots)
    back_send = back_send.reshape(expert_count, capacity, model_dim)
    grad_expert_out = lax.all_to_all(back_send, "expert", split_axis=0, concat_axis=1, tiled=True)
    grad_act = jnp.einsum(
        "erd,efd->erf", grad_expert_out, w_down, preferred_element_type=jnp.float32
    )
    grad_w_down = jnp.einsum(
        "erf,erd->efd", activated, grad_expert_out, preferred_element_type=jnp.float32
    )
    grad_gate = grad_act * up_part * sigmoid_gate * (1.0 + gate_part * (1.0 - sigmoid_gate))
    grad_up = grad_act * silu_gate
    grad_hidden = jnp.concatenate([grad_gate, grad_up], axis=-1).astype(jnp.bfloat16)
    grad_w_gate_up = jnp.einsum(
        "erd,erf->edf", expert_rows, grad_hidden, preferred_element_type=jnp.float32
    )
    grad_rows = jnp.einsum(
        "erf,edf->erd", grad_hidden, w_gate_up, preferred_element_type=jnp.float32
    ).astype(jnp.bfloat16)
    grad_back = lax.all_to_all(
        grad_rows, "expert", split_axis=1, concat_axis=0, tiled=True
    ).reshape(slot_count, model_dim)
    grad_two = contract_rows(dispatch_table, grad_back)
    grad_chosen = gate_values * (
        grad_gates - jnp.sum(gate_values * grad_gates, axis=-1, keepdims=True)
    )
    grad_logits = jnp.sum(chooser * grad_chosen[:, :, None], axis=1).astype(jnp.bfloat16)
    grad_router = contract_rows(hidden_two, grad_logits)
    grad_two = grad_two + contract_cols(grad_logits, router_full)
    grad_gain_mlp = jnp.sum(grad_two * normed_mlp, axis=0)
    grad_resid = grad_out_rows + norm_back(grad_two * gain_mlp, normed_mlp, scale_mlp)
    grad_attn = grad_resid.astype(jnp.bfloat16)
    grad_w_out = contract_rows(attended, grad_attn)
    grad_attended = contract_cols(grad_attn, out_full).astype(jnp.bfloat16).reshape(head_shape)
    attn_again = jnp.exp(masked_scores(query_rot, key_rot, allowed, scaling) - log_total)
    attn_again_low = attn_again.astype(jnp.bfloat16)
    grad_value = jnp.einsum(
        "ghqk,gqhd->gkhd", attn_again_low, grad_attended, preferred_element_type=jnp.float32
    )
    grad_attn_weights = jnp.einsum(
        "gqhd,gkhd->ghqk", grad_attended, value_low, preferred_element_type=jnp.float32
    )
    row_delta = jnp.sum(grad_attn_weights * attn_again, axis=-1, keepdims=True)
    grad_scores = (attn_again * (grad_attn_weights - row_delta)).astype(jnp.bfloat16)
    grad_query_rot = (
        jnp.einsum("ghqk,gkhd->gqhd", grad_scores, key_rot, preferred_element_type=jnp.float32)
        * scaling
    )
    grad_key_rot = (
        jnp.einsum("ghqk,gqhd->gkhd", grad_scores, query_rot, preferred_element_type=jnp.float32)
        * scaling
    )
    grad_query_normed = rotary(grad_query_rot, -1.0).reshape(group_count * row_count, model_dim)
    grad_key_normed = rotary(grad_key_rot, -1.0).reshape(group_count * row_count, model_dim)
    grad_gain_query = jnp.sum(grad_query_normed * normed_query, axis=0)
    grad_gain_key = jnp.sum(grad_key_normed * normed_key, axis=0)
    weighted_query = grad_query_normed * gain_query
    weighted_key = grad_key_normed * gain_key
    dot_query = jnp.sum(weighted_query * normed_query, axis=-1, keepdims=True)
    dot_key = jnp.sum(weighted_key * normed_key, axis=-1, keepdims=True)
    grad_query = scale_query * (weighted_query - normed_query * (dot_query / model_dim))
    grad_key = scale_key * (weighted_key - normed_key * (dot_key / model_dim))
    grad_proj = jnp.concatenate(
        [grad_query, grad_key, grad_value.reshape(group_count * row_count, model_dim)], axis=-1
    ).astype(jnp.bfloat16)
    grad_w_qkv = contract_rows(hidden_one, grad_proj).reshape(model_dim, 3, model_dim)
    grad_one = contract_cols(grad_proj, qkv_full)
    grad_gain_attn = jnp.sum(grad_one * normed_attn, axis=0)
    grad_inputs = grad_resid + norm_back(grad_one * gain_attn, normed_attn, scale_attn)
    gain_pair = jnp.stack([grad_gain_query, grad_gain_key])
    head_qkv, head_out, head_gains = (
        lax.psum_scatter(
            grad_w_qkv.astype(jnp.bfloat16), "expert", scatter_dimension=2, tiled=True
        ).astype(jnp.float32),
        lax.psum_scatter(
            grad_w_out.astype(jnp.bfloat16), "expert", scatter_dimension=0, tiled=True
        ).astype(jnp.float32),
        lax.psum_scatter(
            gain_pair.astype(jnp.bfloat16), "expert", scatter_dimension=1, tiled=True
        ).astype(jnp.float32),
    )
    spread_gains = jnp.broadcast_to(head_gains[None], (dp_count,) + head_gains.shape)
    summed = (
        lax.psum_scatter(
            head_qkv.astype(jnp.bfloat16), "dp", scatter_dimension=0, tiled=True
        ).astype(jnp.float32),
        lax.psum_scatter(
            head_out.astype(jnp.bfloat16), "dp", scatter_dimension=1, tiled=True
        ).astype(jnp.float32),
        lax.psum_scatter(
            spread_gains.astype(jnp.bfloat16), "dp", scatter_dimension=0, tiled=True
        ).astype(jnp.float32),
        lax.psum_scatter(
            grad_w_gate_up.astype(jnp.bfloat16), "dp", scatter_dimension=1, tiled=True
        ).astype(jnp.float32),
        lax.psum_scatter(
            grad_w_down.astype(jnp.bfloat16), "dp", scatter_dimension=1, tiled=True
        ).astype(jnp.float32),
    )
    shared = (
        lax.psum_scatter(grad_router, ("dp", "expert"), scatter_dimension=0, tiled=True),
        lax.psum_scatter(grad_gain_attn, ("dp", "expert"), scatter_dimension=0, tiled=True),
        lax.psum_scatter(grad_gain_mlp, ("dp", "expert"), scatter_dimension=0, tiled=True),
    )
    return (
        output,
        grad_inputs,
        summed[0],
        summed[1],
        shared[0],
        shared[1],
        shared[2],
        summed[2][0, 0],
        summed[2][0, 1],
        summed[3],
        summed[4],
    )


def solution(mesh):
    placed = (
        P(("dp", "expert"), None),
        P(("dp", "expert"), None),
        P(("dp", "expert"), None),
        P(("dp", "expert"), None),
        P(("dp", "expert"), None),
        P(("dp", "expert"), None),
        P(("dp", "expert"), None),
        P(("dp", "expert")),
        P(("dp", "expert")),
        P(("dp", "expert")),
        P(("dp", "expert")),
        P("expert", None, None),
        P("expert", None, None),
    )
    return jax.shard_map(
        on_device,
        mesh=mesh,
        in_specs=placed,
        out_specs=(
            P(("dp", "expert"), None),
            P(("dp", "expert"), None),
            P("dp", None, "expert"),
            P("expert", "dp"),
            P(("dp", "expert"), None),
            P(("dp", "expert")),
            P(("dp", "expert")),
            P("expert"),
            P("expert"),
            P("expert", "dp", None),
            P("expert", "dp", None),
        ),
        check_vma=False,
    )
```

profile of v0, /device:TPU:16, one launch (start us, length us, event | category | flops | bytes accessed | tf_op | source)
XLA Modules:
  0.0 2160.5 jit_solution(9898101751853634901)
XLA Ops:
  12.1 41.8 %all-reduce.8 = (bf16[2048]{0:T(1024)(128)(2,1)S(1)}, bf16[2048]{0:T(1024)(128)(2,1)S(1)}, bf16[2048]{0:T(1024)(128)(2,1)S(1)}, bf16[2048]{0:T(1024)(128)(2,1)S(1)}) all-reduce(bf16[2048]{0:T(1024)(128)(2,1)S(1)} %dynamic-update-slice, bf16[2048]{0:T(1024)(128)(2,1)S(1)} %dynamic-update-slice.2, ...), channel_id=1, replica_groups=mesh['dp'=4,'expert'=8] {'dp','expert'}, use_global_device_ids=true, to_apply=%add | all-reduce | flops 8192 | bytes 32768
  53.9 37.2 %all-gather = bf16[32,64,24]{1,2,0:T(8,128)(2,1)S(1)} all-gather(bf16[1,64,24]{1,2,0:T(8,128)(2,1)} %bitcast.186), channel_id=1, replica_groups=mesh['dp'=4,'expert'=8] {'dp','expert'}, dimensions={0}, use_global_device_ids=true | all-gather | bytes 101376 | tf_op jit(solution)/shard_map/all_gather | solution.py:87
  93.8 74.6 %all-gather.4.cloned.1.call-done = bf16[2048,6144]{1,0:T(8,128)(2,1)} async-done(((bf16[64,6144]{1,0:T(8,128)(2,1)}), bf16[2048,6144]{1,0:T(8,128)(2,1)}) %all-gather.4.cloned.1.call-update) | async-done | bytes 25165840 | tf_op jit(solution)/shard_map/all_gather | solution.py:85
  189.3 58.2 %all-gather.6.cloned.1.call-done = bf16[2048,2048]{1,0:T(8,128)(2,1)} async-done(((bf16[64,2048]{1,0:T(8,128)(2,1)}), bf16[2048,2048]{1,0:T(8,128)(2,1)}) %all-gather.6.cloned.1.call-update) | async-done | bytes 8388624 | tf_op jit(solution)/shard_map/all_gather | solution.py:86
  254.7 19.1 fusion.2
  275.9 156.6 %all_to_all.66 = bf16[24,72,2048]{2,1,0:T(8,128)(2,1)S(1)} all-to-all(bf16[24,72,2048]{2,1,0:T(8,128)(2,1)S(1)} %bitcast.163), channel_id=1, replica_groups=mesh['dp'=4,'expert'=8] {'expert'}, dimensions={0} | all-to-all | bytes 14155776 | tf_op jit(solution)/shard_map/all_to_all | solution.py:153
  436.1 24.6 %fusion.85 = f32[3,576,2048]{2,1,0:T(8,128)} fusion(bf16[3,576,2048]{2,1,0:T(8,128)(2,1)} %bitcast.160, bf16[3,2048,2048]{2,1,0:T(8,128)(2,1)} %param.24), kind=kOutput, calls=%fused_computation.172 | convolution fusion | flops 14495514624 | bytes 46399488 | tf_op jit(solution)/shard_map/erd,edf->erf/dot_general | solution.py:154
  481.0 22.9 %copy.145 = bf16[3,576,2048]{2,0,1:T(4,128)(2,1)} copy(bf16[3,576,2048]{2,1,0:T(8,128)(2,1)S(1)} %convolution_convert_fusion.6) | data formatting | bytes 14155776 | tf_op jit(solution)/shard_map/convert_element_type | solution.py:163
  513.5 202.4 %all-to-all-done.1 = bf16[3,576,2048]{2,0,1:T(4,128)(2,1)} async-done(((bf16[3,576,2048]{2,0,1:T(4,128)(2,1)}), bf16[3,576,2048]{2,0,1:T(4,128)(2,1)}, u32[]{:S(2)}, u32[]{:S(2)}) %all-to-all-start.1) | async-done | bytes 7077920 | tf_op jit(solution)/shard_map/all_to_all | solution.py:164
  727.7 16.6 gather_fusion
  763.8 159.8 %all_to_all.67 = bf16[24,72,2048]{2,1,0:T(8,128)(2,1)S(1)} all-to-all(bf16[24,72,2048]{2,1,0:T(8,128)(2,1)} %bitcast.166), channel_id=1, replica_groups=mesh['dp'=4,'expert'=8] {'expert'}, dimensions={0} | all-to-all | bytes 14155776 | tf_op jit(solution)/shard_map/all_to_all | solution.py:183
  927.4 22.4 %multiply_convert_fusion.1 = (bf16[3,576,1024]{2,1,0:T(8,128)(2,1)}, bf16[3,576,1024]{2,1,0:T(8,128)(2,1)}) fusion(f32[3,576,2048]{2,1,0:T(8,128)} %fusion.85, bf16[3,576,2048]{2,1,0:T(8,128)(2,1)} %bitcast.176, bf16[3,1024,2048]{2,1,0:T(8,128)(2,1)} %param.25), kind=kOutput, calls=%fused_computation.15 | convolution fusion | flops 7270760448 | bytes 40894464 | tf_op jit(solution)/shard_map/erd,efd->erf/dot_general | solution.py:184
  949.7 21.6 convolution_convert_fusion.5
  1000.2 194.1 %all-to-all-done.3 = bf16[3,576,2048]{2,0,1:T(4,128)(2,1)} async-done(((bf16[3,576,2048]{2,0,1:T(4,128)(2,1)}), bf16[3,576,2048]{2,0,1:T(4,128)(2,1)}, u32[]{:S(2)}, u32[]{:S(2)}) %all-to-all-start.3) | async-done | bytes 7077920 | tf_op jit(solution)/shard_map/all_to_all | solution.py:199
  1256.3 32.7 %copy.163 = bf16[2048,6144]{0,1:T(8,128)(2,1)} copy(bf16[2048,6144]{1,0:T(8,128)(2,1)} %convolution_convert_fusion) | data formatting | bytes 50331648 | tf_op jit(solution)/shard_map/convert_element_type | solution.py:252
  1292.9 16.5 convolution_convert_fusion.4
  1310.5 26.6 %convolution_convert_fusion.1 = bf16[3,2048,2048]{2,1,0:T(8,128)(2,1)} fusion(bf16[3,576,2048]{2,1,0:T(8,128)(2,1)} %bitcast.161, bf16[3,576,1024]{2,1,0:T(8,128)(2,1)} %get-tuple-element.80, bf16[3,576,1024]{2,1,0:T(8,128)(2,1)} %get-tuple-element.79), kind=kOutput, calls=%fused_computation.5 | convolution fusion | flops 14522253312 | bytes 39321600 | tf_op jit(solution)/shard_map/erd,erf->edf/dot_general | solution.py:193
  1337.2 218.9 %reduce-scatter.13.cloned.1.call-done = bf16[2048,3,256]{0,2,1:T(8,128)(2,1)} async-done(((bf16[2048,3,2048]{0,2,1:T(8,128)(2,1)}), bf16[2048,3,256]{0,2,1:T(8,128)(2,1)}) %reduce-scatter.13.cloned.1.call-update) | async-done | bytes 3145744 | tf_op jit(solution)/shard_map/reduce_scatter | solution.py:251
  1556.7 127.1 %reduce-scatter.25.cloned.1.call-done = f32[64,24]{1,0:T(8,128)} async-done(((f32[2048,24]{1,0:T(8,128)}), f32[64,24]{1,0:T(8,128)}) %reduce-scatter.25.cloned.1.call-update) | async-done | bytes 6160
  1700.0 48.6 %all-reduce.7 = (f32[2048]{0:T(1024)S(1)}, f32[2048]{0:T(1024)S(1)}) all-reduce(f32[2048]{0:T(1024)S(1)} %get-tuple-element.65, f32[2048]{0:T(1024)S(1)} %get-tuple-element.63), channel_id=7, replica_groups=mesh['dp'=4,'expert'=8] {'dp','expert'}, use_global_device_ids=true, to_apply=%region_28.29.clone | all-reduce | flops 4096 | bytes 32768
  1765.0 82.9 %reduce-scatter.23.cloned.1.call-done = bf16[3,256,2048]{2,1,0:T(8,128)(2,1)} async-done(((bf16[3,1024,2048]{2,1,0:T(8,128)(2,1)}), bf16[3,256,2048]{2,1,0:T(8,128)(2,1)}) %reduce-scatter.23.cloned.1.call-update) | async-done | bytes 3145744 | tf_op jit(solution)/shard_map/reduce_scatter | solution.py:275
  1853.4 25.2 %reduce-scatter.19.cloned.1.call-done = bf16[256,512]{1,0:T(8,128)(2,1)} async-done(((bf16[256,2048]{1,0:T(8,128)(2,1)}), bf16[256,512]{1,0:T(8,128)(2,1)}) %reduce-scatter.19.cloned.1.call-update) | async-done | bytes 262160 | tf_op jit(solution)/shard_map/reduce_scatter | solution.py:266
  1880.4 223.5 %reduce-scatter.21.cloned.1.call-done = bf16[3,512,2048]{2,1,0:T(8,128)(2,1)} async-done(((bf16[3,2048,2048]{2,1,0:T(8,128)(2,1)}), bf16[3,512,2048]{2,1,0:T(8,128)(2,1)}) %reduce-scatter.21.cloned.1.call-update) | async-done | bytes 6291472 | tf_op jit(solution)/shard_map/reduce_scatter | solution.py:272
  2113.0 37.7 %reduce-scatter.15.cloned.1.call-done = bf16[512,3,256]{0,2,1:T(8,128)(2,1)} async-done(((bf16[2048,3,256]{0,2,1:T(8,128)(2,1)}), bf16[512,3,256]{0,2,1:T(8,128)(2,1)}) %reduce-scatter.15.cloned.1.call-update) | async-done | bytes 786448 | tf_op jit(solution)/shard_map/reduce_scatter | solution.py:263
  (250 shorter events, 253.3 us)
Async XLA Ops:
  7.2 85.0 %copy-start.7 = (bf16[192,2048]{1,0:T(8,128)(2,1)S(1)}, bf16[192,2048]{1,0:T(8,128)(2,1)}, u32[]{:S(2)}) copy-start(bf16[192,2048]{1,0:T(8,128)(2,1)} %param.13) | copy-start | bytes 2359300
  7.2 85.4 %copy-start.52 = (s32[1,192]{1,0:T(1,128)S(1)}, s32[1,192]{1,0:T(1,128)}, u32[]{:S(2)}) copy-start(s32[1,192]{1,0:T(1,128)} %param.15) | copy-start | bytes 2308
  7.2 161.2 %all-gather.4.cloned.1.call-start = ((), (), s32[]{:S(2)}) async-start(), calls=%async_computation.12 | async-start | bytes 25952256 | tf_op jit(solution)/shard_map/all_gather | solution.py:85
  7.9 239.5 %all-gather.6.cloned.1.call-start = ((), (), s32[]{:S(2)}) async-start(), calls=%async_computation.13 | async-start | bytes 8650752 | tf_op jit(solution)/shard_map/all_gather | solution.py:86
  53.9 125.7 %copy-start.30 = (f32[2048]{0:T(1024)}, f32[2048]{0:T(1024)S(1)}, u32[]{:S(2)}) copy-start(f32[2048]{0:T(1024)S(1)} %convert_element_type.154) | copy-start | bytes 24580
  53.9 126.1 %copy-start.34 = (f32[2048]{0:T(1024)}, f32[2048]{0:T(1024)S(1)}, u32[]{:S(2)}) copy-start(f32[2048]{0:T(1024)S(1)} %convert_element_type.158) | copy-start | bytes 24580
  53.9 126.1 %copy-start.36 = (f32[2048]{0:T(1024)}, f32[2048]{0:T(1024)S(1)}, u32[]{:S(2)}) copy-start(f32[2048]{0:T(1024)S(1)} %convert_element_type.157) | copy-start | bytes 24580
  53.9 198.9 %copy-start.38 = (f32[2048]{0:T(1024)}, f32[2048]{0:T(1024)S(1)}, u32[]{:S(2)}) copy-start(f32[2048]{0:T(1024)S(1)} %convert_element_type.164) | copy-start | bytes 24580
  91.4 162.7 %copy-start.27 = (bf16[2048,24]{0,1:T(8,128)(2,1)}, bf16[2048,24]{0,1:T(8,128)(2,1)S(1)}, u32[]{:S(2)}) copy-start(bf16[2048,24]{0,1:T(8,128)(2,1)S(1)} %reshape.545) | copy-start | bytes 294916
  92.5 87.2 %copy-start.44 = (f32[192]{0:T(256)}, f32[192]{0:T(256)S(1)}, u32[]{:S(2)}) copy-start(f32[192]{0:T(256)S(1)} %add_rsqrt_fusion.3) | copy-start | bytes 2308
  93.8 88.5 %copy-start.25 = (f32[192,64]{1,0:T(8,128)}, f32[192,64]{1,0:T(8,128)S(1)}, u32[]{:S(2)}) copy-start(f32[192,64]{1,0:T(8,128)S(1)} %get-tuple-element.107) | copy-start | bytes 147460
  189.3 63.5 %copy-start.19 = (bf16[1,192,16,128]{3,2,1,0:T(8,128)(2,1)}, bf16[1,192,16,128]{3,2,1,0:T(8,128)(2,1)S(1)}, u32[]{:S(2)}) copy-start(bf16[1,192,16,128]{3,2,1,0:T(8,128)(2,1)S(1)} %copy.139) | copy-start | bytes 2359300
  503.9 211.9 %all-to-all-start.1 = ((bf16[3,576,2048]{2,0,1:T(4,128)(2,1)}), bf16[3,576,2048]{2,0,1:T(4,128)(2,1)}, u32[]{:S(2)}, u32[]{:S(2)}) async-start(bf16[3,576,2048]{2,0,1:T(4,128)(2,1)} %copy.145), calls=%async_computation.1 | async-start | bytes 18874368 | tf_op jit(solution)/shard_map/all_to_all | solution.py:164
  982.8 211.5 %all-to-all-start.3 = ((bf16[3,576,2048]{2,0,1:T(4,128)(2,1)}), bf16[3,576,2048]{2,0,1:T(4,128)(2,1)}, u32[]{:S(2)}, u32[]{:S(2)}) async-start(bf16[3,576,2048]{2,0,1:T(4,128)(2,1)} %copy.150), calls=%async_computation.3 | async-start | bytes 18874368 | tf_op jit(solution)/shard_map/all_to_all | solution.py:199
  991.3 318.3 %reduce-scatter.17.cloned.1.call-start = ((), (), s32[]{:S(2)}) async-start(), calls=%async_computation.16 | async-start | bytes 9437184 | tf_op jit(solution)/shard_map/reduce_scatter | solution.py:254
  1220.3 335.8 %reduce-scatter.13.cloned.1.call-start = ((), (), s32[]{:S(2)}) async-start(), calls=%async_computation.14 | async-start | bytes 28311552 | tf_op jit(solution)/shard_map/reduce_scatter | solution.py:251
  1289.0 394.8 %reduce-scatter.25.cloned.1.call-start = ((), (), s32[]{:S(2)}) async-start(), calls=%async_computation.20 | async-start | bytes 1081344
  1291.7 461.3 %reduce-scatter.27.cloned.1.call-start = ((), (), s32[]{:S(2)}) async-start(), calls=%async_computation.21 | async-start | bytes 589824
  1292.8 555.1 %reduce-scatter.23.cloned.1.call-start = ((), (), s32[]{:S(2)}) async-start(), calls=%async_computation.19 | async-start | bytes 15728640 | tf_op jit(solution)/shard_map/reduce_scatter | solution.py:275
  1309.5 569.1 %reduce-scatter.19.cloned.1.call-start = ((), (), s32[]{:S(2)}) async-start(), calls=%async_computation.17 | async-start | bytes 1310720 | tf_op jit(solution)/shard_map/reduce_scatter | solution.py:266
  1310.2 793.7 %reduce-scatter.21.cloned.1.call-start = ((), (), s32[]{:S(2)}) async-start(), calls=%async_computation.18 | async-start | bytes 31457280 | tf_op jit(solution)/shard_map/reduce_scatter | solution.py:272
  1337.2 219.0 %copy-start.53 = (u32[32]{0:T(128)S(1)}, u32[32]{0:T(128)}, u32[]{:S(2)}) copy-start(u32[32]{0:T(128)} %constant.82) | copy-start | bytes 388
  1337.2 348.1 %copy-start.9 = (bf16[192,2048]{1,0:T(8,128)(2,1)S(1)}, bf16[192,2048]{1,0:T(8,128)(2,1)}, u32[]{:S(2)}) copy-start(bf16[192,2048]{1,0:T(8,128)(2,1)} %param.13) | copy-start | bytes 2359300
  1337.2 813.5 %reduce-scatter.15.cloned.1.call-start = ((), (), s32[]{:S(2)}) async-start(), calls=%async_computation.15 | async-start | bytes 3932160 | tf_op jit(solution)/shard_map/reduce_scatter | solution.py:263
  (44 other events, 148.5 us)
Sparse Core Ops, SparseCore 0:
  11.0 157.3 all-gather.3
  171.4 75.9 all-gather.5
  1220.5 87.8 reduce-scatter.16
  1310.6 245.5 reduce-scatter.12
  1558.8 124.9 reduce-scatter.24
  1686.6 31.7 reduce-scatter.26
  1722.1 125.8 reduce-scatter.22
  1850.8 27.6 reduce-scatter.18
  1882.0 221.8 reduce-scatter.20
  2106.7 43.9 reduce-scatter.14
where the time goes:
time: 2170 us; the launch traced here: 2160 us
  waiting for transfers between devices  1250 us (58%)
  blocking collectives  454 us (21%)
  matrix products  198 us (9%)
  local copies, waits for them, and re-layouts  140 us (6%)
  other arithmetic  88 us (4%)
    reduce_scatter x1, waiting for transfers between devices, on_device(): lax.psum_scatter(grad_w_gate_up.astype(jnp.bfloat16), 'dp', scatter_dimen...  224 us
    reduce_scatter x1, waiting for transfers between devices, on_device(): lax.psum_scatter(grad_w_qkv.astype(jnp.bfloat16), 'expert', scatter_dimen...  219 us
    all_to_all x1, waiting for transfers between devices, on_device(): lax.all_to_all(expert_out, 'expert', split_axis=1, concat_axis=0, tiled=T...  202 us
    all_to_all x1, waiting for transfers between devices, on_device(): lax.all_to_all(grad_rows, 'expert', split_axis=1, concat_axis=0, tiled=True)  194 us
    all_to_all x1, blocking collectives, on_device(): lax.all_to_all(back_send, 'expert', split_axis=0, concat_axis=1, tiled=True)  160 us
    all_to_all x1, blocking collectives, on_device(): lax.all_to_all(send_rows, 'expert', split_axis=0, concat_axis=1, tiled=True)  157 us
    unnamed x12, waiting for transfers between devices  129 us
    unnamed x3, blocking collectives  100 us
  transfers between devices with their start and end apart: 12, of which 10 were waited for; matrix products, arithmetic and copies ran while one was open for 9% of the time, Pallas kernels for 0%

commit v1 on v0

v1 whole, which is shorter than its diff:
```python
import functools
import math

import jax
import jax.numpy as jnp
from jax import lax
from jax.experimental import pallas as pl
from jax.experimental.pallas import tpu as pltpu
from jax.sharding import PartitionSpec as P

HEADS = 16
NORM_EPS = 1e-05
MESH = pl.DeviceIdType.MESH
ANY = pl.BlockSpec(memory_space=pl.ANY)
LOW = jnp.bfloat16
FULL = jnp.float32


def line_place():
    place = lax.axis_index("expert")
    level, side = lax.div(place, 2), lax.rem(place, 2)
    return place, level, side, place + 1 - 2 * side


def line_barrier(place, other, has_up, has_down):
    barrier = pltpu.get_barrier_semaphore()
    pl.semaphore_signal(barrier, inc=1, device_id={"expert": other}, device_id_type=MESH)

    @pl.when(has_up)
    def _():
        pl.semaphore_signal(barrier, inc=1, device_id={"expert": place + 2}, device_id_type=MESH)

    @pl.when(has_down)
    def _():
        pl.semaphore_signal(barrier, inc=1, device_id={"expert": place - 2}, device_id_type=MESH)

    pl.semaphore_wait(barrier, 1 + has_up.astype(jnp.int32) + has_down.astype(jnp.int32))


def line_gather_kernel(levels, cuts, *refs):
    count = len(cuts)
    ins, outs = refs[:count], refs[count : 2 * count]
    up_sem, down_sem, side_sem, recv_sem, own_sem = refs[2 * count :]
    pieces = [(i, k) for i in range(count) for k in range(cuts[i])]
    place, level, side, other = line_place()
    has_up, has_down = level < levels - 1, level > 0

    def part(ref, i, k):
        rows = ins[i].shape[0] // cuts[i]
        return ref.at[pl.ds(k * rows, rows)]

    def sending(q, block, own, sem, target):
        i, k = pieces[q]
        landing = part(outs[i].at[block], i, k)
        return pltpu.make_async_remote_copy(
            src_ref=part(ins[i], i, k) if own else landing,
            dst_ref=landing,
            send_sem=sem,
            recv_sem=recv_sem.at[block, q],
            device_id={"expert": target},
            device_id_type=MESH,
        )

    def up(q, step):
        return sending(q, place - 2 * step, step == 0, up_sem.at[step, q], place + 2)

    def down(q, step):
        return sending(q, place + 2 * step, step == 0, down_sem.at[step, q], place - 2)

    def across(q, step):
        return sending(q, place - 2 * step, step == 0, side_sem.at[step + levels - 1, q], other)

    own_copies = [
        pltpu.make_async_copy(ins[i], outs[i].at[place], own_sem.at[i]) for i in range(count)
    ]
    line_barrier(place, other, has_up, has_down)
    for q in range(len(pieces)):
        pl.when(has_up)(up(q, 0).start)
        pl.when(has_down)(down(q, 0).start)
    for q in range(len(pieces)):
        across(q, 0).start()
    for copy in own_copies:
        copy.start()
    for step in range(1, levels):
        for q in range(len(pieces)):

            @pl.when(level >= step)
            def _():
                across(q, step).wait_recv()
                pl.when(has_up)(up(q, step).start)
                across(q, step).start()

            @pl.when(level + step < levels)
            def _():
                across(q, -step).wait_recv()
                pl.when(has_down)(down(q, step).start)
                across(q, -step).start()

    for q in range(len(pieces)):
        for far in range(levels):
            sending(q, 2 * far + 1 - side, False, side_sem.at[0, q], other).wait_recv()
        across(q, 0).wait_send()
        for step in range(levels):
            pl.when(has_up & (level >= step))(up(q, step).wait_send)
            pl.when(has_down & (level + step < levels))(down(q, step).wait_send)
            if step:
                pl.when(level >= step)(across(q, step).wait_send)
                pl.when(level + step < levels)(across(q, -step).wait_send)
    for copy in own_copies:
        copy.wait()


def line_gather(size, arrays, cuts, number):
    levels, total = size // 2, sum(cuts)
    sems = pltpu.SemaphoreType.DMA
    return pl.pallas_call(
        functools.partial(line_gather_kernel, levels, tuple(cuts)),
        out_shape=[jax.ShapeDtypeStruct((size,) + a.shape, a.dtype) for a in arrays],
        in_specs=[ANY] * len(arrays),
        out_specs=[ANY] * len(arrays),
        scratch_shapes=[
            sems((levels, total)),
            sems((levels, total)),
            sems((2 * levels - 1, total)),
            sems((size, total)),
            sems((len(arrays),)),
        ],
        compiler_params=pltpu.CompilerParams(collective_id=number, has_side_effects=True),
        cost_estimate=pl.CostEstimate(flops=0, transcendentals=0, bytes_accessed=150_000_000),
        name="line_gather",
    )(*arrays)


def line_reduce_kernel(levels, cuts, part_ref, sum_ref, own, beside, rising, falling, *sems):
    load_sem, side_send, side_recv, up_send, up_recv, down_send, down_recv, out_sem = sems
    place, level, side, other = line_place()
    has_up, has_down = level < levels - 1, level > 0
    rows = part_ref.shape[1] // cuts

    def cut(ref, block, k):
        return ref.at[block, pl.ds(k * rows, rows)]

    def moving(source, target_ref, block, k, send, recv, target):
        return pltpu.make_async_remote_copy(
            src_ref=source,
            dst_ref=cut(target_ref, block, k),
            send_sem=send.at[block, k],
            recv_sem=recv.at[block, k],
            device_id={"expert": target},
            device_id_type=MESH,
        )

    def loading(far, k):
        return pltpu.make_async_copy(
            cut(part_ref, 2 * far + side, k), cut(own, far, k), load_sem.at[far, k]
        )

    def across(far, k):
        source = cut(part_ref, 2 * far + 1 - side, k)
        return moving(source, beside, far, k, side_send, side_recv, other)

    def up(far, k):
        return moving(cut(own, far, k), rising, far, k, up_send, up_recv, place + 2)

    def down(far, k):
        return moving(cut(own, far, k), falling, far, k, down_send, down_recv, place - 2)

    def value(ref, block, k):
        return cut(ref, block, k)[...].astype(jnp.float32)

    order = []
    for step in range(levels):
        for far in (levels - 1 - step, step):
            if far not in order:
                order.append(far)
    for far in order:
        for k in range(cuts):
            loading(far, k).start()
    line_barrier(place, other, has_up, has_down)
    for far in order:
        for k in range(cuts):
            across(far, k).start()

    def pair(far, k):
        loading(far, k).wait()
        across(far, k).wait_recv()
        return value(own, far, k) + value(beside, far, k)

    for step in range(levels - 1):
        for k in range(cuts):
            high, low = levels - 1 - step, step

            @pl.when((level < high) & has_down)
            def _():
                both = pair(high, k)
                up(high, k).wait_recv()
                cut(own, high, k)[...] = (both + value(rising, high, k)).astype(own.dtype)

            @pl.when((level < high) & jnp.logical_not(has_down))
            def _():
                cut(own, high, k)[...] = pair(high, k).astype(own.dtype)

            pl.when(level < high)(up(high, k).start)

            @pl.when((level > low) & has_up)
            def _():
                both = pair(low, k)
                down(low, k).wait_recv()
                cut(own, low, k)[...] = (both + value(falling, low, k)).astype(own.dtype)

            @pl.when((level > low) & jnp.logical_not(has_up))
            def _():
                cut(own, low, k)[...] = pair(low, k).astype(own.dtype)

            pl.when(level > low)(down(low, k).start)

    for k in range(cuts):
        cut(own, level, k)[...] = pair(level, k).astype(own.dtype)

        @pl.when(has_down)
        def _():
            up(level, k).wait_recv()
            total = value(own, level, k) + value(rising, level, k)
            cut(own, level, k)[...] = total.astype(own.dtype)

        @pl.when(has_up)
        def _():
            down(level, k).wait_recv()
            total = value(own, level, k) + value(falling, level, k)
            cut(own, level, k)[...] = total.astype(own.dtype)

        pltpu.make_async_copy(
            cut(own, level, k), sum_ref.at[pl.ds(k * rows, rows)], out_sem.at[k]
        ).start()
    for k in range(cuts):
        pltpu.make_async_copy(
            cut(own, level, k), sum_ref.at[pl.ds(k * rows, rows)], out_sem.at[k]
        ).wait()
        for far in range(levels):
            across(far, k).wait_send()
            pl.when(level < far)(up(far, k).wait_send)
            pl.when(level > far)(down(far, k).wait_send)


def line_reduce(size, parts, cuts, number):
    levels = size // 2
    block = parts.shape[1:]
    sems = pltpu.SemaphoreType.DMA((levels, cuts))
    return pl.pallas_call(
        functools.partial(line_reduce_kernel, levels, cuts),
        out_shape=jax.ShapeDtypeStruct(block, parts.dtype),
        in_specs=[ANY],
        out_specs=ANY,
        scratch_shapes=[pltpu.VMEM((levels,) + block, parts.dtype)] * 4
        + [sems] * 7
        + [pltpu.SemaphoreType.DMA((cuts,))],
        compiler_params=pltpu.CompilerParams(
            collective_id=number, has_side_effects=True, vmem_limit_bytes=40 << 20
        ),
        cost_estimate=pl.CostEstimate(flops=0, transcendentals=0, bytes_accessed=150_000_000),
        name="line_reduce",
    )(parts)


def exchange_kernel(axis, size, spread, *refs):
    count = len(spread)
    ins, outs = refs[:count], refs[count : 2 * count]
    send_sem, recv_sem, own_sem = refs[2 * count :]
    place = lax.axis_index(axis)
    barrier = pltpu.get_barrier_semaphore()
    peers = [lax.rem(place + shift, size) for shift in range(1, size)]
    for peer in peers:
        pl.semaphore_signal(barrier, inc=1, device_id={axis: peer}, device_id_type=MESH)
    pl.semaphore_wait(barrier, size - 1)

    def source(i, block):
        return ins[i] if spread[i] else ins[i].at[block]

    def sending(i, shift, peer, landing):
        return pltpu.make_async_remote_copy(
            src_ref=source(i, peer),
            dst_ref=outs[i].at[landing],
            send_sem=send_sem.at[i, shift],
            recv_sem=recv_sem.at[i, landing],
            device_id={axis: peer},
            device_id_type=MESH,
        )

    own = [
        pltpu.make_async_copy(source(i, place), outs[i].at[place], own_sem.at[i])
        for i in range(count)
    ]
    for shift, peer in enumerate(peers):
        for i in range(count):
            sending(i, shift, peer, place).start()
    for copy in own:
        copy.start()
    for shift, peer in enumerate(peers):
        for i in range(count):
            sending(i, shift, peer, peer).wait_recv()
            sending(i, shift, peer, place).wait_send()
    for copy in own:
        copy.wait()


def exchange(axis, size, arrays, spread, number):
    sems = pltpu.SemaphoreType.DMA
    outs = [
        jax.ShapeDtypeStruct((size,) + a.shape if flat else a.shape, a.dtype)
        for a, flat in zip(arrays, spread)
    ]
    return pl.pallas_call(
        functools.partial(exchange_kernel, axis, size, tuple(spread)),
        out_shape=outs,
        in_specs=[ANY] * len(arrays),
        out_specs=[ANY] * len(arrays),
        scratch_shapes=[
            sems((len(arrays), size)),
            sems((len(arrays), size)),
            sems((len(arrays),)),
        ],
        compiler_params=pltpu.CompilerParams(collective_id=number, has_side_effects=True),
        cost_estimate=pl.CostEstimate(flops=0, transcendentals=0, bytes_accessed=30_000_000),
        name="exchange_" + axis,
    )(*arrays)


def rms_scale(values):
    return lax.rsqrt(jnp.mean(values * values, axis=-1, keepdims=True) + NORM_EPS)


def rotary(values, direction):
    length = values.shape[-3]
    half_size = values.shape[-1] // 2
    index_half = jnp.arange(half_size, dtype=FULL)
    frequency = jnp.exp(index_half * (-2.0 * math.log(10000.0) / values.shape[-1]))
    angles = jnp.arange(length, dtype=FULL)[:, None] * frequency[None, :]
    cosine = jnp.cos(angles)[:, None, :]
    sine_table = direction * jnp.sin(angles)[:, None, :]
    first_half = values[..., :half_size]
    second = values[..., half_size:]
    return jnp.concatenate(
        [first_half * cosine - second * sine_table, second * cosine + first_half * sine_table],
        axis=-1,
    )


def norm_back(grad_normed, normed, scale_rows):
    return scale_rows * (
        grad_normed - normed * jnp.mean(grad_normed * normed, axis=-1, keepdims=True)
    )


def contract_rows(left_side, right_side):
    return lax.dot_general(
        left_side, right_side, (((0,), (0,)), ((), ())), preferred_element_type=FULL
    )


def contract_cols(left_side, right_side):
    return lax.dot_general(
        left_side, right_side, (((1,), (1,)), ((), ())), preferred_element_type=FULL
    )


def einsum(spec, left_side, right_side):
    return jnp.einsum(spec, left_side, right_side, preferred_element_type=FULL)


def on_device(
    dp_count,
    line_count,
    layer_input,
    out_cotangent,
    segments,
    routes,
    w_qkv,
    w_out,
    w_router,
    attn_gain,
    mlp_gain,
    query_gain,
    key_gain,
    w_gate_up,
    w_down,
):
    row_count, model_dim = layer_input.shape
    top_count = routes.shape[1]
    expert_count = w_router.shape[1]
    local_count = w_gate_up.shape[0]
    head_size = model_dim // HEADS
    head_cols = model_dim // line_count
    heads_here = head_cols // head_size
    capacity = (row_count * top_count * 9 // 8 + expert_count - 1) // expert_count
    scaling = 1.0 / math.sqrt(head_size)
    place = lax.axis_index("expert")
    all_rows = line_count * row_count
    shard = w_qkv.shape[0]

    out_full = lax.all_gather(w_out, ("dp", "expert"), axis=0, tiled=True)
    small = jnp.concatenate(
        [w_router] + [g[:, None] for g in (attn_gain, mlp_gain, query_gain, key_gain)], axis=1
    )
    small = jnp.pad(small, ((0, 0), (0, 128 - small.shape[1])))
    columns = w_qkv.reshape(shard, 3, line_count, head_cols).transpose(2, 0, 1, 3)
    columns = columns.reshape(line_count, shard, 3 * head_cols)
    packed = jnp.concatenate(
        [columns, jnp.broadcast_to(small[None], (line_count,) + small.shape)], axis=2
    )
    (packed,) = exchange("expert", line_count, [packed], [False], 1)
    packed = packed.reshape(line_count * shard, packed.shape[2])
    (packed,) = exchange("dp", dp_count, [packed], [True], 2)
    packed = packed.reshape(model_dim, packed.shape[2])
    qkv_here = packed[:, : 3 * head_cols]
    router_full = packed[:, 3 * head_cols : 3 * head_cols + expert_count]
    gains = packed[:, 3 * head_cols + expert_count : 3 * head_cols + expert_count + 4].astype(FULL)
    gain_attn, gain_mlp = gains[:, 0], gains[:, 1]
    own_gains = lax.dynamic_slice_in_dim(gains, place * head_cols, head_cols, axis=0)
    gain_query, gain_key = own_gains[:, 2], own_gains[:, 3]

    numbers = jnp.concatenate([routes.T, segments, jnp.zeros((7, row_count), jnp.int32)], axis=0)
    x_all, numbers_all = line_gather(line_count, [layer_input, numbers], [4, 1], 3)
    routes_all = numbers_all[:, :top_count]
    segments_all = numbers_all[:, top_count]
    (x_all,) = (x_all.reshape(all_rows, model_dim),)
    inputs_all = x_all.astype(FULL)
    hidden_one = (inputs_all * rms_scale(inputs_all) * gain_attn).astype(LOW)
    projected = jnp.dot(hidden_one, qkv_here, preferred_element_type=FULL)
    query_rows = projected[:, :head_cols]
    key_rows = projected[:, head_cols : 2 * head_cols]
    value_rows = projected[:, 2 * head_cols :]
    squares = jnp.stack(
        [jnp.sum(query_rows * query_rows, axis=-1), jnp.sum(key_rows * key_rows, axis=-1)]
    ).reshape(2 * line_count, row_count)
    (squares,) = exchange("expert", line_count, [squares], [True], 4)
    squares = jnp.sum(squares, axis=0).reshape(2, all_rows, 1)
    scale_query = lax.rsqrt(squares[0] / model_dim + NORM_EPS)
    scale_key = lax.rsqrt(squares[1] / model_dim + NORM_EPS)
    normed_query = query_rows * scale_query
    normed_key = key_rows * scale_key
    head_shape = (line_count, row_count, heads_here, head_size)
    query_rot = rotary((normed_query * gain_query).reshape(head_shape), 1.0).astype(LOW)
    key_rot = rotary((normed_key * gain_key).reshape(head_shape), 1.0).astype(LOW)
    value_low = value_rows.reshape(head_shape).astype(LOW)
    position = jnp.arange(row_count)
    allowed = (position[:, None] >= position[None, :])[None] & (
        segments_all[:, :, None] == segments_all[:, None, :]
    )
    scores = einsum("gqhd,gkhd->ghqk", query_rot, key_rot) * scaling
    scores = jnp.where(allowed[:, None], scores, -1e30)
    expanded = jnp.exp(scores - jnp.max(scores, axis=-1, keepdims=True))
    attn = expanded / jnp.sum(expanded, axis=-1, keepdims=True)
    attn_low = attn.astype(LOW)
    attended = einsum("ghqk,gkhd->gqhd", attn_low, value_low).astype(LOW)
    attended = attended.reshape(line_count, row_count, head_cols)
    (own_attended,) = exchange("expert", line_count, [attended], [False], 5)
    own_attended = own_attended.transpose(1, 0, 2).reshape(row_count, model_dim)
    inputs = layer_input.astype(FULL)
    scale_attn = rms_scale(inputs)
    normed_attn = inputs * scale_attn
    residual = inputs + jnp.dot(own_attended, out_full, preferred_element_type=FULL)
    scale_mlp = rms_scale(residual)
    normed_mlp = residual * scale_mlp
    hidden_two = (normed_mlp * gain_mlp).astype(LOW)

    logits = jnp.dot(hidden_two, router_full, preferred_element_type=FULL)
    chosen = jnp.any(routes[:, :, None] == jnp.arange(expert_count)[None, None, :], axis=1)
    masked = jnp.where(chosen, logits, -1e30)
    powers = jnp.where(chosen, jnp.exp(masked - jnp.max(masked, axis=-1, keepdims=True)), 0.0)
    gates = powers / jnp.sum(powers, axis=-1, keepdims=True)

    h_all, gates_all = line_gather(line_count, [hidden_two, gates.T], [4, 1], 6)
    (dy_all,) = line_gather(line_count, [out_cotangent], [4], 7)
    local = place * local_count + jnp.arange(local_count)
    used = jnp.any(routes_all[:, None] == local[None, :, None, None], axis=2)
    lower = (position[:, None] < position[None, :]).astype(LOW)
    rank = einsum("gju,ut->gjt", used.astype(LOW), lower).astype(jnp.int32)
    rank = jnp.where(used, rank, -1)
    table = (rank[:, :, None, :] == jnp.arange(capacity)[None, None, :, None]).astype(LOW)
    local_gates = lax.dynamic_slice_in_dim(gates_all, place * local_count, local_count, axis=1)
    slot_gates = jnp.sum(table.astype(FULL) * local_gates[:, :, None, :], axis=-1)
    slots = line_count * capacity
    slot_gates = slot_gates.transpose(1, 0, 2).reshape(local_count, slots, 1)

    def place_rows(rows):
        return jnp.stack(
            [
                einsum("gst,gtd->gsd", table[:, j], rows).astype(LOW).reshape(slots, model_dim)
                for j in range(local_count)
            ]
        )

    def collect(rows, weights):
        return sum(
            einsum(
                "gst,gsd->gtd", weights[:, j], rows[j].reshape(line_count, capacity, model_dim)
            )
            for j in range(local_count)
        ).astype(LOW)

    expert_rows = place_rows(h_all)
    dy_rows = place_rows(dy_all).astype(FULL)
    hidden = einsum("erd,edf->erf", expert_rows, w_gate_up)
    hidden_size = hidden.shape[2] // 2
    gate_part = hidden[..., :hidden_size]
    up_part = hidden[..., hidden_size:]
    sigmoid_gate = jax.nn.sigmoid(gate_part)
    silu_gate = gate_part * sigmoid_gate
    activated = (silu_gate * up_part).astype(LOW)
    expert_out = einsum("erf,efd->erd", activated, w_down).astype(LOW)
    grad_expert_out = (slot_gates * dy_rows).astype(LOW)
    grad_w_down = einsum("erf,erd->efd", activated, grad_expert_out).astype(LOW)
    sum_down = lax.psum_scatter(grad_w_down, "dp", scatter_dimension=1, tiled=True)
    grad_act = einsum("erd,efd->erf", grad_expert_out, w_down)
    grad_gate = grad_act * up_part * sigmoid_gate * (1.0 + gate_part * (1.0 - sigmoid_gate))
    grad_hidden = jnp.concatenate([grad_gate, grad_act * silu_gate], axis=-1).astype(LOW)
    grad_w_gate_up = einsum("erd,erf->edf", expert_rows, grad_hidden).astype(LOW)
    sum_gate_up = lax.psum_scatter(grad_w_gate_up, "dp", scatter_dimension=1, tiled=True)
    grad_rows = einsum("erf,edf->erd", grad_hidden, w_gate_up).astype(LOW)
    slot_grads = jnp.sum(expert_out.astype(FULL) * dy_rows, axis=-1)
    slot_grads = slot_grads.reshape(local_count, line_count, capacity)
    grad_gates = jnp.sum(
        table.astype(FULL) * slot_grads.transpose(1, 0, 2)[:, :, :, None], axis=2
    )
    (grad_gates,) = exchange("expert", line_count, [grad_gates], [False], 8)
    grad_gates = grad_gates.reshape(expert_count, row_count).T
    grad_two = line_reduce(line_count, collect(grad_rows, table), 4, 9).astype(FULL)
    weighted_table = table * local_gates[:, :, None, :].astype(LOW)
    mixture = line_reduce(line_count, collect(expert_out, weighted_table), 4, 10).astype(FULL)
    output = (residual + mixture).astype(LOW)

    grad_out_rows = out_cotangent.astype(FULL)
    grad_logits = gates * (grad_gates - jnp.sum(gates * grad_gates, axis=-1, keepdims=True))
    grad_logits = grad_logits.astype(LOW)
    grad_router = contract_rows(grad_logits, hidden_two)
    grad_two = grad_two + contract_cols(grad_logits, router_full)
    grad_gain_mlp = jnp.sum(grad_two * normed_mlp, axis=0)
    grad_resid = grad_out_rows + norm_back(grad_two * gain_mlp, normed_mlp, scale_mlp)
    grad_attn = grad_resid.astype(LOW)

    (grad_attn_all,) = line_gather(line_count, [grad_attn], [4], 11)
    grad_attn_all = grad_attn_all.reshape(all_rows, model_dim)
    out_here = lax.dynamic_slice_in_dim(out_full, place * head_cols, head_cols, axis=0)
    grad_w_out = contract_rows(attended.reshape(all_rows, head_cols), grad_attn_all)
    grad_attended = contract_cols(grad_attn_all, out_here).astype(LOW).reshape(head_shape)
    grad_value = einsum("ghqk,gqhd->gkhd", attn_low, grad_attended)
    grad_weights = einsum("gqhd,gkhd->ghqk", grad_attended, value_low)
    row_delta = jnp.sum(grad_weights * attn, axis=-1, keepdims=True)
    grad_scores = (attn * (grad_weights - row_delta)).astype(LOW)
    grad_query_rot = einsum("ghqk,gkhd->gqhd", grad_scores, key_rot) * scaling
    grad_key_rot = einsum("ghqk,gqhd->gkhd", grad_scores, query_rot) * scaling
    grad_query_normed = rotary(grad_query_rot, -1.0).reshape(all_rows, head_cols)
    grad_key_normed = rotary(grad_key_rot, -1.0).reshape(all_rows, head_cols)
    gain_pair = jnp.stack(
        [
            jnp.sum(grad_query_normed * normed_query, axis=0),
            jnp.sum(grad_key_normed * normed_key, axis=0),
        ]
    )
    weighted_query = grad_query_normed * gain_query
    weighted_key = grad_key_normed * gain_key
    dots = jnp.stack(
        [
            jnp.sum(weighted_query * normed_query, axis=-1),
            jnp.sum(weighted_key * normed_key, axis=-1),
        ]
    ).reshape(2 * line_count, row_count)
    (dots,) = exchange("expert", line_count, [dots], [True], 12)
    dots = jnp.sum(dots, axis=0).reshape(2, all_rows, 1) / model_dim
    grad_query = scale_query * (weighted_query - normed_query * dots[0])
    grad_key = scale_key * (weighted_key - normed_key * dots[1])
    grad_proj = jnp.concatenate(
        [grad_query, grad_key, grad_value.reshape(all_rows, head_cols)], axis=-1
    ).astype(LOW)
    grad_one = contract_cols(grad_proj, qkv_here).astype(LOW)
    grad_one = line_reduce(
        line_count, grad_one.reshape(line_count, row_count, model_dim), 4, 13
    ).astype(FULL)
    grad_w_qkv = contract_rows(hidden_one, grad_proj)
    grad_gain_attn = jnp.sum(grad_one * normed_attn, axis=0)
    grad_inputs = grad_resid + norm_back(grad_one * gain_attn, normed_attn, scale_attn)

    out_cols = model_dim // dp_count
    qkv_parts = grad_w_qkv.astype(LOW).reshape(dp_count, out_cols, 3 * head_cols)
    out_parts = grad_w_out.astype(LOW).reshape(head_cols, dp_count, out_cols).transpose(1, 0, 2)
    qkv_parts, out_parts, gain_pair = exchange(
        "dp", dp_count, [qkv_parts, out_parts, gain_pair], [False, False, True], 14
    )
    sum_qkv = jnp.sum(qkv_parts.astype(FULL), axis=0).reshape(out_cols, 3, head_cols)
    sum_out = jnp.sum(out_parts.astype(FULL), axis=0)
    gain_pair = jnp.sum(gain_pair, axis=0)
    shared = jnp.concatenate([grad_router, grad_gain_attn[None], grad_gain_mlp[None]], axis=0)
    kinds = shared.shape[0]
    shared = jnp.pad(shared, ((0, -kinds % 8), (0, 0)))
    tall = shared.shape[0]
    shared = shared.reshape(tall, dp_count, line_count, shard).transpose(2, 0, 1, 3)
    shared = shared.reshape(line_count, tall, dp_count * shard)
    (shared,) = exchange("expert", line_count, [shared], [False], 15)
    shared = jnp.sum(shared, axis=0).reshape(tall, dp_count, shard).transpose(1, 0, 2)
    (shared,) = exchange("dp", dp_count, [shared], [False], 16)
    shared = jnp.sum(shared, axis=0)
    return (
        output,
        grad_inputs,
        sum_qkv,
        sum_out,
        shared[:expert_count].T,
        shared[expert_count],
        shared[expert_count + 1],
        gain_pair[0],
        gain_pair[1],
        sum_gate_up.astype(FULL),
        sum_down.astype(FULL),
    )


def solution(mesh):
    both = ("dp", "expert")
    rows, flat = P(both, None), P(both)
    placed = (rows,) * 7 + (flat,) * 4 + (P("expert", None, None),) * 2
    return jax.shard_map(
        functools.partial(on_device, mesh.shape["dp"], mesh.shape["expert"]),
        mesh=mesh,
        in_specs=placed,
        out_specs=(
            rows,
            rows,
            P("dp", None, "expert"),
            P("expert", "dp"),
            rows,
            flat,
            flat,
            P("expert"),
            P("expert"),
            P("expert", "dp", None),
            P("expert", "dp", None),
        ),
        check_vma=False,
    )
```

time: 2170 us -> 1080 us (0.50)
  waiting for transfers between devices: 1250 us -> 0.72 us
  Pallas kernels: 0 us -> 644 us
  blocking collectives: 454 us -> 0 us
  matrix products: 198 us -> 252 us
  local copies, waits for them, and re-layouts: 140 us -> 88.3 us
    pallas_call x0 -> x16, Pallas kernels: none -> 644 us  [the longest x4 259 us: line_gather(): pl.pallas_call(functools.partial(line_gather_kernel, levels, tuple(cuts))...]
    reduce_scatter x6 -> x2, waiting for transfers between devices: 588 us -> 0.01 us  [the longest x1 0.01 us: on_device(): lax.psum_scatter(grad_w_down, 'dp', scatter_dimension=1, tiled=True)]
    all_to_all x2 -> x0, waiting for transfers between devices: 397 us -> none  [the longest x1 202 us: on_device(): lax.all_to_all(expert_out, 'expert', split_axis=1, concat_axis=0, tiled=T...]
    all_to_all x2 -> x0, blocking collectives: 316 us -> none  [the longest x1 160 us: on_device(): lax.all_to_all(back_send, 'expert', split_axis=0, concat_axis=1, tiled=True)]
    all_gather x2 -> x1, waiting for transfers between devices: 133 us -> 0.01 us  [on_device(): out_full = lax.all_gather(w_out, ('dp', 'expert'), axis=0, tiled=True)]
    unnamed x12 -> x3, waiting for transfers between devices: 129 us -> 0.71 us
    unnamed x3 -> x0, blocking collectives: 100 us -> none
    dot_general x17 -> x27, matrix products: 150 us -> 219 us  [the longest x24 207 us: einsum(): return jnp.einsum(spec, left_side, right_side, preferred_element_type=FULL)]
  transfers between devices with their start and end apart: 12 -> 3, of which waited for: 10 -> 0; matrix products, arithmetic and copies ran while one was open for 9% -> 29% of each run, Pallas kernels for 0% -> 55%
where the time goes in v1:
time: 1080 us; the launch traced here: 1070 us
  Pallas kernels  644 us (60%)
  matrix products  252 us (23%)
  local copies, waits for them, and re-layouts  88.3 us (8%)
  other arithmetic  69.9 us (6%)
  between operations  15.4 us (1%)
    pallas_call x4, Pallas kernels, line_gather(): pl.pallas_call(functools.partial(line_gather_kernel, levels, tuple(cuts))...  259 us
    pallas_call x3, Pallas kernels, line_reduce(): pl.pallas_call(functools.partial(line_reduce_kernel, levels, cuts), out_s...  215 us
    dot_general x24, matrix products, einsum(): return jnp.einsum(spec, left_side, right_side, preferred_element_type=FULL)  207 us
    pallas_call x9, Pallas kernels, exchange(): pl.pallas_call(functools.partial(exchange_kernel, axis, size, tuple(sprea...  170 us
    unnamed x161, local copies, waits for them, and re-layouts  23.4 us
  transfers between devices with their start and end apart: 3, of which 0 were waited for; matrix products, arithmetic and copies ran while one was open for 29% of the time, Pallas kernels for 55%

profile of v1, /device:TPU:16, one launch (start us, length us, event | category | flops | bytes accessed | tf_op | source)
XLA Modules:
  0.0 1070.5 jit_solution(16921763895401012690)
XLA Ops:
  9.4 93.8 %line_gather.4 = (bf16[8,192,2048]{2,1,0:T(8,128)(2,1)}, s32[8,16,192]{2,1,0:T(8,128)}) custom-call(bf16[192,2048]{1,0:T(8,128)(2,1)} %refs_0_.2, s32[16,192]{1,0:T(8,128)} %add_add_fusion.refs_1_), custom_call_target="tpu_custom_call" | custom-call | bytes 150000000 | tf_op jit(solution)/shard_map/line_gather/pallas_call | solution.py:116
  109.6 24.6 %exchange_expert.6 = bf16[8,64,896]{2,1,0:T(8,128)(2,1)} custom-call(bf16[8,64,896]{2,1,0:T(8,128)(2,1)} %pad_maximum_fusion.12.refs_0_), custom_call_target="tpu_custom_call" | custom-call | bytes 30000000 | tf_op jit(solution)/shard_map/exchange_expert/pallas_call | solution.py:312
  134.2 43.0 %exchange_dp.3 = bf16[4,512,896]{2,1,0:T(8,128)(2,1)} custom-call(bf16[512,896]{1,0:T(8,128)(2,1)} %bitcast.218), custom_call_target="tpu_custom_call" | custom-call | bytes 30000000 | tf_op jit(solution)/shard_map/exchange_dp/pallas_call | solution.py:312
  196.0 7.9 exchange_expert.7
  244.2 19.8 %exchange_expert.8 = bf16[8,192,256]{2,1,0:T(8,128)(2,1)} custom-call(bf16[8,192,256]{2,1,0:T(8,128)(2,1)} %copy_bitcast_fusion.1.refs_0_), custom_call_target="tpu_custom_call" | custom-call | bytes 30000000 | tf_op jit(solution)/shard_map/exchange_expert/pallas_call | solution.py:312
  265.2 54.1 %line_gather.6 = bf16[8,192,2048]{2,1,0:T(8,128)(2,1)} custom-call(bf16[192,2048]{1,0:T(8,128)(2,1)} %refs_0_.3), custom_call_target="tpu_custom_call" | custom-call | bytes 150000000 | tf_op jit(solution)/shard_map/line_gather/pallas_call | solution.py:116
  341.2 57.8 %line_gather.5 = (bf16[8,192,2048]{2,1,0:T(8,128)(2,1)}, f32[8,24,192]{2,1,0:T(8,128)}) custom-call(bf16[192,2048]{1,0:T(8,128)(2,1)} %copy-done.8, f32[24,192]{1,0:T(8,128)} %fusion.61.refs_1_), custom_call_target="tpu_custom_call" | custom-call | bytes 150000000 | tf_op jit(solution)/shard_map/line_gather/pallas_call | solution.py:116
  410.0 24.8 %fusion.9 = f32[3,576,2048]{2,1,0:T(8,128)} fusion(bf16[3,2048,2048]{2,1,0:T(8,128)(2,1)} %param.24, bf16[1,576,2048]{2,1,0:T(8,128)(2,1)} %bitcast.211, bf16[1,576,2048]{2,1,0:T(8,128)(2,1)} %bitcast.209, bf16[1,576,2048]{2,1,0:T(8,128)(2,1)} %bitcast.207), kind=kOutput, calls=%fused_computation.37 | convolution fusion | flops 14502592512 | bytes 46399488 | tf_op jit(solution)/shard_map/erd,edf->erf/dot_general | solution.py:367
  442.0 13.0 %fusion.2 = (f32[3,576]{1,0:T(4,128)S(1)}, bf16[3,576,2048]{2,1,0:T(8,128)(2,1)}) fusion(bf16[1,576,2048]{2,1,0:T(8,128)(2,1)S(1)} %bitcast.206, bf16[1,576,2048]{2,1,0:T(8,128)(2,1)S(1)} %bitcast.203, bf16[1,576,2048]{2,1,0:T(8,128)(2,1)S(1)} %bitcast.200, bf16[3,576,1024]{2,1,0:T(8,128)(2,1)S(1)} %multiply_convert_fusion.2, bf16[3,1024,2048]{2,1,0:T(8,128)(2,1)} %param.25), kind=kOutput, calls=%fused_computation.4 | convolution fusion | flops 7272528384 | bytes 30284544 | tf_op jit(solution)/shard_map/erf,efd->erd/dot_general | solution.py:367
  457.9 16.6 %convolution_convert_fusion.2 = bf16[3,1024,2048]{2,1,0:T(8,128)(2,1)} fusion(bf16[3,576,1024]{2,1,0:T(8,128)(2,1)} %copy-done.24, f32[3,576]{1,0:T(4,128)S(1)} %mul.669, bf16[1,576,2048]{2,1,0:T(8,128)(2,1)} %bitcast.204, bf16[1,576,2048]{2,1,0:T(8,128)(2,1)} %bitcast.201, bf16[1,576,2048]{2,1,0:T(8,128)(2,1)} %bitcast.198), kind=kOutput, calls=%fused_computation.21 | convolution fusion | flops 7271743488 | bytes 23206656 | tf_op jit(solution)/shard_map/erf,erd->efd/dot_general | solution.py:367
  474.5 22.4 %multiply_convert_fusion.1 = (bf16[3,576,1024]{2,1,0:T(8,128)(2,1)}, bf16[3,576,1024]{2,1,0:T(8,128)(2,1)}) fusion(f32[3,576,2048]{2,1,0:T(8,128)} %fusion.9, bf16[3,1024,2048]{2,1,0:T(8,128)(2,1)} %param.25, f32[3,576]{1,0:T(4,128)S(1)} %mul.669, bf16[1,576,2048]{2,1,0:T(8,128)(2,1)} %bitcast.205, bf16[1,576,2048]{2,1,0:T(8,128)(2,1)} %bitcast.202, ...), kind=kOutput, calls=%fused_computation.17 | convolution fusion | flops 7288455168 | bytes 40901376 | tf_op jit(solution)/shard_map/erd,efd->erf/dot_general | solution.py:367
  497.0 26.8 %convolution_convert_fusion = bf16[3,2048,2048]{2,1,0:T(8,128)(2,1)} fusion(bf16[3,576,1024]{2,1,0:T(8,128)(2,1)} %get-tuple-element.86, bf16[3,576,1024]{2,1,0:T(8,128)(2,1)} %get-tuple-element.85, bf16[1,576,2048]{2,1,0:T(8,128)(2,1)} %bitcast.212, bf16[1,576,2048]{2,1,0:T(8,128)(2,1)} %bitcast.210, bf16[1,576,2048]{2,1,0:T(8,128)(2,1)} %bitcast.208), kind=kOutput, calls=%fused_computation.5 | convolution fusion | flops 14529331200 | bytes 39321600 | tf_op jit(solution)/shard_map/erd,erf->edf/dot_general | solution.py:367
  526.9 22.1 %convolution_convert_fusion.3 = bf16[3,576,2048]{2,1,0:T(8,128)(2,1)} fusion(bf16[3,2048,2048]{2,1,0:T(8,128)(2,1)} %param.24, bf16[3,576,1024]{2,1,0:T(8,128)(2,1)} %get-tuple-element.86, bf16[3,576,1024]{2,1,0:T(8,128)(2,1)} %get-tuple-element.85), kind=kOutput, calls=%fused_computation.24 | convolution fusion | flops 14513209344 | bytes 39321600 | tf_op jit(solution)/shard_map/erf,edf->erd/dot_general | solution.py:367
  568.3 11.6 %add_convert_fusion.part_ref = bf16[8,192,2048]{2,1,0:T(8,128)(2,1)S(1)} fusion(f32[8,192,2048]{2,1,0:T(8,128)} %fusion.44, f32[8,192,2048]{2,1,0:T(8,128)} %fusion.45, bf16[8,72,2048]{2,1,0:T(8,128)(2,1)} %bitcast.192, pred[8,3,72,192]{3,2,0,1:T(8,128)(4,1)S(1)} %copy-done.5), kind=kOutput, calls=%fused_computation.9 | convolution fusion | flops 462422016 | bytes 33964032 | tf_op jit(solution)/shard_map/gst,gsd->gtd/dot_general | solution.py:367
  580.0 71.8 %line_reduce.4 = bf16[192,2048]{1,0:T(8,128)(2,1)S(1)} custom-call(bf16[8,192,2048]{2,1,0:T(8,128)(2,1)S(1)} %add_convert_fusion.part_ref), custom_call_target="tpu_custom_call" | custom-call | bytes 150000000 | tf_op jit(solution)/shard_map/line_reduce/pallas_call | solution.py:249
  664.9 53.4 %line_gather.7 = bf16[8,192,2048]{2,1,0:T(8,128)(2,1)} custom-call(bf16[192,2048]{1,0:T(8,128)(2,1)} %fusion.78.refs_0_), custom_call_target="tpu_custom_call" | custom-call | bytes 150000000 | tf_op jit(solution)/shard_map/line_gather/pallas_call | solution.py:116
  747.4 9.1 exchange_expert.10
  775.8 70.2 %line_reduce.5 = bf16[192,2048]{1,0:T(8,128)(2,1)S(1)} custom-call(bf16[8,192,2048]{2,1,0:T(8,128)(2,1)S(1)} %bitcast.182), custom_call_target="tpu_custom_call" | custom-call | bytes 150000000 | tf_op jit(solution)/shard_map/line_reduce/pallas_call | solution.py:249
  850.2 7.8 exchange_expert.11
  874.6 9.2 convolution_convert_fusion.5
  883.9 47.5 %exchange_dp.4 = (bf16[4,512,768]{2,1,0:T(8,128)(2,1)}, bf16[4,256,512]{2,1,0:T(8,128)(2,1)}, f32[4,2,256]{2,1,0:T(2,128)}) custom-call(bf16[4,512,768]{2,1,0:T(8,128)(2,1)} %bitcast.222, bf16[4,256,512]{2,1,0:T(8,128)(2,1)} %bitcast.217, f32[2,256]{1,0:T(2,128)} %pad_maximum_fusion.17.refs_2_), custom_call_target="tpu_custom_call" | custom-call | bytes 30000000 | tf_op jit(solution)/shard_map/exchange_dp/pallas_call | solution.py:312
  960.4 10.8 %add_convert_fusion.1.part_ref = bf16[8,192,2048]{2,1,0:T(8,128)(2,1)S(1)} fusion(f32[8,192,2048]{2,1,0:T(8,128)} %fusion.47, f32[8,192,2048]{2,1,0:T(8,128)} %fusion.46, bf16[8,72,2048]{2,1,0:T(8,128)(2,1)} %bitcast.191, bf16[8,3,72,192]{3,2,0,1:T(8,128)(2,1)} %copy-done.23), kind=kOutput, calls=%fused_computation.10 | convolution fusion | flops 462422016 | bytes 34111488 | tf_op jit(solution)/shard_map/gst,gsd->gtd/dot_general | solution.py:367
  971.3 72.8 %line_reduce.3 = bf16[192,2048]{1,0:T(8,128)(2,1)S(1)} custom-call(bf16[8,192,2048]{2,1,0:T(8,128)(2,1)S(1)} %add_convert_fusion.1.part_ref), custom_call_target="tpu_custom_call" | custom-call | bytes 150000000 | tf_op jit(solution)/shard_map/line_reduce/pallas_call | solution.py:249
  1054.5 9.1 convert_element_type.198
  (310 shorter events, 254.8 us)
Async XLA Ops:
  7.2 323.8 %all-gather.2.cloned.1.call-start = ((), (), s32[]{:S(2)}) async-start(), calls=%async_computation.2 | async-start | bytes 8650752 | tf_op jit(solution)/shard_map/all_gather | solution.py:400
  7.9 1041.1 %reduce-scatter.5.cloned.1.call-start = ((), (), s32[]{:S(2)}) async-start(), calls=%async_computation.4 | async-start | bytes 15728640 | tf_op jit(solution)/shard_map/reduce_scatter | solution.py:513
  182.9 153.5 %copy-start.47 = (f32[2048,1]{0,1:T(1,128)}, f32[2048,1]{0,1:T(1,128)S(1)}, u32[]{:S(2)}) copy-start(f32[2048,1]{0,1:T(1,128)S(1)} %get-tuple-element.119) | copy-start | bytes 24580
  265.2 54.2 %copy-start.56 = (s32[192,8]{0,1:T(8,128)S(1)}, s32[192,8]{0,1:T(8,128)}, u32[]{:S(2)}) copy-start(s32[192,8]{0,1:T(8,128)} %param.16) | copy-start | bytes 18436
  265.2 54.2 %copy-start.42 = (s32[8,8,192]{2,1,0:T(8,128)S(1)}, s32[8,8,192]{2,1,0:T(8,128)}, u32[]{:S(2)}) copy-start(s32[8,8,192]{2,1,0:T(8,128)} %slice.155) | copy-start | bytes 147460
  319.4 20.0 %copy-start.43 = (pred[192,24]{0,1:T(8,128)(4,1)}, pred[192,24]{0,1:T(8,128)(4,1)S(1)}, u32[]{:S(2)}) copy-start(pred[192,24]{0,1:T(8,128)(4,1)S(1)} %fusion.50) | copy-start | bytes 13828
  319.7 136.8 %copy-start.45 = (s32[8,3,192]{2,0,1:T(8,128)}, s32[8,3,192]{2,0,1:T(8,128)S(1)}, u32[]{:S(2)}) copy-start(s32[8,3,192]{2,0,1:T(8,128)S(1)} %fusion.29) | copy-start | bytes 55300
  320.0 87.4 %copy-start.4 = (pred[8,3,72,192]{3,2,0,1:T(8,128)(4,1)}, pred[8,3,72,192]{3,2,0,1:T(8,128)(4,1)S(1)}, u32[]{:S(2)}) copy-start(pred[8,3,72,192]{3,2,0,1:T(8,128)(4,1)S(1)} %iota_compare_fusion) | copy-start | bytes 995332
  336.4 68.3 %copy-start.59 = (f32[192]{0:T(256)}, f32[192]{0:T(256)S(1)}, u32[]{:S(2)}) copy-start(f32[192]{0:T(256)S(1)} %add_rsqrt_fusion.2) | copy-start | bytes 2308
  441.3 13.7 %copy-start.24 = (bf16[3,576,1024]{2,1,0:T(8,128)(2,1)}, bf16[3,576,1024]{2,1,0:T(8,128)(2,1)S(1)}, u32[]{:S(2)}) copy-start(bf16[3,576,1024]{2,1,0:T(8,128)(2,1)S(1)} %multiply_convert_fusion.2) | copy-start | bytes 10616836
  474.5 580.0 %reduce-scatter.3.cloned.1.call-start = ((), (), s32[]{:S(2)}) async-start(), calls=%async_computation.3 | async-start | bytes 31457280 | tf_op jit(solution)/shard_map/reduce_scatter | solution.py:518
  579.9 78.4 %copy-start.40 = (f32[192,24]{0,1:T(8,128)S(1)}, f32[192,24]{0,1:T(8,128)}, u32[]{:S(2)}) copy-start(f32[192,24]{0,1:T(8,128)} %copy-done.39) | copy-start | bytes 55300
  579.9 78.4 %copy-start.44 = (pred[192,24]{0,1:T(8,128)(4,1)S(1)}, pred[192,24]{0,1:T(8,128)(4,1)}, u32[]{:S(2)}) copy-start(pred[192,24]{0,1:T(8,128)(4,1)} %copy-done.43) | copy-start | bytes 13828
  579.9 78.4 %copy-start.58 = (f32[192]{0:T(256)S(1)}, f32[192]{0:T(256)}, u32[]{:S(2)}) copy-start(f32[192]{0:T(256)} %copy-done.57) | copy-start | bytes 2308
  579.9 78.4 %copy-start.63 = (f32[192]{0:T(256)S(1)}, f32[192]{0:T(256)}, u32[]{:S(2)}) copy-start(f32[192]{0:T(256)} %copy-done.62) | copy-start | bytes 2308
  579.9 78.5 %copy-start.48 = (f32[2048,1]{0,1:T(1,128)S(1)}, f32[2048,1]{0,1:T(1,128)}, u32[]{:S(2)}) copy-start(f32[2048,1]{0,1:T(1,128)} %copy-done.47) | copy-start | bytes 24580
  580.0 78.5 %copy-start.60 = (f32[192]{0:T(256)S(1)}, f32[192]{0:T(256)}, u32[]{:S(2)}) copy-start(f32[192]{0:T(256)} %copy-done.59) | copy-start | bytes 2308
  775.8 70.3 %copy-start.11 = (bf16[192,2048]{1,0:T(8,128)(2,1)S(1)}, bf16[192,2048]{1,0:T(8,128)(2,1)}, u32[]{:S(2)}) copy-start(bf16[192,2048]{1,0:T(8,128)(2,1)} %refs_0_.2) | copy-start | bytes 2359300
  775.8 70.3 %copy-start.50 = (f32[2048,1]{0,1:T(1,128)S(1)}, f32[2048,1]{0,1:T(1,128)}, u32[]{:S(2)}) copy-start(f32[2048,1]{0,1:T(1,128)} %copy-done.49) | copy-start | bytes 24580
  775.8 70.9 %copy-start.9 = (bf16[192,2048]{1,0:T(8,128)(2,1)S(1)}, bf16[192,2048]{1,0:T(8,128)(2,1)}, u32[]{:S(2)}) copy-start(bf16[192,2048]{1,0:T(8,128)(2,1)} %copy-done.8) | copy-start | bytes 2359300
  847.0 18.7 %copy-start.19 = (bf16[8,192,2,128]{3,2,1,0:T(2,128)(2,1)S(1)}, bf16[8,192,2,128]{3,2,1,0:T(2,128)(2,1)}, u32[]{:S(2)}) copy-start(bf16[8,192,2,128]{3,2,1,0:T(2,128)(2,1)} %copy.166) | copy-start | bytes 2359300
  971.2 72.9 %copy-start.33 = (bf16[4,256,512]{2,1,0:T(8,128)(2,1)S(1)}, bf16[4,256,512]{2,1,0:T(8,128)(2,1)}, u32[]{:S(2)}) copy-start(bf16[4,256,512]{2,1,0:T(8,128)(2,1)} %get-tuple-element.23) | copy-start | bytes 3145732
  971.2 75.5 %copy-start.7 = (f32[192,2048]{1,0:T(8,128)S(1)}, f32[192,2048]{1,0:T(8,128)}, u32[]{:S(2)}) copy-start(f32[192,2048]{1,0:T(8,128)} %copy-done.6) | copy-start | bytes 4718596
  971.2 75.5 %copy-start.18 = (bf16[192,2048]{1,0:T(8,128)(2,1)S(1)}, bf16[192,2048]{1,0:T(8,128)(2,1)}, u32[]{:S(2)}) copy-start(bf16[192,2048]{1,0:T(8,128)(2,1)} %refs_0_.3) | copy-start | bytes 2359300
  (55 other events, 209.9 us)
Sparse Core Ops, SparseCore 0:
  11.0 89.5 all-gather.1
  474.6 123.3 reduce-scatter.4
  601.1 221.8 reduce-scatter.2

commit v2 on v0

v2 whole, which is shorter than its diff:
```python
import functools
import math

import jax
import jax.numpy as jnp
from jax import lax
from jax.experimental import pallas as pl
from jax.experimental.pallas import tpu as pltpu
from jax.sharding import PartitionSpec as P

HEADS = 16
NORM_EPS = 1e-05
MESH = pl.DeviceIdType.MESH
ANY = pl.BlockSpec(memory_space=pl.ANY)
LOW = jnp.bfloat16
FULL = jnp.float32


def line_place():
    place = lax.axis_index("expert")
    level, side = lax.div(place, 2), lax.rem(place, 2)
    return place, level, side, place + 1 - 2 * side


def greet(axis, targets):
    barrier = pltpu.get_barrier_semaphore()
    for target, there in targets:

        def signal(target=target):
            pl.semaphore_signal(barrier, inc=1, device_id={axis: target}, device_id_type=MESH)

        if there is None:
            signal()
        else:
            pl.when(there)(signal)


def line_barrier(levels):
    place, level, _, other = line_place()
    has_up, has_down = level < levels - 1, level > 0
    greet("expert", [(other, None), (place + 2, has_up), (place - 2, has_down)])
    count = 1 + has_up.astype(jnp.int32) + has_down.astype(jnp.int32)
    pl.semaphore_wait(pltpu.get_barrier_semaphore(), count)


def around(axis, size):
    place = lax.axis_index(axis)
    return [lax.rem(place + shift, size) for shift in range(1, size)]


def remote(source, target, send, recv, device):
    return pltpu.make_async_remote_copy(
        src_ref=source,
        dst_ref=target,
        send_sem=send,
        recv_sem=recv,
        device_id=device,
        device_id_type=MESH,
    )


class LineGather:
    def __init__(self, levels, cuts, ins, outs, up_sem, down_sem, side_sem, recv_sem, own_sem):
        self.levels, self.cuts, self.ins, self.outs = levels, cuts, ins, outs
        self.up_sem, self.down_sem, self.side_sem = up_sem, down_sem, side_sem
        self.recv_sem = recv_sem
        self.pieces = [(i, k) for i in range(len(cuts)) for k in range(cuts[i])]
        self.place, self.level, self.side, self.other = line_place()
        self.has_up, self.has_down = self.level < levels - 1, self.level > 0
        self.own = [
            pltpu.make_async_copy(ins[i], outs[i].at[self.place], own_sem.at[i])
            for i in range(len(cuts))
        ]

    @staticmethod
    def scratch(size, cuts):
        levels, total = size // 2, sum(cuts)
        shapes = ((levels, total), (levels, total), (2 * levels - 1, total), (size, total))
        return [pltpu.SemaphoreType.DMA(shape) for shape in shapes + ((len(cuts),),)]

    def part(self, ref, i, k):
        rows = self.ins[i].shape[0] // self.cuts[i]
        return ref.at[pl.ds(k * rows, rows)]

    def sending(self, q, block, own, sem, target):
        i, k = self.pieces[q]
        landing = self.part(self.outs[i].at[block], i, k)
        source = self.part(self.ins[i], i, k) if own else landing
        return remote(source, landing, sem, self.recv_sem.at[block, q], {"expert": target})

    def up(self, q, step):
        block = self.place - 2 * step
        return self.sending(q, block, step == 0, self.up_sem.at[step, q], self.place + 2)

    def down(self, q, step):
        block = self.place + 2 * step
        return self.sending(q, block, step == 0, self.down_sem.at[step, q], self.place - 2)

    def across(self, q, step):
        sem = self.side_sem.at[step + self.levels - 1, q]
        return self.sending(q, self.place - 2 * step, step == 0, sem, self.other)

    def begin(self):
        for q in range(len(self.pieces)):
            pl.when(self.has_up)(self.up(q, 0).start)
            pl.when(self.has_down)(self.down(q, 0).start)
        for q in range(len(self.pieces)):
            self.across(q, 0).start()
        for copy in self.own:
            copy.start()

    def forward(self, step, q):
        @pl.when(self.level >= step)
        def _():
            self.across(q, step).wait_recv()
            pl.when(self.has_up)(self.up(q, step).start)
            self.across(q, step).start()

        @pl.when(self.level + step < self.levels)
        def _():
            self.across(q, -step).wait_recv()
            pl.when(self.has_down)(self.down(q, step).start)
            self.across(q, -step).start()

    def finish(self):
        for q in range(len(self.pieces)):
            for far in range(self.levels):
                block = 2 * far + 1 - self.side
                self.sending(q, block, False, self.side_sem.at[0, q], self.other).wait_recv()
            self.across(q, 0).wait_send()
            for step in range(self.levels):
                above, below = self.level >= step, self.level + step < self.levels
                pl.when(self.has_up & above)(self.up(q, step).wait_send)
                pl.when(self.has_down & below)(self.down(q, step).wait_send)
                if step:
                    pl.when(above)(self.across(q, step).wait_send)
                    pl.when(below)(self.across(q, -step).wait_send)
        for copy in self.own:
            copy.wait()

    def run(self):
        self.begin()
        for step in range(1, self.levels):
            for q in range(len(self.pieces)):
                self.forward(step, q)
        self.finish()


def line_gather_kernel(levels, cuts, *refs):
    count = len(cuts)
    line = LineGather(levels, cuts, refs[:count], refs[count : 2 * count], *refs[2 * count :])
    line_barrier(levels)
    line.run()


def call(kernel, name, number, outs, scratch, arrays, moved):
    return pl.pallas_call(
        kernel,
        out_shape=outs,
        in_specs=[ANY] * len(arrays),
        out_specs=[ANY] * len(outs),
        scratch_shapes=scratch,
        compiler_params=pltpu.CompilerParams(
            collective_id=number, has_side_effects=True, vmem_limit_bytes=48 << 20
        ),
        cost_estimate=pl.CostEstimate(flops=0, transcendentals=0, bytes_accessed=moved),
        name=name,
    )(*arrays)


def line_gather(size, arrays, cuts, number):
    return call(
        functools.partial(line_gather_kernel, size // 2, tuple(cuts)),
        "line_gather",
        number,
        [jax.ShapeDtypeStruct((size,) + a.shape, a.dtype) for a in arrays],
        LineGather.scratch(size, cuts),
        arrays,
        150_000_000,
    )


class LineReduce:
    def __init__(self, levels, cuts, parts, total, own, beside, rising, falling, *sems):
        self.levels, self.cuts, self.parts, self.total = levels, cuts, parts, total
        self.own, self.beside, self.rising, self.falling = own, beside, rising, falling
        self.load_sem, self.side_send, self.side_recv = sems[:3]
        self.up_send, self.up_recv, self.down_send, self.down_recv, self.out_sem = sems[3:]
        self.place, self.level, self.side, self.other = line_place()
        self.has_up, self.has_down = self.level < levels - 1, self.level > 0
        self.rows = parts.shape[1] // cuts
        self.order = []
        for step in range(levels):
            for far in (levels - 1 - step, step):
                if far not in self.order:
                    self.order.append(far)

    @staticmethod
    def scratch(size, block, dtype, cuts):
        levels = size // 2
        return (
            [pltpu.VMEM((levels,) + block, dtype)] * 4
            + [pltpu.SemaphoreType.DMA((levels, cuts))] * 7
            + [pltpu.SemaphoreType.DMA((cuts,))]
        )

    def cut(self, ref, block, k):
        return ref.at[block, pl.ds(k * self.rows, self.rows)]

    def loading(self, far, k):
        source = self.cut(self.parts, 2 * far + self.side, k)
        return pltpu.make_async_copy(source, self.cut(self.own, far, k), self.load_sem.at[far, k])

    def across(self, far, k):
        source = self.cut(self.parts, 2 * far + 1 - self.side, k)
        sems = self.side_send.at[far, k], self.side_recv.at[far, k]
        return remote(source, self.cut(self.beside, far, k), *sems, {"expert": self.other})

    def up(self, far, k):
        sems = self.up_send.at[far, k], self.up_recv.at[far, k]
        target = {"expert": self.place + 2}
        return remote(self.cut(self.own, far, k), self.cut(self.rising, far, k), *sems, target)

    def down(self, far, k):
        sems = self.down_send.at[far, k], self.down_recv.at[far, k]
        target = {"expert": self.place - 2}
        return remote(self.cut(self.own, far, k), self.cut(self.falling, far, k), *sems, target)

    def value(self, ref, block, k):
        return self.cut(ref, block, k)[...].astype(FULL)

    def load(self):
        for far in self.order:
            for k in range(self.cuts):
                self.loading(far, k).start()

    def begin(self):
        for far in self.order:
            for k in range(self.cuts):
                self.across(far, k).start()

    def pair(self, far, k):
        self.loading(far, k).wait()
        self.across(far, k).wait_recv()
        return self.value(self.own, far, k) + self.value(self.beside, far, k)

    def store(self, far, k, total):
        self.cut(self.own, far, k)[...] = total.astype(self.own.dtype)

    def toward(self, far, k, ahead, behind, move, arrived):
        @pl.when(ahead & behind)
        def _():
            both = self.pair(far, k)
            move(far, k).wait_recv()
            self.store(far, k, both + self.value(arrived, far, k))

        @pl.when(ahead & jnp.logical_not(behind))
        def _():
            self.store(far, k, self.pair(far, k))

        pl.when(ahead)(move(far, k).start)

    def main(self, beside=None):
        for step in range(self.levels - 1):
            high, low = self.levels - 1 - step, step
            for k in range(self.cuts):
                if beside:
                    beside(step * self.cuts + k)
                self.toward(high, k, self.level < high, self.has_down, self.up, self.rising)
                self.toward(low, k, self.level > low, self.has_up, self.down, self.falling)
        for k in range(self.cuts):
            self.store(self.level, k, self.pair(self.level, k))
            for there, move, arrived in (
                (self.has_down, self.up, self.rising),
                (self.has_up, self.down, self.falling),
            ):

                @pl.when(there)
                def _():
                    move(self.level, k).wait_recv()
                    total = self.value(self.own, self.level, k) + self.value(arrived, self.level, k)
                    self.store(self.level, k, total)

            self.leaving(k).start()

    def leaving(self, k):
        target = self.total.at[pl.ds(k * self.rows, self.rows)]
        return pltpu.make_async_copy(self.cut(self.own, self.level, k), target, self.out_sem.at[k])

    def finish(self):
        for k in range(self.cuts):
            self.leaving(k).wait()
            for far in range(self.levels):
                self.across(far, k).wait_send()
                pl.when(self.level < far)(self.up(far, k).wait_send)
                pl.when(self.level > far)(self.down(far, k).wait_send)


def line_reduce_kernel(levels, cuts, *refs):
    line = LineReduce(levels, cuts, *refs)
    line.load()
    line_barrier(levels)
    line.begin()
    line.main()
    line.finish()


def line_reduce(size, parts, cuts, number):
    block = parts.shape[1:]
    return call(
        functools.partial(line_reduce_kernel, size // 2, cuts),
        "line_reduce",
        number,
        [jax.ShapeDtypeStruct(block, parts.dtype)],
        LineReduce.scratch(size, block, parts.dtype, cuts),
        [parts],
        150_000_000,
    )[0]


class Exchange:
    def __init__(self, axis, size, spread, cuts, ins, outs, send_sem, recv_sem, own_sem):
        self.axis, self.spread, self.ins, self.outs = axis, spread, ins, outs
        self.send_sem, self.recv_sem, self.own_sem = send_sem, recv_sem, own_sem
        self.cuts = cuts
        self.firsts = [sum(cuts[:i]) for i in range(len(cuts))]
        self.pieces = [(i, k) for i in range(len(cuts)) for k in range(cuts[i])]
        self.place, self.peers = lax.axis_index(axis), around(axis, size)

    @staticmethod
    def scratch(size, cuts):
        sems = pltpu.SemaphoreType.DMA
        return [sems((sum(cuts), size)), sems((sum(cuts), size)), sems((len(cuts),))]

    def source(self, i, block):
        return self.ins[i] if self.spread[i] else self.ins[i].at[block]

    def staying(self, i):
        target = self.outs[i].at[self.place]
        return pltpu.make_async_copy(self.source(i, self.place), target, self.own_sem.at[i])

    def sending(self, i, k, shift, landing):
        peer = self.peers[shift]
        source, target, q = self.source(i, peer), self.outs[i].at[landing], self.firsts[i] + k
        if self.cuts[i] > 1:
            rows = target.shape[0] // self.cuts[i]
            source, target = source.at[pl.ds(k * rows, rows)], target.at[pl.ds(k * rows, rows)]
        sems = self.send_sem.at[q, shift], self.recv_sem.at[q, landing]
        return remote(source, target, *sems, {self.axis: peer})

    def send(self, i, k):
        for shift in range(len(self.peers)):
            self.sending(i, k, shift, self.place).start()

    def stay(self):
        for i in range(len(self.spread)):
            self.staying(i).start()

    def begin(self):
        for i, k in self.pieces:
            self.send(i, k)
        self.stay()

    def land(self):
        for shift, peer in enumerate(self.peers):
            for i, k in self.pieces:
                self.sending(i, k, shift, peer).wait_recv()

    def arrive(self):
        self.land()
        for i in range(len(self.spread)):
            self.staying(i).wait()

    def finish(self):
        for shift in range(len(self.peers)):
            for i, k in self.pieces:
                self.sending(i, k, shift, self.place).wait_send()


def exchange_kernel(axis, size, spread, *refs):
    count = len(spread)
    ins, outs, sems = refs[:count], refs[count : 2 * count], refs[2 * count :]
    moves = Exchange(axis, size, spread, (1,) * count, ins, outs, *sems)
    greet(axis, [(peer, None) for peer in moves.peers])
    pl.semaphore_wait(pltpu.get_barrier_semaphore(), size - 1)
    moves.begin()
    moves.arrive()
    moves.finish()


def exchange_outs(size, arrays, spread):
    return [
        jax.ShapeDtypeStruct((size,) + a.shape if flat else a.shape, a.dtype)
        for a, flat in zip(arrays, spread)
    ]


def exchange(axis, size, arrays, spread, number):
    return call(
        functools.partial(exchange_kernel, axis, size, tuple(spread)),
        "exchange_" + axis,
        number,
        exchange_outs(size, arrays, spread),
        Exchange.scratch(size, (1,) * len(arrays)),
        arrays,
        30_000_000,
    )


def opening_kernel(size, dp_count, cuts, *refs):
    count = len(cuts)
    ins, w_ref, small_ref = refs[:count], refs[count], refs[count + 1]
    outs, w_out, small_out = refs[count + 2 : 2 * count + 2], refs[2 * count + 2], refs[2 * count + 3]
    line_sems, rest = refs[2 * count + 4 : 2 * count + 9], refs[2 * count + 9 :]
    send_sem, recv_sem, own_sem = rest[:3]
    line = LineGather(size // 2, cuts, ins, outs, *line_sems)
    place, mine = line.place, lax.axis_index("dp")
    peers = around("expert", size)
    width = w_out.shape[3] // 3
    mine_refs = [w_out.at[mine], small_out.at[mine]]
    across = Exchange("dp", dp_count, (True,) * 2, (size,) * 2, mine_refs, [w_out, small_out], *rest[3:])
    greet("expert", [(peer, None) for peer in peers])
    greet("dp", [(peer, None) for peer in across.peers])
    pl.semaphore_wait(pltpu.get_barrier_semaphore(), size + dp_count - 2)

    def ends(peer, landing, j):
        if j == 3:
            return small_ref, small_out.at[mine, landing]
        start = pl.multiple_of(j * width * size + peer * width, 128)
        target = w_out.at[mine, landing, :, pl.ds(j * width, width)]
        return w_ref.at[:, pl.ds(start, width)], target

    def sending(shift, landing, j):
        source, target = ends(peers[shift], landing, j)
        sems = send_sem.at[shift, j], recv_sem.at[landing, j]
        return remote(source, target, *sems, {"expert": peers[shift]})

    own = [pltpu.make_async_copy(*ends(place, place, j), own_sem.at[j]) for j in range(4)]
    for shift in range(size - 1):
        for j in range(4):
            sending(shift, place, j).start()
    for copy in own:
        copy.start()
    line.begin()
    for copy in own:
        copy.wait()
    across.send(0, place)
    across.send(1, place)
    for shift, peer in enumerate(peers):
        for j in range(4):
            sending(shift, peer, j).wait_recv()
        across.send(0, peer)
        across.send(1, peer)
    for step in range(1, size // 2):
        for q in range(len(line.pieces)):
            line.forward(step, q)
    line.finish()
    for shift in range(size - 1):
        for j in range(4):
            sending(shift, place, j).wait_send()
    across.land()
    across.finish()


def opening(size, dp_count, arrays, cuts, weights, small, number):
    sems = pltpu.SemaphoreType.DMA
    outs = [jax.ShapeDtypeStruct((size,) + a.shape, a.dtype) for a in arrays]
    rows, columns = weights.shape
    whole = (dp_count, size, rows)
    outs.append(jax.ShapeDtypeStruct(whole + (columns // size,), weights.dtype))
    outs.append(jax.ShapeDtypeStruct(whole + (small.shape[1],), small.dtype))
    return call(
        functools.partial(opening_kernel, size, dp_count, tuple(cuts)),
        "opening",
        number,
        outs,
        LineGather.scratch(size, cuts)
        + [sems((size, 4)), sems((size, 4)), sems((4,))]
        + Exchange.scratch(dp_count, (size, size)),
        list(arrays) + [weights, small],
        200_000_000,
    )


def closing_kernel(size, dp_count, cuts, sum_cuts, *refs):
    ins, outs, rest = refs[:5], refs[5:10], refs[10:]
    line = LineReduce(size // 2, cuts, ins[0], outs[0], *rest[:12])
    sums = Exchange("dp", dp_count, (False, False, True), sum_cuts, ins[1:4], outs[1:4], *rest[12:15])
    got, half, last = rest[15:18]
    first = Exchange("expert", size, (False,), (1,), ins[4:5], [got], *rest[18:21])
    second = Exchange("dp", dp_count, (False,), (1,), [half], [last], *rest[21:24])
    line.load()
    greet("expert", [(peer, None) for peer in first.peers])
    greet("dp", [(peer, None) for peer in sums.peers])
    pl.semaphore_wait(pltpu.get_barrier_semaphore(), size + dp_count - 2)
    first.begin()
    line.begin()
    sums.stay()
    turns = (size // 2 - 1) * cuts
    tall = half.shape[1]

    def beside(turn):
        for q in range(len(sums.pieces)):
            if q * turns // len(sums.pieces) == turn:
                sums.send(*sums.pieces[q])
        if turn == turns // 2:
            first.arrive()
            for copy in range(dp_count):
                rows = pl.ds(copy * tall, tall)
                half[copy] = sum(got[i, rows, :] for i in range(size))
            second.begin()

    line.main(beside)
    second.arrive()
    outs[4][...] = sum(last[i] for i in range(dp_count))
    sums.arrive()
    for moves in (line, first, second, sums):
        moves.finish()


def closing(size, dp_count, parts, cuts, sums, shared, number):
    block = parts.shape[1:]
    tall = shared.shape[1] // dp_count
    wide = shared.shape[2]
    vmem = pl.BlockSpec(memory_space=pltpu.VMEM)
    sum_cuts = (8, 2, 1)
    outs = [jax.ShapeDtypeStruct(block, parts.dtype)]
    outs += exchange_outs(dp_count, sums, (False, False, True))
    outs.append(jax.ShapeDtypeStruct((tall, wide), FULL))
    return pl.pallas_call(
        functools.partial(closing_kernel, size, dp_count, cuts, sum_cuts),
        out_shape=outs,
        in_specs=[ANY] * 5,
        out_specs=[ANY] * 4 + [vmem],
        scratch_shapes=LineReduce.scratch(size, block, parts.dtype, cuts)
        + Exchange.scratch(dp_count, sum_cuts)
        + [pltpu.VMEM((size,) + shared.shape[1:], FULL)]
        + [pltpu.VMEM((dp_count, tall, wide), FULL)] * 2
        + Exchange.scratch(size, (1,))
        + Exchange.scratch(dp_count, (1,)),
        compiler_params=pltpu.CompilerParams(
            collective_id=number, has_side_effects=True, vmem_limit_bytes=48 << 20
        ),
        cost_estimate=pl.CostEstimate(flops=0, transcendentals=0, bytes_accessed=200_000_000),
        name="closing",
    )(parts, *sums, shared)


def rows_kernel(local_count, table_ref, rows_ref, out_ref):
    capacity = out_ref.shape[1]
    placed = jnp.dot(table_ref[0], rows_ref[0], preferred_element_type=FULL)
    for j in range(local_count):
        out_ref[j] = placed[j * capacity : (j + 1) * capacity].astype(LOW)


def place_rows(table, rows, local_count):
    groups, slots, tokens = table.shape
    width = rows.shape[2]
    capacity = slots // local_count
    return pl.pallas_call(
        functools.partial(rows_kernel, local_count),
        out_shape=jax.ShapeDtypeStruct((local_count, groups * capacity, width), LOW),
        grid=(groups,),
        in_specs=[
            pl.BlockSpec((1, slots, tokens), lambda g: (g, 0, 0)),
            pl.BlockSpec((1, tokens, width), lambda g: (g, 0, 0)),
        ],
        out_specs=pl.BlockSpec((local_count, capacity, width), lambda g: (0, g, 0)),
        cost_estimate=pl.CostEstimate(
            flops=2 * table.size * width, transcendentals=0, bytes_accessed=4 * rows.size
        ),
        name="place_rows",
    )(table, rows)


def collect_kernel(*refs):
    tables, rows_refs, out_ref = refs[: len(refs) // 2], refs[len(refs) // 2 : -1], refs[-1]
    total = 0.0
    for table_ref, rows_ref in zip(tables, rows_refs):
        total += jnp.dot(table_ref[0], rows_ref[0], preferred_element_type=FULL)
    out_ref[0] = total.astype(LOW)


def collect(tables, rows):
    groups, tokens, capacity = tables[0].shape
    width = rows[0].shape[2]
    return pl.pallas_call(
        collect_kernel,
        out_shape=jax.ShapeDtypeStruct((groups, tokens, width), LOW),
        grid=(groups,),
        in_specs=[pl.BlockSpec((1, tokens, capacity), lambda g: (g, 0, 0))] * len(rows)
        + [pl.BlockSpec((1, capacity, width), lambda g: (0, g, 0))] * len(rows),
        out_specs=pl.BlockSpec((1, tokens, width), lambda g: (g, 0, 0)),
        cost_estimate=pl.CostEstimate(
            flops=2 * len(rows) * tables[0].size * width,
            transcendentals=0,
            bytes_accessed=4 * groups * tokens * width,
        ),
        name="collect",
    )(*tables, *rows)


def across_cols(left_side, right_side):
    return lax.dot_general(
        left_side, right_side, (((1,), (1,)), ((), ())), preferred_element_type=FULL
    )


def expert_kernel(
    tiles,
    x_ref,
    dy_ref,
    scale_ref,
    gate_ref,
    up_ref,
    down_ref,
    grads_ref,
    out_ref,
    back_ref,
    dots_ref,
    turned,
    weighted,
    out_sum,
    back_sum,
    side_buf,
    down_buf,
    sems,
):
    tile = pl.program_id(0)
    slot = lax.rem(tile, 2)
    width = gate_ref.shape[2]
    copies, high = side_buf.shape[2], side_buf.shape[3]
    some, low = down_buf.shape[1], down_buf.shape[2]
    hidden = tiles * width

    def leaving(at, half, slot):
        columns = pl.ds(pl.multiple_of(half * hidden + at * width, 128), width)
        target = grads_ref.at[:, pl.ds(0, high), columns]
        return pltpu.make_async_copy(side_buf.at[slot, half], target, sems.at[slot, half])

    def leaving_down(at, slot):
        target = grads_ref.at[pl.ds(at * some, some), pl.ds(high, low), :]
        return pltpu.make_async_copy(down_buf.at[slot], target, sems.at[slot, 2])

    def settle(at, slot):
        leaving(at, 0, slot).wait()
        leaving(at, 1, slot).wait()
        leaving_down(at, slot).wait()

    @pl.when(tile == 0)
    def _():
        turned[...] = x_ref[0].T
        weighted[...] = (scale_ref[0] * dy_ref[0].astype(FULL)).astype(LOW)
        out_sum[...] = jnp.zeros_like(out_sum)
        back_sum[...] = jnp.zeros_like(back_sum)

    @pl.when(tile >= 2)
    def _():
        settle(tile - 2, slot)

    rows, grads = x_ref[0], weighted[...]
    w_gate, w_up, w_down = gate_ref[0], up_ref[0], down_ref[0]
    gate = jnp.dot(rows, w_gate, preferred_element_type=FULL)
    up = jnp.dot(rows, w_up, preferred_element_type=FULL)
    sigmoid = jax.nn.sigmoid(gate)
    silu = gate * sigmoid
    act = (silu * up).astype(LOW)
    out_sum[...] += jnp.dot(act, w_down, preferred_element_type=FULL)
    grad_act = across_cols(grads, w_down)
    grad_gate = (grad_act * up * sigmoid * (1.0 + gate * (1.0 - sigmoid))).astype(LOW)
    grad_up = (grad_act * silu).astype(LOW)
    back_sum[...] += across_cols(grad_gate, w_gate) + across_cols(grad_up, w_up)
    turned_rows = turned[...]
    for half, grad in enumerate((grad_gate, grad_up)):
        total = jnp.dot(turned_rows, grad, preferred_element_type=FULL).astype(LOW)
        side_buf[slot, half] = total.reshape(copies, high, width)
        leaving(tile, half, slot).start()
    total = jnp.dot(act.T, grads, preferred_element_type=FULL).astype(LOW)
    down_buf[slot] = total.reshape(some, low, total.shape[1])
    leaving_down(tile, slot).start()

    @pl.when(tile == tiles - 1)
    def _():
        final = out_sum[...]
        dots_ref[0] = jnp.sum(final * dy_ref[0].astype(FULL), axis=-1, keepdims=True)
        out_ref[0] = (scale_ref[0] * final).astype(LOW)
        back_ref[0] = back_sum[...].astype(LOW)
        settle(tile - 1, 1 - slot)
        settle(tile, slot)


def expert(j, dp_count, x_rows, dy_rows, scales, w_gate_up, w_down, tiles=4):
    _, slots, width = x_rows.shape
    hidden = w_down.shape[1]
    tile = hidden // tiles
    high, low = width // dp_count, hidden // dp_count
    some = tile // low
    once = pl.Buffered(1)
    row_spec = pl.BlockSpec((1, slots, width), lambda f: (j, 0, 0), pipeline_mode=once)
    out_spec = pl.BlockSpec((1, slots, width), lambda f: (0, 0, 0), pipeline_mode=once)
    return pl.pallas_call(
        functools.partial(expert_kernel, tiles),
        out_shape=[
            jax.ShapeDtypeStruct((dp_count, high + low, width), LOW),
            jax.ShapeDtypeStruct((1, slots, width), LOW),
            jax.ShapeDtypeStruct((1, slots, width), LOW),
            jax.ShapeDtypeStruct((1, slots, 1), FULL),
        ],
        grid=(tiles,),
        in_specs=[
            row_spec,
            row_spec,
            pl.BlockSpec((1, slots, 1), lambda f: (j, 0, 0), pipeline_mode=once),
            pl.BlockSpec((1, width, tile), lambda f: (j, 0, f)),
            pl.BlockSpec((1, width, tile), lambda f: (j, 0, tiles + f)),
            pl.BlockSpec((1, tile, width), lambda f: (j, f, 0)),
        ],
        out_specs=[
            ANY,
            out_spec,
            out_spec,
            pl.BlockSpec((1, slots, 1), lambda f: (0, 0, 0), pipeline_mode=once),
        ],
        scratch_shapes=[
            pltpu.VMEM((width, slots), LOW),
            pltpu.VMEM((slots, width), LOW),
            pltpu.VMEM((slots, width), FULL),
            pltpu.VMEM((slots, width), FULL),
            pltpu.VMEM((2, 2, dp_count, high, tile), LOW),
            pltpu.VMEM((2, some, low, width), LOW),
            pltpu.SemaphoreType.DMA((2, 3)),
        ],
        compiler_params=pltpu.CompilerParams(vmem_limit_bytes=60 << 20),
        cost_estimate=pl.CostEstimate(
            flops=18 * slots * width * hidden,
            transcendentals=slots * hidden,
            bytes_accessed=12 * width * hidden,
        ),
        name="expert",
    )(x_rows, dy_rows, scales, w_gate_up, w_gate_up, w_down)


def rms_scale(values):
    return lax.rsqrt(jnp.mean(values * values, axis=-1, keepdims=True) + NORM_EPS)


def rotary_tables(length, size):
    index = jnp.arange(size // 2, dtype=FULL)
    frequency = jnp.exp(index * (-2.0 * math.log(10000.0) / size))
    angles = jnp.arange(length, dtype=FULL)[:, None] * frequency[None, :]
    cosine, sine = jnp.cos(angles), jnp.sin(angles)
    return jnp.stack(
        [jnp.concatenate([cosine, cosine], axis=1), jnp.concatenate([-sine, sine], axis=1)]
    )


def norm_back(grad_normed, normed, scale_rows):
    return scale_rows * (
        grad_normed - normed * jnp.mean(grad_normed * normed, axis=-1, keepdims=True)
    )


def contract_rows(left_side, right_side):
    return lax.dot_general(
        left_side, right_side, (((0,), (0,)), ((), ())), preferred_element_type=FULL
    )


def contract_cols(left_side, right_side):
    return lax.dot_general(
        left_side, right_side, (((1,), (1,)), ((), ())), preferred_element_type=FULL
    )


def einsum(spec, left_side, right_side):
    return jnp.einsum(spec, left_side, right_side, preferred_element_type=FULL)


def turn(values, cosine, sine):
    return values * cosine + pltpu.roll(values, values.shape[1] // 2, 1) * sine


def allowed_pairs(column_ref, row_ref):
    shape = (column_ref.shape[1], row_ref.shape[2])
    later = lax.broadcasted_iota(jnp.int32, shape, 0) >= lax.broadcasted_iota(jnp.int32, shape, 1)
    return later & (column_ref[0] == row_ref[0])


def softmax(query, key, allowed):
    scores = across_cols(query, key) * (1.0 / math.sqrt(query.shape[1]))
    scores = jnp.where(allowed, scores, -1e30)
    powers = jnp.exp(scores - jnp.max(scores, axis=-1, keepdims=True))
    return powers / jnp.sum(powers, axis=-1, keepdims=True)


def attend_kernel(
    heads, rows_ref, scale_ref, gain_ref, turn_ref, column_ref, row_ref, kept_ref, out_ref
):
    width = out_ref.shape[2]
    size = width // heads
    allowed = allowed_pairs(column_ref, row_ref)
    cosine, sine = turn_ref[0], turn_ref[1]
    for h in range(heads):
        parts = []
        for part in range(3):
            columns = pl.ds(part * width + h * size, size)
            values = rows_ref[0, :, columns]
            if part < 2:
                values = values * scale_ref[0, :, part : part + 1]
                values = values * gain_ref[part : part + 1, h * size : (h + 1) * size]
                values = turn(values, cosine, sine)
            parts.append(values.astype(LOW))
            kept_ref[0, :, columns] = parts[-1]
        query, key, value = parts
        probs = softmax(query, key, allowed).astype(LOW)
        out_ref[0, :, pl.ds(h * size, size)] = jnp.dot(
            probs, value, preferred_element_type=FULL
        ).astype(LOW)


def block_of(array):
    rest = array.shape[1:]
    return pl.BlockSpec((1,) + rest, lambda g: (g,) + (0,) * len(rest))


def whole_of(array):
    return pl.BlockSpec(array.shape, lambda g: (0,) * array.ndim, pipeline_mode=pl.Buffered(1))


def attend(heads, rows, scales, gains, turns, column, row):
    groups, length, width = rows.shape
    kept = jax.ShapeDtypeStruct((groups, length, width), LOW)
    out = jax.ShapeDtypeStruct((groups, length, width // 3), LOW)
    return pl.pallas_call(
        functools.partial(attend_kernel, heads),
        out_shape=[kept, out],
        grid=(groups,),
        in_specs=[
            block_of(rows),
            block_of(scales),
            whole_of(gains),
            whole_of(turns),
            block_of(column),
            block_of(row),
        ],
        out_specs=[block_of(kept), block_of(out)],
        cost_estimate=pl.CostEstimate(
            flops=4 * groups * length * length * width, transcendentals=0, bytes_accessed=8 * rows.size
        ),
        name="attend",
    )(rows, scales, gains, turns, column, row)


def attend_back_kernel(
    heads,
    grad_ref,
    w_ref,
    kept_ref,
    out_ref,
    rows_ref,
    scale_ref,
    gain_ref,
    turn_ref,
    column_ref,
    row_ref,
    back_ref,
    dots_ref,
    gains_ref,
    w_grad_ref,
    w_sum,
):
    step = pl.program_id(0)
    width = out_ref.shape[2]
    size = width // heads
    scaling = 1.0 / math.sqrt(size)
    allowed = allowed_pairs(column_ref, row_ref)
    cosine, sine = turn_ref[0], turn_ref[1]

    @pl.when(step == 0)
    def _():
        w_sum[...] = jnp.zeros_like(w_sum)
        gains_ref[...] = jnp.zeros_like(gains_ref)

    grad_rows = grad_ref[0]
    grad_out = across_cols(grad_rows, w_ref[...]).astype(LOW)
    w_sum[...] += contract_rows(out_ref[0], grad_rows)
    dots = [0.0, 0.0]
    for h in range(heads):
        mine = slice(h * size, (h + 1) * size)
        query, key, value = (kept_ref[0, :, pl.ds(p * width + h * size, size)] for p in range(3))
        probs = softmax(query, key, allowed)
        grad = grad_out[:, mine]
        grad_value = contract_rows(probs.astype(LOW), grad)
        grad_probs = across_cols(grad, value)
        delta = jnp.sum(grad_probs * probs, axis=-1, keepdims=True)
        grad_scores = (probs * (grad_probs - delta)).astype(LOW)
        grad_query = jnp.dot(grad_scores, key, preferred_element_type=FULL) * scaling
        grad_key = contract_rows(grad_scores, query) * scaling
        for part, grad_turned in enumerate((grad_query, grad_key)):
            columns = pl.ds(part * width + h * size, size)
            grad_normed = turn(grad_turned, cosine, -sine)
            normed = rows_ref[0, :, columns] * scale_ref[0, :, part : part + 1]
            gains_ref[part : part + 1, mine] += jnp.sum(grad_normed * normed, axis=0, keepdims=True)
            weighted = grad_normed * gain_ref[part : part + 1, mine]
            dots[part] += jnp.sum(weighted * normed, axis=-1, keepdims=True)
            back_ref[0, :, columns] = weighted
        back_ref[0, :, pl.ds(2 * width + h * size, size)] = grad_value
    dots_ref[0] = jnp.concatenate(dots, axis=1)

    @pl.when(step == pl.num_programs(0) - 1)
    def _():
        for copy in range(w_grad_ref.shape[0]):
            wide = w_grad_ref.shape[2]
            w_grad_ref[copy] = w_sum[:, copy * wide : (copy + 1) * wide].astype(LOW)


def attend_back(heads, dp_count, grad, w_here, kept, out, rows, scales, gains, turns, column, row):
    groups, length, model_dim = grad.shape
    width = out.shape[2]
    back = jax.ShapeDtypeStruct((groups, length, 3 * width), FULL)
    dots = jax.ShapeDtypeStruct((groups, length, 2), FULL)
    gain_sums = jax.ShapeDtypeStruct((2, width), FULL)
    w_grad = jax.ShapeDtypeStruct((dp_count, width, model_dim // dp_count), LOW)
    blocks = [block_of, whole_of, block_of, block_of, block_of, block_of, whole_of, whole_of]
    arrays = [grad, w_here, kept, out, rows, scales, gains, turns, column, row]
    return pl.pallas_call(
        functools.partial(attend_back_kernel, heads),
        out_shape=[back, dots, gain_sums, w_grad],
        grid=(groups,),
        in_specs=[f(a) for f, a in zip(blocks + [block_of] * 2, arrays)],
        out_specs=[block_of(back), block_of(dots), whole_of(gain_sums), whole_of(w_grad)],
        scratch_shapes=[pltpu.VMEM((width, model_dim), FULL)],
        compiler_params=pltpu.CompilerParams(vmem_limit_bytes=48 << 20),
        cost_estimate=pl.CostEstimate(
            flops=4 * grad.size * width, transcendentals=0, bytes_accessed=10 * grad.size
        ),
        name="attend_back",
    )(*arrays)


def on_device(
    dp_count,
    line_count,
    layer_input,
    out_cotangent,
    segments,
    routes,
    w_qkv,
    w_out,
    w_router,
    attn_gain,
    mlp_gain,
    query_gain,
    key_gain,
    w_gate_up,
    w_down,
):
    row_count, model_dim = layer_input.shape
    top_count = routes.shape[1]
    expert_count = w_router.shape[1]
    local_count = w_gate_up.shape[0]
    head_size = model_dim // HEADS
    head_cols = model_dim // line_count
    heads_here = head_cols // head_size
    capacity = (row_count * top_count * 9 // 8 + expert_count - 1) // expert_count
    scaling = 1.0 / math.sqrt(head_size)
    place = lax.axis_index("expert")
    all_rows = line_count * row_count
    shard = w_qkv.shape[0]

    small = jnp.concatenate(
        [w_router] + [g[:, None] for g in (attn_gain, mlp_gain, query_gain, key_gain)], axis=1
    )
    small = jnp.pad(small, ((0, 0), (0, 128 - small.shape[1])))
    numbers = jnp.concatenate([routes.T, segments, jnp.zeros((7, row_count), jnp.int32)], axis=0)
    x_all, numbers_all, qkv_here, small = opening(
        line_count, dp_count, [layer_input, numbers], [4, 1], w_qkv, small, 1
    )
    out_full = lax.all_gather(w_out, ("dp", "expert"), axis=0, tiled=True)
    late_cotangent, x_all = lax.optimization_barrier((out_cotangent, x_all))
    dy_all = lax.all_gather(late_cotangent, "expert", axis=0)
    qkv_here = qkv_here.reshape(model_dim, 3 * head_cols)
    small = small.reshape(model_dim, small.shape[3])
    router_full = small[:, :expert_count]
    gains = small[:, expert_count : expert_count + 4].astype(FULL)
    gain_attn, gain_mlp = gains[:, 0], gains[:, 1]
    own_gains = lax.dynamic_slice_in_dim(gains, place * head_cols, head_cols, axis=0)
    gain_query, gain_key = own_gains[:, 2], own_gains[:, 3]

    routes_all = numbers_all[:, :top_count]
    segments_all = numbers_all[:, top_count]
    inputs_all = x_all.reshape(all_rows, model_dim).astype(FULL)
    normed_all = inputs_all * rms_scale(inputs_all)
    hidden_one = (normed_all * gain_attn).astype(LOW)
    projected = jnp.dot(hidden_one, qkv_here, preferred_element_type=FULL)
    query_rows = projected[:, :head_cols]
    key_rows = projected[:, head_cols : 2 * head_cols]
    value_rows = projected[:, 2 * head_cols :]
    squares = jnp.stack(
        [jnp.sum(query_rows * query_rows, axis=-1), jnp.sum(key_rows * key_rows, axis=-1)]
    ).reshape(2 * line_count, row_count)
    (squares,) = exchange("expert", line_count, [squares], [True], 4)
    squares = jnp.sum(squares, axis=0).reshape(2, line_count, row_count)
    scales = lax.rsqrt(squares / model_dim + NORM_EPS).transpose(1, 2, 0)
    tables = rotary_tables(row_count, head_size)
    both_gains = jnp.stack([gain_query, gain_key])
    column, row = segments_all[:, :, None], segments_all[:, None, :]
    projected = projected.reshape(line_count, row_count, 3 * head_cols)
    kept, attended = attend(heads_here, projected, scales, both_gains, tables, column, row)
    (own_attended,) = exchange("expert", line_count, [attended], [False], 5)
    own_attended = own_attended.transpose(1, 0, 2).reshape(row_count, model_dim)
    inputs = layer_input.astype(FULL)
    scale_attn = rms_scale(inputs)
    normed_attn = inputs * scale_attn
    residual = inputs + jnp.dot(own_attended, out_full, preferred_element_type=FULL)
    scale_mlp = rms_scale(residual)
    normed_mlp = residual * scale_mlp
    hidden_two = (normed_mlp * gain_mlp).astype(LOW)

    logits = jnp.dot(hidden_two, router_full, preferred_element_type=FULL)
    chosen = jnp.any(routes[:, :, None] == jnp.arange(expert_count)[None, None, :], axis=1)
    masked = jnp.where(chosen, logits, -1e30)
    powers = jnp.where(chosen, jnp.exp(masked - jnp.max(masked, axis=-1, keepdims=True)), 0.0)
    gates = powers / jnp.sum(powers, axis=-1, keepdims=True)

    h_all, gates_all = line_gather(line_count, [hidden_two, gates.T], [4, 1], 6)
    local = place * local_count + jnp.arange(local_count)
    used = jnp.any(routes_all[:, None] == local[None, :, None, None], axis=2)
    position = jnp.arange(row_count)
    lower = (position[:, None] < position[None, :]).astype(LOW)
    rank = einsum("gju,ut->gjt", used.astype(LOW), lower).astype(jnp.int32)
    rank = jnp.where(used, rank, -1)
    spots = jnp.arange(capacity)
    table = (rank[:, :, None, :] == spots[None, None, :, None]).astype(LOW)
    returns = [(rank[:, j, :, None] == spots[None, None, :]).astype(LOW) for j in range(local_count)]
    slots = line_count * capacity
    flat_table = table.reshape(line_count, local_count * capacity, row_count)
    expert_rows = place_rows(flat_table, h_all, local_count)
    dy_all, _ = lax.optimization_barrier((dy_all, expert_rows))
    dy_rows = place_rows(flat_table, dy_all, local_count)
    local_gates = lax.dynamic_slice_in_dim(gates_all, place * local_count, local_count, axis=1)
    slot_gates = jnp.sum(table.astype(FULL) * local_gates[:, :, None, :], axis=-1)
    slot_gates = slot_gates.transpose(1, 0, 2).reshape(local_count, slots, 1)
    out_rows, back_rows, slot_grads, grad_sums = [], [], [], []
    for j in range(local_count):
        grads, out_row, back_row, dots = expert(
            j, dp_count, expert_rows, dy_rows, slot_gates, w_gate_up, w_down
        )
        grads = grads.reshape(-1, model_dim)
        grad_sums.append(lax.psum_scatter(grads, "dp", scatter_dimension=0, tiled=True))
        out_rows.append(out_row)
        back_rows.append(back_row)
        slot_grads.append(dots.reshape(line_count, capacity))
    gate_rows = model_dim // dp_count
    sum_gate_up = jnp.stack([both[:gate_rows] for both in grad_sums]).astype(FULL)
    sum_down = jnp.stack([both[gate_rows:] for both in grad_sums]).astype(FULL)
    slot_grads = jnp.stack(slot_grads, axis=1)
    grad_gates = jnp.sum(table.astype(FULL) * slot_grads[:, :, :, None], axis=2)
    (grad_gates,) = exchange("expert", line_count, [grad_gates], [False], 8)
    grad_gates = grad_gates.reshape(expert_count, row_count).T
    grad_two = line_reduce(line_count, collect(returns, back_rows), 4, 9).astype(FULL)
    grad_out_rows = out_cotangent.astype(FULL)
    grad_logits = gates * (grad_gates - jnp.sum(gates * grad_gates, axis=-1, keepdims=True))
    grad_logits = grad_logits.astype(LOW)
    grad_router = contract_rows(grad_logits, hidden_two)
    grad_two = grad_two + contract_cols(grad_logits, router_full)
    grad_gain_mlp = jnp.sum(grad_two * normed_mlp, axis=0)
    grad_resid = grad_out_rows + norm_back(grad_two * gain_mlp, normed_mlp, scale_mlp)
    grad_attn = grad_resid.astype(LOW)

    (grad_attn_all,) = line_gather(line_count, [grad_attn], [4], 11)
    out_here = lax.dynamic_slice_in_dim(out_full, place * head_cols, head_cols, axis=0)
    back, dots, gain_pair, out_parts = attend_back(
        heads_here,
        dp_count,
        grad_attn_all,
        out_here,
        kept,
        attended,
        projected,
        scales,
        both_gains,
        tables,
        column,
        row,
    )
    dots = dots.transpose(2, 0, 1).reshape(2 * line_count, row_count)
    (dots,) = exchange("expert", line_count, [dots], [True], 12)
    dots = jnp.sum(dots, axis=0).reshape(2, all_rows, 1) / model_dim
    flat_scales = scales.reshape(all_rows, 2)
    back = back.reshape(all_rows, 3 * head_cols)
    projected = projected.reshape(all_rows, 3 * head_cols)
    grads = []
    for part in range(2):
        columns = slice(part * head_cols, (part + 1) * head_cols)
        scale = flat_scales[:, part : part + 1]
        normed = projected[:, columns] * scale
        grads.append(scale * (back[:, columns] - normed * dots[part]))
    grad_proj = jnp.concatenate(grads + [back[:, 2 * head_cols :]], axis=-1).astype(LOW)
    grad_one = contract_cols(grad_proj, qkv_here)
    grad_gain_attn = jnp.sum(grad_one * normed_all, axis=0)
    grad_one = grad_one.astype(LOW).reshape(line_count, row_count, model_dim)
    grad_w_qkv = contract_rows(hidden_one, grad_proj)

    out_cols = model_dim // dp_count
    qkv_parts = grad_w_qkv.astype(LOW).reshape(dp_count, out_cols, 3 * head_cols)
    shared = jnp.concatenate([grad_router, grad_gain_attn[None], grad_gain_mlp[None]], axis=0)
    tall = shared.shape[0] + -shared.shape[0] % 8
    shared = jnp.pad(shared, ((0, tall - shared.shape[0]), (0, 0)))
    shared = shared.reshape(tall, dp_count, line_count, shard).transpose(2, 1, 0, 3)
    shared = shared.reshape(line_count, dp_count * tall, shard)
    shared = jnp.pad(shared, ((0, 0), (0, 0), (0, 128 - shard)))
    grad_one, qkv_parts, out_parts, gain_pair, shared = closing(
        line_count, dp_count, grad_one, 4, [qkv_parts, out_parts, gain_pair], shared, 14
    )
    out_rows = lax.optimization_barrier((out_rows, grad_one))[0]
    mixture = line_reduce(line_count, collect(returns, out_rows), 4, 10).astype(FULL)
    output = (residual + mixture).astype(LOW)
    sum_qkv = jnp.sum(qkv_parts.astype(FULL), axis=0).reshape(out_cols, 3, head_cols)
    sum_out = jnp.sum(out_parts.astype(FULL), axis=0)
    gain_pair = jnp.sum(gain_pair, axis=0)
    shared = shared[:, :shard]
    grad_one = grad_one.astype(FULL)
    grad_inputs = grad_resid + norm_back(grad_one * gain_attn, normed_attn, scale_attn)
    return (
        output,
        grad_inputs,
        sum_qkv,
        sum_out,
        shared[:expert_count].T,
        shared[expert_count],
        shared[expert_count + 1],
        gain_pair[0],
        gain_pair[1],
        sum_gate_up.astype(FULL),
        sum_down.astype(FULL),
    )


def solution(mesh):
    both = ("dp", "expert")
    rows, flat = P(both, None), P(both)
    placed = (rows,) * 7 + (flat,) * 4 + (P("expert", None, None),) * 2
    return jax.shard_map(
        functools.partial(on_device, mesh.shape["dp"], mesh.shape["expert"]),
        mesh=mesh,
        in_specs=placed,
        out_specs=(
            rows,
            rows,
            P("dp", None, "expert"),
            P("expert", "dp"),
            rows,
            flat,
            flat,
            P("expert"),
            P("expert"),
            P("expert", "dp", None),
            P("expert", "dp", None),
        ),
        check_vma=False,
    )
```

time: 2170 us -> 842 us (0.39)
  waiting for transfers between devices: 1250 us -> 0.82 us
  Pallas kernels: 0 us -> 702 us
  blocking collectives: 454 us -> 0 us
  matrix products: 198 us -> 33.9 us
  local copies, waits for them, and re-layouts: 140 us -> 43.6 us
  other arithmetic: 88 us -> 41 us
    pallas_call x0 -> x19, Pallas kernels: none -> 702 us  [the longest x9 425 us: call(): pl.pallas_call(kernel, out_shape=outs, in_specs=[ANY] * len(arrays), out_...]
    reduce_scatter x6 -> x3, waiting for transfers between devices: 588 us -> 0.04 us  [on_device(): lax.psum_scatter(grads, 'dp', scatter_dimension=0, tiled=True)]
    all_to_all x2 -> x0, waiting for transfers between devices: 397 us -> none  [the longest x1 202 us: on_device(): lax.all_to_all(expert_out, 'expert', split_axis=1, concat_axis=0, tiled=T...]
    all_to_all x2 -> x0, blocking collectives: 316 us -> none  [the longest x1 160 us: on_device(): lax.all_to_all(back_send, 'expert', split_axis=0, concat_axis=1, tiled=True)]
    dot_general x17 -> x4, matrix products: 150 us -> 12.4 us  [the longest x1 6.59 us: on_device(): projected = jnp.dot(hidden_one, qkv_here, preferred_element_type=FULL)]
    all_gather x2, waiting for transfers between devices: 133 us -> 0.02 us  [the longest x1 0.02 us: on_device(): out_full = lax.all_gather(w_out, ('dp', 'expert'), axis=0, tiled=True)]
    unnamed x12 -> x5, waiting for transfers between devices: 129 us -> 0.75 us
    unnamed x3 -> x0, blocking collectives: 100 us -> none
  transfers between devices with their start and end apart: 12 -> 5, of which waited for: 10 -> 0; matrix products, arithmetic and copies ran while one was open for 9% -> 11% of each run, Pallas kernels for 0% -> 78%
where the time goes in v2:
time: 842 us; the launch traced here: 837 us
  Pallas kernels  702 us (83%)
  local copies, waits for them, and re-layouts  43.6 us (5%)
  other arithmetic  41 us (5%)
  matrix products  33.9 us (4%)
  between operations  14.8 us (2%)
    pallas_call x9, Pallas kernels, call(): pl.pallas_call(kernel, out_shape=outs, in_specs=[ANY] * len(arrays), out_...  425 us
    pallas_call x3, Pallas kernels, expert(): pl.pallas_call(functools.partial(expert_kernel, tiles), out_shape=[jax.Sh...  119 us
    pallas_call x1, Pallas kernels, closing(): pl.pallas_call(functools.partial(closing_kernel, size, dp_count, cuts, su...  82.7 us
    pallas_call x2, Pallas kernels, collect(): pl.pallas_call(collect_kernel, out_shape=jax.ShapeDtypeStruct((groups, to...  21.9 us
    pallas_call x1, Pallas kernels, attend_back(): pl.pallas_call(functools.partial(attend_back_kernel, heads), out_shape=[b...  21.8 us
    pallas_call x2, Pallas kernels, place_rows(): pl.pallas_call(functools.partial(rows_kernel, local_count), out_shape=jax...  19.3 us
    unnamed x93, local copies, waits for them, and re-layouts  17.5 us
  transfers between devices with their start and end apart: 5, of which 0 were waited for; matrix products, arithmetic and copies ran while one was open for 11% of the time, Pallas kernels for 78%

profile of v2, /device:TPU:16, one launch (start us, length us, event | category | flops | bytes accessed | tf_op | source)
XLA Modules:
  0.0 837.4 jit_solution(3028011788225919696)
XLA Ops:
  15.1 111.2 %opening.1 = (bf16[8,192,2048]{2,1,0:T(8,128)(2,1)}, s32[8,16,192]{2,1,0:T(8,128)S(1)}, bf16[4,8,64,768]{3,2,1,0:T(8,128)(2,1)S(1)}, bf16[4,8,64,128]{3,2,1,0:T(8,128)(2,1)S(1)}) custom-call(bf16[192,2048]{1,0:T(8,128)(2,1)S(1)} %copy-done.1, s32[16,192]{1,0:T(8,128)S(1)} %add_add_fusion.refs_1_, bf16[64,6144]{1,0:T(8,128)(2,1)S(1)} %copy-done.9, ...), custom_call_target="tpu_custom_call" | custom-call | bytes 200000000 | tf_op jit(solution)/shard_map/opening/pallas_call | solution.py:157
  138.0 6.6 fusion.47
  147.1 12.6 %exchange_expert.4 = f32[8,16,192]{2,1,0:T(8,128)S(1)} custom-call(f32[16,192]{1,0:T(8,128)S(1)} %reshape.186.refs_0_), custom_call_target="tpu_custom_call" | custom-call | bytes 30000000 | tf_op jit(solution)/shard_map/exchange_expert/pallas_call | solution.py:157
  162.9 12.6 %attend.1 = (bf16[8,192,768]{2,1,0:T(8,128)(2,1)}, bf16[8,192,256]{2,1,0:T(8,128)(2,1)}) custom-call(f32[8,192,768]{2,1,0:T(8,128)} %bitcast.9.rows_ref, f32[8,192,2]{2,1,0:T(8,128)} %bitcast.115, f32[2,256]{1,0:T(2,128)} %pad_maximum_fusion.6.gain_ref, f32[2,192,128]{2,1,0:T(8,128)} %pad_maximum_fusion.3.turn_ref, s32[8,192,1]{2,1,0:T(8,128)} %copy.87.column_ref, ...), custom_call_target="tpu_custom_call" | custom-call | flops 905969664 | bytes 9437184 | tf_op jit(solution)/shard_map/attend/pallas_call | solution.py:834
  176.6 34.5 %exchange_expert.5 = bf16[8,192,256]{2,1,0:T(8,128)(2,1)S(1)} custom-call(bf16[8,192,256]{2,1,0:T(8,128)(2,1)S(1)} %copy-done.4), custom_call_target="tpu_custom_call" | custom-call | bytes 30000000 | tf_op jit(solution)/shard_map/exchange_expert/pallas_call | solution.py:157
  212.4 5.3 multiply_reduce_fusion.4
  219.1 53.5 %line_gather.2 = (bf16[8,192,2048]{2,1,0:T(8,128)(2,1)}, f32[8,24,192]{2,1,0:T(8,128)S(1)}) custom-call(bf16[192,2048]{1,0:T(8,128)(2,1)S(1)} %multiply_convert_fusion.2.refs_0_, f32[24,192]{1,0:T(8,128)S(1)} %fusion.35.refs_1_), custom_call_target="tpu_custom_call" | custom-call | bytes 150000000 | tf_op jit(solution)/shard_map/line_gather/pallas_call | solution.py:157
  273.1 9.7 %place_rows.2.x_ref = bf16[3,576,2048]{2,1,0:T(8,128)(2,1)} custom-call(bf16[8,216,192]{2,1,0:T(8,128)(2,1)} %fusion.5.table_ref, bf16[8,192,2048]{2,1,0:T(8,128)(2,1)} %get-tuple-element.52.rows_ref), custom_call_target="tpu_custom_call" | custom-call | flops 1358954496 | bytes 12582912 | tf_op jit(solution)/shard_map/place_rows/pallas_call | solution.py:560
  282.8 9.6 %place_rows.3.dy_ref = bf16[3,576,2048]{2,1,0:T(8,128)(2,1)} custom-call(bf16[8,216,192]{2,1,0:T(8,128)(2,1)} %fusion.5.table_ref, bf16[8,192,2048]{2,1,0:T(8,128)(2,1)} %bitcast.129), custom_call_target="tpu_custom_call" | custom-call | flops 1358954496 | bytes 12582912 | tf_op jit(solution)/shard_map/place_rows/pallas_call | solution.py:560
  293.6 39.6 %expert.5 = (bf16[4,768,2048]{2,1,0:T(8,128)(2,1)}, bf16[1,576,2048]{2,1,0:T(8,128)(2,1)}, bf16[1,576,2048]{2,1,0:T(8,128)(2,1)}, f32[1,576,1]{2,1,0:T(8,128)}) custom-call(bf16[3,576,2048]{2,1,0:T(8,128)(2,1)} %place_rows.2.x_ref, bf16[3,576,2048]{2,1,0:T(8,128)(2,1)} %place_rows.3.dy_ref, f32[3,576,1]{2,1,0:T(8,128)} %reshape.204.scale_ref, ...), custom_call_target="tpu_custom_call" | custom-call | flops 21743271936 | bytes 25165824 | tf_op jit(solution)/shard_map/expert/pallas_call | solution.py:701
  333.8 39.7 %expert.4 = (bf16[4,768,2048]{2,1,0:T(8,128)(2,1)}, bf16[1,576,2048]{2,1,0:T(8,128)(2,1)}, bf16[1,576,2048]{2,1,0:T(8,128)(2,1)}, f32[1,576,1]{2,1,0:T(8,128)}) custom-call(bf16[3,576,2048]{2,1,0:T(8,128)(2,1)} %place_rows.2.x_ref, bf16[3,576,2048]{2,1,0:T(8,128)(2,1)} %place_rows.3.dy_ref, f32[3,576,1]{2,1,0:T(8,128)} %reshape.204.scale_ref, ...), custom_call_target="tpu_custom_call" | custom-call | flops 21743271936 | bytes 25165824 | tf_op jit(solution)/shard_map/expert/pallas_call | solution.py:701
  373.7 39.6 %expert.3 = (bf16[4,768,2048]{2,1,0:T(8,128)(2,1)}, bf16[1,576,2048]{2,1,0:T(8,128)(2,1)}, bf16[1,576,2048]{2,1,0:T(8,128)(2,1)}, f32[1,576,1]{2,1,0:T(8,128)}) custom-call(bf16[3,576,2048]{2,1,0:T(8,128)(2,1)} %place_rows.2.x_ref, bf16[3,576,2048]{2,1,0:T(8,128)(2,1)} %place_rows.3.dy_ref, f32[3,576,1]{2,1,0:T(8,128)} %reshape.204.scale_ref, ...), custom_call_target="tpu_custom_call" | custom-call | flops 21743271936 | bytes 25165824 | tf_op jit(solution)/shard_map/expert/pallas_call | solution.py:701
  423.0 9.8 %exchange_expert.6 = f32[8,3,192]{2,1,0:T(4,128)S(1)} custom-call(f32[8,3,192]{2,1,0:T(4,128)S(1)} %fusion.3.refs_0_), custom_call_target="tpu_custom_call" | custom-call | bytes 30000000 | tf_op jit(solution)/shard_map/exchange_expert/pallas_call | solution.py:157
  432.8 11.1 %collect.2.refs_0_ = bf16[8,192,2048]{2,1,0:T(8,128)(2,1)} custom-call(bf16[8,192,72]{2,1,0:T(8,128)(2,1)} %get-tuple-element.153.refs_0_, bf16[8,192,72]{2,1,0:T(8,128)(2,1)} %get-tuple-element.154.refs_1_, bf16[8,192,72]{2,1,0:T(8,128)(2,1)} %fusion.19.refs_2_, bf16[1,576,2048]{2,1,0:T(8,128)(2,1)} %get-tuple-element.59.refs_3_, ...), custom_call_target="tpu_custom_call" | custom-call | flops 1358954496 | bytes 12582912 | tf_op jit(solution)/shard_map/collect/pallas_call | solution.py:587
  443.9 67.0 %line_reduce.2 = bf16[192,2048]{1,0:T(8,128)(2,1)S(1)} custom-call(bf16[8,192,2048]{2,1,0:T(8,128)(2,1)} %collect.2.refs_0_), custom_call_target="tpu_custom_call" | custom-call | bytes 150000000 | tf_op jit(solution)/shard_map/line_reduce/pallas_call | solution.py:157
  513.0 52.4 %line_gather.3.grad_ref = bf16[8,192,2048]{2,1,0:T(8,128)(2,1)} custom-call(bf16[192,2048]{1,0:T(8,128)(2,1)S(1)} %fusion.42.refs_0_), custom_call_target="tpu_custom_call" | custom-call | bytes 150000000 | tf_op jit(solution)/shard_map/line_gather/pallas_call | solution.py:157
  567.1 21.8 %attend_back.1 = (f32[8,192,768]{2,1,0:T(8,128)}, f32[8,192,2]{2,1,0:T(8,128)S(1)}, f32[2,256]{1,0:T(2,128)S(1)}, bf16[4,256,512]{2,1,0:T(8,128)(2,1)S(1)}) custom-call(bf16[8,192,2048]{2,1,0:T(8,128)(2,1)} %line_gather.3.grad_ref, bf16[256,2048]{1,0:T(8,128)(2,1)S(1)} %constant_dynamic-slice_fusion.w_ref, bf16[8,192,768]{2,1,0:T(8,128)(2,1)} %get-tuple-element.65.kept_ref, ...), custom_call_target="tpu_custom_call" | custom-call | flops 3221225472 | bytes 31457280 | tf_op jit(solution)/shard_map/attend_back/pallas_call | solution.py:926
  591.2 9.1 %exchange_expert.7 = f32[8,16,192]{2,1,0:T(8,128)S(1)} custom-call(f32[16,192]{1,0:T(8,128)S(1)} %bitcast.123), custom_call_target="tpu_custom_call" | custom-call | bytes 30000000 | tf_op jit(solution)/shard_map/exchange_expert/pallas_call | solution.py:157
  606.5 11.1 %multiply_reduce_fusion = (f32[2048]{0:T(1024)S(1)}, bf16[1536,2048]{1,0:T(8,128)(2,1)}, bf16[1536,2048]{1,0:T(8,128)(2,1)}) fusion(bf16[8,192,2048]{2,1,0:T(8,128)(2,1)} %get-tuple-element.47, f32[1536]{0:T(1024)S(1)} %copy-done.44, f32[2048]{0:T(1024)S(1)} %bitcast.143, bf16[2048,768]{1,0:T(8,128)(2,1)S(1)} %bitcast.125, ...), kind=kOutput, calls=%fused_computation.1 | convolution fusion | flops 4860934144 | bytes 24401920 | tf_op jit(solution)/shard_map/dot_general | solution.py:770
  618.3 9.4 %convolution_convert_fusion = bf16[2048,768]{1,0:T(8,128)(2,1)} fusion(bf16[1536,2048]{1,0:T(8,128)(2,1)} %get-tuple-element.124, bf16[1536,256]{1,0:T(8,128)(2,1)} %copy-done.26, bf16[1536,256]{1,0:T(8,128)(2,1)} %copy-done.28, bf16[1536,256]{1,0:T(8,128)(2,1)} %copy-done.27), kind=kOutput, calls=%fused_computation.7 | convolution fusion | flops 4840488960 | bytes 11796480 | tf_op jit(solution)/shard_map/dot_general | solution.py:764
  627.6 82.7 %closing.1 = (bf16[192,2048]{1,0:T(8,128)(2,1)S(1)}, bf16[4,512,768]{2,1,0:T(8,128)(2,1)}, bf16[4,256,512]{2,1,0:T(8,128)(2,1)S(1)}, f32[4,2,256]{2,1,0:T(2,128)S(1)}, f32[32,128]{1,0:T(8,128)S(1)}) custom-call(bf16[8,192,2048]{2,1,0:T(8,128)(2,1)} %bitcast.130, bf16[4,512,768]{2,1,0:T(8,128)(2,1)} %bitcast.135, ...), custom_call_target="tpu_custom_call" | custom-call | bytes 200000000 | tf_op jit(solution)/shard_map/closing/pallas_call | solution.py:530
  721.5 10.8 %collect.3.refs_0_ = bf16[8,192,2048]{2,1,0:T(8,128)(2,1)} custom-call(bf16[8,192,72]{2,1,0:T(8,128)(2,1)} %get-tuple-element.153.refs_0_, bf16[8,192,72]{2,1,0:T(8,128)(2,1)} %get-tuple-element.154.refs_1_, bf16[8,192,72]{2,1,0:T(8,128)(2,1)} %fusion.19.refs_2_, bf16[1,576,2048]{2,1,0:T(8,128)(2,1)} %get-tuple-element.71.refs_3_, ...), custom_call_target="tpu_custom_call" | custom-call | flops 1358954496 | bytes 12582912 | tf_op jit(solution)/shard_map/collect/pallas_call | solution.py:587
  732.3 74.9 %line_reduce.3 = bf16[192,2048]{1,0:T(8,128)(2,1)S(1)} custom-call(bf16[8,192,2048]{2,1,0:T(8,128)(2,1)} %collect.3.refs_0_), custom_call_target="tpu_custom_call" | custom-call | bytes 150000000 | tf_op jit(solution)/shard_map/line_reduce/pallas_call | solution.py:157
  824.9 5.8 maximum_convert_fusion
  (211 shorter events, 82.3 us)
Async XLA Ops:
  7.2 205.2 %all-gather.4.cloned.1.call-start = ((), (), s32[]{:S(2)}) async-start(), calls=%async_computation.3 | async-start | bytes 8650752 | tf_op jit(solution)/shard_map/all_gather | solution.py:979
  7.9 274.9 %all-gather.6.cloned.1.call-start = ((), (), s32[]{:S(2)}) async-start(), calls=%async_computation.7 | async-start | bytes 7077888 | tf_op jit(solution)/shard_map/all_gather | solution.py:981
  127.9 685.7 %reduce-scatter.8.cloned.1.call-start = ((), (), s32[]{:S(2)}) async-start(), calls=%async_computation.6 | async-start | bytes 15728640 | tf_op jit(solution)/shard_map/reduce_scatter | solution.py:1050
  175.4 37.0 %copy-start.2 = (bf16[192,2048]{1,0:T(8,128)(2,1)S(1)}, bf16[192,2048]{1,0:T(8,128)(2,1)}, u32[]{:S(2)}) copy-start(bf16[192,2048]{1,0:T(8,128)(2,1)} %refs_0_.1) | copy-start | bytes 2359300
  176.6 35.7 %copy-start.34 = (s32[192,8]{0,1:T(8,128)S(1)}, s32[192,8]{0,1:T(8,128)}, u32[]{:S(2)}) copy-start(s32[192,8]{0,1:T(8,128)} %param.16) | copy-start | bytes 18436
  219.0 53.6 %copy-start.37 = (f32[192]{0:T(256)}, f32[192]{0:T(256)S(1)}, u32[]{:S(2)}) copy-start(f32[192]{0:T(256)S(1)} %get-tuple-element.147) | copy-start | bytes 2308
  219.0 53.6 %copy-start.41 = (f32[192]{0:T(256)}, f32[192]{0:T(256)S(1)}, u32[]{:S(2)}) copy-start(f32[192]{0:T(256)S(1)} %fusion.38) | copy-start | bytes 2308
  333.3 481.7 %reduce-scatter.6.cloned.1.call-start = ((), (), s32[]{:S(2)}) async-start(), calls=%async_computation.5 | async-start | bytes 15728640 | tf_op jit(solution)/shard_map/reduce_scatter | solution.py:1050
  373.5 442.8 %reduce-scatter.4.cloned.1.call-start = ((), (), s32[]{:S(2)}) async-start(), calls=%async_computation.4 | async-start | bytes 15728640 | tf_op jit(solution)/shard_map/reduce_scatter | solution.py:1050
  413.4 5.9 copy-start.29
  413.4 7.4 copy-start.30
  443.9 67.0 %copy-start.38 = (f32[192]{0:T(256)S(1)}, f32[192]{0:T(256)}, u32[]{:S(2)}) copy-start(f32[192]{0:T(256)} %copy-done.37) | copy-start | bytes 2308
  443.9 67.0 %copy-start.42 = (f32[192]{0:T(256)S(1)}, f32[192]{0:T(256)}, u32[]{:S(2)}) copy-start(f32[192]{0:T(256)} %copy-done.41) | copy-start | bytes 2308
  443.9 67.1 %copy-start.18 = (f32[192,2048]{1,0:T(8,128)S(1)}, f32[192,2048]{1,0:T(8,128)}, u32[]{:S(2)}) copy-start(f32[192,2048]{1,0:T(8,128)} %copy-done.17) | copy-start | bytes 4718596
  443.9 67.1 %copy-start.40 = (f32[192]{0:T(256)S(1)}, f32[192]{0:T(256)}, u32[]{:S(2)}) copy-start(f32[192]{0:T(256)} %copy-done.39) | copy-start | bytes 2308
  513.0 53.9 %copy-start.6 = (f32[2,192,128]{2,1,0:T(8,128)S(1)}, f32[2,192,128]{2,1,0:T(8,128)}, u32[]{:S(2)}) copy-start(f32[2,192,128]{2,1,0:T(8,128)} %pad_maximum_fusion.3.turn_ref) | copy-start | bytes 589828
  513.0 53.9 %copy-start.11 = (s32[8,1,192]{2,1,0:T(1,128)S(1)}, s32[8,1,192]{2,1,0:T(1,128)}, u32[]{:S(2)}) copy-start(s32[8,1,192]{2,1,0:T(1,128)} %get-tuple-element.127.row_ref) | copy-start | bytes 18436
  513.0 53.9 %copy-start.12 = (f32[2,256]{1,0:T(2,128)S(1)}, f32[2,256]{1,0:T(2,128)}, u32[]{:S(2)}) copy-start(f32[2,256]{1,0:T(2,128)} %pad_maximum_fusion.6.gain_ref) | copy-start | bytes 6148
  589.7 12.5 %copy-start.35 = (f32[1536]{0:T(1024)S(1)}, f32[1536]{0:T(1024)}, u32[]{:S(2)}) copy-start(f32[1536]{0:T(1024)} %get-tuple-element.118) | copy-start | bytes 18436
  589.7 12.5 %copy-start.36 = (f32[1536]{0:T(1024)S(1)}, f32[1536]{0:T(1024)}, u32[]{:S(2)}) copy-start(f32[1536]{0:T(1024)} %get-tuple-element.119) | copy-start | bytes 18436
  606.3 11.4 %copy-start.27 = (bf16[1536,256]{1,0:T(8,128)(2,1)}, bf16[1536,256]{1,0:T(8,128)(2,1)S(1)}, u32[]{:S(2)}) copy-start(bf16[1536,256]{1,0:T(8,128)(2,1)S(1)} %get-tuple-element.122) | copy-start | bytes 2359300
  606.3 11.4 %copy-start.28 = (bf16[1536,256]{1,0:T(8,128)(2,1)}, bf16[1536,256]{1,0:T(8,128)(2,1)S(1)}, u32[]{:S(2)}) copy-start(bf16[1536,256]{1,0:T(8,128)(2,1)S(1)} %get-tuple-element.123) | copy-start | bytes 2359300
  732.3 74.9 %copy-start.8 = (bf16[4,256,512]{2,1,0:T(8,128)(2,1)S(1)}, bf16[4,256,512]{2,1,0:T(8,128)(2,1)}, u32[]{:S(2)}) copy-start(bf16[4,256,512]{2,1,0:T(8,128)(2,1)} %copy-done.7) | copy-start | bytes 3145732
  732.3 75.9 %copy-start.43 = (f32[192]{0:T(256)S(1)}, f32[192]{0:T(256)}, u32[]{:S(2)}) copy-start(f32[192]{0:T(256)} %add_rsqrt_fusion.1) | copy-start | bytes 2308
  (26 other events, 53.0 us)
Sparse Core Ops, SparseCore 0:
  11.0 104.9 all-gather.3
  128.1 81.9 all-gather.5
  333.4 124.6 reduce-scatter.7
  461.0 120.7 reduce-scatter.5
  584.7 165.3 reduce-scatter.3

commit v3 on v2

--- a/solution.py
+++ b/solution.py
@@ -122,11 +122,15 @@
             pl.when(self.has_down)(self.down(q, step).start)
             self.across(q, -step).start()
 
-    def finish(self):
+    def land_across(self, block):
         for q in range(len(self.pieces)):
+            self.sending(q, block, False, self.side_sem.at[0, q], self.other).wait_recv()
+
+    def finish(self, landed=False, held=0):
+        if not landed:
             for far in range(self.levels):
-                block = 2 * far + 1 - self.side
-                self.sending(q, block, False, self.side_sem.at[0, q], self.other).wait_recv()
+                self.land_across(2 * far + 1 - self.side)
+        for q in range(len(self.pieces)):
             self.across(q, 0).wait_send()
             for step in range(self.levels):
                 above, below = self.level >= step, self.level + step < self.levels
@@ -135,7 +139,7 @@
                 if step:
                     pl.when(above)(self.across(q, step).wait_send)
                     pl.when(below)(self.across(q, -step).wait_send)
-        for copy in self.own:
+        for copy in self.own[held:]:
             copy.wait()
 
     def run(self):
@@ -183,6 +187,7 @@
 class LineReduce:
     def __init__(self, levels, cuts, parts, total, own, beside, rising, falling, *sems):
         self.levels, self.cuts, self.parts, self.total = levels, cuts, parts, total
+        self.made = parts.shape[0] == levels
         self.own, self.beside, self.rising, self.falling = own, beside, rising, falling
         self.load_sem, self.side_send, self.side_recv = sems[:3]
         self.up_send, self.up_recv, self.down_send, self.down_recv, self.out_sem = sems[3:]
@@ -212,7 +217,7 @@
         return pltpu.make_async_copy(source, self.cut(self.own, far, k), self.load_sem.at[far, k])
 
     def across(self, far, k):
-        source = self.cut(self.parts, 2 * far + 1 - self.side, k)
+        source = self.cut(self.parts, far if self.made else 2 * far + 1 - self.side, k)
         sems = self.side_send.at[far, k], self.side_recv.at[far, k]
         return remote(source, self.cut(self.beside, far, k), *sems, {"expert": self.other})
 
@@ -239,8 +244,17 @@
             for k in range(self.cuts):
                 self.across(far, k).start()
 
+    def prepare(self, far, which, make):
+        if which == 0:
+            make(2 * far + 1 - self.side, self.parts.at[far])
+            for k in range(self.cuts):
+                self.across(far, k).start()
+        else:
+            make(2 * far + self.side, self.own.at[far])
+
     def pair(self, far, k):
-        self.loading(far, k).wait()
+        if not self.made:
+            self.loading(far, k).wait()
         self.across(far, k).wait_recv()
         return self.value(self.own, far, k) + self.value(self.beside, far, k)
 
@@ -296,28 +310,6 @@
                 pl.when(self.level > far)(self.down(far, k).wait_send)
 
 
-def line_reduce_kernel(levels, cuts, *refs):
-    line = LineReduce(levels, cuts, *refs)
-    line.load()
-    line_barrier(levels)
-    line.begin()
-    line.main()
-    line.finish()
-
-
-def line_reduce(size, parts, cuts, number):
-    block = parts.shape[1:]
-    return call(
-        functools.partial(line_reduce_kernel, size // 2, cuts),
-        "line_reduce",
-        number,
-        [jax.ShapeDtypeStruct(block, parts.dtype)],
-        LineReduce.scratch(size, block, parts.dtype, cuts),
-        [parts],
-        150_000_000,
-    )[0]
-
-
 class Exchange:
     def __init__(self, axis, size, spread, cuts, ins, outs, send_sem, recv_sem, own_sem):
         self.axis, self.spread, self.ins, self.outs = axis, spread, ins, outs
@@ -408,17 +400,21 @@
 
 
 def opening_kernel(size, dp_count, cuts, *refs):
-    count = len(cuts)
-    ins, w_ref, small_ref = refs[:count], refs[count], refs[count + 1]
-    outs, w_out, small_out = refs[count + 2 : 2 * count + 2], refs[2 * count + 2], refs[2 * count + 3]
-    line_sems, rest = refs[2 * count + 4 : 2 * count + 9], refs[2 * count + 9 :]
-    send_sem, recv_sem, own_sem = rest[:3]
-    line = LineGather(size // 2, cuts, ins, outs, *line_sems)
+    count, levels = len(cuts), size // 2
+    ins, (w_ref, small_ref, sheet_ref) = refs[:count], refs[count : count + 3]
+    outs, rest = refs[count + 3 : 2 * count + 3], refs[2 * count + 3 :]
+    w_out, small_out, sheet_out = rest[:3]
+    line = LineGather(levels, cuts, ins, outs, *rest[3:8])
+    send_sem, recv_sem, own_sem = rest[8:11]
+    level, side, other = line.level, line.side, line.other
     place, mine = line.place, lax.axis_index("dp")
     peers = around("expert", size)
     width = w_out.shape[3] // 3
     mine_refs = [w_out.at[mine], small_out.at[mine]]
-    across = Exchange("dp", dp_count, (True,) * 2, (size,) * 2, mine_refs, [w_out, small_out], *rest[3:])
+    across = Exchange(
+        "dp", dp_count, (True,) * 2, (size,) * 2, mine_refs, [w_out, small_out], *rest[11:14]
+    )
+    up_send, down_send, line_recv, dp_send, dp_recv, side_send, side_recv, sheet_own = rest[14:]
     greet("expert", [(peer, None) for peer in peers])
     greet("dp", [(peer, None) for peer in across.peers])
     pl.semaphore_wait(pltpu.get_barrier_semaphore(), size + dp_count - 2)
@@ -435,12 +431,45 @@
         sems = send_sem.at[shift, j], recv_sem.at[landing, j]
         return remote(source, target, *sems, {"expert": peers[shift]})
 
+    def sheet_line(far, own, send, target):
+        landing = sheet_out.at[mine, 2 * far + side]
+        source = sheet_ref if own else landing
+        return remote(source, landing, send.at[far], line_recv.at[far], {"expert": target})
+
+    def sheet_up(far, own=False):
+        return sheet_line(far, own, up_send, place + 2)
+
+    def sheet_down(far, own=False):
+        return sheet_line(far, own, down_send, place - 2)
+
+    def sheet_dp(far, shift, copy, own=False):
+        landing = sheet_out.at[copy, 2 * far + side]
+        source = sheet_ref if own else landing
+        sems = dp_send.at[shift, far], dp_recv.at[copy, far]
+        return remote(source, landing, *sems, {"dp": across.peers[shift]})
+
+    def sheet_side(far, copy, whose, own=False):
+        landing = sheet_out.at[copy, 2 * far + whose]
+        source = sheet_ref if own else landing
+        sems = side_send.at[copy, far], side_recv.at[copy, far]
+        return remote(source, landing, *sems, {"expert": other})
+
+    def spread_sheet(far, own=False):
+        for shift in range(dp_count - 1):
+            sheet_dp(far, shift, mine, own).start()
+        sheet_side(far, mine, side, own).start()
+
     own = [pltpu.make_async_copy(*ends(place, place, j), own_sem.at[j]) for j in range(4)]
+    sheet_stays = pltpu.make_async_copy(sheet_ref, sheet_out.at[mine, place], sheet_own.at[0])
     for shift in range(size - 1):
         for j in range(4):
             sending(shift, place, j).start()
     for copy in own:
         copy.start()
+    sheet_stays.start()
+    pl.when(line.has_up)(sheet_up(level, True).start)
+    pl.when(line.has_down)(sheet_down(level, True).start)
+    spread_sheet(level, True)
     line.begin()
     for copy in own:
         copy.wait()
@@ -451,24 +480,52 @@
             sending(shift, peer, j).wait_recv()
         across.send(0, peer)
         across.send(1, peer)
-    for step in range(1, size // 2):
+    for step in range(1, levels):
+
+        @pl.when(level >= step)
+        def _():
+            sheet_up(level - step).wait_recv()
+            pl.when(line.has_up)(sheet_up(level - step).start)
+            spread_sheet(level - step)
+
+        @pl.when(level + step < levels)
+        def _():
+            sheet_down(level + step).wait_recv()
+            pl.when(line.has_down)(sheet_down(level + step).start)
+            spread_sheet(level + step)
+
         for q in range(len(line.pieces)):
             line.forward(step, q)
+    for shift, peer in enumerate(across.peers):
+        for far in range(levels):
+            sheet_dp(far, shift, peer).wait_recv()
+            sheet_side(far, peer, side).start()
     line.finish()
     for shift in range(size - 1):
         for j in range(4):
             sending(shift, place, j).wait_send()
     across.land()
     across.finish()
-
-
-def opening(size, dp_count, arrays, cuts, weights, small, number):
+    for far in range(levels):
+        pl.when(line.has_up & (level >= far))(sheet_up(far).wait_send)
+        pl.when(line.has_down & (level <= far))(sheet_down(far).wait_send)
+        for shift in range(dp_count - 1):
+            sheet_dp(far, shift, mine).wait_send()
+        for copy in range(dp_count):
+            sheet_side(far, copy, 1 - side).wait_recv()
+            sheet_side(far, copy, side).wait_send()
+    sheet_stays.wait()
+
+
+def opening(size, dp_count, arrays, cuts, weights, small, sheet, number):
     sems = pltpu.SemaphoreType.DMA
+    levels = size // 2
     outs = [jax.ShapeDtypeStruct((size,) + a.shape, a.dtype) for a in arrays]
     rows, columns = weights.shape
     whole = (dp_count, size, rows)
     outs.append(jax.ShapeDtypeStruct(whole + (columns // size,), weights.dtype))
     outs.append(jax.ShapeDtypeStruct(whole + (small.shape[1],), small.dtype))
+    outs.append(jax.ShapeDtypeStruct((dp_count, size) + sheet.shape, sheet.dtype))
     return call(
         functools.partial(opening_kernel, size, dp_count, tuple(cuts)),
         "opening",
@@ -476,25 +533,185 @@
         outs,
         LineGather.scratch(size, cuts)
         + [sems((size, 4)), sems((size, 4)), sems((4,))]
-        + Exchange.scratch(dp_count, (size, size)),
-        list(arrays) + [weights, small],
+        + Exchange.scratch(dp_count, (size, size))
+        + [sems((levels,))] * 3
+        + [sems((dp_count, levels))] * 4
+        + [sems((1,))],
+        list(arrays) + [weights, small, sheet],
         200_000_000,
     )
 
 
+VMEM = pl.BlockSpec(memory_space=pltpu.VMEM)
+COLUMNS = 512
+
+
+def gather_place_kernel(levels, cuts, *refs):
+    rows_ref, gates_ref, table_ref, dy_ref, x_out, dy_out, gates_out = refs[:7]
+    held, dy_held, x_stage, dy_stage = refs[7:11]
+    line_sems, (dy_sem, x_sems, dy_sems) = refs[11:16], refs[16:]
+    line = LineGather(levels, cuts, [rows_ref, gates_ref], [held, gates_out], *line_sems)
+    size, width = 2 * levels, held.shape[2]
+    _, local_count, capacity, _ = x_stage.shape
+
+    def leaving(block, stage, out, sems):
+        target = out.at[:, pl.ds(pl.multiple_of(block * capacity, 8), capacity)]
+        return pltpu.make_async_copy(stage.at[block], target, sems.at[block])
+
+    def place(block, rows, stage, out, sems):
+        table = table_ref[block]
+
+        @pl.loop(0, width // COLUMNS)
+        def _(n):
+            columns = pl.ds(pl.multiple_of(n * COLUMNS, COLUMNS), COLUMNS)
+            placed = jnp.dot(table, rows[block, :, columns], preferred_element_type=FULL)
+            for j in range(local_count):
+                part = placed[j * capacity : (j + 1) * capacity]
+                stage[block, j, :, columns] = part.astype(stage.dtype)
+
+        leaving(block, stage, out, sems).start()
+
+    def place_x(block):
+        place(block, held, x_stage, x_out, x_sems)
+
+    loading = pltpu.make_async_copy(dy_ref, dy_held, dy_sem.at[0])
+    loading.start()
+    line_barrier(levels)
+    line.begin()
+    loading.wait()
+
+    @pl.loop(0, size)
+    def _(block):
+        place(block, dy_held, dy_stage, dy_out, dy_sems)
+
+    line.own[0].wait()
+    place_x(line.place)
+    for step in range(1, levels + 1):
+        if step < levels:
+            for q in range(len(line.pieces)):
+                line.forward(step, q)
+        for sign in (-1, 1):
+            far = line.level + sign * (step - 1)
+            there = (far >= 0) & (far < levels)
+            if step > 1 or sign > 0:
+
+                @pl.when(there)
+                def _():
+                    line.land_across(2 * far + 1 - line.side)
+                    place_x(2 * far + 1 - line.side)
+
+            near = line.level + sign * step
+            if step < levels:
+
+                @pl.when((near >= 0) & (near < levels))
+                def _():
+                    place_x(2 * near + line.side)
+
+    line.finish(landed=True, held=1)
+    for block in range(size):
+        leaving(block, x_stage, x_out, x_sems).wait()
+        leaving(block, dy_stage, dy_out, dy_sems).wait()
+
+
+def gather_place(size, rows, gates, table, dy, local_count, number):
+    cuts = (4, 1)
+    tokens, width = rows.shape
+    capacity = table.shape[1] // local_count
+    placed = jax.ShapeDtypeStruct((local_count, size * capacity, width), rows.dtype)
+    sems = pltpu.SemaphoreType.DMA
+    return pl.pallas_call(
+        functools.partial(gather_place_kernel, size // 2, cuts),
+        out_shape=[placed, placed, jax.ShapeDtypeStruct((size,) + gates.shape, gates.dtype)],
+        in_specs=[ANY, ANY, VMEM, ANY],
+        out_specs=[ANY] * 3,
+        scratch_shapes=[pltpu.VMEM((size, tokens, width), rows.dtype)] * 2
+        + [pltpu.VMEM((size, local_count, capacity, width), rows.dtype)] * 2
+        + LineGather.scratch(size, cuts)
+        + [sems((1,)), sems((size,)), sems((size,))],
+        compiler_params=pltpu.CompilerParams(
+            collective_id=number, has_side_effects=True, vmem_limit_bytes=48 << 20
+        ),
+        cost_estimate=pl.CostEstimate(
+            flops=4 * table.size * width, transcendentals=0, bytes_accessed=150_000_000
+        ),
+        name="gather_place",
+    )(rows, gates, table, dy)
+
+
+def collect_reduce_kernel(levels, cuts, local_count, *refs):
+    tables, slots, small_ref = refs[:local_count], refs[local_count : 2 * local_count], refs[2 * local_count]
+    total_ref, small_out = refs[2 * local_count + 1 : 2 * local_count + 3]
+    away, rest = refs[2 * local_count + 3], refs[2 * local_count + 4 :]
+    line = LineReduce(levels, cuts, away, total_ref, *rest[:12])
+    small = Exchange("expert", 2 * levels, (False,), (1,), [small_ref], [small_out], *rest[12:])
+    width = away.shape[2]
+    greet("expert", [(peer, None) for peer in small.peers])
+    pl.semaphore_wait(pltpu.get_barrier_semaphore(), 2 * levels - 1)
+
+    def make(block, target):
+        @pl.loop(0, width // COLUMNS)
+        def _(n):
+            columns = pl.ds(pl.multiple_of(n * COLUMNS, COLUMNS), COLUMNS)
+            total = 0.0
+            for table, rows in zip(tables, slots):
+                total += jnp.dot(table[block], rows[block, :, columns], preferred_element_type=FULL)
+            target[:, columns] = total.astype(target.dtype)
+
+    small.begin()
+    for far in line.order[:2]:
+        line.prepare(far, 0, make)
+        line.prepare(far, 1, make)
+    later = [(far, which) for far in line.order[2:] for which in (0, 1)]
+
+    def beside(turn):
+        if turn < len(later):
+            line.prepare(*later[turn], make)
+
+    line.main(beside)
+    small.arrive()
+    line.finish()
+    small.finish()
+
+
+def collect_reduce(size, tables, slots, small, number):
+    levels, cuts = size // 2, 4
+    block = (tables[0].shape[1], slots[0].shape[2])
+    kind = slots[0].dtype
+    return pl.pallas_call(
+        functools.partial(collect_reduce_kernel, levels, cuts, len(tables)),
+        out_shape=[
+            jax.ShapeDtypeStruct(block, kind),
+            jax.ShapeDtypeStruct(small.shape, small.dtype),
+        ],
+        in_specs=[VMEM] * (2 * len(tables)) + [ANY],
+        out_specs=[ANY, ANY],
+        scratch_shapes=[pltpu.VMEM((levels,) + block, kind)]
+        + LineReduce.scratch(size, block, kind, cuts)
+        + Exchange.scratch(size, (1,)),
+        compiler_params=pltpu.CompilerParams(
+            collective_id=number, has_side_effects=True, vmem_limit_bytes=48 << 20
+        ),
+        cost_estimate=pl.CostEstimate(flops=0, transcendentals=0, bytes_accessed=150_000_000),
+        name="collect_reduce",
+    )(*tables, *slots, small)
+
+
 def closing_kernel(size, dp_count, cuts, sum_cuts, *refs):
-    ins, outs, rest = refs[:5], refs[5:10], refs[10:]
-    line = LineReduce(size // 2, cuts, ins[0], outs[0], *rest[:12])
-    sums = Exchange("dp", dp_count, (False, False, True), sum_cuts, ins[1:4], outs[1:4], *rest[12:15])
-    got, half, last = rest[15:18]
-    first = Exchange("expert", size, (False,), (1,), ins[4:5], [got], *rest[18:21])
-    second = Exchange("dp", dp_count, (False,), (1,), [half], [last], *rest[21:24])
-    line.load()
+    ins, outs, rest = refs[:6], refs[6:12], refs[12:]
+    lines = [LineReduce(size // 2, cuts, ins[i], outs[i], *rest[12 * i : 12 * i + 12]) for i in (0, 1)]
+    rest = rest[24:]
+    sums = Exchange("dp", dp_count, (False, False, True), sum_cuts, ins[2:5], outs[2:5], *rest[:3])
+    got, half, last = rest[3:6]
+    first = Exchange("expert", size, (False,), (1,), ins[5:6], [got], *rest[6:9])
+    second = Exchange("dp", dp_count, (False,), (1,), [half], [last], *rest[9:12])
+    for line in lines:
+        line.load()
     greet("expert", [(peer, None) for peer in first.peers])
     greet("dp", [(peer, None) for peer in sums.peers])
     pl.semaphore_wait(pltpu.get_barrier_semaphore(), size + dp_count - 2)
     first.begin()
-    line.begin()
+    for line in lines:
+        line.begin()
     sums.stay()
     turns = (size // 2 - 1) * cuts
     tall = half.shape[1]
@@ -510,29 +727,29 @@
                 half[copy] = sum(got[i, rows, :] for i in range(size))
             second.begin()
 
-    line.main(beside)
+    lines[0].main(beside)
+    lines[1].main()
     second.arrive()
-    outs[4][...] = sum(last[i] for i in range(dp_count))
+    outs[5][...] = sum(last[i] for i in range(dp_count))
     sums.arrive()
-    for moves in (line, first, second, sums):
+    for moves in lines + [first, second, sums]:
         moves.finish()
 
 
 def closing(size, dp_count, parts, cuts, sums, shared, number):
-    block = parts.shape[1:]
+    block = parts[0].shape[1:]
     tall = shared.shape[1] // dp_count
     wide = shared.shape[2]
-    vmem = pl.BlockSpec(memory_space=pltpu.VMEM)
     sum_cuts = (8, 2, 1)
-    outs = [jax.ShapeDtypeStruct(block, parts.dtype)]
+    outs = [jax.ShapeDtypeStruct(block, parts[0].dtype)] * 2
     outs += exchange_outs(dp_count, sums, (False, False, True))
     outs.append(jax.ShapeDtypeStruct((tall, wide), FULL))
     return pl.pallas_call(
         functools.partial(closing_kernel, size, dp_count, cuts, sum_cuts),
         out_shape=outs,
-        in_specs=[ANY] * 5,
-        out_specs=[ANY] * 4 + [vmem],
-        scratch_shapes=LineReduce.scratch(size, block, parts.dtype, cuts)
+        in_specs=[ANY] * 6,
+        out_specs=[ANY] * 5 + [VMEM],
+        scratch_shapes=LineReduce.scratch(size, block, parts[0].dtype, cuts) * 2
         + Exchange.scratch(dp_count, sum_cuts)
         + [pltpu.VMEM((size,) + shared.shape[1:], FULL)]
         + [pltpu.VMEM((dp_count, tall, wide), FULL)] * 2
@@ -543,34 +760,7 @@
         ),
         cost_estimate=pl.CostEstimate(flops=0, transcendentals=0, bytes_accessed=200_000_000),
         name="closing",
-    )(parts, *sums, shared)
-
-
-def rows_kernel(local_count, table_ref, rows_ref, out_ref):
-    capacity = out_ref.shape[1]
-    placed = jnp.dot(table_ref[0], rows_ref[0], preferred_element_type=FULL)
-    for j in range(local_count):
-        out_ref[j] = placed[j * capacity : (j + 1) * capacity].astype(LOW)
-
-
-def place_rows(table, rows, local_count):
-    groups, slots, tokens = table.shape
-    width = rows.shape[2]
-    capacity = slots // local_count
-    return pl.pallas_call(
-        functools.partial(rows_kernel, local_count),
-        out_shape=jax.ShapeDtypeStruct((local_count, groups * capacity, width), LOW),
-        grid=(groups,),
-        in_specs=[
-            pl.BlockSpec((1, slots, tokens), lambda g: (g, 0, 0)),
-            pl.BlockSpec((1, tokens, width), lambda g: (g, 0, 0)),
-        ],
-        out_specs=pl.BlockSpec((local_count, capacity, width), lambda g: (0, g, 0)),
-        cost_estimate=pl.CostEstimate(
-            flops=2 * table.size * width, transcendentals=0, bytes_accessed=4 * rows.size
-        ),
-        name="place_rows",
-    )(table, rows)
+    )(*parts, *sums, shared)
 
 
 def collect_kernel(*refs):
@@ -973,10 +1163,10 @@
     )
     small = jnp.pad(small, ((0, 0), (0, 128 - small.shape[1])))
     numbers = jnp.concatenate([routes.T, segments, jnp.zeros((7, row_count), jnp.int32)], axis=0)
-    x_all, numbers_all, qkv_here, small = opening(
-        line_count, dp_count, [layer_input, numbers], [4, 1], w_qkv, small, 1
-    )
-    out_full = lax.all_gather(w_out, ("dp", "expert"), axis=0, tiled=True)
+    x_all, numbers_all, qkv_here, small, out_full = opening(
+        line_count, dp_count, [layer_input, numbers], [4, 1], w_qkv, small, w_out, 1
+    )
+    out_full = out_full.reshape(model_dim, model_dim)
     late_cotangent, x_all = lax.optimization_barrier((out_cotangent, x_all))
     dy_all = lax.all_gather(late_cotangent, "expert", axis=0)
     qkv_here = qkv_here.reshape(model_dim, 3 * head_cols)
@@ -1023,7 +1213,6 @@
     powers = jnp.where(chosen, jnp.exp(masked - jnp.max(masked, axis=-1, keepdims=True)), 0.0)
     gates = powers / jnp.sum(powers, axis=-1, keepdims=True)
 
-    h_all, gates_all = line_gather(line_count, [hidden_two, gates.T], [4, 1], 6)
     local = place * local_count + jnp.arange(local_count)
     used = jnp.any(routes_all[:, None] == local[None, :, None, None], axis=2)
     position = jnp.arange(row_count)
@@ -1035,9 +1224,9 @@
     returns = [(rank[:, j, :, None] == spots[None, None, :]).astype(LOW) for j in range(local_count)]
     slots = line_count * capacity
     flat_table = table.reshape(line_count, local_count * capacity, row_count)
-    expert_rows = place_rows(flat_table, h_all, local_count)
-    dy_all, _ = lax.optimization_barrier((dy_all, expert_rows))
-    dy_rows = place_rows(flat_table, dy_all, local_count)
+    expert_rows, dy_rows, gates_all = gather_place(
+        line_count, hidden_two, gates.T, flat_table, dy_all, local_count, 6
+    )
     local_gates = lax.dynamic_slice_in_dim(gates_all, place * local_count, local_count, axis=1)
     slot_gates = jnp.sum(table.astype(FULL) * local_gates[:, :, None, :], axis=-1)
     slot_gates = slot_gates.transpose(1, 0, 2).reshape(local_count, slots, 1)
@@ -1049,16 +1238,17 @@
         grads = grads.reshape(-1, model_dim)
         grad_sums.append(lax.psum_scatter(grads, "dp", scatter_dimension=0, tiled=True))
         out_rows.append(out_row)
-        back_rows.append(back_row)
+        back_rows.append(back_row.reshape(line_count, capacity, model_dim))
         slot_grads.append(dots.reshape(line_count, capacity))
     gate_rows = model_dim // dp_count
     sum_gate_up = jnp.stack([both[:gate_rows] for both in grad_sums]).astype(FULL)
     sum_down = jnp.stack([both[gate_rows:] for both in grad_sums]).astype(FULL)
     slot_grads = jnp.stack(slot_grads, axis=1)
     grad_gates = jnp.sum(table.astype(FULL) * slot_grads[:, :, :, None], axis=2)
-    (grad_gates,) = exchange("expert", line_count, [grad_gates], [False], 8)
+    grad_two, grad_gates = collect_reduce(line_count, returns, back_rows, grad_gates, 8)
     grad_gates = grad_gates.reshape(expert_count, row_count).T
-    grad_two = line_reduce(line_count, collect(returns, back_rows), 4, 9).astype(FULL)
+    grad_two = grad_two.astype(FULL)
+
     grad_out_rows = out_cotangent.astype(FULL)
     grad_logits = gates * (grad_gates - jnp.sum(gates * grad_gates, axis=-1, keepdims=True))
     grad_logits = grad_logits.astype(LOW)
@@ -1110,12 +1300,17 @@
     shared = shared.reshape(tall, dp_count, line_count, shard).transpose(2, 1, 0, 3)
     shared = shared.reshape(line_count, dp_count * tall, shard)
     shared = jnp.pad(shared, ((0, 0), (0, 0), (0, 128 - shard)))
-    grad_one, qkv_parts, out_parts, gain_pair, shared = closing(
-        line_count, dp_count, grad_one, 4, [qkv_parts, out_parts, gain_pair], shared, 14
-    )
     out_rows = lax.optimization_barrier((out_rows, grad_one))[0]
-    mixture = line_reduce(line_count, collect(returns, out_rows), 4, 10).astype(FULL)
-    output = (residual + mixture).astype(LOW)
+    grad_one, mixture, qkv_parts, out_parts, gain_pair, shared = closing(
+        line_count,
+        dp_count,
+        [grad_one, collect(returns, out_rows)],
+        4,
+        [qkv_parts, out_parts, gain_pair],
+        shared,
+        14,
+    )
+    output = (residual + mixture.astype(FULL)).astype(LOW)
     sum_qkv = jnp.sum(qkv_parts.astype(FULL), axis=0).reshape(out_cols, 3, head_cols)
     sum_out = jnp.sum(out_parts.astype(FULL), axis=0)
     gain_pair = jnp.sum(gain_pair, axis=0)

time: 842 us -> 775 us (0.920)
  Pallas kernels: 702 us -> 630 us
    pallas_call x9 -> x5, Pallas kernels: 425 us -> 203 us  [call(): pl.pallas_call(kernel, out_shape=outs, in_specs=[ANY] * len(arrays), out_...]
    pallas_call x2, Pallas kernels: 19.3 us -> 135 us  [the longest x1 81.9 us: collect_reduce(): pl.pallas_call(functools.partial(collect_reduce_kernel, levels, cuts, len...]
    pallas_call x1, Pallas kernels: 82.7 us -> 127 us  [closing(): pl.pallas_call(functools.partial(closing_kernel, size, dp_count, cuts, su...]
    pallas_call x2 -> x1, Pallas kernels: 21.9 us -> 10.8 us  [collect(): pl.pallas_call(collect_kernel, out_shape=jax.ShapeDtypeStruct((groups, to...]
    unnamed x93 -> x85, local copies, waits for them, and re-layouts: 17.5 us -> 26 us
  transfers between devices with their start and end apart: 5 -> 4, of which waited for: 0 -> 0; matrix products, arithmetic and copies ran while one was open for 11% -> 11% of each run, Pallas kernels for 78% -> 57%
where the time goes in v3:
time: 775 us; the launch traced here: 770 us
  Pallas kernels  630 us (81%)
  local copies, waits for them, and re-layouts  49.1 us (6%)
  other arithmetic  39.7 us (5%)
  matrix products  35.1 us (5%)
  between operations  14.8 us (2%)
    pallas_call x5, Pallas kernels, call(): pl.pallas_call(kernel, out_shape=outs, in_specs=[ANY] * len(arrays), out_...  203 us
    pallas_call x1, Pallas kernels, closing(): pl.pallas_call(functools.partial(closing_kernel, size, dp_count, cuts, su...  127 us
    pallas_call x3, Pallas kernels, expert(): pl.pallas_call(functools.partial(expert_kernel, tiles), out_shape=[jax.Sh...  119 us
    pallas_call x1, Pallas kernels, collect_reduce(): pl.pallas_call(functools.partial(collect_reduce_kernel, levels, cuts, len...  81.9 us
    pallas_call x1, Pallas kernels, gather_place(): pl.pallas_call(functools.partial(gather_place_kernel, size // 2, cuts), o...  53.2 us
    unnamed x85, local copies, waits for them, and re-layouts  26 us
    pallas_call x1, Pallas kernels, attend_back(): pl.pallas_call(functools.partial(attend_back_kernel, heads), out_shape=[b...  21.9 us
  transfers between devices with their start and end apart: 4, of which 0 were waited for; matrix products, arithmetic and copies ran while one was open for 11% of the time, Pallas kernels for 57%

profile of v3, /device:TPU:16, one launch (start us, length us, event | category | flops | bytes accessed | tf_op | source)
XLA Modules:
  0.0 769.9 jit_solution(18088702414777945111)
XLA Ops:
  15.3 97.6 %opening.1 = (bf16[8,192,2048]{2,1,0:T(8,128)(2,1)}, s32[8,16,192]{2,1,0:T(8,128)S(1)}, bf16[4,8,64,768]{3,2,1,0:T(8,128)(2,1)S(1)}, bf16[4,8,64,128]{3,2,1,0:T(8,128)(2,1)S(1)}, bf16[4,8,64,2048]{3,2,1,0:T(8,128)(2,1)}) custom-call(bf16[192,2048]{1,0:T(8,128)(2,1)S(1)} %copy-done.1, s32[16,192]{1,0:T(8,128)S(1)} %add_add_fusion.refs_1_, ...), custom_call_target="tpu_custom_call" | custom-call | bytes 200000000 | tf_op jit(solution)/shard_map/opening/pallas_call | solution.py:161
  117.6 4.2 multiply_reduce_fusion.1
  124.4 6.6 fusion.47
  133.6 8.9 %exchange_expert.3 = f32[8,16,192]{2,1,0:T(8,128)S(1)} custom-call(f32[16,192]{1,0:T(8,128)S(1)} %reshape.198.refs_0_), custom_call_target="tpu_custom_call" | custom-call | bytes 30000000 | tf_op jit(solution)/shard_map/exchange_expert/pallas_call | solution.py:161
  145.7 12.6 %attend.1 = (bf16[8,192,768]{2,1,0:T(8,128)(2,1)}, bf16[8,192,256]{2,1,0:T(8,128)(2,1)}) custom-call(f32[8,192,768]{2,1,0:T(8,128)} %bitcast.9.rows_ref, f32[8,192,2]{2,1,0:T(8,128)} %bitcast.119, f32[2,256]{1,0:T(2,128)} %pad_maximum_fusion.6.gain_ref, f32[2,192,128]{2,1,0:T(8,128)} %pad_maximum_fusion.3.turn_ref, s32[8,192,1]{2,1,0:T(8,128)} %copy.87.column_ref, ...), custom_call_target="tpu_custom_call" | custom-call | flops 905969664 | bytes 9437184 | tf_op jit(solution)/shard_map/attend/pallas_call | solution.py:1024
  159.5 35.3 %exchange_expert.4 = bf16[8,192,256]{2,1,0:T(8,128)(2,1)S(1)} custom-call(bf16[8,192,256]{2,1,0:T(8,128)(2,1)S(1)} %copy-done.8), custom_call_target="tpu_custom_call" | custom-call | bytes 30000000 | tf_op jit(solution)/shard_map/exchange_expert/pallas_call | solution.py:161
  196.1 5.3 multiply_reduce_fusion.4
  203.8 53.2 %gather_place.1 = (bf16[3,576,2048]{2,1,0:T(8,128)(2,1)}, bf16[3,576,2048]{2,1,0:T(8,128)(2,1)}, f32[8,24,192]{2,1,0:T(8,128)S(1)}) custom-call(bf16[192,2048]{1,0:T(8,128)(2,1)S(1)} %multiply_convert_fusion.2.refs_0_, f32[24,192]{1,0:T(8,128)S(1)} %fusion.35.refs_1_, bf16[8,216,192]{2,1,0:T(8,128)(2,1)S(1)} %copy-done.14, bf16[8,192,2048]{2,1,0:T(8,128)(2,1)} %bitcast.164), custom_call_target="tpu_custom_call" | custom-call | flops 2717908992 | bytes 150000000 | tf_op jit(solution)/shard_map/gather_place/pallas_call | solution.py:622
  258.7 39.6 %expert.5 = (bf16[4,768,2048]{2,1,0:T(8,128)(2,1)}, bf16[1,576,2048]{2,1,0:T(8,128)(2,1)}, bf16[1,576,2048]{2,1,0:T(8,128)(2,1)}, f32[1,576,1]{2,1,0:T(8,128)}) custom-call(bf16[3,576,2048]{2,1,0:T(8,128)(2,1)} %get-tuple-element.58.x_ref, bf16[3,576,2048]{2,1,0:T(8,128)(2,1)} %get-tuple-element.59.dy_ref, f32[3,576,1]{2,1,0:T(8,128)} %reshape.220.scale_ref, ...), custom_call_target="tpu_custom_call" | custom-call | flops 21743271936 | bytes 25165824 | tf_op jit(solution)/shard_map/expert/pallas_call | solution.py:891
  298.9 39.7 %expert.4 = (bf16[4,768,2048]{2,1,0:T(8,128)(2,1)}, bf16[1,576,2048]{2,1,0:T(8,128)(2,1)}, bf16[1,576,2048]{2,1,0:T(8,128)(2,1)}, f32[1,576,1]{2,1,0:T(8,128)}) custom-call(bf16[3,576,2048]{2,1,0:T(8,128)(2,1)} %get-tuple-element.58.x_ref, bf16[3,576,2048]{2,1,0:T(8,128)(2,1)} %get-tuple-element.59.dy_ref, f32[3,576,1]{2,1,0:T(8,128)} %reshape.220.scale_ref, ...), custom_call_target="tpu_custom_call" | custom-call | flops 21743271936 | bytes 25165824 | tf_op jit(solution)/shard_map/expert/pallas_call | solution.py:891
  338.8 40.0 %expert.3 = (bf16[4,768,2048]{2,1,0:T(8,128)(2,1)}, bf16[1,576,2048]{2,1,0:T(8,128)(2,1)}, bf16[1,576,2048]{2,1,0:T(8,128)(2,1)}, f32[1,576,1]{2,1,0:T(8,128)}) custom-call(bf16[3,576,2048]{2,1,0:T(8,128)(2,1)} %get-tuple-element.58.x_ref, bf16[3,576,2048]{2,1,0:T(8,128)(2,1)} %get-tuple-element.59.dy_ref, f32[3,576,1]{2,1,0:T(8,128)} %reshape.220.scale_ref, ...), custom_call_target="tpu_custom_call" | custom-call | flops 21743271936 | bytes 25165824 | tf_op jit(solution)/shard_map/expert/pallas_call | solution.py:891
  392.9 81.9 %collect_reduce.1 = (bf16[192,2048]{1,0:T(8,128)(2,1)S(1)}, f32[8,3,192]{2,1,0:T(4,128)S(1)}) custom-call(bf16[8,192,72]{2,1,0:T(8,128)(2,1)S(1)} %copy-done.6, bf16[8,192,72]{2,1,0:T(8,128)(2,1)S(1)} %copy-done.7, bf16[8,192,72]{2,1,0:T(8,128)(2,1)S(1)} %fusion.19.refs_2_, bf16[8,72,2048]{2,1,0:T(8,128)(2,1)S(1)} %bitcast.126, ...), custom_call_target="tpu_custom_call" | custom-call | bytes 150000000 | tf_op jit(solution)/shard_map/collect_reduce/pallas_call | solution.py:680
  480.1 52.4 %line_gather.1.grad_ref = bf16[8,192,2048]{2,1,0:T(8,128)(2,1)} custom-call(bf16[192,2048]{1,0:T(8,128)(2,1)S(1)} %fusion.42.refs_0_), custom_call_target="tpu_custom_call" | custom-call | bytes 150000000 | tf_op jit(solution)/shard_map/line_gather/pallas_call | solution.py:161
  532.6 21.9 %attend_back.1 = (f32[8,192,768]{2,1,0:T(8,128)}, f32[8,192,2]{2,1,0:T(8,128)S(1)}, f32[2,256]{1,0:T(2,128)S(1)}, bf16[4,256,512]{2,1,0:T(8,128)(2,1)S(1)}) custom-call(bf16[8,192,2048]{2,1,0:T(8,128)(2,1)} %line_gather.1.grad_ref, bf16[256,2048]{1,0:T(8,128)(2,1)S(1)} %copy-done.4, bf16[8,192,768]{2,1,0:T(8,128)(2,1)} %get-tuple-element.69.kept_ref, ...), custom_call_target="tpu_custom_call" | custom-call | flops 3221225472 | bytes 31457280 | tf_op jit(solution)/shard_map/attend_back/pallas_call | solution.py:1116
  556.8 9.2 %exchange_expert.5 = f32[8,16,192]{2,1,0:T(8,128)S(1)} custom-call(f32[16,192]{1,0:T(8,128)S(1)} %bitcast.128), custom_call_target="tpu_custom_call" | custom-call | bytes 30000000 | tf_op jit(solution)/shard_map/exchange_expert/pallas_call | solution.py:161
  567.7 3.8 fusion.14
  571.9 10.9 %multiply_reduce_fusion = (f32[2048]{0:T(1024)S(1)}, bf16[1536,2048]{1,0:T(8,128)(2,1)}, bf16[1536,2048]{1,0:T(8,128)(2,1)}) fusion(bf16[8,192,2048]{2,1,0:T(8,128)(2,1)} %get-tuple-element.51, f32[1536]{0:T(1024)S(1)} %rsqrt.38, f32[2048]{0:T(1024)S(1)} %bitcast.151, bf16[2048,768]{1,0:T(8,128)(2,1)S(1)} %bitcast.130, bf16[1536,256]{1,0:T(8,128)(2,1)S(1)} %slice.191, ...), kind=kOutput, calls=%fused_computation.1 | convolution fusion | flops 4860934144 | bytes 24401920 | tf_op jit(solution)/shard_map/dot_general | solution.py:960
  583.6 10.8 %collect.1.refs_1_ = bf16[8,192,2048]{2,1,0:T(8,128)(2,1)} custom-call(bf16[8,192,72]{2,1,0:T(8,128)(2,1)} %get-tuple-element.161.refs_0_, bf16[8,192,72]{2,1,0:T(8,128)(2,1)} %get-tuple-element.162.refs_1_, bf16[8,192,72]{2,1,0:T(8,128)(2,1)} %copy-done.5, bf16[1,576,2048]{2,1,0:T(8,128)(2,1)} %get-tuple-element.75.refs_3_, ...), custom_call_target="tpu_custom_call" | custom-call | flops 1358954496 | bytes 12582912 | tf_op jit(solution)/shard_map/collect/pallas_call | solution.py:777
  594.5 8.9 %convolution_convert_fusion = bf16[2048,768]{1,0:T(8,128)(2,1)} fusion(bf16[1536,2048]{1,0:T(8,128)(2,1)} %get-tuple-element.132, bf16[1536,256]{1,0:T(8,128)(2,1)S(1)} %copy-done.37, bf16[1536,256]{1,0:T(8,128)(2,1)} %copy-done.39, bf16[1536,256]{1,0:T(8,128)(2,1)} %copy-done.38), kind=kOutput, calls=%fused_computation.7 | convolution fusion | flops 4840488960 | bytes 11796480 | tf_op jit(solution)/shard_map/dot_general | solution.py:954
  603.4 126.9 %closing.1 = (bf16[192,2048]{1,0:T(8,128)(2,1)S(1)}, bf16[192,2048]{1,0:T(8,128)(2,1)S(1)}, bf16[4,512,768]{2,1,0:T(8,128)(2,1)}, bf16[4,256,512]{2,1,0:T(8,128)...) custom-call(bf16[8,192,2048]{2,1,0:T(8,128)(2,1)} %bitcast.134, bf16[8,192,2048]{2,1,0:T(8,128)(2,1)} %collect.1.refs_1_, ...), custom_call_target="tpu_custom_call" | custom-call | bytes 200000000 | tf_op jit(solution)/shard_map/closing/pallas_call | solution.py:747
  736.3 3.1 copy.103
  742.5 3.7 fusion.9
  750.2 3.2 maximum_convert_fusion.1
  757.4 5.8 maximum_convert_fusion
  (195 shorter events, 69.5 us)
Async XLA Ops:
  7.2 195.4 %all-gather.3.cloned.1.call-start = ((), (), s32[]{:S(2)}) async-start(), calls=%async_computation.6 | async-start | bytes 7077888 | tf_op jit(solution)/shard_map/all_gather | solution.py:1171
  114.5 631.6 %reduce-scatter.8.cloned.1.call-start = ((), (), s32[]{:S(2)}) async-start(), calls=%async_computation.5 | async-start | bytes 15728640 | tf_op jit(solution)/shard_map/reduce_scatter | solution.py:1239
  117.6 4.7 copy-start.26
  158.2 37.8 %copy-start.2 = (bf16[192,2048]{1,0:T(8,128)(2,1)S(1)}, bf16[192,2048]{1,0:T(8,128)(2,1)}, u32[]{:S(2)}) copy-start(bf16[192,2048]{1,0:T(8,128)(2,1)} %refs_0_.1) | copy-start | bytes 2359300
  159.5 36.5 %copy-start.40 = (s32[192,8]{0,1:T(8,128)S(1)}, s32[192,8]{0,1:T(8,128)}, u32[]{:S(2)}) copy-start(s32[192,8]{0,1:T(8,128)} %param.16) | copy-start | bytes 18436
  298.4 449.1 %reduce-scatter.6.cloned.1.call-start = ((), (), s32[]{:S(2)}) async-start(), calls=%async_computation.4 | async-start | bytes 15728640 | tf_op jit(solution)/shard_map/reduce_scatter | solution.py:1239
  338.6 410.2 %reduce-scatter.4.cloned.1.call-start = ((), (), s32[]{:S(2)}) async-start(), calls=%async_computation.3 | async-start | bytes 15728640 | tf_op jit(solution)/shard_map/reduce_scatter | solution.py:1239
  381.2 93.6 %copy-start.5 = (bf16[8,192,72]{2,1,0:T(8,128)(2,1)}, bf16[8,192,72]{2,1,0:T(8,128)(2,1)S(1)}, u32[]{:S(2)}) copy-start(bf16[8,192,72]{2,1,0:T(8,128)(2,1)S(1)} %fusion.19.refs_2_) | copy-start | bytes 663556
  475.8 3.8 copy-start.28
  475.8 3.8 copy-start.31
  480.0 52.5 %copy-start.3 = (s32[8,192,1]{2,1,0:T(8,128)S(1)}, s32[8,192,1]{2,1,0:T(8,128)}, u32[]{:S(2)}) copy-start(s32[8,192,1]{2,1,0:T(8,128)} %copy.87.column_ref) | copy-start | bytes 18436
  480.0 52.5 %copy-start.4 = (bf16[256,2048]{1,0:T(8,128)(2,1)S(1)}, bf16[256,2048]{1,0:T(8,128)(2,1)}, u32[]{:S(2)}) copy-start(bf16[256,2048]{1,0:T(8,128)(2,1)} %constant_dynamic-slice_fusion.w_ref) | copy-start | bytes 3145732
  480.0 52.5 %copy-start.9 = (bf16[8,192,256]{2,1,0:T(8,128)(2,1)S(1)}, bf16[8,192,256]{2,1,0:T(8,128)(2,1)}, u32[]{:S(2)}) copy-start(bf16[8,192,256]{2,1,0:T(8,128)(2,1)} %get-tuple-element.55.refs_0_.out_ref) | copy-start | bytes 2359300
  480.0 52.5 %copy-start.11 = (f32[2,192,128]{2,1,0:T(8,128)S(1)}, f32[2,192,128]{2,1,0:T(8,128)}, u32[]{:S(2)}) copy-start(f32[2,192,128]{2,1,0:T(8,128)} %pad_maximum_fusion.3.turn_ref) | copy-start | bytes 589828
  480.1 52.5 %copy-start.21 = (s32[8,1,192]{2,1,0:T(1,128)S(1)}, s32[8,1,192]{2,1,0:T(1,128)}, u32[]{:S(2)}) copy-start(s32[8,1,192]{2,1,0:T(1,128)} %get-tuple-element.135.row_ref) | copy-start | bytes 18436
  480.1 52.5 %copy-start.22 = (f32[2,256]{1,0:T(2,128)S(1)}, f32[2,256]{1,0:T(2,128)}, u32[]{:S(2)}) copy-start(f32[2,256]{1,0:T(2,128)} %pad_maximum_fusion.6.gain_ref) | copy-start | bytes 6148
  567.7 3.9 copy-start.36
  567.7 4.2 copy-start.25
  571.6 11.2 %copy-start.38 = (bf16[1536,256]{1,0:T(8,128)(2,1)}, bf16[1536,256]{1,0:T(8,128)(2,1)S(1)}, u32[]{:S(2)}) copy-start(bf16[1536,256]{1,0:T(8,128)(2,1)S(1)} %get-tuple-element.130) | copy-start | bytes 2359300
  571.6 11.2 %copy-start.39 = (bf16[1536,256]{1,0:T(8,128)(2,1)}, bf16[1536,256]{1,0:T(8,128)(2,1)S(1)}, u32[]{:S(2)}) copy-start(bf16[1536,256]{1,0:T(8,128)(2,1)S(1)} %get-tuple-element.131) | copy-start | bytes 2359300
  583.6 10.8 %copy-start.37 = (bf16[1536,256]{1,0:T(8,128)(2,1)S(1)}, bf16[1536,256]{1,0:T(8,128)(2,1)}, u32[]{:S(2)}) copy-start(bf16[1536,256]{1,0:T(8,128)(2,1)} %copy-done.36) | copy-start | bytes 2359300
  736.3 3.1 copy-start.13
  739.4 3.1 copy-start.32
  750.1 3.2 copy-start.33
  (21 other events, 30.1 us)
Sparse Core Ops, SparseCore 0:
  114.7 80.2 all-gather.2
  298.5 127.3 reduce-scatter.7
  429.0 120.7 reduce-scatter.5
  553.3 165.9 reduce-scatter.3

commit v4 on v3

--- a/solution.py
+++ b/solution.py
@@ -63,98 +63,117 @@
     def __init__(self, levels, cuts, ins, outs, up_sem, down_sem, side_sem, recv_sem, own_sem):
         self.levels, self.cuts, self.ins, self.outs = levels, cuts, ins, outs
         self.up_sem, self.down_sem, self.side_sem = up_sem, down_sem, side_sem
-        self.recv_sem = recv_sem
-        self.pieces = [(i, k) for i in range(len(cuts)) for k in range(cuts[i])]
+        self.recv_sem, self.own_sem = recv_sem, own_sem
         self.place, self.level, self.side, self.other = line_place()
         self.has_up, self.has_down = self.level < levels - 1, self.level > 0
-        self.own = [
-            pltpu.make_async_copy(ins[i], outs[i].at[self.place], own_sem.at[i])
-            for i in range(len(cuts))
-        ]
 
     @staticmethod
-    def scratch(size, cuts):
-        levels, total = size // 2, sum(cuts)
+    def scratch(size, cuts, count):
+        levels, total = size // 2, cuts + count - 1
         shapes = ((levels, total), (levels, total), (2 * levels - 1, total), (size, total))
-        return [pltpu.SemaphoreType.DMA(shape) for shape in shapes + ((len(cuts),),)]
-
-    def part(self, ref, i, k):
-        rows = self.ins[i].shape[0] // self.cuts[i]
-        return ref.at[pl.ds(k * rows, rows)]
-
-    def sending(self, q, block, own, sem, target):
-        i, k = self.pieces[q]
-        landing = self.part(self.outs[i].at[block], i, k)
-        source = self.part(self.ins[i], i, k) if own else landing
-        return remote(source, landing, sem, self.recv_sem.at[block, q], {"expert": target})
-
-    def up(self, q, step):
+        return [pltpu.SemaphoreType.DMA(shape) for shape in shapes + ((count,),)]
+
+    def pieces(self):
+        return [(0, k) for k in range(self.cuts)] + [(i, 0) for i in range(1, len(self.ins))]
+
+    def staying(self, i):
+        target = self.outs[i].at[self.place]
+        return pltpu.make_async_copy(self.ins[i], target, self.own_sem.at[i])
+
+    def sending(self, piece, block, own, sem, target):
+        i, k = piece
+        landing, source, q = self.outs[i].at[block], self.ins[i], k
+        if i:
+            q = self.cuts + i - 1
+        else:
+            rows = source.shape[0] // self.cuts
+            landing, source = landing.at[pl.ds(k * rows, rows)], source.at[pl.ds(k * rows, rows)]
+        sems = sem.at[q], self.recv_sem.at[block, q]
+        return remote(source if own else landing, landing, *sems, {"expert": target})
+
+    def up(self, piece, step, own=False):
         block = self.place - 2 * step
-        return self.sending(q, block, step == 0, self.up_sem.at[step, q], self.place + 2)
-
-    def down(self, q, step):
+        return self.sending(piece, block, own, self.up_sem.at[step], self.place + 2)
+
+    def down(self, piece, step, own=False):
         block = self.place + 2 * step
-        return self.sending(q, block, step == 0, self.down_sem.at[step, q], self.place - 2)
-
-    def across(self, q, step):
-        sem = self.side_sem.at[step + self.levels - 1, q]
-        return self.sending(q, self.place - 2 * step, step == 0, sem, self.other)
+        return self.sending(piece, block, own, self.down_sem.at[step], self.place - 2)
+
+    def across(self, piece, step, own=False):
+        sem = self.side_sem.at[step + self.levels - 1]
+        return self.sending(piece, self.place - 2 * step, own, sem, self.other)
 
     def begin(self):
-        for q in range(len(self.pieces)):
-            pl.when(self.has_up)(self.up(q, 0).start)
-            pl.when(self.has_down)(self.down(q, 0).start)
-        for q in range(len(self.pieces)):
-            self.across(q, 0).start()
-        for copy in self.own:
-            copy.start()
-
-    def forward(self, step, q):
+        for piece in self.pieces():
+            pl.when(self.has_up)(self.up(piece, 0, True).start)
+            pl.when(self.has_down)(self.down(piece, 0, True).start)
+        for piece in self.pieces():
+            self.across(piece, 0, True).start()
+        for i in range(len(self.ins)):
+            self.staying(i).start()
+
+    def forward(self, step, piece):
         @pl.when(self.level >= step)
         def _():
-            self.across(q, step).wait_recv()
-            pl.when(self.has_up)(self.up(q, step).start)
-            self.across(q, step).start()
+            self.across(piece, step).wait_recv()
+            pl.when(self.has_up)(self.up(piece, step).start)
+            self.across(piece, step).start()
 
         @pl.when(self.level + step < self.levels)
         def _():
-            self.across(q, -step).wait_recv()
-            pl.when(self.has_down)(self.down(q, step).start)
-            self.across(q, -step).start()
+            self.across(piece, -step).wait_recv()
+            pl.when(self.has_down)(self.down(piece, step).start)
+            self.across(piece, -step).start()
 
     def land_across(self, block):
-        for q in range(len(self.pieces)):
-            self.sending(q, block, False, self.side_sem.at[0, q], self.other).wait_recv()
-
-    def finish(self, landed=False, held=0):
-        if not landed:
-            for far in range(self.levels):
-                self.land_across(2 * far + 1 - self.side)
-        for q in range(len(self.pieces)):
-            self.across(q, 0).wait_send()
+        for piece in self.pieces():
+            self.sending(piece, block, False, self.side_sem.at[0], self.other).wait_recv()
+
+    def main(self, landed=None, before=None):
+        levels, cuts = self.levels, self.cuts
+
+        @pl.loop(0, levels * cuts)
+        def _(turn):
+            step, k = lax.div(turn, cuts) + 1, lax.rem(turn, cuts)
+
+            @pl.when(step < levels)
+            def _():
+                if before:
+                    pl.when(k == 0)(lambda: before(step))
+                self.forward(step, (0, k))
+
+                @pl.when(k == cuts - 1)
+                def _():
+                    for i in range(1, len(self.ins)):
+                        self.forward(step, (i, 0))
+
+            group, sign, crossed = step - 1, 2 * lax.rem(k, 2) - 1, lax.div(k, 2)
+            crossed = jnp.where(group == 0, k, crossed)
+            far = jnp.where(group == 0, self.level, self.level + sign * group)
+
+            @pl.when((far >= 0) & (far < levels) & (k < 4) & ((group > 0) | (k < 2)))
+            def _():
+                block = 2 * far + self.side + crossed * (1 - 2 * self.side)
+
+                @pl.when(crossed == 1)
+                def _():
+                    self.land_across(block)
+
+                if landed:
+                    landed(block)
+
+    def finish(self, held=0):
+        for piece in self.pieces():
+            self.across(piece, 0).wait_send()
             for step in range(self.levels):
                 above, below = self.level >= step, self.level + step < self.levels
-                pl.when(self.has_up & above)(self.up(q, step).wait_send)
-                pl.when(self.has_down & below)(self.down(q, step).wait_send)
+                pl.when(self.has_up & above)(self.up(piece, step).wait_send)
+                pl.when(self.has_down & below)(self.down(piece, step).wait_send)
                 if step:
-                    pl.when(above)(self.across(q, step).wait_send)
-                    pl.when(below)(self.across(q, -step).wait_send)
-        for copy in self.own[held:]:
-            copy.wait()
-
-    def run(self):
-        self.begin()
-        for step in range(1, self.levels):
-            for q in range(len(self.pieces)):
-                self.forward(step, q)
-        self.finish()
-
-
-def line_gather_kernel(levels, cuts, *refs):
-    count = len(cuts)
-    line = LineGather(levels, cuts, refs[:count], refs[count : 2 * count], *refs[2 * count :])
-    line_barrier(levels)
-    line.run()
+                    pl.when(above)(self.across(piece, step).wait_send)
+                    pl.when(below)(self.across(piece, -step).wait_send)
+        for i in range(held, len(self.ins)):
+            self.staying(i).wait()
 
 
 def call(kernel, name, number, outs, scratch, arrays, moved):
@@ -172,18 +191,6 @@
     )(*arrays)
 
 
-def line_gather(size, arrays, cuts, number):
-    return call(
-        functools.partial(line_gather_kernel, size // 2, tuple(cuts)),
-        "line_gather",
-        number,
-        [jax.ShapeDtypeStruct((size,) + a.shape, a.dtype) for a in arrays],
-        LineGather.scratch(size, cuts),
-        arrays,
-        150_000_000,
-    )
-
-
 class LineReduce:
     def __init__(self, levels, cuts, parts, total, own, beside, rising, falling, *sems):
         self.levels, self.cuts, self.parts, self.total = levels, cuts, parts, total
@@ -194,11 +201,6 @@
         self.place, self.level, self.side, self.other = line_place()
         self.has_up, self.has_down = self.level < levels - 1, self.level > 0
         self.rows = parts.shape[1] // cuts
-        self.order = []
-        for step in range(levels):
-            for far in (levels - 1 - step, step):
-                if far not in self.order:
-                    self.order.append(far)
 
     @staticmethod
     def scratch(size, block, dtype, cuts):
@@ -235,21 +237,29 @@
         return self.cut(ref, block, k)[...].astype(FULL)
 
     def load(self):
-        for far in self.order:
+        for i in range(self.levels):
             for k in range(self.cuts):
-                self.loading(far, k).start()
+                self.loading(self.far(i), k).start()
 
     def begin(self):
-        for far in self.order:
+        for i in range(self.levels):
             for k in range(self.cuts):
-                self.across(far, k).start()
-
-    def prepare(self, far, which, make):
-        if which == 0:
+                self.across(self.far(i), k).start()
+
+    def far(self, i):
+        return jnp.where(lax.rem(i, 2) == 0, self.levels - 1 - lax.div(i, 2), lax.div(i, 2))
+
+    def prepare(self, turn, make):
+        far = self.far(lax.div(turn, 2))
+
+        @pl.when(lax.rem(turn, 2) == 0)
+        def _():
             make(2 * far + 1 - self.side, self.parts.at[far])
             for k in range(self.cuts):
                 self.across(far, k).start()
-        else:
+
+        @pl.when(lax.rem(turn, 2) == 1)
+        def _():
             make(2 * far + self.side, self.own.at[far])
 
     def pair(self, far, k):
@@ -275,14 +285,17 @@
         pl.when(ahead)(move(far, k).start)
 
     def main(self, beside=None):
-        for step in range(self.levels - 1):
+        @pl.loop(0, (self.levels - 1) * self.cuts)
+        def _(turn):
+            step, k = lax.div(turn, self.cuts), lax.rem(turn, self.cuts)
             high, low = self.levels - 1 - step, step
-            for k in range(self.cuts):
-                if beside:
-                    beside(step * self.cuts + k)
-                self.toward(high, k, self.level < high, self.has_down, self.up, self.rising)
-                self.toward(low, k, self.level > low, self.has_up, self.down, self.falling)
-        for k in range(self.cuts):
+            if beside:
+                beside(turn)
+            self.toward(high, k, self.level < high, self.has_down, self.up, self.rising)
+            self.toward(low, k, self.level > low, self.has_up, self.down, self.falling)
+
+        @pl.loop(0, self.cuts)
+        def _(k):
             self.store(self.level, k, self.pair(self.level, k))
             for there, move, arrived in (
                 (self.has_down, self.up, self.rising),
@@ -399,8 +412,8 @@
     )
 
 
-def opening_kernel(size, dp_count, cuts, *refs):
-    count, levels = len(cuts), size // 2
+def opening_kernel(size, dp_count, count, cuts, *refs):
+    levels = size // 2
     ins, (w_ref, small_ref, sheet_ref) = refs[:count], refs[count : count + 3]
     outs, rest = refs[count + 3 : 2 * count + 3], refs[2 * count + 3 :]
     w_out, small_out, sheet_out = rest[:3]
@@ -480,8 +493,8 @@
             sending(shift, peer, j).wait_recv()
         across.send(0, peer)
         across.send(1, peer)
-    for step in range(1, levels):
-
+
+    def pass_sheets(step):
         @pl.when(level >= step)
         def _():
             sheet_up(level - step).wait_recv()
@@ -494,8 +507,7 @@
             pl.when(line.has_down)(sheet_down(level + step).start)
             spread_sheet(level + step)
 
-        for q in range(len(line.pieces)):
-            line.forward(step, q)
+    line.main(before=pass_sheets)
     for shift, peer in enumerate(across.peers):
         for far in range(levels):
             sheet_dp(far, shift, peer).wait_recv()
@@ -527,11 +539,11 @@
     outs.append(jax.ShapeDtypeStruct(whole + (small.shape[1],), small.dtype))
     outs.append(jax.ShapeDtypeStruct((dp_count, size) + sheet.shape, sheet.dtype))
     return call(
-        functools.partial(opening_kernel, size, dp_count, tuple(cuts)),
+        functools.partial(opening_kernel, size, dp_count, len(arrays), cuts),
         "opening",
         number,
         outs,
-        LineGather.scratch(size, cuts)
+        LineGather.scratch(size, cuts, len(arrays))
         + [sems((size, 4)), sems((size, 4)), sems((4,))]
         + Exchange.scratch(dp_count, (size, size))
         + [sems((levels,))] * 3
@@ -584,37 +596,18 @@
     def _(block):
         place(block, dy_held, dy_stage, dy_out, dy_sems)
 
-    line.own[0].wait()
-    place_x(line.place)
-    for step in range(1, levels + 1):
-        if step < levels:
-            for q in range(len(line.pieces)):
-                line.forward(step, q)
-        for sign in (-1, 1):
-            far = line.level + sign * (step - 1)
-            there = (far >= 0) & (far < levels)
-            if step > 1 or sign > 0:
-
-                @pl.when(there)
-                def _():
-                    line.land_across(2 * far + 1 - line.side)
-                    place_x(2 * far + 1 - line.side)
-
-            near = line.level + sign * step
-            if step < levels:
-
-                @pl.when((near >= 0) & (near < levels))
-                def _():
-                    place_x(2 * near + line.side)
-
-    line.finish(landed=True, held=1)
-    for block in range(size):
+    line.staying(0).wait()
+    line.main(place_x)
+    line.finish(held=1)
+
+    @pl.loop(0, size)
+    def _(block):
         leaving(block, x_stage, x_out, x_sems).wait()
         leaving(block, dy_stage, dy_out, dy_sems).wait()
 
 
 def gather_place(size, rows, gates, table, dy, local_count, number):
-    cuts = (4, 1)
+    cuts = 4
     tokens, width = rows.shape
     capacity = table.shape[1] // local_count
     placed = jax.ShapeDtypeStruct((local_count, size * capacity, width), rows.dtype)
@@ -626,7 +619,7 @@
         out_specs=[ANY] * 3,
         scratch_shapes=[pltpu.VMEM((size, tokens, width), rows.dtype)] * 2
         + [pltpu.VMEM((size, local_count, capacity, width), rows.dtype)] * 2
-        + LineGather.scratch(size, cuts)
+        + LineGather.scratch(size, cuts, 2)
         + [sems((1,)), sems((size,)), sems((size,))],
         compiler_params=pltpu.CompilerParams(
             collective_id=number, has_side_effects=True, vmem_limit_bytes=48 << 20
@@ -638,34 +631,34 @@
     )(rows, gates, table, dy)
 
 
+def collect_block(tables, slots, block, target):
+    @pl.loop(0, target.shape[1] // COLUMNS)
+    def _(n):
+        columns = pl.ds(pl.multiple_of(n * COLUMNS, COLUMNS), COLUMNS)
+        total = 0.0
+        for table, rows in zip(tables, slots):
+            total += jnp.dot(table[block], rows[block, :, columns], preferred_element_type=FULL)
+        target[:, columns] = total.astype(target.dtype)
+
+
 def collect_reduce_kernel(levels, cuts, local_count, *refs):
     tables, slots, small_ref = refs[:local_count], refs[local_count : 2 * local_count], refs[2 * local_count]
     total_ref, small_out = refs[2 * local_count + 1 : 2 * local_count + 3]
     away, rest = refs[2 * local_count + 3], refs[2 * local_count + 4 :]
     line = LineReduce(levels, cuts, away, total_ref, *rest[:12])
     small = Exchange("expert", 2 * levels, (False,), (1,), [small_ref], [small_out], *rest[12:])
-    width = away.shape[2]
     greet("expert", [(peer, None) for peer in small.peers])
     pl.semaphore_wait(pltpu.get_barrier_semaphore(), 2 * levels - 1)
 
-    def make(block, target):
-        @pl.loop(0, width // COLUMNS)
-        def _(n):
-            columns = pl.ds(pl.multiple_of(n * COLUMNS, COLUMNS), COLUMNS)
-            total = 0.0
-            for table, rows in zip(tables, slots):
-                total += jnp.dot(table[block], rows[block, :, columns], preferred_element_type=FULL)
-            target[:, columns] = total.astype(target.dtype)
-
+    make = functools.partial(collect_block, tables, slots)
     small.begin()
-    for far in line.order[:2]:
-        line.prepare(far, 0, make)
-        line.prepare(far, 1, make)
-    later = [(far, which) for far in line.order[2:] for which in (0, 1)]
+
+    @pl.loop(0, 4)
+    def _(turn):
+        line.prepare(turn, make)
 
     def beside(turn):
-        if turn < len(later):
-            line.prepare(*later[turn], make)
+        pl.when(turn + 4 < 2 * levels)(lambda: line.prepare(turn + 4, make))
 
     line.main(beside)
     small.arrive()
@@ -696,98 +689,90 @@
     )(*tables, *slots, small)
 
 
-def closing_kernel(size, dp_count, cuts, sum_cuts, *refs):
-    ins, outs, rest = refs[:6], refs[6:12], refs[12:]
-    lines = [LineReduce(size // 2, cuts, ins[i], outs[i], *rest[12 * i : 12 * i + 12]) for i in (0, 1)]
-    rest = rest[24:]
-    sums = Exchange("dp", dp_count, (False, False, True), sum_cuts, ins[2:5], outs[2:5], *rest[:3])
-    got, half, last = rest[3:6]
-    first = Exchange("expert", size, (False,), (1,), ins[5:6], [got], *rest[6:9])
-    second = Exchange("dp", dp_count, (False,), (1,), [half], [last], *rest[9:12])
-    for line in lines:
-        line.load()
+def closing_kernel(size, dp_count, local_count, cuts, sum_cuts, *refs):
+    tables, slots = refs[:local_count], refs[local_count : 2 * local_count]
+    parts_ref, *sum_refs = refs[2 * local_count : 2 * local_count + 5]
+    outs, rest = refs[2 * local_count + 5 : 2 * local_count + 11], refs[2 * local_count + 11 :]
+    levels = size // 2
+    back = LineReduce(levels, cuts, parts_ref, outs[0], *rest[:12])
+    mixed = LineReduce(levels, cuts, rest[12], outs[1], *rest[13:25])
+    qkv_got, out_got, gain_got, got, half, last = rest[25:31]
+    sems = rest[31:]
+    lands = [qkv_got, out_got, gain_got]
+    sums = Exchange("dp", dp_count, (False, False, True), sum_cuts, sum_refs[:3], lands, *sems[:3])
+    first = Exchange("expert", size, (False,), (1,), sum_refs[3:], [got], *sems[3:6])
+    second = Exchange("dp", dp_count, (False,), (1,), [half], [last], *sems[6:9])
+    back.load()
     greet("expert", [(peer, None) for peer in first.peers])
     greet("dp", [(peer, None) for peer in sums.peers])
     pl.semaphore_wait(pltpu.get_barrier_semaphore(), size + dp_count - 2)
     first.begin()
-    for line in lines:
-        line.begin()
+    back.begin()
     sums.stay()
-    turns = (size // 2 - 1) * cuts
     tall = half.shape[1]
+    make = functools.partial(collect_block, tables, slots)
 
     def beside(turn):
-        for q in range(len(sums.pieces)):
-            if q * turns // len(sums.pieces) == turn:
-                sums.send(*sums.pieces[q])
-        if turn == turns // 2:
+        pl.when(turn < sum_cuts[0])(lambda: sums.send(0, turn))
+        after = turn - sum_cuts[0]
+        pl.when((after >= 0) & (after < sum_cuts[1]))(lambda: sums.send(1, after))
+
+        @pl.when(after == sum_cuts[1])
+        def _():
+            sums.send(2, 0)
             first.arrive()
             for copy in range(dp_count):
                 rows = pl.ds(copy * tall, tall)
                 half[copy] = sum(got[i, rows, :] for i in range(size))
             second.begin()
 
-    lines[0].main(beside)
-    lines[1].main()
+        pl.when(turn < 2 * levels)(lambda: mixed.prepare(turn, make))
+
+    back.main(beside)
+    mixed.main()
     second.arrive()
     outs[5][...] = sum(last[i] for i in range(dp_count))
     sums.arrive()
-    for moves in lines + [first, second, sums]:
+    wide = outs[2].shape[2]
+    for j in range(3):
+        columns = slice(j * wide, (j + 1) * wide)
+        outs[2][j] = sum(qkv_got[copy, :, columns].astype(FULL) for copy in range(dp_count))
+    outs[3][...] = sum(out_got[copy].astype(FULL) for copy in range(dp_count))
+    outs[4][...] = sum(gain_got[copy] for copy in range(dp_count))
+    for moves in (back, mixed, first, second, sums):
         moves.finish()
 
 
-def closing(size, dp_count, parts, cuts, sums, shared, number):
-    block = parts[0].shape[1:]
+def closing(size, dp_count, parts, tables, slots, cuts, sums, shared, number):
+    block = parts.shape[1:]
     tall = shared.shape[1] // dp_count
     wide = shared.shape[2]
     sum_cuts = (8, 2, 1)
-    outs = [jax.ShapeDtypeStruct(block, parts[0].dtype)] * 2
-    outs += exchange_outs(dp_count, sums, (False, False, True))
-    outs.append(jax.ShapeDtypeStruct((tall, wide), FULL))
+    qkv, out, gain = exchange_outs(dp_count, sums, (False, False, True))
+    shapes = [(3, qkv.shape[1], qkv.shape[2] // 3), out.shape[1:], gain.shape[1:], (tall, wide)]
+    outs = [jax.ShapeDtypeStruct(block, parts.dtype)] * 2
+    outs += [jax.ShapeDtypeStruct(shape, FULL) for shape in shapes]
+    line = LineReduce.scratch(size, block, parts.dtype, cuts)
     return pl.pallas_call(
-        functools.partial(closing_kernel, size, dp_count, cuts, sum_cuts),
+        functools.partial(closing_kernel, size, dp_count, len(tables), cuts, sum_cuts),
         out_shape=outs,
-        in_specs=[ANY] * 6,
-        out_specs=[ANY] * 5 + [VMEM],
-        scratch_shapes=LineReduce.scratch(size, block, parts[0].dtype, cuts) * 2
-        + Exchange.scratch(dp_count, sum_cuts)
+        in_specs=[VMEM] * (2 * len(tables)) + [ANY] * 5,
+        out_specs=[ANY] * 2 + [VMEM] * 4,
+        scratch_shapes=line
+        + [pltpu.VMEM((size // 2,) + block, parts.dtype)]
+        + line
+        + [pltpu.VMEM(a.shape, a.dtype) for a in (qkv, out, gain)]
         + [pltpu.VMEM((size,) + shared.shape[1:], FULL)]
         + [pltpu.VMEM((dp_count, tall, wide), FULL)] * 2
+        + Exchange.scratch(dp_count, sum_cuts)
         + Exchange.scratch(size, (1,))
         + Exchange.scratch(dp_count, (1,)),
         compiler_params=pltpu.CompilerParams(
-            collective_id=number, has_side_effects=True, vmem_limit_bytes=48 << 20
+            collective_id=number, has_side_effects=True, vmem_limit_bytes=56 << 20
         ),
         cost_estimate=pl.CostEstimate(flops=0, transcendentals=0, bytes_accessed=200_000_000),
         name="closing",
-    )(*parts, *sums, shared)
-
-
-def collect_kernel(*refs):
-    tables, rows_refs, out_ref = refs[: len(refs) // 2], refs[len(refs) // 2 : -1], refs[-1]
-    total = 0.0
-    for table_ref, rows_ref in zip(tables, rows_refs):
-        total += jnp.dot(table_ref[0], rows_ref[0], preferred_element_type=FULL)
-    out_ref[0] = total.astype(LOW)
-
-
-def collect(tables, rows):
-    groups, tokens, capacity = tables[0].shape
-    width = rows[0].shape[2]
-    return pl.pallas_call(
-        collect_kernel,
-        out_shape=jax.ShapeDtypeStruct((groups, tokens, width), LOW),
-        grid=(groups,),
-        in_specs=[pl.BlockSpec((1, tokens, capacity), lambda g: (g, 0, 0))] * len(rows)
-        + [pl.BlockSpec((1, capacity, width), lambda g: (0, g, 0))] * len(rows),
-        out_specs=pl.BlockSpec((1, tokens, width), lambda g: (g, 0, 0)),
-        cost_estimate=pl.CostEstimate(
-            flops=2 * len(rows) * tables[0].size * width,
-            transcendentals=0,
-            bytes_accessed=4 * groups * tokens * width,
-        ),
-        name="collect",
-    )(*tables, *rows)
+    )(*tables, *slots, parts, *sums, shared)
 
 
 def across_cols(left_side, right_side):
@@ -796,138 +781,125 @@
     )
 
 
-def expert_kernel(
-    tiles,
-    x_ref,
-    dy_ref,
-    scale_ref,
-    gate_ref,
-    up_ref,
-    down_ref,
-    grads_ref,
-    out_ref,
-    back_ref,
-    dots_ref,
-    turned,
-    weighted,
-    out_sum,
-    back_sum,
-    side_buf,
-    down_buf,
-    sems,
-):
-    tile = pl.program_id(0)
-    slot = lax.rem(tile, 2)
-    width = gate_ref.shape[2]
-    copies, high = side_buf.shape[2], side_buf.shape[3]
-    some, low = down_buf.shape[1], down_buf.shape[2]
-    hidden = tiles * width
-
-    def leaving(at, half, slot):
-        columns = pl.ds(pl.multiple_of(half * hidden + at * width, 128), width)
-        target = grads_ref.at[:, pl.ds(0, high), columns]
-        return pltpu.make_async_copy(side_buf.at[slot, half], target, sems.at[slot, half])
-
-    def leaving_down(at, slot):
-        target = grads_ref.at[pl.ds(at * some, some), pl.ds(high, low), :]
-        return pltpu.make_async_copy(down_buf.at[slot], target, sems.at[slot, 2])
-
-    def settle(at, slot):
-        leaving(at, 0, slot).wait()
-        leaving(at, 1, slot).wait()
-        leaving_down(at, slot).wait()
-
-    @pl.when(tile == 0)
+def expert_kernel(first, count, tiles, x_ref, dy_ref, scale_ref, side_ref, down_ref, grads_ref, out_ref, back_ref, dots_ref,
+                  side_w, down_w, turned, turned_act, act, grad_side, side_buf, down_buf, w_sems, sems):
+    e, step = pl.program_id(0), pl.program_id(1)
+    slot = lax.rem(e, 2)
+    hidden, model = down_w.shape[1], down_w.shape[2]
+    width, wide = hidden // tiles, model // tiles
+    copies = grads_ref.shape[0]
+    high, low = model // copies, hidden // copies
+    part = side_buf.shape[1]
+
+    def loads(e, tile):
+        slot = lax.rem(e, 2)
+        out = []
+        for half in range(2):
+            columns = pl.ds(pl.multiple_of(half * hidden + tile * width, 128), width)
+            out.append(pltpu.make_async_copy(side_ref.at[first + e, :, columns], side_w.at[slot, :, columns], w_sems.at[slot, tile, half]))
+        rows = pl.ds(pl.multiple_of(tile * width, 128), width)
+        out.append(pltpu.make_async_copy(down_ref.at[first + e, rows], down_w.at[slot, rows], w_sems.at[slot, tile, 2]))
+        return out
+
+    def leaving(at):
+        e, chunk = lax.div(at, tiles), lax.rem(at, tiles)
+        slot = lax.rem(at, 2)
+        base = e * (high + low)
+        columns = pl.ds(pl.multiple_of(chunk * wide, 128), wide)
+        if wide >= high:
+            target = grads_ref.at[pl.ds(chunk * part, part), pl.ds(base, high)]
+        else:
+            target = grads_ref.at[pl.ds(lax.div(chunk * wide, high), 1), pl.ds(base + lax.rem(chunk * wide, high), wide)]
+        return (pltpu.make_async_copy(side_buf.at[slot], target, sems.at[slot, 0]),
+                pltpu.make_async_copy(down_buf.at[slot], grads_ref.at[:, pl.ds(base + high, low), columns], sems.at[slot, 1]))
+
+    @pl.when((e == 0) & (step == 0))
+    def _():
+        for tile in range(tiles):
+            for copy in loads(e, tile): copy.start()
+
+    @pl.when((e + 1 < count) & (step == 0))
+    def _():
+        for tile in range(tiles):
+            for copy in loads(e + 1, tile): copy.start()
+
+    @pl.when(step == 0)
     def _():
         turned[...] = x_ref[0].T
-        weighted[...] = (scale_ref[0] * dy_ref[0].astype(FULL)).astype(LOW)
-        out_sum[...] = jnp.zeros_like(out_sum)
-        back_sum[...] = jnp.zeros_like(back_sum)
-
-    @pl.when(tile >= 2)
+        dots_ref[...] = jnp.zeros_like(dots_ref)
+
+    @pl.when(step < tiles)
     def _():
-        settle(tile - 2, slot)
-
-    rows, grads = x_ref[0], weighted[...]
-    w_gate, w_up, w_down = gate_ref[0], up_ref[0], down_ref[0]
-    gate = jnp.dot(rows, w_gate, preferred_element_type=FULL)
-    up = jnp.dot(rows, w_up, preferred_element_type=FULL)
-    sigmoid = jax.nn.sigmoid(gate)
-    silu = gate * sigmoid
-    act = (silu * up).astype(LOW)
-    out_sum[...] += jnp.dot(act, w_down, preferred_element_type=FULL)
-    grad_act = across_cols(grads, w_down)
-    grad_gate = (grad_act * up * sigmoid * (1.0 + gate * (1.0 - sigmoid))).astype(LOW)
-    grad_up = (grad_act * silu).astype(LOW)
-    back_sum[...] += across_cols(grad_gate, w_gate) + across_cols(grad_up, w_up)
-    turned_rows = turned[...]
-    for half, grad in enumerate((grad_gate, grad_up)):
-        total = jnp.dot(turned_rows, grad, preferred_element_type=FULL).astype(LOW)
-        side_buf[slot, half] = total.reshape(copies, high, width)
-        leaving(tile, half, slot).start()
-    total = jnp.dot(act.T, grads, preferred_element_type=FULL).astype(LOW)
-    down_buf[slot] = total.reshape(some, low, total.shape[1])
-    leaving_down(tile, slot).start()
-
-    @pl.when(tile == tiles - 1)
+        for copy in loads(e, step): copy.wait()
+        rows, grads, scale = x_ref[0], dy_ref[0], scale_ref[0]
+        columns = pl.ds(pl.multiple_of(step * width, 128), width)
+        others = pl.ds(pl.multiple_of(hidden + step * width, 128), width)
+        gate = jnp.dot(rows, side_w[slot, :, columns], preferred_element_type=FULL)
+        up = jnp.dot(rows, side_w[slot, :, others], preferred_element_type=FULL)
+        grad_act = across_cols(grads, down_w[slot, columns, :])
+        sigmoid = jax.nn.sigmoid(gate)
+        silu = gate * sigmoid
+        raw = silu * up
+        dots_ref[0] += jnp.sum(raw * grad_act, axis=-1, keepdims=True)
+        weighted = (scale * raw).astype(LOW)
+        act[:, columns] = weighted
+        turned_act[columns, :] = weighted.T
+        grad_act = grad_act * scale
+        grad_side[:, columns] = (grad_act * up * sigmoid * (1.0 + gate * (1.0 - sigmoid))).astype(LOW)
+        grad_side[:, others] = (grad_act * silu).astype(LOW)
+
+    @pl.when(step >= tiles)
     def _():
-        final = out_sum[...]
-        dots_ref[0] = jnp.sum(final * dy_ref[0].astype(FULL), axis=-1, keepdims=True)
-        out_ref[0] = (scale_ref[0] * final).astype(LOW)
-        back_ref[0] = back_sum[...].astype(LOW)
-        settle(tile - 1, 1 - slot)
-        settle(tile, slot)
-
-
-def expert(j, dp_count, x_rows, dy_rows, scales, w_gate_up, w_down, tiles=4):
+        chunk = step - tiles
+        at = e * tiles + chunk
+        spot = lax.rem(at, 2)
+        columns = pl.ds(pl.multiple_of(chunk * wide, 128), wide)
+
+        @pl.when(at >= 2)
+        def _():
+            for copy in leaving(at - 2): copy.wait()
+        total = jnp.dot(turned[columns, :], grad_side[...], preferred_element_type=FULL)
+        side_buf[spot] = total.astype(LOW).reshape(side_buf.shape[1:])
+        leaving(at)[0].start()
+        total = jnp.dot(turned_act[...], dy_ref[0, :, columns], preferred_element_type=FULL)
+        down_buf[spot] = total.astype(LOW).reshape(down_buf.shape[1:])
+        leaving(at)[1].start()
+        back_ref[0, :, columns] = across_cols(grad_side[...], side_w[slot, columns, :]).astype(LOW)
+        out_ref[0, :, columns] = jnp.dot(act[...], down_w[slot, :, columns], preferred_element_type=FULL).astype(LOW)
+
+        @pl.when(at == count * tiles - 1)
+        def _():
+            for copy in leaving(at - 1) + leaving(at): copy.wait()
+
+def expert(first, count, dp_count, x_rows, dy_rows, scales, w_gate_up, w_down, tiles=4):
     _, slots, width = x_rows.shape
     hidden = w_down.shape[1]
-    tile = hidden // tiles
     high, low = width // dp_count, hidden // dp_count
-    some = tile // low
-    once = pl.Buffered(1)
-    row_spec = pl.BlockSpec((1, slots, width), lambda f: (j, 0, 0), pipeline_mode=once)
-    out_spec = pl.BlockSpec((1, slots, width), lambda f: (0, 0, 0), pipeline_mode=once)
+    wide = width // tiles
+    part = max(1, wide // high)
+    rs = pl.BlockSpec((1, slots, width), lambda e, f: (first + e, 0, 0))
+    os = pl.BlockSpec((1, slots, width), lambda e, f: (e, 0, 0))
+    sems = pltpu.SemaphoreType.DMA
     return pl.pallas_call(
-        functools.partial(expert_kernel, tiles),
-        out_shape=[
-            jax.ShapeDtypeStruct((dp_count, high + low, width), LOW),
-            jax.ShapeDtypeStruct((1, slots, width), LOW),
-            jax.ShapeDtypeStruct((1, slots, width), LOW),
-            jax.ShapeDtypeStruct((1, slots, 1), FULL),
-        ],
-        grid=(tiles,),
-        in_specs=[
-            row_spec,
-            row_spec,
-            pl.BlockSpec((1, slots, 1), lambda f: (j, 0, 0), pipeline_mode=once),
-            pl.BlockSpec((1, width, tile), lambda f: (j, 0, f)),
-            pl.BlockSpec((1, width, tile), lambda f: (j, 0, tiles + f)),
-            pl.BlockSpec((1, tile, width), lambda f: (j, f, 0)),
-        ],
-        out_specs=[
-            ANY,
-            out_spec,
-            out_spec,
-            pl.BlockSpec((1, slots, 1), lambda f: (0, 0, 0), pipeline_mode=once),
-        ],
-        scratch_shapes=[
-            pltpu.VMEM((width, slots), LOW),
-            pltpu.VMEM((slots, width), LOW),
-            pltpu.VMEM((slots, width), FULL),
-            pltpu.VMEM((slots, width), FULL),
-            pltpu.VMEM((2, 2, dp_count, high, tile), LOW),
-            pltpu.VMEM((2, some, low, width), LOW),
-            pltpu.SemaphoreType.DMA((2, 3)),
-        ],
-        compiler_params=pltpu.CompilerParams(vmem_limit_bytes=60 << 20),
+        functools.partial(expert_kernel, first, count, tiles),
+        out_shape=[jax.ShapeDtypeStruct((dp_count, count * (high + low), width), LOW),
+                   jax.ShapeDtypeStruct((count, slots, width), LOW), jax.ShapeDtypeStruct((count, slots, width), LOW),
+                   jax.ShapeDtypeStruct((count, slots, 1), FULL)],
+        grid=(count, 2 * tiles),
+        in_specs=[rs, rs, pl.BlockSpec((1, slots, 1), lambda e, f: (first + e, 0, 0)), ANY, ANY],
+        out_specs=[ANY, os, os, pl.BlockSpec((1, slots, 1), lambda e, f: (e, 0, 0))],
+        scratch_shapes=[pltpu.VMEM((min(2, count), width, 2 * hidden), LOW), pltpu.VMEM((min(2, count), hidden, width), LOW),
+                        pltpu.VMEM((width, slots), LOW), pltpu.VMEM((hidden, slots), LOW), pltpu.VMEM((slots, hidden), LOW), pltpu.VMEM((slots, 2 * hidden), LOW),
+                        pltpu.VMEM((2, part, min(wide, high), 2 * hidden), LOW), pltpu.VMEM((2, dp_count, low, wide), LOW),
+                        sems((min(2, count), tiles, 3)), sems((2, 2))],
+        compiler_params=pltpu.CompilerParams(vmem_limit_bytes=62 << 20),
         cost_estimate=pl.CostEstimate(
-            flops=18 * slots * width * hidden,
-            transcendentals=slots * hidden,
-            bytes_accessed=12 * width * hidden,
+            flops=18 * count * slots * width * hidden,
+            transcendentals=count * slots * hidden,
+            bytes_accessed=12 * count * width * hidden,
         ),
         name="expert",
-    )(x_rows, dy_rows, scales, w_gate_up, w_gate_up, w_down)
+    )(x_rows, dy_rows, scales, w_gate_up, w_down)
 
 
 def rms_scale(values):
@@ -970,10 +942,10 @@
     return values * cosine + pltpu.roll(values, values.shape[1] // 2, 1) * sine
 
 
-def allowed_pairs(column_ref, row_ref):
-    shape = (column_ref.shape[1], row_ref.shape[2])
+def allowed_pairs(column, row):
+    shape = (column.shape[0], row.shape[1])
     later = lax.broadcasted_iota(jnp.int32, shape, 0) >= lax.broadcasted_iota(jnp.int32, shape, 1)
-    return later & (column_ref[0] == row_ref[0])
+    return later & (column == row)
 
 
 def softmax(query, key, allowed):
@@ -988,7 +960,7 @@
 ):
     width = out_ref.shape[2]
     size = width // heads
-    allowed = allowed_pairs(column_ref, row_ref)
+    allowed = allowed_pairs(column_ref[0], row_ref[0])
     cosine, sine = turn_ref[0], turn_ref[1]
     for h in range(heads):
         parts = []
@@ -1041,43 +1013,22 @@
     )(rows, scales, gains, turns, column, row)
 
 
-def attend_back_kernel(
-    heads,
-    grad_ref,
-    w_ref,
-    kept_ref,
-    out_ref,
-    rows_ref,
-    scale_ref,
-    gain_ref,
-    turn_ref,
-    column_ref,
-    row_ref,
-    back_ref,
-    dots_ref,
-    gains_ref,
-    w_grad_ref,
-    w_sum,
-):
-    step = pl.program_id(0)
+def attend_back_block(heads, block, grad_ref, refs, back_ref, dots_ref, gains_ref, w_sum):
+    w_ref, kept_ref, out_ref, rows_ref, scale_ref, gain_ref, turn_ref, column_ref, row_ref = refs
     width = out_ref.shape[2]
     size = width // heads
     scaling = 1.0 / math.sqrt(size)
-    allowed = allowed_pairs(column_ref, row_ref)
+    allowed = allowed_pairs(column_ref[block], row_ref[block])
     cosine, sine = turn_ref[0], turn_ref[1]
-
-    @pl.when(step == 0)
-    def _():
-        w_sum[...] = jnp.zeros_like(w_sum)
-        gains_ref[...] = jnp.zeros_like(gains_ref)
-
-    grad_rows = grad_ref[0]
+    grad_rows = grad_ref[block]
     grad_out = across_cols(grad_rows, w_ref[...]).astype(LOW)
-    w_sum[...] += contract_rows(out_ref[0], grad_rows)
+    w_sum[...] += contract_rows(out_ref[block], grad_rows)
     dots = [0.0, 0.0]
     for h in range(heads):
         mine = slice(h * size, (h + 1) * size)
-        query, key, value = (kept_ref[0, :, pl.ds(p * width + h * size, size)] for p in range(3))
+        query, key, value = (
+            kept_ref[block, :, pl.ds(p * width + h * size, size)] for p in range(3)
+        )
         probs = softmax(query, key, allowed)
         grad = grad_out[:, mine]
         grad_value = contract_rows(probs.astype(LOW), grad)
@@ -1089,43 +1040,59 @@
         for part, grad_turned in enumerate((grad_query, grad_key)):
             columns = pl.ds(part * width + h * size, size)
             grad_normed = turn(grad_turned, cosine, -sine)
-            normed = rows_ref[0, :, columns] * scale_ref[0, :, part : part + 1]
+            normed = rows_ref[block, :, columns] * scale_ref[block, :, part : part + 1]
             gains_ref[part : part + 1, mine] += jnp.sum(grad_normed * normed, axis=0, keepdims=True)
             weighted = grad_normed * gain_ref[part : part + 1, mine]
             dots[part] += jnp.sum(weighted * normed, axis=-1, keepdims=True)
-            back_ref[0, :, columns] = weighted
-        back_ref[0, :, pl.ds(2 * width + h * size, size)] = grad_value
-    dots_ref[0] = jnp.concatenate(dots, axis=1)
-
-    @pl.when(step == pl.num_programs(0) - 1)
-    def _():
-        for copy in range(w_grad_ref.shape[0]):
-            wide = w_grad_ref.shape[2]
-            w_grad_ref[copy] = w_sum[:, copy * wide : (copy + 1) * wide].astype(LOW)
-
-
-def attend_back(heads, dp_count, grad, w_here, kept, out, rows, scales, gains, turns, column, row):
-    groups, length, model_dim = grad.shape
+            back_ref[block, :, columns] = weighted
+        back_ref[block, :, pl.ds(2 * width + h * size, size)] = grad_value
+    dots_ref[block] = jnp.concatenate(dots, axis=1)
+
+
+def attend_back_kernel(levels, cuts, heads, grad_ref, *refs):
+    reads, (back_ref, dots_ref, gains_ref, w_grad_ref, w_sum, held), sems = refs[:9], refs[9:15], refs[15:]
+    line = LineGather(levels, cuts, [grad_ref], [held], *sems)
+    line_barrier(levels)
+    line.begin()
+    w_sum[...] = jnp.zeros_like(w_sum)
+    gains_ref[...] = jnp.zeros_like(gains_ref)
+    line.staying(0).wait()
+
+    def landed(block):
+        attend_back_block(heads, block, held, reads, back_ref, dots_ref, gains_ref, w_sum)
+
+    line.main(landed)
+    wide = w_grad_ref.shape[2]
+    for copy in range(w_grad_ref.shape[0]):
+        w_grad_ref[copy] = w_sum[:, copy * wide : (copy + 1) * wide].astype(LOW)
+    line.finish(held=1)
+
+
+def attend_back(size, dp_count, heads, grad, arrays, number):
+    w_here, _, out, rows = arrays[:4]
     width = out.shape[2]
-    back = jax.ShapeDtypeStruct((groups, length, 3 * width), FULL)
-    dots = jax.ShapeDtypeStruct((groups, length, 2), FULL)
-    gain_sums = jax.ShapeDtypeStruct((2, width), FULL)
-    w_grad = jax.ShapeDtypeStruct((dp_count, width, model_dim // dp_count), LOW)
-    blocks = [block_of, whole_of, block_of, block_of, block_of, block_of, whole_of, whole_of]
-    arrays = [grad, w_here, kept, out, rows, scales, gains, turns, column, row]
+    tokens, model_dim = grad.shape
     return pl.pallas_call(
-        functools.partial(attend_back_kernel, heads),
-        out_shape=[back, dots, gain_sums, w_grad],
-        grid=(groups,),
-        in_specs=[f(a) for f, a in zip(blocks + [block_of] * 2, arrays)],
-        out_specs=[block_of(back), block_of(dots), whole_of(gain_sums), whole_of(w_grad)],
-        scratch_shapes=[pltpu.VMEM((width, model_dim), FULL)],
-        compiler_params=pltpu.CompilerParams(vmem_limit_bytes=48 << 20),
-        cost_estimate=pl.CostEstimate(
-            flops=4 * grad.size * width, transcendentals=0, bytes_accessed=10 * grad.size
+        functools.partial(attend_back_kernel, size // 2, 4, heads),
+        out_shape=[
+            jax.ShapeDtypeStruct(rows.shape, FULL),
+            jax.ShapeDtypeStruct((size, tokens, 2), FULL),
+            jax.ShapeDtypeStruct((2, width), FULL),
+            jax.ShapeDtypeStruct((dp_count, width, model_dim // dp_count), LOW),
+        ],
+        in_specs=[ANY] + [VMEM] * len(arrays),
+        out_specs=[VMEM] * 4,
+        scratch_shapes=[
+            pltpu.VMEM((width, model_dim), FULL),
+            pltpu.VMEM((size, tokens, model_dim), LOW),
+        ]
+        + LineGather.scratch(size, 4, 1),
+        compiler_params=pltpu.CompilerParams(
+            collective_id=number, has_side_effects=True, vmem_limit_bytes=48 << 20
         ),
+        cost_estimate=pl.CostEstimate(flops=0, transcendentals=0, bytes_accessed=150_000_000),
         name="attend_back",
-    )(*arrays)
+    )(grad, *arrays)
 
 
 def on_device(
@@ -1164,7 +1131,7 @@
     small = jnp.pad(small, ((0, 0), (0, 128 - small.shape[1])))
     numbers = jnp.concatenate([routes.T, segments, jnp.zeros((7, row_count), jnp.int32)], axis=0)
     x_all, numbers_all, qkv_here, small, out_full = opening(
-        line_count, dp_count, [layer_input, numbers], [4, 1], w_qkv, small, w_out, 1
+        line_count, dp_count, [layer_input, numbers], 4, w_qkv, small, w_out, 1
     )
     out_full = out_full.reshape(model_dim, model_dim)
     late_cotangent, x_all = lax.optimization_barrier((out_cotangent, x_all))
@@ -1231,19 +1198,21 @@
     slot_gates = jnp.sum(table.astype(FULL) * local_gates[:, :, None, :], axis=-1)
     slot_gates = slot_gates.transpose(1, 0, 2).reshape(local_count, slots, 1)
     out_rows, back_rows, slot_grads, grad_sums = [], [], [], []
-    for j in range(local_count):
+    both_rows = model_dim // dp_count + w_down.shape[1] // dp_count
+    for first, count in ((0, 1), (1, local_count - 1)):
         grads, out_row, back_row, dots = expert(
-            j, dp_count, expert_rows, dy_rows, slot_gates, w_gate_up, w_down
+            first, count, dp_count, expert_rows, dy_rows, slot_gates, w_gate_up, w_down
         )
         grads = grads.reshape(-1, model_dim)
-        grad_sums.append(lax.psum_scatter(grads, "dp", scatter_dimension=0, tiled=True))
-        out_rows.append(out_row)
-        back_rows.append(back_row.reshape(line_count, capacity, model_dim))
-        slot_grads.append(dots.reshape(line_count, capacity))
+        grads = lax.psum_scatter(grads, "dp", scatter_dimension=0, tiled=True)
+        grad_sums.append(grads.reshape(count, both_rows, model_dim))
+        for kept_list, rows in ((out_rows, out_row), (back_rows, back_row), (slot_grads, dots)):
+            for j in range(count):
+                kept_list.append(rows[j].reshape(line_count, capacity, rows.shape[2]))
     gate_rows = model_dim // dp_count
-    sum_gate_up = jnp.stack([both[:gate_rows] for both in grad_sums]).astype(FULL)
-    sum_down = jnp.stack([both[gate_rows:] for both in grad_sums]).astype(FULL)
-    slot_grads = jnp.stack(slot_grads, axis=1)
+    sum_gate_up = jnp.concatenate([both[:, :gate_rows] for both in grad_sums]).astype(FULL)
+    sum_down = jnp.concatenate([both[:, gate_rows:] for both in grad_sums]).astype(FULL)
+    slot_grads = jnp.stack([dots[:, :, 0] for dots in slot_grads], axis=1)
     grad_gates = jnp.sum(table.astype(FULL) * slot_grads[:, :, :, None], axis=2)
     grad_two, grad_gates = collect_reduce(line_count, returns, back_rows, grad_gates, 8)
     grad_gates = grad_gates.reshape(expert_count, row_count).T
@@ -1258,21 +1227,10 @@
     grad_resid = grad_out_rows + norm_back(grad_two * gain_mlp, normed_mlp, scale_mlp)
     grad_attn = grad_resid.astype(LOW)
 
-    (grad_attn_all,) = line_gather(line_count, [grad_attn], [4], 11)
     out_here = lax.dynamic_slice_in_dim(out_full, place * head_cols, head_cols, axis=0)
+    arrays = [out_here, kept, attended, projected, scales, both_gains, tables, column, row]
     back, dots, gain_pair, out_parts = attend_back(
-        heads_here,
-        dp_count,
-        grad_attn_all,
-        out_here,
-        kept,
-        attended,
-        projected,
-        scales,
-        both_gains,
-        tables,
-        column,
-        row,
+        line_count, dp_count, heads_here, grad_attn, arrays, 11
     )
     dots = dots.transpose(2, 0, 1).reshape(2 * line_count, row_count)
     (dots,) = exchange("expert", line_count, [dots], [True], 12)
@@ -1300,20 +1258,19 @@
     shared = shared.reshape(tall, dp_count, line_count, shard).transpose(2, 1, 0, 3)
     shared = shared.reshape(line_count, dp_count * tall, shard)
     shared = jnp.pad(shared, ((0, 0), (0, 0), (0, 128 - shard)))
-    out_rows = lax.optimization_barrier((out_rows, grad_one))[0]
-    grad_one, mixture, qkv_parts, out_parts, gain_pair, shared = closing(
+    grad_one, mixture, sum_qkv, sum_out, gain_pair, shared = closing(
         line_count,
         dp_count,
-        [grad_one, collect(returns, out_rows)],
+        grad_one,
+        returns,
+        out_rows,
         4,
         [qkv_parts, out_parts, gain_pair],
         shared,
         14,
     )
     output = (residual + mixture.astype(FULL)).astype(LOW)
-    sum_qkv = jnp.sum(qkv_parts.astype(FULL), axis=0).reshape(out_cols, 3, head_cols)
-    sum_out = jnp.sum(out_parts.astype(FULL), axis=0)
-    gain_pair = jnp.sum(gain_pair, axis=0)
+    sum_qkv = sum_qkv.transpose(1, 0, 2)
     shared = shared[:, :shard]
     grad_one = grad_one.astype(FULL)
     grad_inputs = grad_resid + norm_back(grad_one * gain_attn, normed_attn, scale_attn)

time: 775 us -> 744 us (0.960)
  Pallas kernels: 630 us -> 598 us
    pallas_call x5 -> x4, Pallas kernels: 203 us -> 152 us  [call(): pl.pallas_call(kernel, out_shape=outs, in_specs=[ANY] * len(arrays), out_...]
    slice x0 -> x7, local copies, waits for them, and re-layouts: none -> 18.5 us  [the longest x3 11.2 us: on_device(): kept_list.append(rows[j].reshape(line_count, capacity, rows.shape[2]))]
    pallas_call x6 -> x4, Pallas kernels: 279 us -> 296 us  [the longest x1 137 us: closing(): pl.pallas_call(functools.partial(closing_kernel, size, dp_count, len(tabl...]
    unnamed x85 -> x106, local copies, waits for them, and re-layouts: 26 us -> 16.8 us
  transfers between devices with their start and end apart: 4 -> 3, of which waited for: 0 -> 0; matrix products, arithmetic and copies ran while one was open for 11% -> 12% of each run, Pallas kernels for 57% -> 56%
where the time goes in v4:
time: 744 us; the launch traced here: 740 us
  Pallas kernels  598 us (80%)
  local copies, waits for them, and re-layouts  55.2 us (7%)
  other arithmetic  36.8 us (5%)
  matrix products  34.2 us (5%)
  between operations  14.8 us (2%)
    pallas_call x4, Pallas kernels, call(): pl.pallas_call(kernel, out_shape=outs, in_specs=[ANY] * len(arrays), out_...  152 us
    pallas_call x1, Pallas kernels, closing(): pl.pallas_call(functools.partial(closing_kernel, size, dp_count, len(tabl...  137 us
    pallas_call x2, Pallas kernels, expert(): pl.pallas_call(functools.partial(expert_kernel, first, count, tiles), out...  101 us
    pallas_call x1, Pallas kernels, collect_reduce(): pl.pallas_call(functools.partial(collect_reduce_kernel, levels, cuts, len...  83.7 us
    pallas_call x1, Pallas kernels, attend_back(): pl.pallas_call(functools.partial(attend_back_kernel, size // 2, 4, heads)...  57.9 us
    pallas_call x1, Pallas kernels, gather_place(): pl.pallas_call(functools.partial(gather_place_kernel, size // 2, cuts), o...  53.7 us
    unnamed x106, local copies, waits for them, and re-layouts  16.8 us
  transfers between devices with their start and end apart: 3, of which 0 were waited for; matrix products, arithmetic and copies ran while one was open for 12% of the time, Pallas kernels for 56%

profile of v4, /device:TPU:16, one launch (start us, length us, event | category | flops | bytes accessed | tf_op | source)
XLA Modules:
  0.0 740.3 jit_solution(5394987227642237163)
XLA Ops:
  15.3 97.6 %opening.1 = (bf16[8,192,2048]{2,1,0:T(8,128)(2,1)}, s32[8,16,192]{2,1,0:T(8,128)S(1)}, bf16[4,8,64,768]{3,2,1,0:T(8,128)(2,1)S(1)}, bf16[4,8,64,128]{3,2,1,0:T(8,128)(2,1)S(1)}, bf16[4,8,64,2048]{3,2,1,0:T(8,128)(2,1)}) custom-call(bf16[192,2048]{1,0:T(8,128)(2,1)S(1)} %copy-done.1, s32[16,192]{1,0:T(8,128)S(1)} %add_add_fusion.refs_1_, ...), custom_call_target="tpu_custom_call" | custom-call | bytes 200000000 | tf_op jit(solution)/shard_map/opening/pallas_call | solution.py:180
  117.5 4.2 multiply_reduce_fusion.1
  122.2 4.2 multiply_convert_fusion.1
  126.4 8.6 %fusion.49 = f32[1536,768]{1,0:T(8,128)} fusion(bf16[1536,2048]{1,0:T(8,128)(2,1)} %bitcast.130, bf16[2048,768]{1,0:T(8,128)(2,1)S(1)} %bitcast.121), kind=kOutput, calls=%fused_computation.124 | convolution fusion | flops 4831838208 | bytes 14155776 | tf_op jit(solution)/shard_map/dot_general | solution.py:1152
  137.6 9.3 %exchange_expert.3 = f32[8,16,192]{2,1,0:T(8,128)S(1)} custom-call(f32[16,192]{1,0:T(8,128)S(1)} %reshape.189.refs_0_), custom_call_target="tpu_custom_call" | custom-call | bytes 30000000 | tf_op jit(solution)/shard_map/exchange_expert/pallas_call | solution.py:180
  150.0 12.6 %attend.1 = (bf16[8,192,768]{2,1,0:T(8,128)(2,1)}, bf16[8,192,256]{2,1,0:T(8,128)(2,1)}) custom-call(f32[8,192,768]{2,1,0:T(8,128)} %bitcast.9.rows_ref.refs_3_, f32[8,192,2]{2,1,0:T(8,128)} %bitcast.111, f32[2,256]{1,0:T(2,128)} %pad_maximum_fusion.6.gain_ref.refs_5_, f32[2,192,128]{2,1,0:T(8,128)} %pad_maximum_fusion.3.turn_ref.refs_6_, ...), custom_call_target="tpu_custom_call" | custom-call | flops 905969664 | bytes 9437184 | tf_op jit(solution)/shard_map/attend/pallas_call | solution.py:996
  163.8 31.3 %exchange_expert.4 = bf16[8,192,256]{2,1,0:T(8,128)(2,1)S(1)} custom-call(bf16[8,192,256]{2,1,0:T(8,128)(2,1)S(1)} %copy-done.9), custom_call_target="tpu_custom_call" | custom-call | bytes 30000000 | tf_op jit(solution)/shard_map/exchange_expert/pallas_call | solution.py:180
  195.5 5.3 multiply_reduce_fusion.4
  202.2 53.7 %gather_place.1 = (bf16[3,576,2048]{2,1,0:T(8,128)(2,1)}, bf16[3,576,2048]{2,1,0:T(8,128)(2,1)}, f32[8,24,192]{2,1,0:T(8,128)S(1)}) custom-call(bf16[192,2048]{1,0:T(8,128)(2,1)S(1)} %multiply_convert_fusion.2.refs_0_, f32[24,192]{1,0:T(8,128)S(1)} %fusion.35.refs_1_, bf16[8,216,192]{2,1,0:T(8,128)(2,1)S(1)} %fusion.5.refs_2_, bf16[8,192,2048]{2,1,0:T(8,128)(2,1)} %bitcast.162), custom_call_target="tpu_custom_call" | custom-call | flops 2717908992 | bytes 150000000 | tf_op jit(solution)/shard_map/gather_place/pallas_call | solution.py:615
  257.7 35.5 %expert.2 = (bf16[4,768,2048]{2,1,0:T(8,128)(2,1)}, bf16[1,576,2048]{2,1,0:T(8,128)(2,1)}, bf16[1,576,2048]{2,1,0:T(8,128)(2,1)}, f32[1,576,1]{2,1,0:T(8,128)}) custom-call(bf16[3,576,2048]{2,1,0:T(8,128)(2,1)} %get-tuple-element.51.x_ref, bf16[3,576,2048]{2,1,0:T(8,128)(2,1)} %get-tuple-element.52.dy_ref, f32[3,576,1]{2,1,0:T(8,128)} %reshape.208.scale_ref, ...), custom_call_target="tpu_custom_call" | custom-call | flops 21743271936 | bytes 25165824 | tf_op jit(solution)/shard_map/expert/pallas_call | solution.py:883
  293.7 65.7 %expert.3 = (bf16[4,1536,2048]{2,1,0:T(8,128)(2,1)}, bf16[2,576,2048]{2,1,0:T(8,128)(2,1)}, bf16[2,576,2048]{2,1,0:T(8,128)(2,1)}, f32[2,576,1]{2,1,0:T(8,128)}) custom-call(bf16[3,576,2048]{2,1,0:T(8,128)(2,1)} %get-tuple-element.51.x_ref, bf16[3,576,2048]{2,1,0:T(8,128)(2,1)} %get-tuple-element.52.dy_ref, f32[3,576,1]{2,1,0:T(8,128)} %reshape.208.scale_ref, ...), custom_call_target="tpu_custom_call" | custom-call | flops 43486543872 | bytes 50331648 | tf_op jit(solution)/shard_map/expert/pallas_call | solution.py:883
  368.0 5.5 fusion.43
  373.6 83.7 %collect_reduce.1 = (bf16[192,2048]{1,0:T(8,128)(2,1)S(1)}, f32[8,3,192]{2,1,0:T(4,128)S(1)}) custom-call(bf16[8,192,72]{2,1,0:T(8,128)(2,1)S(1)} %copy-done.7, bf16[8,192,72]{2,1,0:T(8,128)(2,1)S(1)} %copy-done.8, bf16[8,192,72]{2,1,0:T(8,128)(2,1)S(1)} %fusion.19.refs_2_, bf16[8,72,2048]{2,1,0:T(8,128)(2,1)S(1)} %bitcast.118, ...), custom_call_target="tpu_custom_call" | custom-call | bytes 150000000 | tf_op jit(solution)/shard_map/collect_reduce/pallas_call | solution.py:673
  458.4 2.7 multiply_reduce_fusion.2
  463.1 57.9 %attend_back.1 = (f32[8,192,768]{2,1,0:T(8,128)}, f32[8,192,2]{2,1,0:T(8,128)S(1)}, f32[2,256]{1,0:T(2,128)S(1)}, bf16[4,256,512]{2,1,0:T(8,128)(2,1)S(1)}) custom-call(bf16[192,2048]{1,0:T(8,128)(2,1)S(1)} %fusion.42.grad_ref, bf16[256,2048]{1,0:T(8,128)(2,1)} %constant_dynamic-slice_fusion.refs_0_, bf16[8,192,768]{2,1,0:T(8,128)(2,1)} %get-tuple-element.62.refs_1_, ...), custom_call_target="tpu_custom_call" | custom-call | bytes 150000000 | tf_op jit(solution)/shard_map/attend_back/pallas_call | solution.py:1075
  524.3 14.2 %exchange_expert.5 = f32[8,16,192]{2,1,0:T(8,128)S(1)} custom-call(f32[16,192]{1,0:T(8,128)S(1)} %bitcast.120), custom_call_target="tpu_custom_call" | custom-call | bytes 30000000 | tf_op jit(solution)/shard_map/exchange_expert/pallas_call | solution.py:180
  540.6 3.9 fusion.14
  544.8 10.3 %multiply_reduce_fusion = (f32[2048]{0:T(1024)S(1)}, bf16[1536,2048]{1,0:T(8,128)(2,1)}, bf16[1536,2048]{1,0:T(8,128)(2,1)}) fusion(bf16[8,192,2048]{2,1,0:T(8,128)(2,1)} %get-tuple-element.44, f32[1536]{0:T(1024)S(1)} %rsqrt.38, f32[2048]{0:T(1024)S(1)} %bitcast.149, bf16[2048,768]{1,0:T(8,128)(2,1)S(1)} %bitcast.122, bf16[1536,256]{1,0:T(8,128)(2,1)S(1)} %slice.199, ...), kind=kOutput, calls=%fused_computation.1 | convolution fusion | flops 4860934144 | bytes 24401920 | tf_op jit(solution)/shard_map/dot_general | solution.py:932
  556.5 5.5 fusion.44
  562.7 6.7 convolution_convert_fusion
  569.4 136.7 %closing.1 = (bf16[192,2048]{1,0:T(8,128)(2,1)}, bf16[192,2048]{1,0:T(8,128)(2,1)}, f32[3,512,256]{2,1,0:T(8,128)}, f32[256,512]{1,0:T(8,128)}, f32[2,256]{1,0:T(2,128)}, /*index=5*/f32[32,128]{1,0:T(8,128)}) custom-call(bf16[8,192,72]{2,1,0:T(8,128)(2,1)} %get-tuple-element.118.refs_0_, bf16[8,192,72]{2,1,0:T(8,128)(2,1)} %get-tuple-element.119.refs_1_, ...), custom_call_target="tpu_custom_call" | custom-call | bytes 200000000 | tf_op jit(solution)/shard_map/closing/pallas_call | solution.py:756
  711.7 3.6 fusion.9
  722.6 3.1 maximum_convert_fusion.1
  725.8 5.6 maximum_convert_fusion
  (205 shorter events, 58.0 us)
Async XLA Ops:
  7.2 195.0 %all-gather.3.cloned.1.call-start = ((), (), s32[]{:S(2)}) async-start(), calls=%async_computation.4 | async-start | bytes 7077888 | tf_op jit(solution)/shard_map/all_gather | solution.py:1138
  114.6 87.1 %copy-start.4 = (bf16[4,8,64,128]{3,2,1,0:T(8,128)(2,1)}, bf16[4,8,64,128]{3,2,1,0:T(8,128)(2,1)S(1)}, u32[]{:S(2)}) copy-start(bf16[4,8,64,128]{3,2,1,0:T(8,128)(2,1)S(1)} %get-tuple-element.45) | copy-start | bytes 1572868
  114.6 600.7 %reduce-scatter.3.cloned.1.call-start = ((), (), s32[]{:S(2)}) async-start(), calls=%async_computation.2 | async-start | bytes 15728640 | tf_op jit(solution)/shard_map/reduce_scatter | solution.py:1207
  121.8 79.1 %copy-start.39 = (f32[2048,1]{0,1:T(1,128)}, f32[2048,1]{0,1:T(1,128)S(1)}, u32[]{:S(2)}) copy-start(f32[2048,1]{0,1:T(1,128)S(1)} %get-tuple-element.105) | copy-start | bytes 24580
  162.6 32.9 %copy-start.2 = (bf16[192,2048]{1,0:T(8,128)(2,1)S(1)}, bf16[192,2048]{1,0:T(8,128)(2,1)}, u32[]{:S(2)}) copy-start(bf16[192,2048]{1,0:T(8,128)(2,1)} %refs_0_.1) | copy-start | bytes 2359300
  163.8 31.6 %copy-start.43 = (s32[192,8]{0,1:T(8,128)S(1)}, s32[192,8]{0,1:T(8,128)}, u32[]{:S(2)}) copy-start(s32[192,8]{0,1:T(8,128)} %param.16) | copy-start | bytes 18436
  202.1 53.8 %copy-start.44 = (f32[192]{0:T(256)}, f32[192]{0:T(256)S(1)}, u32[]{:S(2)}) copy-start(f32[192]{0:T(256)S(1)} %get-tuple-element.114) | copy-start | bytes 2308
  202.1 53.8 %copy-start.48 = (f32[192]{0:T(256)}, f32[192]{0:T(256)S(1)}, u32[]{:S(2)}) copy-start(f32[192]{0:T(256)S(1)} %fusion.38) | copy-start | bytes 2308
  293.2 425.2 %reduce-scatter.5.cloned.1.call-start = ((), (), s32[]{:S(2)}) async-start(), calls=%async_computation.3 | async-start | bytes 31457280 | tf_op jit(solution)/shard_map/reduce_scatter | solution.py:1207
  362.0 11.5 %copy-start.6 = (bf16[8,192,72]{2,1,0:T(8,128)(2,1)}, bf16[8,192,72]{2,1,0:T(8,128)(2,1)S(1)}, u32[]{:S(2)}) copy-start(bf16[8,192,72]{2,1,0:T(8,128)(2,1)S(1)} %fusion.19.refs_2_) | copy-start | bytes 663556
  368.0 5.6 copy-start.7
  368.0 5.6 copy-start.8
  373.5 84.7 %copy-start.45 = (f32[192]{0:T(256)S(1)}, f32[192]{0:T(256)}, u32[]{:S(2)}) copy-start(f32[192]{0:T(256)} %copy-done.44) | copy-start | bytes 2308
  373.6 84.7 %copy-start.49 = (f32[192]{0:T(256)S(1)}, f32[192]{0:T(256)}, u32[]{:S(2)}) copy-start(f32[192]{0:T(256)} %copy-done.48) | copy-start | bytes 2308
  373.6 84.8 %copy-start.5 = (bf16[4,8,64,128]{3,2,1,0:T(8,128)(2,1)S(1)}, bf16[4,8,64,128]{3,2,1,0:T(8,128)(2,1)}, u32[]{:S(2)}) copy-start(bf16[4,8,64,128]{3,2,1,0:T(8,128)(2,1)} %copy-done.4) | copy-start | bytes 1572868
  373.6 84.8 %copy-start.40 = (f32[2048,1]{0,1:T(1,128)S(1)}, f32[2048,1]{0,1:T(1,128)}, u32[]{:S(2)}) copy-start(f32[2048,1]{0,1:T(1,128)} %copy-done.39) | copy-start | bytes 24580
  373.6 84.8 %copy-start.47 = (f32[192]{0:T(256)S(1)}, f32[192]{0:T(256)}, u32[]{:S(2)}) copy-start(f32[192]{0:T(256)} %copy-done.46) | copy-start | bytes 2308
  522.8 21.6 %copy-start.20 = (f32[2,256]{1,0:T(2,128)}, f32[2,256]{1,0:T(2,128)S(1)}, u32[]{:S(2)}) copy-start(f32[2,256]{1,0:T(2,128)S(1)} %get-tuple-element.66.refs_9_) | copy-start | bytes 6148
  544.5 10.6 %copy-start.35 = (bf16[1536,256]{1,0:T(8,128)(2,1)}, bf16[1536,256]{1,0:T(8,128)(2,1)S(1)}, u32[]{:S(2)}) copy-start(bf16[1536,256]{1,0:T(8,128)(2,1)S(1)} %get-tuple-element.86) | copy-start | bytes 2359300
  556.5 6.2 copy-start.50
  569.4 142.3 %copy-start.29 = (f32[192,2048]{1,0:T(8,128)S(1)}, f32[192,2048]{1,0:T(8,128)}, u32[]{:S(2)}) copy-start(f32[192,2048]{1,0:T(8,128)} %copy-done.28) | copy-start | bytes 4718596
  569.4 142.3 %copy-start.31 = (bf16[192,2048]{1,0:T(8,128)(2,1)S(1)}, bf16[192,2048]{1,0:T(8,128)(2,1)}, u32[]{:S(2)}) copy-start(bf16[192,2048]{1,0:T(8,128)(2,1)} %param.14) | copy-start | bytes 2359300
  706.1 5.6 copy-start.27
  725.7 5.6 copy-start.32
  (30 other events, 77.8 us)
Sparse Core Ops, SparseCore 0:
  114.7 78.5 all-gather.2
  293.3 126.5 reduce-scatter.2
  423.0 267.5 reduce-scatter.4

commit v5 on v4

--- a/solution.py
+++ b/solution.py
@@ -413,21 +413,17 @@
 
 
 def opening_kernel(size, dp_count, count, cuts, *refs):
-    levels = size // 2
-    ins, (w_ref, small_ref, sheet_ref) = refs[:count], refs[count : count + 3]
-    outs, rest = refs[count + 3 : 2 * count + 3], refs[2 * count + 3 :]
-    w_out, small_out, sheet_out = rest[:3]
-    line = LineGather(levels, cuts, ins, outs, *rest[3:8])
-    send_sem, recv_sem, own_sem = rest[8:11]
-    level, side, other = line.level, line.side, line.other
+    ins, (w_ref, small_ref) = refs[:count], refs[count : count + 2]
+    outs, (w_out, small_out), rest = refs[count + 2 : 2 * count + 2], refs[2 * count + 2 :][:2], refs[2 * count + 4 :]
+    line = LineGather(size // 2, cuts, ins, outs, *rest[:5])
+    send_sem, recv_sem, own_sem = rest[5:8]
     place, mine = line.place, lax.axis_index("dp")
     peers = around("expert", size)
     width = w_out.shape[3] // 3
     mine_refs = [w_out.at[mine], small_out.at[mine]]
     across = Exchange(
-        "dp", dp_count, (True,) * 2, (size,) * 2, mine_refs, [w_out, small_out], *rest[11:14]
-    )
-    up_send, down_send, line_recv, dp_send, dp_recv, side_send, side_recv, sheet_own = rest[14:]
+        "dp", dp_count, (True,) * 2, (size,) * 2, mine_refs, [w_out, small_out], *rest[8:]
+    )
     greet("expert", [(peer, None) for peer in peers])
     greet("dp", [(peer, None) for peer in across.peers])
     pl.semaphore_wait(pltpu.get_barrier_semaphore(), size + dp_count - 2)
@@ -444,45 +440,12 @@
         sems = send_sem.at[shift, j], recv_sem.at[landing, j]
         return remote(source, target, *sems, {"expert": peers[shift]})
 
-    def sheet_line(far, own, send, target):
-        landing = sheet_out.at[mine, 2 * far + side]
-        source = sheet_ref if own else landing
-        return remote(source, landing, send.at[far], line_recv.at[far], {"expert": target})
-
-    def sheet_up(far, own=False):
-        return sheet_line(far, own, up_send, place + 2)
-
-    def sheet_down(far, own=False):
-        return sheet_line(far, own, down_send, place - 2)
-
-    def sheet_dp(far, shift, copy, own=False):
-        landing = sheet_out.at[copy, 2 * far + side]
-        source = sheet_ref if own else landing
-        sems = dp_send.at[shift, far], dp_recv.at[copy, far]
-        return remote(source, landing, *sems, {"dp": across.peers[shift]})
-
-    def sheet_side(far, copy, whose, own=False):
-        landing = sheet_out.at[copy, 2 * far + whose]
-        source = sheet_ref if own else landing
-        sems = side_send.at[copy, far], side_recv.at[copy, far]
-        return remote(source, landing, *sems, {"expert": other})
-
-    def spread_sheet(far, own=False):
-        for shift in range(dp_count - 1):
-            sheet_dp(far, shift, mine, own).start()
-        sheet_side(far, mine, side, own).start()
-
     own = [pltpu.make_async_copy(*ends(place, place, j), own_sem.at[j]) for j in range(4)]
-    sheet_stays = pltpu.make_async_copy(sheet_ref, sheet_out.at[mine, place], sheet_own.at[0])
     for shift in range(size - 1):
         for j in range(4):
             sending(shift, place, j).start()
     for copy in own:
         copy.start()
-    sheet_stays.start()
-    pl.when(line.has_up)(sheet_up(level, True).start)
-    pl.when(line.has_down)(sheet_down(level, True).start)
-    spread_sheet(level, True)
     line.begin()
     for copy in own:
         copy.wait()
@@ -493,51 +456,22 @@
             sending(shift, peer, j).wait_recv()
         across.send(0, peer)
         across.send(1, peer)
-
-    def pass_sheets(step):
-        @pl.when(level >= step)
-        def _():
-            sheet_up(level - step).wait_recv()
-            pl.when(line.has_up)(sheet_up(level - step).start)
-            spread_sheet(level - step)
-
-        @pl.when(level + step < levels)
-        def _():
-            sheet_down(level + step).wait_recv()
-            pl.when(line.has_down)(sheet_down(level + step).start)
-            spread_sheet(level + step)
-
-    line.main(before=pass_sheets)
-    for shift, peer in enumerate(across.peers):
-        for far in range(levels):
-            sheet_dp(far, shift, peer).wait_recv()
-            sheet_side(far, peer, side).start()
+    line.main()
     line.finish()
     for shift in range(size - 1):
         for j in range(4):
             sending(shift, place, j).wait_send()
     across.land()
     across.finish()
-    for far in range(levels):
-        pl.when(line.has_up & (level >= far))(sheet_up(far).wait_send)
-        pl.when(line.has_down & (level <= far))(sheet_down(far).wait_send)
-        for shift in range(dp_count - 1):
-            sheet_dp(far, shift, mine).wait_send()
-        for copy in range(dp_count):
-            sheet_side(far, copy, 1 - side).wait_recv()
-            sheet_side(far, copy, side).wait_send()
-    sheet_stays.wait()
-
-
-def opening(size, dp_count, arrays, cuts, weights, small, sheet, number):
+
+
+def opening(size, dp_count, arrays, cuts, weights, small, number):
     sems = pltpu.SemaphoreType.DMA
-    levels = size // 2
     outs = [jax.ShapeDtypeStruct((size,) + a.shape, a.dtype) for a in arrays]
     rows, columns = weights.shape
     whole = (dp_count, size, rows)
     outs.append(jax.ShapeDtypeStruct(whole + (columns // size,), weights.dtype))
     outs.append(jax.ShapeDtypeStruct(whole + (small.shape[1],), small.dtype))
-    outs.append(jax.ShapeDtypeStruct((dp_count, size) + sheet.shape, sheet.dtype))
     return call(
         functools.partial(opening_kernel, size, dp_count, len(arrays), cuts),
         "opening",
@@ -545,13 +479,94 @@
         outs,
         LineGather.scratch(size, cuts, len(arrays))
         + [sems((size, 4)), sems((size, 4)), sems((4,))]
-        + Exchange.scratch(dp_count, (size, size))
-        + [sems((levels,))] * 3
-        + [sems((dp_count, levels))] * 4
-        + [sems((1,))],
-        list(arrays) + [weights, small, sheet],
+        + Exchange.scratch(dp_count, (size, size)),
+        list(arrays) + [weights, small],
         200_000_000,
     )
+
+
+class Sheets:
+    def __init__(self, size, dp_count, source, target, *sems):
+        self.levels, self.dp_count, self.ins, self.out = size // 2, dp_count, source, target
+        self.up_send, self.down_send, self.line_recv, self.dp_send, self.dp_recv = sems[:5]
+        self.side_send, self.side_recv, self.own_sem = sems[5:]
+        self.place, self.level, self.side, self.other = line_place()
+        self.has_up, self.has_down = self.level < self.levels - 1, self.level > 0
+        self.mine, self.peers = lax.axis_index("dp"), around("dp", dp_count)
+
+    @staticmethod
+    def scratch(size, dp_count):
+        sems, levels = pltpu.SemaphoreType.DMA, size // 2
+        return [sems((levels,))] * 3 + [sems((dp_count, levels))] * 4 + [sems((1,))]
+
+    def along(self, far, own, send, target):
+        landing = self.out.at[self.mine, 2 * far + self.side]
+        source = self.ins if own else landing
+        return remote(source, landing, send.at[far], self.line_recv.at[far], {"expert": target})
+
+    def up(self, far, own=False):
+        return self.along(far, own, self.up_send, self.place + 2)
+
+    def down(self, far, own=False):
+        return self.along(far, own, self.down_send, self.place - 2)
+
+    def over(self, far, shift, copy, own=False):
+        landing = self.out.at[copy, 2 * far + self.side]
+        source = self.ins if own else landing
+        sems = self.dp_send.at[shift, far], self.dp_recv.at[copy, far]
+        return remote(source, landing, *sems, {"dp": self.peers[shift]})
+
+    def across(self, far, copy, whose, own=False):
+        landing = self.out.at[copy, 2 * far + whose]
+        source = self.ins if own else landing
+        sems = self.side_send.at[copy, far], self.side_recv.at[copy, far]
+        return remote(source, landing, *sems, {"expert": self.other})
+
+    def spread(self, far, own=False):
+        for shift in range(self.dp_count - 1):
+            self.over(far, shift, self.mine, own).start()
+        self.across(far, self.mine, self.side, own).start()
+
+    def staying(self):
+        target = self.out.at[self.mine, self.place]
+        return pltpu.make_async_copy(self.ins, target, self.own_sem.at[0])
+
+    def begin(self):
+        pl.when(self.has_up)(self.up(self.level, True).start)
+        pl.when(self.has_down)(self.down(self.level, True).start)
+        self.spread(self.level, True)
+        self.staying().start()
+
+    def forward(self, step):
+        @pl.when(self.level >= step)
+        def _():
+            self.up(self.level - step).wait_recv()
+            pl.when(self.has_up)(self.up(self.level - step).start)
+            self.spread(self.level - step)
+
+        @pl.when(self.level + step < self.levels)
+        def _():
+            self.down(self.level + step).wait_recv()
+            pl.when(self.has_down)(self.down(self.level + step).start)
+            self.spread(self.level + step)
+
+    def cross(self, far):
+        for shift, peer in enumerate(self.peers):
+            self.over(far, shift, peer).wait_recv()
+            self.across(far, peer, self.side).start()
+
+    def finish(self):
+        @pl.loop(0, self.levels)
+        def _(far):
+            pl.when(self.has_up & (self.level >= far))(self.up(far).wait_send)
+            pl.when(self.has_down & (self.level <= far))(self.down(far).wait_send)
+            for shift in range(self.dp_count - 1):
+                self.over(far, shift, self.mine).wait_send()
+            for copy in range(self.dp_count):
+                self.across(far, copy, 1 - self.side).wait_recv()
+                self.across(far, copy, self.side).wait_send()
+
+        self.staying().wait()
 
 
 VMEM = pl.BlockSpec(memory_space=pltpu.VMEM)
@@ -955,62 +970,164 @@
     return powers / jnp.sum(powers, axis=-1, keepdims=True)
 
 
-def attend_kernel(
-    heads, rows_ref, scale_ref, gain_ref, turn_ref, column_ref, row_ref, kept_ref, out_ref
-):
+def attend_block(heads, block, rows_ref, scales, gain_ref, turn_ref, column, row, kept_ref, out_ref):
     width = out_ref.shape[2]
     size = width // heads
-    allowed = allowed_pairs(column_ref[0], row_ref[0])
+    allowed = allowed_pairs(column, row)
     cosine, sine = turn_ref[0], turn_ref[1]
     for h in range(heads):
         parts = []
         for part in range(3):
             columns = pl.ds(part * width + h * size, size)
-            values = rows_ref[0, :, columns]
+            values = rows_ref[block, :, columns]
             if part < 2:
-                values = values * scale_ref[0, :, part : part + 1]
+                values = values * scales[part]
                 values = values * gain_ref[part : part + 1, h * size : (h + 1) * size]
                 values = turn(values, cosine, sine)
             parts.append(values.astype(LOW))
-            kept_ref[0, :, columns] = parts[-1]
+            kept_ref[block, :, columns] = parts[-1]
         query, key, value = parts
         probs = softmax(query, key, allowed).astype(LOW)
-        out_ref[0, :, pl.ds(h * size, size)] = jnp.dot(
+        out_ref[block, :, pl.ds(h * size, size)] = jnp.dot(
             probs, value, preferred_element_type=FULL
         ).astype(LOW)
 
 
-def block_of(array):
-    rest = array.shape[1:]
-    return pl.BlockSpec((1,) + rest, lambda g: (g,) + (0,) * len(rest))
-
-
-def whole_of(array):
-    return pl.BlockSpec(array.shape, lambda g: (0,) * array.ndim, pipeline_mode=pl.Buffered(1))
-
-
-def attend(heads, rows, scales, gains, turns, column, row):
-    groups, length, width = rows.shape
-    kept = jax.ShapeDtypeStruct((groups, length, width), LOW)
-    out = jax.ShapeDtypeStruct((groups, length, width // 3), LOW)
+def attention_kernel(size, dp_count, heads, *refs):
+    x_ref, w_ref, gain_ref, gains_ref, turn_ref, column_ref, row_ref, sheet_ref = refs[:8]
+    h_out, rows_out, scale_ref, kept_ref, out_ref, own_out, sheet_out = refs[8:15]
+    x_held, h_held, rows, sums, squares, got = refs[15:21]
+    x_sem, h_sem, rows_sem, send_sem, recv_sem, stay_sem = refs[21:27]
+    square_sems, sheet_sems = refs[27:30], refs[30:]
+    sheets = Sheets(size, dp_count, sheet_ref, sheet_out, *sheet_sems)
+    small = Exchange("expert", size, (True,), (1,), [squares], [got], *square_sems)
+    place, model_dim = sheets.place, x_ref.shape[2]
+    width = out_ref.shape[2]
+
+    def loading(g):
+        return pltpu.make_async_copy(x_ref.at[g], x_held.at[g], x_sem.at[g])
+
+    def leaving(g):
+        return (
+            pltpu.make_async_copy(h_held.at[g], h_out.at[g], h_sem.at[g]),
+            pltpu.make_async_copy(rows.at[g], rows_out.at[g], rows_sem.at[g]),
+        )
+
+    for g in range(size):
+        loading(g).start()
+    greet("expert", [(peer, None) for peer in small.peers])
+    greet("dp", [(peer, None) for peer in sheets.peers])
+    pl.semaphore_wait(pltpu.get_barrier_semaphore(), size + dp_count - 2)
+    sheets.begin()
+    sums[...] = jnp.zeros_like(sums)
+    lanes = lax.broadcasted_iota(jnp.int32, sums.shape, 1)
+
+    @pl.loop(0, size)
+    def _(g):
+        loading(g).wait()
+        values = x_held[g].astype(FULL)
+        hidden = (values * rms_scale(values) * gain_ref[...]).astype(LOW)
+        h_held[g] = hidden
+        projected = jnp.dot(hidden, w_ref[...], preferred_element_type=FULL)
+        rows[g] = projected
+        for copy in leaving(g):
+            copy.start()
+        for part in range(2):
+            half = projected[:, part * width : (part + 1) * width]
+            total = jnp.sum(half * half, axis=-1, keepdims=True)
+            sums[...] += jnp.where(lanes == part * size + g, total, 0.0)
+        pl.when((lax.rem(g, 2) == 0) & (g > 0))(lambda: sheets.forward(lax.div(g, 2)))
+
+    squares[...] = sums[...].T[: 2 * size]
+    small.begin()
+    small.arrive()
+    total = sum(got[i] for i in range(size))
+    sums[:, : 2 * size] = lax.rsqrt(total / model_dim + NORM_EPS).T
+
+    def sending(g, source):
+        columns = pl.ds(pl.multiple_of(source * width, 128), width)
+        target = own_out.at[:, columns]
+        return remote(out_ref.at[g], target, send_sem.at[g], recv_sem.at[source], {"expert": g})
+
+    own_columns = pl.ds(pl.multiple_of(place * width, 128), width)
+    staying = pltpu.make_async_copy(out_ref.at[place], own_out.at[:, own_columns], stay_sem.at[0])
+
+    @pl.loop(0, size)
+    def _(i):
+        g = lax.rem(place + 1 + i, size)
+        scales = [
+            jnp.sum(jnp.where(lanes == part * size + g, sums[...], 0.0), axis=-1, keepdims=True)
+            for part in range(2)
+        ]
+        scale_ref[g] = jnp.concatenate(scales, axis=1)
+        attend_block(
+            heads, g, rows, scales, gains_ref, turn_ref, column_ref[g], row_ref[g], kept_ref, out_ref
+        )
+        pl.when(g != place)(lambda: sending(g, place).start())
+        pl.when((lax.rem(i, 2) == 1) & (i < 2 * (size // 2)))(lambda: sheets.cross(lax.div(i, 2)))
+
+    staying.start()
+
+    @pl.loop(1, size)
+    def _(i):
+        peer = lax.rem(place + i, size)
+        sending(peer, peer).wait_recv()
+        sending(peer, place).wait_send()
+
+    @pl.loop(0, size)
+    def _(g):
+        for copy in leaving(g):
+            copy.wait()
+
+    staying.wait()
+    small.finish()
+    sheets.finish()
+
+
+def attention(size, dp_count, heads, x_all, w_here, gain, gains, turns, column, row, sheet, number):
+    _, tokens, model_dim = x_all.shape
+    columns = w_here.shape[1]
+    width = columns // 3
+    sems = pltpu.SemaphoreType.DMA
+    seqs = (size, tokens)
+    small = (2 * size, tokens)
     return pl.pallas_call(
-        functools.partial(attend_kernel, heads),
-        out_shape=[kept, out],
-        grid=(groups,),
-        in_specs=[
-            block_of(rows),
-            block_of(scales),
-            whole_of(gains),
-            whole_of(turns),
-            block_of(column),
-            block_of(row),
+        functools.partial(attention_kernel, size, dp_count, heads),
+        out_shape=[
+            jax.ShapeDtypeStruct(x_all.shape, LOW),
+            jax.ShapeDtypeStruct(seqs + (columns,), FULL),
+            jax.ShapeDtypeStruct(seqs + (2,), FULL),
+            jax.ShapeDtypeStruct(seqs + (columns,), LOW),
+            jax.ShapeDtypeStruct(seqs + (width,), LOW),
+            jax.ShapeDtypeStruct((tokens, model_dim), LOW),
+            jax.ShapeDtypeStruct((dp_count, size) + sheet.shape, LOW),
         ],
-        out_specs=[block_of(kept), block_of(out)],
+        in_specs=[ANY] + [VMEM] * 6 + [ANY],
+        out_specs=[ANY] * 2 + [VMEM] * 3 + [ANY] * 2,
+        scratch_shapes=[
+            pltpu.VMEM(x_all.shape, LOW),
+            pltpu.VMEM(x_all.shape, LOW),
+            pltpu.VMEM(seqs + (columns,), FULL),
+            pltpu.VMEM((tokens, 128), FULL),
+            pltpu.VMEM(small, FULL),
+            pltpu.VMEM((size,) + small, FULL),
+            sems((size,)),
+            sems((size,)),
+            sems((size,)),
+            sems((size,)),
+            sems((size,)),
+            sems((1,)),
+        ]
+        + Exchange.scratch(size, (1,))
+        + Sheets.scratch(size, dp_count),
+        compiler_params=pltpu.CompilerParams(
+            collective_id=number, has_side_effects=True, vmem_limit_bytes=48 << 20
+        ),
         cost_estimate=pl.CostEstimate(
-            flops=4 * groups * length * length * width, transcendentals=0, bytes_accessed=8 * rows.size
+            flops=2 * x_all.size * columns, transcendentals=0, bytes_accessed=100_000_000
         ),
-        name="attend",
-    )(rows, scales, gains, turns, column, row)
+        name="attention",
+    )(x_all, w_here, gain, gains, turns, column, row, sheet)
 
 
 def attend_back_block(heads, block, grad_ref, refs, back_ref, dots_ref, gains_ref, w_sum):
@@ -1130,10 +1247,9 @@
     )
     small = jnp.pad(small, ((0, 0), (0, 128 - small.shape[1])))
     numbers = jnp.concatenate([routes.T, segments, jnp.zeros((7, row_count), jnp.int32)], axis=0)
-    x_all, numbers_all, qkv_here, small, out_full = opening(
-        line_count, dp_count, [layer_input, numbers], 4, w_qkv, small, w_out, 1
-    )
-    out_full = out_full.reshape(model_dim, model_dim)
+    x_all, numbers_all, qkv_here, small = opening(
+        line_count, dp_count, [layer_input, numbers], 4, w_qkv, small, 1
+    )
     late_cotangent, x_all = lax.optimization_barrier((out_cotangent, x_all))
     dy_all = lax.all_gather(late_cotangent, "expert", axis=0)
     qkv_here = qkv_here.reshape(model_dim, 3 * head_cols)
@@ -1146,26 +1262,27 @@
 
     routes_all = numbers_all[:, :top_count]
     segments_all = numbers_all[:, top_count]
+    turns = rotary_tables(row_count, head_size)
+    both_gains = jnp.stack([gain_query, gain_key])
+    column, row = segments_all[:, :, None], segments_all[:, None, :]
+    hidden_one, projected, scales, kept, attended, own_attended, out_full = attention(
+        line_count,
+        dp_count,
+        heads_here,
+        x_all,
+        qkv_here,
+        gain_attn[None],
+        both_gains,
+        turns,
+        column,
+        row,
+        w_out,
+        4,
+    )
+    out_full = out_full.reshape(model_dim, model_dim)
+    hidden_one = hidden_one.reshape(all_rows, model_dim)
     inputs_all = x_all.reshape(all_rows, model_dim).astype(FULL)
     normed_all = inputs_all * rms_scale(inputs_all)
-    hidden_one = (normed_all * gain_attn).astype(LOW)
-    projected = jnp.dot(hidden_one, qkv_here, preferred_element_type=FULL)
-    query_rows = projected[:, :head_cols]
-    key_rows = projected[:, head_cols : 2 * head_cols]
-    value_rows = projected[:, 2 * head_cols :]
-    squares = jnp.stack(
-        [jnp.sum(query_rows * query_rows, axis=-1), jnp.sum(key_rows * key_rows, axis=-1)]
-    ).reshape(2 * line_count, row_count)
-    (squares,) = exchange("expert", line_count, [squares], [True], 4)
-    squares = jnp.sum(squares, axis=0).reshape(2, line_count, row_count)
-    scales = lax.rsqrt(squares / model_dim + NORM_EPS).transpose(1, 2, 0)
-    tables = rotary_tables(row_count, head_size)
-    both_gains = jnp.stack([gain_query, gain_key])
-    column, row = segments_all[:, :, None], segments_all[:, None, :]
-    projected = projected.reshape(line_count, row_count, 3 * head_cols)
-    kept, attended = attend(heads_here, projected, scales, both_gains, tables, column, row)
-    (own_attended,) = exchange("expert", line_count, [attended], [False], 5)
-    own_attended = own_attended.transpose(1, 0, 2).reshape(row_count, model_dim)
     inputs = layer_input.astype(FULL)
     scale_attn = rms_scale(inputs)
     normed_attn = inputs * scale_attn
@@ -1228,7 +1345,7 @@
     grad_attn = grad_resid.astype(LOW)
 
     out_here = lax.dynamic_slice_in_dim(out_full, place * head_cols, head_cols, axis=0)
-    arrays = [out_here, kept, attended, projected, scales, both_gains, tables, column, row]
+    arrays = [out_here, kept, attended, projected, scales, both_gains, turns, column, row]
     back, dots, gain_pair, out_parts = attend_back(
         line_count, dp_count, heads_here, grad_attn, arrays, 11
     )

time: 744 us -> 753 us (1.012)
  Pallas kernels: 598 us -> 622 us
    pallas_call x1, Pallas kernels: 12.6 us -> 103 us  [attention(): pl.pallas_call(functools.partial(attention_kernel, size, dp_count, heads)...]
    pallas_call x4 -> x2, Pallas kernels: 152 us -> 85.9 us  [call(): pl.pallas_call(kernel, out_shape=outs, in_specs=[ANY] * len(arrays), out_...]
    dot_general x1 -> x0, matrix products: 8.56 us -> none  [on_device(): projected = jnp.dot(hidden_one, qkv_here, preferred_element_type=FULL)]
    unnamed x106 -> x102, local copies, waits for them, and re-layouts: 16.8 us -> 14.1 us
  transfers between devices with their start and end apart: 3 -> 3, of which waited for: 0 -> 0; matrix products, arithmetic and copies ran while one was open for 12% -> 10% of each run, Pallas kernels for 56% -> 62%
where the time goes in v5:
time: 753 us; the launch traced here: 745 us
  Pallas kernels  622 us (83%)
  local copies, waits for them, and re-layouts  49.5 us (7%)
  other arithmetic  29.4 us (4%)
  matrix products  29.2 us (4%)
  between operations  14.8 us (2%)
    pallas_call x1, Pallas kernels, closing(): pl.pallas_call(functools.partial(closing_kernel, size, dp_count, len(tabl...  138 us
    pallas_call x1, Pallas kernels, attention(): pl.pallas_call(functools.partial(attention_kernel, size, dp_count, heads)...  103 us
    pallas_call x2, Pallas kernels, expert(): pl.pallas_call(functools.partial(expert_kernel, first, count, tiles), out...  101 us
    pallas_call x2, Pallas kernels, call(): pl.pallas_call(kernel, out_shape=outs, in_specs=[ANY] * len(arrays), out_...  85.9 us
    pallas_call x1, Pallas kernels, collect_reduce(): pl.pallas_call(functools.partial(collect_reduce_kernel, levels, cuts, len...  81.7 us
    pallas_call x1, Pallas kernels, attend_back(): pl.pallas_call(functools.partial(attend_back_kernel, size // 2, 4, heads)...  58.2 us
    pallas_call x1, Pallas kernels, gather_place(): pl.pallas_call(functools.partial(gather_place_kernel, size // 2, cuts), o...  54.1 us
  transfers between devices with their start and end apart: 3, of which 0 were waited for; matrix products, arithmetic and copies ran while one was open for 10% of the time, Pallas kernels for 62%

profile of v5, /device:TPU:16, one launch (start us, length us, event | category | flops | bytes accessed | tf_op | source)
XLA Modules:
  0.0 745.4 jit_solution(13737396640343005112)
XLA Ops:
  14.3 71.8 %opening.1 = (bf16[8,192,2048]{2,1,0:T(8,128)(2,1)}, s32[8,16,192]{2,1,0:T(8,128)S(1)}, bf16[4,8,64,768]{3,2,1,0:T(8,128)(2,1)S(1)}, bf16[4,8,64,128]{3,2,1,0:T(8,128)(2,1)S(1)}) custom-call(bf16[192,2048]{1,0:T(8,128)(2,1)S(1)} %copy-done, s32[16,192]{1,0:T(8,128)S(1)} %add_add_fusion.refs_1_, bf16[64,6144]{1,0:T(8,128)(2,1)S(1)} %copy-done.16, ...), custom_call_target="tpu_custom_call" | custom-call | bytes 200000000 | tf_op jit(solution)/shard_map/opening/pallas_call | solution.py:180
  91.5 103.1 %attention.1 = (bf16[8,192,2048]{2,1,0:T(8,128)(2,1)}, f32[8,192,768]{2,1,0:T(8,128)}, f32[8,192,2]{2,1,0:T(8,128)S(1)}, bf16[8,192,768]{2,1,0:T(8,128)(2,1)S(1)...) custom-call(bf16[8,192,2048]{2,1,0:T(8,128)(2,1)} %get-tuple-element.48.refs_0_,, ...), custom_call_target="tpu_custom_call" | custom-call | flops 4831838208 | bytes 100000000 | tf_op jit(solution)/shard_map/attention/pallas_call | solution.py:1094
  194.7 6.7 multiply_reduce_fusion.3
  203.2 54.1 %gather_place.1 = (bf16[3,576,2048]{2,1,0:T(8,128)(2,1)}, bf16[3,576,2048]{2,1,0:T(8,128)(2,1)}, f32[8,24,192]{2,1,0:T(8,128)S(1)}) custom-call(bf16[192,2048]{1,0:T(8,128)(2,1)S(1)} %multiply_convert_fusion.refs_0_, f32[24,192]{1,0:T(8,128)S(1)} %fusion.41.refs_1_, bf16[8,216,192]{2,1,0:T(8,128)(2,1)S(1)} %copy-done.14, bf16[8,192,2048]{2,1,0:T(8,128)(2,1)} %bitcast.149), custom_call_target="tpu_custom_call" | custom-call | flops 2717908992 | bytes 150000000 | tf_op jit(solution)/shard_map/gather_place/pallas_call | solution.py:630
  259.1 35.2 %expert.2 = (bf16[4,768,2048]{2,1,0:T(8,128)(2,1)}, bf16[1,576,2048]{2,1,0:T(8,128)(2,1)}, bf16[1,576,2048]{2,1,0:T(8,128)(2,1)}, f32[1,576,1]{2,1,0:T(8,128)}) custom-call(bf16[3,576,2048]{2,1,0:T(8,128)(2,1)} %get-tuple-element.55.x_ref, bf16[3,576,2048]{2,1,0:T(8,128)(2,1)} %get-tuple-element.56.dy_ref, f32[3,576,1]{2,1,0:T(8,128)} %reshape.187.scale_ref, ...), custom_call_target="tpu_custom_call" | custom-call | flops 21743271936 | bytes 25165824 | tf_op jit(solution)/shard_map/expert/pallas_call | solution.py:898
  294.9 65.7 %expert.3 = (bf16[4,1536,2048]{2,1,0:T(8,128)(2,1)}, bf16[2,576,2048]{2,1,0:T(8,128)(2,1)}, bf16[2,576,2048]{2,1,0:T(8,128)(2,1)}, f32[2,576,1]{2,1,0:T(8,128)}) custom-call(bf16[3,576,2048]{2,1,0:T(8,128)(2,1)} %get-tuple-element.55.x_ref, bf16[3,576,2048]{2,1,0:T(8,128)(2,1)} %get-tuple-element.56.dy_ref, f32[3,576,1]{2,1,0:T(8,128)} %reshape.187.scale_ref, ...), custom_call_target="tpu_custom_call" | custom-call | flops 43486543872 | bytes 50331648 | tf_op jit(solution)/shard_map/expert/pallas_call | solution.py:898
  360.6 4.2 multiply_reduce_fusion
  367.5 2.3 constant_dynamic-slice_fusion.refs_0_
  372.1 5.6 fusion.49
  377.7 81.7 %collect_reduce.1 = (bf16[192,2048]{1,0:T(8,128)(2,1)S(1)}, f32[8,3,192]{2,1,0:T(4,128)S(1)}) custom-call(bf16[8,192,72]{2,1,0:T(8,128)(2,1)S(1)} %copy-done.7, bf16[8,192,72]{2,1,0:T(8,128)(2,1)S(1)} %copy-done.8, bf16[8,192,72]{2,1,0:T(8,128)(2,1)S(1)} %fusion.25.refs_2_, bf16[8,72,2048]{2,1,0:T(8,128)(2,1)S(1)} %bitcast.108, ...), custom_call_target="tpu_custom_call" | custom-call | bytes 150000000 | tf_op jit(solution)/shard_map/collect_reduce/pallas_call | solution.py:688
  460.4 2.5 multiply_reduce_fusion.1
  465.0 58.2 %attend_back.1 = (f32[8,192,768]{2,1,0:T(8,128)}, f32[8,192,2]{2,1,0:T(8,128)S(1)}, f32[2,256]{1,0:T(2,128)S(1)}, bf16[4,256,512]{2,1,0:T(8,128)(2,1)S(1)}) custom-call(bf16[192,2048]{1,0:T(8,128)(2,1)S(1)} %fusion.48.grad_ref, bf16[256,2048]{1,0:T(8,128)(2,1)} %constant_dynamic-slice_fusion.refs_0_, bf16[8,192,768]{2,1,0:T(8,128)(2,1)} %copy-done.11, ...), custom_call_target="tpu_custom_call" | custom-call | bytes 150000000 | tf_op jit(solution)/shard_map/attend_back/pallas_call | solution.py:1192
  527.3 14.2 %exchange_expert.1 = f32[8,16,192]{2,1,0:T(8,128)S(1)} custom-call(f32[16,192]{1,0:T(8,128)S(1)} %bitcast.110), custom_call_target="tpu_custom_call" | custom-call | bytes 30000000 | tf_op jit(solution)/shard_map/exchange_expert/pallas_call | solution.py:180
  543.4 3.6 fusion.20
  547.3 9.1 %fusion.1 = (f32[2048]{0:T(1024)S(1)}, bf16[1536,2048]{1,0:T(8,128)(2,1)}) fusion(f32[1536]{0:T(1024)S(1)} %rsqrt.29, bf16[8,192,2048]{2,1,0:T(8,128)(2,1)} %get-tuple-element.48.refs_0_, bf16[2048,768]{1,0:T(8,128)(2,1)S(1)} %bitcast.112, bf16[1536,256]{1,0:T(8,128)(2,1)S(1)} %slice.204, bf16[1536,256]{1,0:T(8,128)(2,1)S(1)} %get-tuple-element.92, ...), kind=kOutput, calls=%fused_computation.2 | convolution fusion | flops 4854642688 | bytes 18102272 | tf_op jit(solution)/shard_map/dot_general | solution.py:947
  557.9 5.3 fusion.50
  563.2 10.2 %convolution_convert_fusion = bf16[2048,768]{1,0:T(8,128)(2,1)} fusion(bf16[1536,2048]{1,0:T(8,128)(2,1)} %bitcast.150, bf16[1536,256]{1,0:T(8,128)(2,1)S(1)} %copy-done.35, bf16[1536,256]{1,0:T(8,128)(2,1)S(1)} %copy-done.37, bf16[1536,256]{1,0:T(8,128)(2,1)S(1)} %get-tuple-element.91), kind=kOutput, calls=%fused_computation.5 | convolution fusion | flops 4840488960 | bytes 11796480 | tf_op jit(solution)/shard_map/dot_general | solution.py:941
  573.4 137.9 %closing.1 = (bf16[192,2048]{1,0:T(8,128)(2,1)}, bf16[192,2048]{1,0:T(8,128)(2,1)}, f32[3,512,256]{2,1,0:T(8,128)}, f32[256,512]{1,0:T(8,128)}, f32[2,256]{1,0:T(2,128)}, /*index=5*/f32[32,128]{1,0:T(8,128)}) custom-call(bf16[8,192,72]{2,1,0:T(8,128)(2,1)} %get-tuple-element.123.refs_0_, bf16[8,192,72]{2,1,0:T(8,128)(2,1)} %get-tuple-element.124.refs_1_, ...), custom_call_target="tpu_custom_call" | custom-call | bytes 200000000 | tf_op jit(solution)/shard_map/closing/pallas_call | solution.py:771
  716.9 3.6 fusion.11
  721.8 1.7 slice.163
  723.5 1.7 slice.166
  725.3 2.5 slice.164
  727.8 3.1 maximum_convert_fusion.1
  730.9 5.6 maximum_convert_fusion
  (189 shorter events, 41.0 us)
Async XLA Ops:
  7.2 195.6 %all-gather.3.cloned.1.call-start = ((), (), s32[]{:S(2)}) async-start(), calls=%async_computation.4 | async-start | bytes 7077888 | tf_op jit(solution)/shard_map/all_gather | solution.py:1254
  87.8 114.5 %copy-start.4 = (bf16[4,8,64,128]{3,2,1,0:T(8,128)(2,1)}, bf16[4,8,64,128]{3,2,1,0:T(8,128)(2,1)S(1)}, u32[]{:S(2)}) copy-start(bf16[4,8,64,128]{3,2,1,0:T(8,128)(2,1)S(1)} %get-tuple-element.50) | copy-start | bytes 1572868
  87.8 632.7 %reduce-scatter.3.cloned.1.call-start = ((), (), s32[]{:S(2)}) async-start(), calls=%async_computation.2 | async-start | bytes 15728640 | tf_op jit(solution)/shard_map/reduce_scatter | solution.py:1324
  88.3 169.1 %copy-start.39 = (s32[8,3,192]{2,1,0:T(4,128)}, s32[8,3,192]{2,1,0:T(4,128)S(1)}, u32[]{:S(2)}) copy-start(s32[8,3,192]{2,1,0:T(4,128)S(1)} %copy.80) | copy-start | bytes 55300
  89.7 105.0 %copy-start.9 = (s32[8,192,1]{2,1,0:T(8,128)}, s32[8,192,1]{2,1,0:T(8,128)S(1)}, u32[]{:S(2)}) copy-start(s32[8,192,1]{2,1,0:T(8,128)S(1)} %copy.77.refs_5_.refs_7_) | copy-start | bytes 18436
  91.5 103.1 %copy-start.18 = (f32[2,192,128]{2,1,0:T(8,128)}, f32[2,192,128]{2,1,0:T(8,128)S(1)}, u32[]{:S(2)}) copy-start(f32[2,192,128]{2,1,0:T(8,128)S(1)} %pad_maximum_fusion.3.refs_4_.refs_6_) | copy-start | bytes 589828
  91.5 103.1 %copy-start.1 = (bf16[192,2048]{1,0:T(8,128)(2,1)S(1)}, bf16[192,2048]{1,0:T(8,128)(2,1)}, u32[]{:S(2)}) copy-start(bf16[192,2048]{1,0:T(8,128)(2,1)} %refs_0_.1) | copy-start | bytes 2359300
  194.6 6.8 copy-start.2
  194.7 6.8 copy-start.11
  194.7 6.8 copy-start.20
  202.7 54.7 %copy-start.47 = (f32[192]{0:T(256)}, f32[192]{0:T(256)S(1)}, u32[]{:S(2)}) copy-start(f32[192]{0:T(256)S(1)} %fusion.44) | copy-start | bytes 2308
  294.4 429.1 %reduce-scatter.5.cloned.1.call-start = ((), (), s32[]{:S(2)}) async-start(), calls=%async_computation.3 | async-start | bytes 31457280 | tf_op jit(solution)/shard_map/reduce_scatter | solution.py:1324
  366.2 11.5 %copy-start.6 = (bf16[8,192,72]{2,1,0:T(8,128)(2,1)}, bf16[8,192,72]{2,1,0:T(8,128)(2,1)S(1)}, u32[]{:S(2)}) copy-start(bf16[8,192,72]{2,1,0:T(8,128)(2,1)S(1)} %fusion.25.refs_2_) | copy-start | bytes 663556
  372.1 5.6 copy-start.7
  372.1 5.6 copy-start.8
  372.1 5.6 copy-start.12
  377.7 82.6 %copy-start.48 = (f32[192]{0:T(256)S(1)}, f32[192]{0:T(256)}, u32[]{:S(2)}) copy-start(f32[192]{0:T(256)} %copy-done.47) | copy-start | bytes 2308
  377.7 82.7 %copy-start.5 = (bf16[4,8,64,128]{3,2,1,0:T(8,128)(2,1)S(1)}, bf16[4,8,64,128]{3,2,1,0:T(8,128)(2,1)}, u32[]{:S(2)}) copy-start(bf16[4,8,64,128]{3,2,1,0:T(8,128)(2,1)} %copy-done.4) | copy-start | bytes 1572868
  377.7 82.7 %copy-start.46 = (f32[192]{0:T(256)S(1)}, f32[192]{0:T(256)}, u32[]{:S(2)}) copy-start(f32[192]{0:T(256)} %copy-done.45) | copy-start | bytes 2308
  547.0 9.5 %copy-start.36 = (bf16[1536,256]{1,0:T(8,128)(2,1)}, bf16[1536,256]{1,0:T(8,128)(2,1)S(1)}, u32[]{:S(2)}) copy-start(bf16[1536,256]{1,0:T(8,128)(2,1)S(1)} %get-tuple-element.92) | copy-start | bytes 2359300
  573.4 143.5 %copy-start.30 = (f32[192,2048]{1,0:T(8,128)S(1)}, f32[192,2048]{1,0:T(8,128)}, u32[]{:S(2)}) copy-start(f32[192,2048]{1,0:T(8,128)} %copy-done.29) | copy-start | bytes 4718596
  573.4 143.5 %copy-start.32 = (bf16[192,2048]{1,0:T(8,128)(2,1)S(1)}, bf16[192,2048]{1,0:T(8,128)(2,1)}, u32[]{:S(2)}) copy-start(bf16[192,2048]{1,0:T(8,128)(2,1)} %param.14) | copy-start | bytes 2359300
  711.2 5.6 copy-start.28
  730.9 5.6 copy-start.33
  (28 other events, 63.6 us)
Sparse Core Ops, SparseCore 0:
  87.9 79.9 all-gather.2
  294.5 125.5 reduce-scatter.2
  423.2 267.1 reduce-scatter.4

commit v6 on v5

--- a/solution.py
+++ b/solution.py
@@ -129,38 +129,38 @@
         for piece in self.pieces():
             self.sending(piece, block, False, self.side_sem.at[0], self.other).wait_recv()
 
-    def main(self, landed=None, before=None):
+    def turn(self, turn, landed=None):
         levels, cuts = self.levels, self.cuts
-
-        @pl.loop(0, levels * cuts)
+        step, k = lax.div(turn, cuts) + 1, lax.rem(turn, cuts)
+
+        @pl.when(step < levels)
+        def _():
+            self.forward(step, (0, k))
+
+            @pl.when(k == cuts - 1)
+            def _():
+                for i in range(1, len(self.ins)):
+                    self.forward(step, (i, 0))
+
+        group, sign, crossed = step - 1, 2 * lax.rem(k, 2) - 1, lax.div(k, 2)
+        crossed = jnp.where(group == 0, k, crossed)
+        far = jnp.where(group == 0, self.level, self.level + sign * group)
+
+        @pl.when((far >= 0) & (far < levels) & (k < 4) & ((group > 0) | (k < 2)))
+        def _():
+            block = 2 * far + self.side + crossed * (1 - 2 * self.side)
+
+            @pl.when(crossed == 1)
+            def _():
+                self.land_across(block)
+
+            if landed:
+                landed(block)
+
+    def main(self, landed=None):
+        @pl.loop(0, self.levels * self.cuts)
         def _(turn):
-            step, k = lax.div(turn, cuts) + 1, lax.rem(turn, cuts)
-
-            @pl.when(step < levels)
-            def _():
-                if before:
-                    pl.when(k == 0)(lambda: before(step))
-                self.forward(step, (0, k))
-
-                @pl.when(k == cuts - 1)
-                def _():
-                    for i in range(1, len(self.ins)):
-                        self.forward(step, (i, 0))
-
-            group, sign, crossed = step - 1, 2 * lax.rem(k, 2) - 1, lax.div(k, 2)
-            crossed = jnp.where(group == 0, k, crossed)
-            far = jnp.where(group == 0, self.level, self.level + sign * group)
-
-            @pl.when((far >= 0) & (far < levels) & (k < 4) & ((group > 0) | (k < 2)))
-            def _():
-                block = 2 * far + self.side + crossed * (1 - 2 * self.side)
-
-                @pl.when(crossed == 1)
-                def _():
-                    self.land_across(block)
-
-                if landed:
-                    landed(block)
+            self.turn(turn, landed)
 
     def finish(self, held=0):
         for piece in self.pieces():
@@ -657,20 +657,29 @@
 
 
 def collect_reduce_kernel(levels, cuts, local_count, *refs):
-    tables, slots, small_ref = refs[:local_count], refs[local_count : 2 * local_count], refs[2 * local_count]
-    total_ref, small_out = refs[2 * local_count + 1 : 2 * local_count + 3]
-    away, rest = refs[2 * local_count + 3], refs[2 * local_count + 4 :]
-    line = LineReduce(levels, cuts, away, total_ref, *rest[:12])
-    small = Exchange("expert", 2 * levels, (False,), (1,), [small_ref], [small_out], *rest[12:])
+    tables, slots = refs[:local_count], refs[local_count : 2 * local_count]
+    dots, table_ref = refs[2 * local_count : 3 * local_count], refs[3 * local_count]
+    total_ref, gates_out, away = refs[3 * local_count + 1 : 3 * local_count + 4]
+    rest, (gates, *sems) = refs[3 * local_count + 4 :][:12], refs[3 * local_count + 16 :]
+    line = LineReduce(levels, cuts, away, total_ref, *rest)
+    small = Exchange("expert", 2 * levels, (False,), (1,), [gates], [gates_out], *sems)
     greet("expert", [(peer, None) for peer in small.peers])
     pl.semaphore_wait(pltpu.get_barrier_semaphore(), 2 * levels - 1)
-
     make = functools.partial(collect_block, tables, slots)
-    small.begin()
 
     @pl.loop(0, 4)
     def _(turn):
         line.prepare(turn, make)
+
+    @pl.loop(0, 2 * levels)
+    def _(block):
+        table = table_ref[block].astype(FULL)
+        capacity = table.shape[0] // local_count
+        for j in range(local_count):
+            part = table[j * capacity : (j + 1) * capacity] * dots[j][block]
+            gates[block, j : j + 1] = jnp.sum(part, axis=0, keepdims=True)
+
+    small.begin()
 
     def beside(turn):
         pl.when(turn + 4 < 2 * levels)(lambda: line.prepare(turn + 4, make))
@@ -681,27 +690,26 @@
     small.finish()
 
 
-def collect_reduce(size, tables, slots, small, number):
+def collect_reduce(size, tables, slots, dots, table, number):
     levels, cuts = size // 2, 4
     block = (tables[0].shape[1], slots[0].shape[2])
     kind = slots[0].dtype
+    gates = (size, len(tables), block[0])
     return pl.pallas_call(
         functools.partial(collect_reduce_kernel, levels, cuts, len(tables)),
-        out_shape=[
-            jax.ShapeDtypeStruct(block, kind),
-            jax.ShapeDtypeStruct(small.shape, small.dtype),
-        ],
-        in_specs=[VMEM] * (2 * len(tables)) + [ANY],
+        out_shape=[jax.ShapeDtypeStruct(block, kind), jax.ShapeDtypeStruct(gates, FULL)],
+        in_specs=[VMEM] * (3 * len(tables) + 1),
         out_specs=[ANY, ANY],
         scratch_shapes=[pltpu.VMEM((levels,) + block, kind)]
         + LineReduce.scratch(size, block, kind, cuts)
+        + [pltpu.VMEM(gates, FULL)]
         + Exchange.scratch(size, (1,)),
         compiler_params=pltpu.CompilerParams(
             collective_id=number, has_side_effects=True, vmem_limit_bytes=48 << 20
         ),
         cost_estimate=pl.CostEstimate(flops=0, transcendentals=0, bytes_accessed=150_000_000),
         name="collect_reduce",
-    )(*tables, *slots, small)
+    )(*tables, *slots, *dots, table)
 
 
 def closing_kernel(size, dp_count, local_count, cuts, sum_cuts, *refs):
@@ -953,6 +961,45 @@
     return jnp.einsum(spec, left_side, right_side, preferred_element_type=FULL)
 
 
+def widen_kernel(steps, *refs):
+    low_ref, high_ref, down_ref = refs[0], refs[-2], refs[-1]
+    step = pl.program_id(1)
+
+    @pl.when(step < steps)
+    def _():
+        high_ref[...] = low_ref[...].astype(FULL)
+
+    @pl.when(step >= steps)
+    def _():
+        down_ref[...] = low_ref[...].astype(FULL)
+
+
+def widen(first, total, high, grads, held=()):
+    count, both, width = grads.shape
+    low = both - high
+    rows = low // 2
+    steps = high // rows
+    block = (1, rows, width)
+    return pl.pallas_call(
+        functools.partial(widen_kernel, steps),
+        out_shape=[
+            jax.ShapeDtypeStruct((total, high, width), FULL),
+            jax.ShapeDtypeStruct((total, low, width), FULL),
+        ],
+        grid=(count, steps + 2),
+        in_specs=[pl.BlockSpec(block, lambda e, r: (e, r, 0))] + [ANY] * len(held),
+        out_specs=[
+            pl.BlockSpec(block, lambda e, r: (first + e, jnp.minimum(r, steps - 1), 0)),
+            pl.BlockSpec(block, lambda e, r: (first + e, jnp.maximum(r - steps, 0), 0)),
+        ],
+        input_output_aliases={1: 0, 2: 1} if held else {},
+        cost_estimate=pl.CostEstimate(
+            flops=grads.size, transcendentals=0, bytes_accessed=6 * grads.size
+        ),
+        name="widen",
+    )(grads, *held)
+
+
 def turn(values, cosine, sine):
     return values * cosine + pltpu.roll(values, values.shape[1] // 2, 1) * sine
 
@@ -994,11 +1041,12 @@
 
 
 def attention_kernel(size, dp_count, heads, *refs):
-    x_ref, w_ref, gain_ref, gains_ref, turn_ref, column_ref, row_ref, sheet_ref = refs[:8]
-    h_out, rows_out, scale_ref, kept_ref, out_ref, own_out, sheet_out = refs[8:15]
-    x_held, h_held, rows, sums, squares, got = refs[15:21]
-    x_sem, h_sem, rows_sem, send_sem, recv_sem, stay_sem = refs[21:27]
-    square_sems, sheet_sems = refs[27:30], refs[30:]
+    x_ref, w_ref, gain_ref, gains_ref, turn_ref, column_ref, row_ref, sheet_ref, dy_ref = refs[:9]
+    h_out, rows_out, scale_ref, root_ref, kept_ref, out_ref, own_out, sheet_out, dy_out = refs[9:18]
+    x_held, h_held, rows, sums, squares, got = refs[18:24]
+    x_sem, h_sem, rows_sem, send_sem, recv_sem, stay_sem = refs[24:30]
+    square_sems, line_sems, sheet_sems = refs[30:33], refs[33:38], refs[38:]
+    line = LineGather(size // 2, 4, [dy_ref], [dy_out], *line_sems)
     sheets = Sheets(size, dp_count, sheet_ref, sheet_out, *sheet_sems)
     small = Exchange("expert", size, (True,), (1,), [squares], [got], *square_sems)
     place, model_dim = sheets.place, x_ref.shape[2]
@@ -1019,6 +1067,7 @@
     greet("dp", [(peer, None) for peer in sheets.peers])
     pl.semaphore_wait(pltpu.get_barrier_semaphore(), size + dp_count - 2)
     sheets.begin()
+    line.begin()
     sums[...] = jnp.zeros_like(sums)
     lanes = lax.broadcasted_iota(jnp.int32, sums.shape, 1)
 
@@ -1026,7 +1075,9 @@
     def _(g):
         loading(g).wait()
         values = x_held[g].astype(FULL)
-        hidden = (values * rms_scale(values) * gain_ref[...]).astype(LOW)
+        root = rms_scale(values)
+        root_ref[g] = root
+        hidden = (values * root * gain_ref[...]).astype(LOW)
         h_held[g] = hidden
         projected = jnp.dot(hidden, w_ref[...], preferred_element_type=FULL)
         rows[g] = projected
@@ -1036,6 +1087,7 @@
             half = projected[:, part * width : (part + 1) * width]
             total = jnp.sum(half * half, axis=-1, keepdims=True)
             sums[...] += jnp.where(lanes == part * size + g, total, 0.0)
+        line.turn(g)
         pl.when((lax.rem(g, 2) == 0) & (g > 0))(lambda: sheets.forward(lax.div(g, 2)))
 
     squares[...] = sums[...].T[: 2 * size]
@@ -1064,6 +1116,7 @@
             heads, g, rows, scales, gains_ref, turn_ref, column_ref[g], row_ref[g], kept_ref, out_ref
         )
         pl.when(g != place)(lambda: sending(g, place).start())
+        line.turn(size + i)
         pl.when((lax.rem(i, 2) == 1) & (i < 2 * (size // 2)))(lambda: sheets.cross(lax.div(i, 2)))
 
     staying.start()
@@ -1081,10 +1134,12 @@
 
     staying.wait()
     small.finish()
+    line.finish()
     sheets.finish()
 
 
-def attention(size, dp_count, heads, x_all, w_here, gain, gains, turns, column, row, sheet, number):
+def attention(size, dp_count, heads, arrays, number):
+    x_all, w_here, sheet, dy = arrays[0], arrays[1], arrays[7], arrays[8]
     _, tokens, model_dim = x_all.shape
     columns = w_here.shape[1]
     width = columns // 3
@@ -1097,13 +1152,15 @@
             jax.ShapeDtypeStruct(x_all.shape, LOW),
             jax.ShapeDtypeStruct(seqs + (columns,), FULL),
             jax.ShapeDtypeStruct(seqs + (2,), FULL),
+            jax.ShapeDtypeStruct(seqs + (1,), FULL),
             jax.ShapeDtypeStruct(seqs + (columns,), LOW),
             jax.ShapeDtypeStruct(seqs + (width,), LOW),
             jax.ShapeDtypeStruct((tokens, model_dim), LOW),
             jax.ShapeDtypeStruct((dp_count, size) + sheet.shape, LOW),
+            jax.ShapeDtypeStruct((size,) + dy.shape, LOW),
         ],
-        in_specs=[ANY] + [VMEM] * 6 + [ANY],
-        out_specs=[ANY] * 2 + [VMEM] * 3 + [ANY] * 2,
+        in_specs=[ANY] + [VMEM] * 6 + [ANY] * 2,
+        out_specs=[ANY] * 2 + [VMEM] * 4 + [ANY] * 3,
         scratch_shapes=[
             pltpu.VMEM(x_all.shape, LOW),
             pltpu.VMEM(x_all.shape, LOW),
@@ -1119,6 +1176,7 @@
             sems((1,)),
         ]
         + Exchange.scratch(size, (1,))
+        + LineGather.scratch(size, 4, 1)
         + Sheets.scratch(size, dp_count),
         compiler_params=pltpu.CompilerParams(
             collective_id=number, has_side_effects=True, vmem_limit_bytes=48 << 20
@@ -1127,7 +1185,7 @@
             flops=2 * x_all.size * columns, transcendentals=0, bytes_accessed=100_000_000
         ),
         name="attention",
-    )(x_all, w_here, gain, gains, turns, column, row, sheet)
+    )(*arrays)
 
 
 def attend_back_block(heads, block, grad_ref, refs, back_ref, dots_ref, gains_ref, w_sum):
@@ -1167,12 +1225,18 @@
 
 
 def attend_back_kernel(levels, cuts, heads, grad_ref, *refs):
-    reads, (back_ref, dots_ref, gains_ref, w_grad_ref, w_sum, held), sems = refs[:9], refs[9:15], refs[15:]
+    w_ref, others = refs[0], refs[1:9]
+    back_ref, dots_ref, gains_ref, w_grad_ref, w_sum, held, w_held, w_sem, *sems = refs[9:]
+    reads = (w_held,) + tuple(others)
     line = LineGather(levels, cuts, [grad_ref], [held], *sems)
+    mine = pl.ds(pl.multiple_of(line.place * w_held.shape[0], 128), w_held.shape[0])
+    loading = pltpu.make_async_copy(w_ref.at[mine], w_held, w_sem.at[0])
+    loading.start()
     line_barrier(levels)
     line.begin()
     w_sum[...] = jnp.zeros_like(w_sum)
     gains_ref[...] = jnp.zeros_like(gains_ref)
+    loading.wait()
     line.staying(0).wait()
 
     def landed(block):
@@ -1186,7 +1250,7 @@
 
 
 def attend_back(size, dp_count, heads, grad, arrays, number):
-    w_here, _, out, rows = arrays[:4]
+    _, _, out, rows = arrays[:4]
     width = out.shape[2]
     tokens, model_dim = grad.shape
     return pl.pallas_call(
@@ -1197,11 +1261,13 @@
             jax.ShapeDtypeStruct((2, width), FULL),
             jax.ShapeDtypeStruct((dp_count, width, model_dim // dp_count), LOW),
         ],
-        in_specs=[ANY] + [VMEM] * len(arrays),
+        in_specs=[ANY] * 2 + [VMEM] * (len(arrays) - 1),
         out_specs=[VMEM] * 4,
         scratch_shapes=[
             pltpu.VMEM((width, model_dim), FULL),
             pltpu.VMEM((size, tokens, model_dim), LOW),
+            pltpu.VMEM((width, model_dim), LOW),
+            pltpu.SemaphoreType.DMA((1,)),
         ]
         + LineGather.scratch(size, 4, 1),
         compiler_params=pltpu.CompilerParams(
@@ -1250,8 +1316,6 @@
     x_all, numbers_all, qkv_here, small = opening(
         line_count, dp_count, [layer_input, numbers], 4, w_qkv, small, 1
     )
-    late_cotangent, x_all = lax.optimization_barrier((out_cotangent, x_all))
-    dy_all = lax.all_gather(late_cotangent, "expert", axis=0)
     qkv_here = qkv_here.reshape(model_dim, 3 * head_cols)
     small = small.reshape(model_dim, small.shape[3])
     router_full = small[:, :expert_count]
@@ -1265,24 +1329,14 @@
     turns = rotary_tables(row_count, head_size)
     both_gains = jnp.stack([gain_query, gain_key])
     column, row = segments_all[:, :, None], segments_all[:, None, :]
-    hidden_one, projected, scales, kept, attended, own_attended, out_full = attention(
-        line_count,
-        dp_count,
-        heads_here,
-        x_all,
-        qkv_here,
-        gain_attn[None],
-        both_gains,
-        turns,
-        column,
-        row,
-        w_out,
-        4,
+    arrays = [x_all, qkv_here, gain_attn[None], both_gains, turns, column, row, w_out, out_cotangent]
+    hidden_one, projected, scales, roots, kept, attended, own_attended, out_full, dy_all = attention(
+        line_count, dp_count, heads_here, arrays, 4
     )
     out_full = out_full.reshape(model_dim, model_dim)
     hidden_one = hidden_one.reshape(all_rows, model_dim)
     inputs_all = x_all.reshape(all_rows, model_dim).astype(FULL)
-    normed_all = inputs_all * rms_scale(inputs_all)
+    normed_all = inputs_all * roots.reshape(all_rows, 1)
     inputs = layer_input.astype(FULL)
     scale_attn = rms_scale(inputs)
     normed_attn = inputs * scale_attn
@@ -1327,11 +1381,9 @@
             for j in range(count):
                 kept_list.append(rows[j].reshape(line_count, capacity, rows.shape[2]))
     gate_rows = model_dim // dp_count
-    sum_gate_up = jnp.concatenate([both[:, :gate_rows] for both in grad_sums]).astype(FULL)
-    sum_down = jnp.concatenate([both[:, gate_rows:] for both in grad_sums]).astype(FULL)
-    slot_grads = jnp.stack([dots[:, :, 0] for dots in slot_grads], axis=1)
-    grad_gates = jnp.sum(table.astype(FULL) * slot_grads[:, :, :, None], axis=2)
-    grad_two, grad_gates = collect_reduce(line_count, returns, back_rows, grad_gates, 8)
+    grad_two, grad_gates = collect_reduce(
+        line_count, returns, back_rows, slot_grads, flat_table, 8
+    )
     grad_gates = grad_gates.reshape(expert_count, row_count).T
     grad_two = grad_two.astype(FULL)
 
@@ -1344,8 +1396,7 @@
     grad_resid = grad_out_rows + norm_back(grad_two * gain_mlp, normed_mlp, scale_mlp)
     grad_attn = grad_resid.astype(LOW)
 
-    out_here = lax.dynamic_slice_in_dim(out_full, place * head_cols, head_cols, axis=0)
-    arrays = [out_here, kept, attended, projected, scales, both_gains, turns, column, row]
+    arrays = [out_full, kept, attended, projected, scales, both_gains, turns, column, row]
     back, dots, gain_pair, out_parts = attend_back(
         line_count, dp_count, heads_here, grad_attn, arrays, 11
     )
@@ -1388,6 +1439,9 @@
     )
     output = (residual + mixture.astype(FULL)).astype(LOW)
     sum_qkv = sum_qkv.transpose(1, 0, 2)
+    first_sums, output = lax.optimization_barrier((grad_sums[0], output))
+    wide = widen(0, local_count, gate_rows, first_sums)
+    sum_gate_up, sum_down = widen(1, local_count, gate_rows, grad_sums[1], wide)
     shared = shared[:, :shard]
     grad_one = grad_one.astype(FULL)
     grad_inputs = grad_resid + norm_back(grad_one * gain_attn, normed_attn, scale_attn)
@@ -1401,8 +1455,8 @@
         shared[expert_count + 1],
         gain_pair[0],
         gain_pair[1],
-        sum_gate_up.astype(FULL),
-        sum_down.astype(FULL),
+        sum_gate_up,
+        sum_down,
     )
 
 

time: 753 us -> 741 us (0.984)
  other arithmetic: 29.4 us -> 14.3 us
  Pallas kernels: 622 us -> 637 us
  local copies, waits for them, and re-layouts: 49.5 us -> 38.1 us
    pallas_call x0 -> x2, Pallas kernels: none -> 17 us  [widen(): pl.pallas_call(functools.partial(widen_kernel, steps), out_shape=[jax.Sha...]
    convert_element_type x2 -> x0, other arithmetic: 8.7 us -> none  [the longest x1 5.59 us: on_device(): jnp.concatenate([both[:, :gate_rows] for both in grad_sums]).astype(FULL)]
  transfers between devices with their start and end apart: 3 -> 2, of which waited for: 0 -> 0; matrix products, arithmetic and copies ran while one was open for 10% -> 7% of each run, Pallas kernels for 62% -> 49%
where the time goes in v6:
time: 741 us; the launch traced here: 734 us
  Pallas kernels  637 us (86%)
  local copies, waits for them, and re-layouts  38.1 us (5%)
  matrix products  28.7 us (4%)
  between operations  15.3 us (2%)
  other arithmetic  14.3 us (2%)
    pallas_call x1, Pallas kernels, closing(): pl.pallas_call(functools.partial(closing_kernel, size, dp_count, len(tabl...  137 us
    pallas_call x2, Pallas kernels, expert(): pl.pallas_call(functools.partial(expert_kernel, first, count, tiles), out...  101 us
    pallas_call x1, Pallas kernels, attention(): pl.pallas_call(functools.partial(attention_kernel, size, dp_count, heads)...  100 us
    pallas_call x2, Pallas kernels, call(): pl.pallas_call(kernel, out_shape=outs, in_specs=[ANY] * len(arrays), out_...  86.1 us
    pallas_call x1, Pallas kernels, collect_reduce(): pl.pallas_call(functools.partial(collect_reduce_kernel, levels, cuts, len...  80.9 us
    pallas_call x1, Pallas kernels, attend_back(): pl.pallas_call(functools.partial(attend_back_kernel, size // 2, 4, heads)...  57.5 us
    pallas_call x1, Pallas kernels, gather_place(): pl.pallas_call(functools.partial(gather_place_kernel, size // 2, cuts), o...  57.1 us
    pallas_call x2, Pallas kernels, widen(): pl.pallas_call(functools.partial(widen_kernel, steps), out_shape=[jax.Sha...  17 us
  transfers between devices with their start and end apart: 2, of which 0 were waited for; matrix products, arithmetic and copies ran while one was open for 7% of the time, Pallas kernels for 49%

profile of v6, /device:TPU:16, one launch (start us, length us, event | category | flops | bytes accessed | tf_op | source)
XLA Modules:
  0.0 733.5 jit_solution(4812403891593847005)
XLA Ops:
  15.1 71.8 %opening.1 = (bf16[8,192,2048]{2,1,0:T(8,128)(2,1)}, s32[8,16,192]{2,1,0:T(8,128)S(1)}, bf16[4,8,64,768]{3,2,1,0:T(8,128)(2,1)S(1)}, bf16[4,8,64,128]{3,2,1,0:T(8,128)(2,1)S(1)}) custom-call(bf16[192,2048]{1,0:T(8,128)(2,1)S(1)} %copy-done, s32[16,192]{1,0:T(8,128)S(1)} %add_add_fusion.refs_1_, bf16[64,6144]{1,0:T(8,128)(2,1)S(1)} %copy-done.22, ...), custom_call_target="tpu_custom_call" | custom-call | bytes 200000000 | tf_op jit(solution)/shard_map/opening/pallas_call | solution.py:180
  86.9 1.7 copy-done.28
  90.5 1.2 copy-done.13
  91.7 100.4 %attention.1 = (bf16[8,192,2048]{2,1,0:T(8,128)(2,1)}, f32[8,192,768]{2,1,0:T(8,128)}, f32[8,192,2]{2,1,0:T(8,128)S(1)}, f32[8,192,1]{2,1,0:T(8,128)S(1)}, bf16[...) custom-call(bf16[8,192,2048]{2,1,0:T(8,128)(2,1)} %get-tuple-element, ...), custom_call_target="tpu_custom_call" | custom-call | flops 4831838208 | bytes 100000000 | tf_op jit(solution)/shard_map/attention/pallas_call | solution.py:1149
  192.1 5.9 multiply_reduce_fusion.3
  199.5 57.1 %gather_place.1 = (bf16[3,576,2048]{2,1,0:T(8,128)(2,1)}, bf16[3,576,2048]{2,1,0:T(8,128)(2,1)}, f32[8,24,192]{2,1,0:T(8,128)S(1)}) custom-call(bf16[192,2048]{1,0:T(8,128)(2,1)S(1)} %multiply_convert_fusion.refs_0_, f32[24,192]{1,0:T(8,128)S(1)} %fusion.39.refs_1_, bf16[8,216,192]{2,1,0:T(8,128)(2,1)S(1)} %fusion.5.refs_2_.refs_9_, ...), custom_call_target="tpu_custom_call" | custom-call | flops 2717908992 | bytes 150000000 | tf_op jit(solution)/shard_map/gather_place/pallas_call | solution.py:630
  258.3 35.3 %expert.2 = (bf16[4,768,2048]{2,1,0:T(8,128)(2,1)}, bf16[1,576,2048]{2,1,0:T(8,128)(2,1)}, bf16[1,576,2048]{2,1,0:T(8,128)(2,1)}, f32[1,576,1]{2,1,0:T(8,128)}) custom-call(bf16[3,576,2048]{2,1,0:T(8,128)(2,1)} %get-tuple-element.60.x_ref, bf16[3,576,2048]{2,1,0:T(8,128)(2,1)} %get-tuple-element.61.dy_ref, f32[3,576,1]{2,1,0:T(8,128)} %reshape.170.scale_ref, ...), custom_call_target="tpu_custom_call" | custom-call | flops 21743271936 | bytes 25165824 | tf_op jit(solution)/shard_map/expert/pallas_call | solution.py:906
  293.9 65.7 %expert.3 = (bf16[4,1536,2048]{2,1,0:T(8,128)(2,1)}, bf16[2,576,2048]{2,1,0:T(8,128)(2,1)}, bf16[2,576,2048]{2,1,0:T(8,128)(2,1)}, f32[2,576,1]{2,1,0:T(8,128)}) custom-call(bf16[3,576,2048]{2,1,0:T(8,128)(2,1)} %get-tuple-element.60.x_ref, bf16[3,576,2048]{2,1,0:T(8,128)(2,1)} %get-tuple-element.61.dy_ref, f32[3,576,1]{2,1,0:T(8,128)} %reshape.170.scale_ref, ...), custom_call_target="tpu_custom_call" | custom-call | flops 43486543872 | bytes 50331648 | tf_op jit(solution)/shard_map/expert/pallas_call | solution.py:906
  362.2 5.7 fusion.47
  367.9 80.9 %collect_reduce.1 = (bf16[192,2048]{1,0:T(8,128)(2,1)S(1)}, f32[8,3,192]{2,1,0:T(4,128)S(1)}) custom-call(bf16[8,192,72]{2,1,0:T(8,128)(2,1)S(1)} %get-tuple-element.137.refs_0_, bf16[8,192,72]{2,1,0:T(8,128)(2,1)S(1)} %get-tuple-element.138.refs_1_, bf16[8,192,72]{2,1,0:T(8,128)(2,1)S(1)} %fusion.23.refs_2_, bf16[8,72,2048]{2,1,0:T(8,128)(2,1)S(1)} %bitcast.107, ...), custom_call_target="tpu_custom_call" | custom-call | bytes 150000000 | tf_op jit(solution)/shard_map/collect_reduce/pallas_call | solution.py:698
  449.8 2.5 multiply_reduce_fusion.1
  454.6 57.5 %attend_back.1 = (f32[8,192,768]{2,1,0:T(8,128)}, f32[8,192,2]{2,1,0:T(8,128)S(1)}, f32[2,256]{1,0:T(2,128)S(1)}, bf16[4,256,512]{2,1,0:T(8,128)(2,1)S(1)}) custom-call(bf16[192,2048]{1,0:T(8,128)(2,1)S(1)} %fusion.46.grad_ref, bf16[2048,2048]{1,0:T(8,128)(2,1)} %bitcast.123, bf16[8,192,768]{2,1,0:T(8,128)(2,1)} %get-tuple-element.73.refs_1_, ...), custom_call_target="tpu_custom_call" | custom-call | bytes 150000000 | tf_op jit(solution)/shard_map/attend_back/pallas_call | solution.py:1256
  513.9 1.5 copy.85
  515.4 14.3 %exchange_expert.1 = f32[8,16,192]{2,1,0:T(8,128)S(1)} custom-call(f32[16,192]{1,0:T(8,128)S(1)} %bitcast.112), custom_call_target="tpu_custom_call" | custom-call | bytes 30000000 | tf_op jit(solution)/shard_map/exchange_expert/pallas_call | solution.py:180
  529.9 1.6 slice.182
  532.5 4.0 fusion.18
  536.7 9.5 %fusion.1 = (f32[2048]{0:T(1024)S(1)}, bf16[1536,2048]{1,0:T(8,128)(2,1)}) fusion(bf16[8,192,2048]{2,1,0:T(8,128)(2,1)} %get-tuple-element.53.refs_0_, f32[1536]{0:T(1024)S(1)} %mul.254, bf16[2048,768]{1,0:T(8,128)(2,1)S(1)} %bitcast.114, bf16[1536,256]{1,0:T(8,128)(2,1)S(1)} %slice.182, bf16[1536,256]{1,0:T(8,128)(2,1)S(1)} %get-tuple-element.102, ...), kind=kOutput, calls=%fused_computation.2 | convolution fusion | flops 4854642688 | bytes 18102272 | tf_op jit(solution)/shard_map/dot_general | solution.py:955
  547.6 5.3 fusion.48
  552.9 10.1 %convolution_convert_fusion = bf16[2048,768]{1,0:T(8,128)(2,1)} fusion(bf16[1536,2048]{1,0:T(8,128)(2,1)} %bitcast.149, bf16[1536,256]{1,0:T(8,128)(2,1)S(1)} %copy-done.39, bf16[1536,256]{1,0:T(8,128)(2,1)S(1)} %copy-done.41, bf16[1536,256]{1,0:T(8,128)(2,1)S(1)} %get-tuple-element.101), kind=kOutput, calls=%fused_computation.3 | convolution fusion | flops 4840488960 | bytes 11796480 | tf_op jit(solution)/shard_map/dot_general | solution.py:949
  563.0 136.8 %closing.1 = (bf16[192,2048]{1,0:T(8,128)(2,1)}, bf16[192,2048]{1,0:T(8,128)(2,1)}, f32[3,512,256]{2,1,0:T(8,128)}, f32[256,512]{1,0:T(8,128)}, f32[2,256]{1,0:T(2,128)}, /*index=5*/f32[32,128]{1,0:T(8,128)}) custom-call(bf16[8,192,72]{2,1,0:T(8,128)(2,1)} %copy-done.9, bf16[8,192,72]{2,1,0:T(8,128)(2,1)} %copy-done.10, bf16[8,192,72]{2,1,0:T(8,128)(2,1)} %copy-done.8, ...), custom_call_target="tpu_custom_call" | custom-call | bytes 200000000 | tf_op jit(solution)/shard_map/closing/pallas_call | solution.py:779
  700.2 1.7 fusion.6
  703.6 3.4 fusion.9
  707.0 6.1 widen.2
  713.1 10.9 %widen.3 = (f32[3,512,2048]{2,1,0:T(8,128)}, f32[3,256,2048]{2,1,0:T(8,128)}) custom-call(bf16[2,768,2048]{2,1,0:T(8,128)(2,1)} %bitcast.125, f32[3,512,2048]{2,1,0:T(8,128)} %get-tuple-element.91.refs_1_, f32[3,256,2048]{2,1,0:T(8,128)} %get-tuple-element.92.refs_2_), custom_call_target="tpu_custom_call", output_to_operand_aliasing={{0}: (1, {}), {1}: (2, {})} | custom-call | flops 3145728 | bytes 18874368 | tf_op jit(solution)/shard_map/widen/pallas_call | solution.py:983
  (167 shorter events, 27.4 us)
Async XLA Ops:
  7.2 699.8 %reduce-scatter.3.cloned.1.call-start = ((), (), s32[]{:S(2)}) async-start(), calls=%async_computation.2 | async-start | bytes 15728640 | tf_op jit(solution)/shard_map/reduce_scatter | solution.py:1378
  88.6 109.7 %copy-start.4 = (bf16[4,8,64,128]{3,2,1,0:T(8,128)(2,1)}, bf16[4,8,64,128]{3,2,1,0:T(8,128)(2,1)S(1)}, u32[]{:S(2)}) copy-start(bf16[4,8,64,128]{3,2,1,0:T(8,128)(2,1)S(1)} %get-tuple-element.55) | copy-start | bytes 1572868
  90.2 101.9 %copy-start.11 = (s32[8,192,1]{2,1,0:T(8,128)}, s32[8,192,1]{2,1,0:T(8,128)S(1)}, u32[]{:S(2)}) copy-start(s32[8,192,1]{2,1,0:T(8,128)S(1)} %copy.76.refs_5_.refs_7_) | copy-start | bytes 18436
  90.4 101.7 %copy-start.17 = (f32[2,192,128]{2,1,0:T(8,128)}, f32[2,192,128]{2,1,0:T(8,128)S(1)}, u32[]{:S(2)}) copy-start(f32[2,192,128]{2,1,0:T(8,128)S(1)} %pad_maximum_fusion.3.refs_4_.refs_6_) | copy-start | bytes 589828
  91.7 100.4 %copy-start.1 = (bf16[192,2048]{1,0:T(8,128)(2,1)S(1)}, bf16[192,2048]{1,0:T(8,128)(2,1)}, u32[]{:S(2)}) copy-start(bf16[192,2048]{1,0:T(8,128)(2,1)} %refs_0_.1) | copy-start | bytes 2359300
  192.1 5.9 copy-start.19
  192.1 5.9 copy-start.24
  198.3 58.3 %copy-start.2 = (bf16[192,2048]{1,0:T(8,128)(2,1)}, bf16[192,2048]{1,0:T(8,128)(2,1)S(1)}, u32[]{:S(2)}) copy-start(bf16[192,2048]{1,0:T(8,128)(2,1)S(1)} %multiply_convert_fusion.refs_0_) | copy-start | bytes 2359300
  199.4 57.1 %copy-start.6 = (bf16[8,216,192]{2,1,0:T(8,128)(2,1)}, bf16[8,216,192]{2,1,0:T(8,128)(2,1)S(1)}, u32[]{:S(2)}) copy-start(bf16[8,216,192]{2,1,0:T(8,128)(2,1)S(1)} %fusion.5.refs_2_.refs_9_) | copy-start | bytes 1990660
  293.6 419.5 %reduce-scatter.5.cloned.1.call-start = ((), (), s32[]{:S(2)}) async-start(), calls=%async_computation.3 | async-start | bytes 31457280 | tf_op jit(solution)/shard_map/reduce_scatter | solution.py:1378
  361.5 6.4 copy-start.8
  362.1 5.8 copy-start.9
  362.1 5.8 copy-start.10
  362.2 5.7 copy-start.7
  362.2 5.7 copy-start.15
  362.2 5.7 copy-start.26
  367.9 81.9 %copy-start.5 = (bf16[4,8,64,128]{3,2,1,0:T(8,128)(2,1)S(1)}, bf16[4,8,64,128]{3,2,1,0:T(8,128)(2,1)}, u32[]{:S(2)}) copy-start(bf16[4,8,64,128]{3,2,1,0:T(8,128)(2,1)} %copy-done.4) | copy-start | bytes 1572868
  513.9 18.3 %copy-start.27 = (f32[2,256]{1,0:T(2,128)}, f32[2,256]{1,0:T(2,128)S(1)}, u32[]{:S(2)}) copy-start(f32[2,256]{1,0:T(2,128)S(1)} %get-tuple-element.80.refs_9_) | copy-start | bytes 6148
  531.5 5.0 copy-start.38
  536.5 9.7 %copy-start.40 = (bf16[1536,256]{1,0:T(8,128)(2,1)}, bf16[1536,256]{1,0:T(8,128)(2,1)S(1)}, u32[]{:S(2)}) copy-start(bf16[1536,256]{1,0:T(8,128)(2,1)S(1)} %get-tuple-element.102) | copy-start | bytes 2359300
  547.5 5.3 copy-start.39
  547.6 5.3 copy-start.41
  563.0 140.6 %copy-start.35 = (f32[192,2048]{1,0:T(8,128)S(1)}, f32[192,2048]{1,0:T(8,128)}, u32[]{:S(2)}) copy-start(f32[192,2048]{1,0:T(8,128)} %copy-done.34) | copy-start | bytes 4718596
  713.1 10.9 %copy-start.37 = (f32[3,512,256]{2,1,0:T(8,128)S(1)}, f32[3,512,256]{2,1,0:T(8,128)}, u32[]{:S(2)}) copy-start(f32[3,512,256]{2,1,0:T(8,128)} %get-tuple-element.85) | copy-start | bytes 4718596
  (24 other events, 46.2 us)
Sparse Core Ops, SparseCore 0:
  293.7 125.0 reduce-scatter.2
  421.9 263.4 reduce-scatter.4

commit v7 on v6

--- a/solution.py
+++ b/solution.py
@@ -3,6 +3,7 @@
 
 import jax
 import jax.numpy as jnp
+import numpy as np
 from jax import lax
 from jax.experimental import pallas as pl
 from jax.experimental.pallas import tpu as pltpu
@@ -206,7 +207,8 @@
     def scratch(size, block, dtype, cuts):
         levels = size // 2
         return (
-            [pltpu.VMEM((levels,) + block, dtype)] * 4
+            [pltpu.VMEM((levels,) + block, dtype)] * 2
+            + [pltpu.VMEM((levels - 1,) + block, dtype)] * 2
             + [pltpu.SemaphoreType.DMA((levels, cuts))] * 7
             + [pltpu.SemaphoreType.DMA((cuts,))]
         )
@@ -226,7 +228,7 @@
     def up(self, far, k):
         sems = self.up_send.at[far, k], self.up_recv.at[far, k]
         target = {"expert": self.place + 2}
-        return remote(self.cut(self.own, far, k), self.cut(self.rising, far, k), *sems, target)
+        return remote(self.cut(self.own, far, k), self.cut(self.rising, far - 1, k), *sems, target)
 
     def down(self, far, k):
         sems = self.down_send.at[far, k], self.down_recv.at[far, k]
@@ -271,12 +273,12 @@
     def store(self, far, k, total):
         self.cut(self.own, far, k)[...] = total.astype(self.own.dtype)
 
-    def toward(self, far, k, ahead, behind, move, arrived):
+    def toward(self, far, k, ahead, behind, move, arrived, shift):
         @pl.when(ahead & behind)
         def _():
             both = self.pair(far, k)
             move(far, k).wait_recv()
-            self.store(far, k, both + self.value(arrived, far, k))
+            self.store(far, k, both + self.value(arrived, far - shift, k))
 
         @pl.when(ahead & jnp.logical_not(behind))
         def _():
@@ -291,21 +293,22 @@
             high, low = self.levels - 1 - step, step
             if beside:
                 beside(turn)
-            self.toward(high, k, self.level < high, self.has_down, self.up, self.rising)
-            self.toward(low, k, self.level > low, self.has_up, self.down, self.falling)
+            self.toward(high, k, self.level < high, self.has_down, self.up, self.rising, 1)
+            self.toward(low, k, self.level > low, self.has_up, self.down, self.falling, 0)
 
         @pl.loop(0, self.cuts)
         def _(k):
             self.store(self.level, k, self.pair(self.level, k))
-            for there, move, arrived in (
-                (self.has_down, self.up, self.rising),
-                (self.has_up, self.down, self.falling),
+            for there, move, arrived, shift in (
+                (self.has_down, self.up, self.rising, 1),
+                (self.has_up, self.down, self.falling, 0),
             ):
 
                 @pl.when(there)
                 def _():
                     move(self.level, k).wait_recv()
-                    total = self.value(self.own, self.level, k) + self.value(arrived, self.level, k)
+                    total = self.value(self.own, self.level, k)
+                    total += self.value(arrived, self.level - shift, k)
                     self.store(self.level, k, total)
 
             self.leaving(k).start()
@@ -413,24 +416,25 @@
 
 
 def opening_kernel(size, dp_count, count, cuts, *refs):
-    ins, (w_ref, small_ref) = refs[:count], refs[count : count + 2]
-    outs, (w_out, small_out), rest = refs[count + 2 : 2 * count + 2], refs[2 * count + 2 :][:2], refs[2 * count + 4 :]
+    ins, (w_ref, *small_refs) = refs[:count], refs[count : count + 3]
+    outs, rest = refs[count + 3 : 2 * count + 3], refs[2 * count + 6 :]
+    w_out, *small_outs = refs[2 * count + 3 : 2 * count + 6]
     line = LineGather(size // 2, cuts, ins, outs, *rest[:5])
     send_sem, recv_sem, own_sem = rest[5:8]
     place, mine = line.place, lax.axis_index("dp")
     peers = around("expert", size)
     width = w_out.shape[3] // 3
-    mine_refs = [w_out.at[mine], small_out.at[mine]]
+    lands = [w_out] + small_outs
     across = Exchange(
-        "dp", dp_count, (True,) * 2, (size,) * 2, mine_refs, [w_out, small_out], *rest[8:]
+        "dp", dp_count, (True,) * 3, (size,) * 3, [a.at[mine] for a in lands], lands, *rest[8:]
     )
     greet("expert", [(peer, None) for peer in peers])
     greet("dp", [(peer, None) for peer in across.peers])
     pl.semaphore_wait(pltpu.get_barrier_semaphore(), size + dp_count - 2)
 
     def ends(peer, landing, j):
-        if j == 3:
-            return small_ref, small_out.at[mine, landing]
+        if j >= 3:
+            return small_refs[j - 3], small_outs[j - 3].at[mine, landing]
         start = pl.multiple_of(j * width * size + peer * width, 128)
         target = w_out.at[mine, landing, :, pl.ds(j * width, width)]
         return w_ref.at[:, pl.ds(start, width)], target
@@ -440,26 +444,26 @@
         sems = send_sem.at[shift, j], recv_sem.at[landing, j]
         return remote(source, target, *sems, {"expert": peers[shift]})
 
-    own = [pltpu.make_async_copy(*ends(place, place, j), own_sem.at[j]) for j in range(4)]
+    own = [pltpu.make_async_copy(*ends(place, place, j), own_sem.at[j]) for j in range(5)]
     for shift in range(size - 1):
-        for j in range(4):
+        for j in range(5):
             sending(shift, place, j).start()
     for copy in own:
         copy.start()
     line.begin()
     for copy in own:
         copy.wait()
-    across.send(0, place)
-    across.send(1, place)
+    for i in range(3):
+        across.send(i, place)
     for shift, peer in enumerate(peers):
-        for j in range(4):
+        for j in range(5):
             sending(shift, peer, j).wait_recv()
-        across.send(0, peer)
-        across.send(1, peer)
+        for i in range(3):
+            across.send(i, peer)
     line.main()
     line.finish()
     for shift in range(size - 1):
-        for j in range(4):
+        for j in range(5):
             sending(shift, place, j).wait_send()
     across.land()
     across.finish()
@@ -471,16 +475,16 @@
     rows, columns = weights.shape
     whole = (dp_count, size, rows)
     outs.append(jax.ShapeDtypeStruct(whole + (columns // size,), weights.dtype))
-    outs.append(jax.ShapeDtypeStruct(whole + (small.shape[1],), small.dtype))
+    outs += [jax.ShapeDtypeStruct((dp_count, size) + a.shape, a.dtype) for a in small]
     return call(
         functools.partial(opening_kernel, size, dp_count, len(arrays), cuts),
         "opening",
         number,
         outs,
         LineGather.scratch(size, cuts, len(arrays))
-        + [sems((size, 4)), sems((size, 4)), sems((4,))]
-        + Exchange.scratch(dp_count, (size, size)),
-        list(arrays) + [weights, small],
+        + [sems((size, 5)), sems((size, 5)), sems((5,))]
+        + Exchange.scratch(dp_count, (size,) * 3),
+        list(arrays) + [weights] + small,
         200_000_000,
     )
 
@@ -646,21 +650,28 @@
     )(rows, gates, table, dy)
 
 
+def split_at(arrays, j, block):
+    for array in arrays:
+        if j < array.shape[0]:
+            return array.at[j, block]
+        j -= array.shape[0]
+
+
 def collect_block(tables, slots, block, target):
     @pl.loop(0, target.shape[1] // COLUMNS)
     def _(n):
         columns = pl.ds(pl.multiple_of(n * COLUMNS, COLUMNS), COLUMNS)
         total = 0.0
-        for table, rows in zip(tables, slots):
-            total += jnp.dot(table[block], rows[block, :, columns], preferred_element_type=FULL)
+        for j, table in enumerate(tables):
+            rows = split_at(slots, j, block)[:, columns]
+            total += jnp.dot(table[block], rows, preferred_element_type=FULL)
         target[:, columns] = total.astype(target.dtype)
 
 
 def collect_reduce_kernel(levels, cuts, local_count, *refs):
-    tables, slots = refs[:local_count], refs[local_count : 2 * local_count]
-    dots, table_ref = refs[2 * local_count : 3 * local_count], refs[3 * local_count]
-    total_ref, gates_out, away = refs[3 * local_count + 1 : 3 * local_count + 4]
-    rest, (gates, *sems) = refs[3 * local_count + 4 :][:12], refs[3 * local_count + 16 :]
+    tables, refs = refs[:local_count], refs[local_count:]
+    slots, dots, (table_ref, total_ref, gates_out, away) = refs[:2], refs[2:4], refs[4:8]
+    rest, (gates, *sems) = refs[8:20], refs[20:]
     line = LineReduce(levels, cuts, away, total_ref, *rest)
     small = Exchange("expert", 2 * levels, (False,), (1,), [gates], [gates_out], *sems)
     greet("expert", [(peer, None) for peer in small.peers])
@@ -676,7 +687,7 @@
         table = table_ref[block].astype(FULL)
         capacity = table.shape[0] // local_count
         for j in range(local_count):
-            part = table[j * capacity : (j + 1) * capacity] * dots[j][block]
+            part = table[j * capacity : (j + 1) * capacity] * split_at(dots, j, block)[...]
             gates[block, j : j + 1] = jnp.sum(part, axis=0, keepdims=True)
 
     small.begin()
@@ -692,13 +703,13 @@
 
 def collect_reduce(size, tables, slots, dots, table, number):
     levels, cuts = size // 2, 4
-    block = (tables[0].shape[1], slots[0].shape[2])
+    block = (tables[0].shape[1], slots[0].shape[3])
     kind = slots[0].dtype
     gates = (size, len(tables), block[0])
     return pl.pallas_call(
         functools.partial(collect_reduce_kernel, levels, cuts, len(tables)),
         out_shape=[jax.ShapeDtypeStruct(block, kind), jax.ShapeDtypeStruct(gates, FULL)],
-        in_specs=[VMEM] * (3 * len(tables) + 1),
+        in_specs=[VMEM] * (len(tables) + 5),
         out_specs=[ANY, ANY],
         scratch_shapes=[pltpu.VMEM((levels,) + block, kind)]
         + LineReduce.scratch(size, block, kind, cuts)
@@ -713,89 +724,142 @@
 
 
 def closing_kernel(size, dp_count, local_count, cuts, sum_cuts, *refs):
-    tables, slots = refs[:local_count], refs[local_count : 2 * local_count]
-    parts_ref, *sum_refs = refs[2 * local_count : 2 * local_count + 5]
-    outs, rest = refs[2 * local_count + 5 : 2 * local_count + 11], refs[2 * local_count + 11 :]
-    levels = size // 2
-    back = LineReduce(levels, cuts, parts_ref, outs[0], *rest[:12])
-    mixed = LineReduce(levels, cuts, rest[12], outs[1], *rest[13:25])
-    qkv_got, out_got, gain_got, got, half, last = rest[25:31]
-    sems = rest[31:]
-    lands = [qkv_got, out_got, gain_got]
-    sums = Exchange("dp", dp_count, (False, False, True), sum_cuts, sum_refs[:3], lands, *sems[:3])
-    first = Exchange("expert", size, (False,), (1,), sum_refs[3:], [got], *sems[3:6])
-    second = Exchange("dp", dp_count, (False,), (1,), [half], [last], *sems[6:9])
-    back.load()
+    refs, levels = list(refs), size // 2
+
+    def take(count):
+        taken = refs[:count]
+        del refs[:count]
+        return taken
+
+    tables, slots = take(local_count), take(2)
+    proj_ref, w_ref, h_ref, gain_ref, out_parts, gain_pair, shared_ref = take(7)
+    back_out, mixed_out, qkv_out, w_out, gains_out, gain_out, shared_out = take(7)
+    back = LineReduce(levels, cuts, *take(1), back_out, *take(12))
+    mixed = LineReduce(levels, cuts, *take(1), mixed_out, *take(12))
+    qkv_parts, qkv_got, out_got, gains_got = take(4)
+    got, half, last, gain_sum, gain_got, gain_half, gain_last = take(7)
+    parts, lands = [qkv_parts, out_parts, gain_pair], [qkv_got, out_got, gains_got]
+    sums = Exchange("dp", dp_count, (False, False, True), sum_cuts, parts, lands, *take(3))
+    first = Exchange("expert", size, (False,), (1,), [shared_ref], [got], *take(3))
+    second = Exchange("dp", dp_count, (False,), (1,), [half], [last], *take(3))
+    gain_first = Exchange("expert", size, (True,), (1,), [gain_sum], [gain_got], *take(3))
+    gain_second = Exchange("dp", dp_count, (True,), (1,), [gain_half], [gain_last], *take(3))
     greet("expert", [(peer, None) for peer in first.peers])
     greet("dp", [(peer, None) for peer in sums.peers])
     pl.semaphore_wait(pltpu.get_barrier_semaphore(), size + dp_count - 2)
     first.begin()
-    back.begin()
-    sums.stay()
-    tall = half.shape[1]
-    make = functools.partial(collect_block, tables, slots)
+    sums.staying(1).start()
+    sums.staying(2).start()
+    gain_sum[...] = jnp.zeros_like(gain_sum)
+    groups, tokens, model_dim = h_ref.shape
+    tall, high = half.shape[1], model_dim // dp_count
+
+    def make_back(block, target):
+        @pl.loop(0, model_dim // COLUMNS)
+        def _(n):
+            columns = pl.ds(pl.multiple_of(n * COLUMNS, COLUMNS), COLUMNS)
+            grad = across_cols(proj_ref[block], w_ref[columns, :])
+            target[:, columns] = grad.astype(target.dtype)
+            weighted = grad * h_ref[block, :, columns].astype(FULL)
+            gain_sum[:, columns] += jnp.sum(weighted, axis=0, keepdims=True)
+
+    def piece(k):
+        @pl.loop(0, dp_count)
+        def _(copy):
+            columns = pl.ds(pl.multiple_of(copy * high + k * 128, 128), 128)
+            rows = h_ref[:, :, columns].reshape(groups * tokens, 128)
+            grads = proj_ref[...].reshape(groups * tokens, proj_ref.shape[2])
+            qkv_parts[copy, pl.ds(k * 128, 128)] = contract_rows(rows, grads).astype(LOW)
+
+        sums.send(0, k)
+        pl.when(k == sum_cuts[0] - 1)(sums.staying(0).start)
+
+    make_mixed = functools.partial(collect_block, tables, slots)
+    ahead = levels
+
+    @pl.loop(0, ahead)
+    def _(turn):
+        back.prepare(turn, make_back)
 
     def beside(turn):
-        pl.when(turn < sum_cuts[0])(lambda: sums.send(0, turn))
-        after = turn - sum_cuts[0]
-        pl.when((after >= 0) & (after < sum_cuts[1]))(lambda: sums.send(1, after))
-
-        @pl.when(after == sum_cuts[1])
+        later = turn - ahead
+        pl.when(turn + ahead < 2 * levels)(lambda: back.prepare(turn + ahead, make_back))
+        pl.when(turn < sum_cuts[1])(lambda: sums.send(1, turn))
+        pl.when(turn == sum_cuts[1])(lambda: sums.send(2, 0))
+        pl.when(later == 0)(gain_first.begin)
+        pl.when((later >= 0) & (later < 2 * levels))(lambda: mixed.prepare(later, make_mixed))
+        pl.when((later >= 0) & (later < sum_cuts[0]))(lambda: piece(later))
+
+        @pl.when(later == ahead)
         def _():
-            sums.send(2, 0)
             first.arrive()
             for copy in range(dp_count):
                 rows = pl.ds(copy * tall, tall)
                 half[copy] = sum(got[i, rows, :] for i in range(size))
             second.begin()
-
-        pl.when(turn < 2 * levels)(lambda: mixed.prepare(turn, make))
+            gain_first.arrive()
+            gain_half[...] = sum(gain_got[i] for i in range(size))
+            gain_second.begin()
 
     back.main(beside)
     mixed.main()
     second.arrive()
-    outs[5][...] = sum(last[i] for i in range(dp_count))
+    shared_out[...] = sum(last[i] for i in range(dp_count))
+    gain_second.arrive()
+    gain_out[...] = sum(gain_last[i] for i in range(dp_count)) / gain_ref[...]
     sums.arrive()
-    wide = outs[2].shape[2]
+    wide = qkv_out.shape[2]
     for j in range(3):
         columns = slice(j * wide, (j + 1) * wide)
-        outs[2][j] = sum(qkv_got[copy, :, columns].astype(FULL) for copy in range(dp_count))
-    outs[3][...] = sum(out_got[copy].astype(FULL) for copy in range(dp_count))
-    outs[4][...] = sum(gain_got[copy] for copy in range(dp_count))
-    for moves in (back, mixed, first, second, sums):
+        qkv_out[j] = sum(qkv_got[copy, :, columns].astype(FULL) for copy in range(dp_count))
+    w_out[...] = sum(out_got[copy].astype(FULL) for copy in range(dp_count))
+    gains_out[...] = sum(gains_got[copy] for copy in range(dp_count))
+    for moves in (back, mixed, first, second, sums, gain_first, gain_second):
         moves.finish()
 
 
-def closing(size, dp_count, parts, tables, slots, cuts, sums, shared, number):
-    block = parts.shape[1:]
+def closing(size, dp_count, tables, slots, arrays, sums, shared, number):
+    proj, _, hidden, gain = arrays
+    levels, cuts = size // 2, 4
+    _, tokens, model_dim = hidden.shape
+    columns, high = proj.shape[2], model_dim // dp_count
+    block = (tokens, model_dim)
     tall = shared.shape[1] // dp_count
     wide = shared.shape[2]
-    sum_cuts = (8, 2, 1)
-    qkv, out, gain = exchange_outs(dp_count, sums, (False, False, True))
-    shapes = [(3, qkv.shape[1], qkv.shape[2] // 3), out.shape[1:], gain.shape[1:], (tall, wide)]
-    outs = [jax.ShapeDtypeStruct(block, parts.dtype)] * 2
+    sum_cuts = (high // 128, 2, 1)
+    out, pair = exchange_outs(dp_count, sums, (False, True))
+    shapes = [(3, high, columns // 3), out.shape[1:], pair.shape[1:], gain.shape, (tall, wide)]
+    outs = [jax.ShapeDtypeStruct(block, LOW)] * 2
     outs += [jax.ShapeDtypeStruct(shape, FULL) for shape in shapes]
-    line = LineReduce.scratch(size, block, parts.dtype, cuts)
+    line = [pltpu.VMEM((levels,) + block, LOW)] + LineReduce.scratch(size, block, LOW, cuts)
     return pl.pallas_call(
         functools.partial(closing_kernel, size, dp_count, len(tables), cuts, sum_cuts),
         out_shape=outs,
-        in_specs=[VMEM] * (2 * len(tables)) + [ANY] * 5,
-        out_specs=[ANY] * 2 + [VMEM] * 4,
+        in_specs=[VMEM] * (len(tables) + 6) + [ANY] * 3,
+        out_specs=[ANY] * 2 + [VMEM] * 5,
         scratch_shapes=line
-        + [pltpu.VMEM((size // 2,) + block, parts.dtype)]
         + line
-        + [pltpu.VMEM(a.shape, a.dtype) for a in (qkv, out, gain)]
+        + [pltpu.VMEM((dp_count, high, columns), LOW)] * 2
+        + [pltpu.VMEM(a.shape, a.dtype) for a in (out, pair)]
         + [pltpu.VMEM((size,) + shared.shape[1:], FULL)]
         + [pltpu.VMEM((dp_count, tall, wide), FULL)] * 2
+        + [
+            pltpu.VMEM(gain.shape, FULL),
+            pltpu.VMEM((size,) + gain.shape, FULL),
+            pltpu.VMEM(gain.shape, FULL),
+            pltpu.VMEM((dp_count,) + gain.shape, FULL),
+        ]
         + Exchange.scratch(dp_count, sum_cuts)
+        + Exchange.scratch(size, (1,))
+        + Exchange.scratch(dp_count, (1,))
         + Exchange.scratch(size, (1,))
         + Exchange.scratch(dp_count, (1,)),
         compiler_params=pltpu.CompilerParams(
-            collective_id=number, has_side_effects=True, vmem_limit_bytes=56 << 20
+            collective_id=number, has_side_effects=True, vmem_limit_bytes=62 << 20
         ),
         cost_estimate=pl.CostEstimate(flops=0, transcendentals=0, bytes_accessed=200_000_000),
         name="closing",
-    )(*tables, *slots, parts, *sums, shared)
+    )(*tables, *slots, *arrays, *sums, shared)
 
 
 def across_cols(left_side, right_side):
@@ -930,13 +994,12 @@
 
 
 def rotary_tables(length, size):
-    index = jnp.arange(size // 2, dtype=FULL)
-    frequency = jnp.exp(index * (-2.0 * math.log(10000.0) / size))
-    angles = jnp.arange(length, dtype=FULL)[:, None] * frequency[None, :]
-    cosine, sine = jnp.cos(angles), jnp.sin(angles)
-    return jnp.stack(
-        [jnp.concatenate([cosine, cosine], axis=1), jnp.concatenate([-sine, sine], axis=1)]
-    )
+    index = np.arange(size // 2, dtype=np.float32)
+    frequency = np.exp(index * np.float32(-2.0 * math.log(10000.0) / size))
+    angles = np.arange(length, dtype=np.float32)[:, None] * frequency[None, :]
+    cosine, sine = np.cos(angles), np.sin(angles)
+    halves = [np.concatenate([cosine, cosine], axis=1), np.concatenate([-sine, sine], axis=1)]
+    return jnp.asarray(np.stack(halves).astype(np.float32))
 
 
 def norm_back(grad_normed, normed, scale_rows):
@@ -1087,8 +1150,8 @@
             half = projected[:, part * width : (part + 1) * width]
             total = jnp.sum(half * half, axis=-1, keepdims=True)
             sums[...] += jnp.where(lanes == part * size + g, total, 0.0)
-        line.turn(g)
-        pl.when((lax.rem(g, 2) == 0) & (g > 0))(lambda: sheets.forward(lax.div(g, 2)))
+        pl.when(g >= size // 2)(lambda: line.turn(g - size // 2))
+        pl.when(g == size // 2)(lambda: sheets.forward(1))
 
     squares[...] = sums[...].T[: 2 * size]
     small.begin()
@@ -1116,10 +1179,19 @@
             heads, g, rows, scales, gains_ref, turn_ref, column_ref[g], row_ref[g], kept_ref, out_ref
         )
         pl.when(g != place)(lambda: sending(g, place).start())
-        line.turn(size + i)
-        pl.when((lax.rem(i, 2) == 1) & (i < 2 * (size // 2)))(lambda: sheets.cross(lax.div(i, 2)))
+        pl.when(i >= size // 2)(lambda: line.turn(i))
+        pl.when(i == size // 2)(lambda: sheets.forward(2))
 
     staying.start()
+
+    @pl.loop(size, 2 * size)
+    def _(i):
+        line.turn(i)
+        for step in range(3, size // 2):
+            pl.when(i == size)(lambda: sheets.forward(step))
+        after = i - size - size // 2
+        pl.when((after >= 0) & (after < size // 2))(lambda: sheets.cross(after))
+
 
     @pl.loop(1, size)
     def _(i):
@@ -1188,7 +1260,7 @@
     )(*arrays)
 
 
-def attend_back_block(heads, block, grad_ref, refs, back_ref, dots_ref, gains_ref, w_sum):
+def attend_back_block(heads, block, grad_ref, refs, back_ref, dots_ref, lanes, gains_ref, w_sum):
     w_ref, kept_ref, out_ref, rows_ref, scale_ref, gain_ref, turn_ref, column_ref, row_ref = refs
     width = out_ref.shape[2]
     size = width // heads
@@ -1221,55 +1293,87 @@
             dots[part] += jnp.sum(weighted * normed, axis=-1, keepdims=True)
             back_ref[block, :, columns] = weighted
         back_ref[block, :, pl.ds(2 * width + h * size, size)] = grad_value
-    dots_ref[block] = jnp.concatenate(dots, axis=1)
+    groups = grad_ref.shape[0]
+    for part in range(2):
+        dots_ref[...] += jnp.where(lanes == part * groups + block, dots[part], 0.0)
 
 
 def attend_back_kernel(levels, cuts, heads, grad_ref, *refs):
-    w_ref, others = refs[0], refs[1:9]
-    back_ref, dots_ref, gains_ref, w_grad_ref, w_sum, held, w_held, w_sem, *sems = refs[9:]
+    w_ref, others, refs = refs[0], refs[1:9], refs[9:]
+    proj_ref, gains_ref, w_grad_ref, w_sum, held, w_held, back, dots, squares, got, w_sem = refs[:11]
     reads = (w_held,) + tuple(others)
-    line = LineGather(levels, cuts, [grad_ref], [held], *sems)
+    rows_ref, scale_ref = others[2:4]
+    size, model_dim = 2 * levels, grad_ref.shape[1]
+    line = LineGather(levels, cuts, [grad_ref], [held], *refs[11:16])
+    small = Exchange("expert", size, (True,), (1,), [squares], [got], *refs[16:])
     mine = pl.ds(pl.multiple_of(line.place * w_held.shape[0], 128), w_held.shape[0])
     loading = pltpu.make_async_copy(w_ref.at[mine], w_held, w_sem.at[0])
     loading.start()
-    line_barrier(levels)
+    greet("expert", [(peer, None) for peer in small.peers])
+    pl.semaphore_wait(pltpu.get_barrier_semaphore(), size - 1)
     line.begin()
     w_sum[...] = jnp.zeros_like(w_sum)
     gains_ref[...] = jnp.zeros_like(gains_ref)
+    dots[...] = jnp.zeros_like(dots)
+    lanes = lax.broadcasted_iota(jnp.int32, dots.shape, 1)
     loading.wait()
     line.staying(0).wait()
 
     def landed(block):
-        attend_back_block(heads, block, held, reads, back_ref, dots_ref, gains_ref, w_sum)
+        attend_back_block(heads, block, held, reads, back, dots, lanes, gains_ref, w_sum)
 
     line.main(landed)
+    squares[...] = dots[...].T[: 2 * size]
+    small.begin()
     wide = w_grad_ref.shape[2]
     for copy in range(w_grad_ref.shape[0]):
         w_grad_ref[copy] = w_sum[:, copy * wide : (copy + 1) * wide].astype(LOW)
+    small.arrive()
+    dots[:, : 2 * size] = sum(got[i] for i in range(size)).T / model_dim
+    width = w_held.shape[0]
+
+    @pl.loop(0, size)
+    def _(block):
+        for part in range(2):
+            columns = pl.ds(part * width, width)
+            scale = scale_ref[block, :, part : part + 1]
+            mean = jnp.where(lanes == part * size + block, dots[...], 0.0)
+            mean = jnp.sum(mean, axis=-1, keepdims=True)
+            normed = rows_ref[block, :, columns] * scale
+            proj_ref[block, :, columns] = (scale * (back[block, :, columns] - normed * mean)).astype(LOW)
+        columns = pl.ds(2 * width, width)
+        proj_ref[block, :, columns] = back[block, :, columns].astype(LOW)
+
     line.finish(held=1)
+    small.finish()
 
 
 def attend_back(size, dp_count, heads, grad, arrays, number):
     _, _, out, rows = arrays[:4]
     width = out.shape[2]
     tokens, model_dim = grad.shape
+    small = (2 * size, tokens)
     return pl.pallas_call(
         functools.partial(attend_back_kernel, size // 2, 4, heads),
         out_shape=[
-            jax.ShapeDtypeStruct(rows.shape, FULL),
-            jax.ShapeDtypeStruct((size, tokens, 2), FULL),
+            jax.ShapeDtypeStruct(rows.shape, LOW),
             jax.ShapeDtypeStruct((2, width), FULL),
             jax.ShapeDtypeStruct((dp_count, width, model_dim // dp_count), LOW),
         ],
         in_specs=[ANY] * 2 + [VMEM] * (len(arrays) - 1),
-        out_specs=[VMEM] * 4,
+        out_specs=[VMEM] * 3,
         scratch_shapes=[
             pltpu.VMEM((width, model_dim), FULL),
             pltpu.VMEM((size, tokens, model_dim), LOW),
             pltpu.VMEM((width, model_dim), LOW),
+            pltpu.VMEM(rows.shape, FULL),
+            pltpu.VMEM((tokens, 128), FULL),
+            pltpu.VMEM(small, FULL),
+            pltpu.VMEM((size,) + small, FULL),
             pltpu.SemaphoreType.DMA((1,)),
         ]
-        + LineGather.scratch(size, 4, 1),
+        + LineGather.scratch(size, 4, 1)
+        + Exchange.scratch(size, (1,)),
         compiler_params=pltpu.CompilerParams(
             collective_id=number, has_side_effects=True, vmem_limit_bytes=48 << 20
         ),
@@ -1305,38 +1409,33 @@
     capacity = (row_count * top_count * 9 // 8 + expert_count - 1) // expert_count
     scaling = 1.0 / math.sqrt(head_size)
     place = lax.axis_index("expert")
-    all_rows = line_count * row_count
     shard = w_qkv.shape[0]
 
-    small = jnp.concatenate(
-        [w_router] + [g[:, None] for g in (attn_gain, mlp_gain, query_gain, key_gain)], axis=1
-    )
-    small = jnp.pad(small, ((0, 0), (0, 128 - small.shape[1])))
     numbers = jnp.concatenate([routes.T, segments, jnp.zeros((7, row_count), jnp.int32)], axis=0)
-    x_all, numbers_all, qkv_here, small = opening(
-        line_count, dp_count, [layer_input, numbers], 4, w_qkv, small, 1
+    x_all, numbers_all, qkv_here, router_full, gains = opening(
+        line_count,
+        dp_count,
+        [layer_input, numbers],
+        4,
+        w_qkv,
+        [w_router, jnp.stack([attn_gain, mlp_gain, query_gain, key_gain])],
+        1,
     )
     qkv_here = qkv_here.reshape(model_dim, 3 * head_cols)
-    small = small.reshape(model_dim, small.shape[3])
-    router_full = small[:, :expert_count]
-    gains = small[:, expert_count : expert_count + 4].astype(FULL)
-    gain_attn, gain_mlp = gains[:, 0], gains[:, 1]
-    own_gains = lax.dynamic_slice_in_dim(gains, place * head_cols, head_cols, axis=0)
-    gain_query, gain_key = own_gains[:, 2], own_gains[:, 3]
+    router_full = router_full.reshape(model_dim, expert_count)
+    gains = gains.transpose(2, 0, 1, 3).reshape(4, model_dim).astype(FULL)
+    gain_attn, gain_mlp = gains[0], gains[1]
+    both_gains = lax.dynamic_slice_in_dim(gains[2:], place * head_cols, head_cols, axis=1)
 
     routes_all = numbers_all[:, :top_count]
     segments_all = numbers_all[:, top_count]
     turns = rotary_tables(row_count, head_size)
-    both_gains = jnp.stack([gain_query, gain_key])
     column, row = segments_all[:, :, None], segments_all[:, None, :]
     arrays = [x_all, qkv_here, gain_attn[None], both_gains, turns, column, row, w_out, out_cotangent]
     hidden_one, projected, scales, roots, kept, attended, own_attended, out_full, dy_all = attention(
         line_count, dp_count, heads_here, arrays, 4
     )
     out_full = out_full.reshape(model_dim, model_dim)
-    hidden_one = hidden_one.reshape(all_rows, model_dim)
-    inputs_all = x_all.reshape(all_rows, model_dim).astype(FULL)
-    normed_all = inputs_all * roots.reshape(all_rows, 1)
     inputs = layer_input.astype(FULL)
     scale_attn = rms_scale(inputs)
     normed_attn = inputs * scale_attn
@@ -1378,8 +1477,7 @@
         grads = lax.psum_scatter(grads, "dp", scatter_dimension=0, tiled=True)
         grad_sums.append(grads.reshape(count, both_rows, model_dim))
         for kept_list, rows in ((out_rows, out_row), (back_rows, back_row), (slot_grads, dots)):
-            for j in range(count):
-                kept_list.append(rows[j].reshape(line_count, capacity, rows.shape[2]))
+            kept_list.append(rows.reshape(count, line_count, capacity, rows.shape[2]))
     gate_rows = model_dim // dp_count
     grad_two, grad_gates = collect_reduce(
         line_count, returns, back_rows, slot_grads, flat_table, 8
@@ -1397,46 +1495,22 @@
     grad_attn = grad_resid.astype(LOW)
 
     arrays = [out_full, kept, attended, projected, scales, both_gains, turns, column, row]
-    back, dots, gain_pair, out_parts = attend_back(
+    grad_proj, gain_pair, out_parts = attend_back(
         line_count, dp_count, heads_here, grad_attn, arrays, 11
     )
-    dots = dots.transpose(2, 0, 1).reshape(2 * line_count, row_count)
-    (dots,) = exchange("expert", line_count, [dots], [True], 12)
-    dots = jnp.sum(dots, axis=0).reshape(2, all_rows, 1) / model_dim
-    flat_scales = scales.reshape(all_rows, 2)
-    back = back.reshape(all_rows, 3 * head_cols)
-    projected = projected.reshape(all_rows, 3 * head_cols)
-    grads = []
-    for part in range(2):
-        columns = slice(part * head_cols, (part + 1) * head_cols)
-        scale = flat_scales[:, part : part + 1]
-        normed = projected[:, columns] * scale
-        grads.append(scale * (back[:, columns] - normed * dots[part]))
-    grad_proj = jnp.concatenate(grads + [back[:, 2 * head_cols :]], axis=-1).astype(LOW)
-    grad_one = contract_cols(grad_proj, qkv_here)
-    grad_gain_attn = jnp.sum(grad_one * normed_all, axis=0)
-    grad_one = grad_one.astype(LOW).reshape(line_count, row_count, model_dim)
-    grad_w_qkv = contract_rows(hidden_one, grad_proj)
-
-    out_cols = model_dim // dp_count
-    qkv_parts = grad_w_qkv.astype(LOW).reshape(dp_count, out_cols, 3 * head_cols)
-    shared = jnp.concatenate([grad_router, grad_gain_attn[None], grad_gain_mlp[None]], axis=0)
+
+    shared = jnp.concatenate([grad_router, grad_gain_mlp[None]], axis=0)
     tall = shared.shape[0] + -shared.shape[0] % 8
     shared = jnp.pad(shared, ((0, tall - shared.shape[0]), (0, 0)))
     shared = shared.reshape(tall, dp_count, line_count, shard).transpose(2, 1, 0, 3)
     shared = shared.reshape(line_count, dp_count * tall, shard)
     shared = jnp.pad(shared, ((0, 0), (0, 0), (0, 128 - shard)))
-    grad_one, mixture, sum_qkv, sum_out, gain_pair, shared = closing(
-        line_count,
-        dp_count,
-        grad_one,
-        returns,
-        out_rows,
-        4,
-        [qkv_parts, out_parts, gain_pair],
-        shared,
-        14,
+    arrays = [grad_proj, qkv_here, hidden_one, gain_attn[None]]
+    grad_one, mixture, sum_qkv, sum_out, gain_pair, gain_sum, shared = closing(
+        line_count, dp_count, returns, out_rows, arrays, [out_parts, gain_pair], shared, 14
     )
+    here = (lax.axis_index("dp") * line_count + place) * shard
+    grad_gain_attn = lax.dynamic_slice_in_dim(gain_sum[0], here, shard)
     output = (residual + mixture.astype(FULL)).astype(LOW)
     sum_qkv = sum_qkv.transpose(1, 0, 2)
     first_sums, output = lax.optimization_barrier((grad_sums[0], output))
@@ -1451,8 +1525,8 @@
         sum_qkv,
         sum_out,
         shared[:expert_count].T,
+        grad_gain_attn,
         shared[expert_count],
-        shared[expert_count + 1],
         gain_pair[0],
         gain_pair[1],
         sum_gate_up,

time: 741 us -> 732 us (0.988)
  Pallas kernels: 637 us -> 669 us
  matrix products: 28.7 us -> 10.4 us
  local copies, waits for them, and re-layouts: 38.1 us -> 22 us
    pallas_call x1, Pallas kernels: 137 us -> 161 us  [closing(): pl.pallas_call(functools.partial(closing_kernel, size, dp_count, len(tabl...]
    pallas_call x1, Pallas kernels: 57.5 us -> 73.2 us  [attend_back(): pl.pallas_call(functools.partial(attend_back_kernel, size // 2, 4, heads)...]
    pallas_call x2 -> x1, Pallas kernels: 86.1 us -> 72.8 us  [call(): pl.pallas_call(kernel, out_shape=outs, in_specs=[ANY] * len(arrays), out_...]
    slice x8 -> x5, local copies, waits for them, and re-layouts: 13.5 us -> 0.29 us  [the longest x2 0.18 us: on_device(): gain_attn, gain_mlp = (gains[0], gains[1])]
    dot_general x2 -> x1, matrix products: 10.4 us -> 0.22 us  [contract_rows(): lax.dot_general(left_side, right_side, (((0,), (0,)), ((), ())), preferre...]
    dot_general x2 -> x1, matrix products: 11.9 us -> 3.72 us  [contract_cols(): lax.dot_general(left_side, right_side, (((1,), (1,)), ((), ())), preferre...]
    unnamed x96 -> x75, local copies, waits for them, and re-layouts: 14.8 us -> 15.3 us
  transfers between devices with their start and end apart: 2 -> 2, of which waited for: 0 -> 0; matrix products, arithmetic and copies ran while one was open for 7% -> 2% of each run, Pallas kernels for 49% -> 53%
where the time goes in v7:
time: 732 us; the launch traced here: 731 us
  Pallas kernels  669 us (91%)
  local copies, waits for them, and re-layouts  22 us (3%)
  between operations  14.6 us (2%)
  other arithmetic  14 us (2%)
  matrix products  10.4 us (1%)
    pallas_call x1, Pallas kernels, closing(): pl.pallas_call(functools.partial(closing_kernel, size, dp_count, len(tabl...  161 us
    pallas_call x2, Pallas kernels, expert(): pl.pallas_call(functools.partial(expert_kernel, first, count, tiles), out...  101 us
    pallas_call x1, Pallas kernels, attention(): pl.pallas_call(functools.partial(attention_kernel, size, dp_count, heads)...  98.7 us
    pallas_call x1, Pallas kernels, collect_reduce(): pl.pallas_call(functools.partial(collect_reduce_kernel, levels, cuts, len...  83.3 us
    pallas_call x1, Pallas kernels, attend_back(): pl.pallas_call(functools.partial(attend_back_kernel, size // 2, 4, heads)...  73.2 us
    pallas_call x1, Pallas kernels, call(): pl.pallas_call(kernel, out_shape=outs, in_specs=[ANY] * len(arrays), out_...  72.8 us
    pallas_call x1, Pallas kernels, gather_place(): pl.pallas_call(functools.partial(gather_place_kernel, size // 2, cuts), o...  62.7 us
    pallas_call x2, Pallas kernels, widen(): pl.pallas_call(functools.partial(widen_kernel, steps), out_shape=[jax.Sha...  17 us
  transfers between devices with their start and end apart: 2, of which 0 were waited for; matrix products, arithmetic and copies ran while one was open for 2% of the time, Pallas kernels for 53%

profile of v7, /device:TPU:16, one launch (start us, length us, event | category | flops | bytes accessed | tf_op | source)
XLA Modules:
  0.0 730.8 jit_solution(6143134012339127149)
XLA Ops:
  7.3 1.4 fusion.8
  11.7 1.1 copy-done
  12.9 1.1 copy-done.22
  14.0 72.8 %opening.1 = (bf16[8,192,2048]{2,1,0:T(8,128)(2,1)}, s32[8,16,192]{2,1,0:T(8,128)S(1)}, bf16[4,8,64,768]{3,2,1,0:T(8,128)(2,1)S(1)}, bf16[4,8,64,24]{3,2,1,0:T(8,128)(2,1)S(1)}, bf16[4,8,4,64]{3,2,1,0:T(4,128)(2,1)S(1)}) custom-call(bf16[192,2048]{1,0:T(8,128)(2,1)S(1)} %copy-done, s32[16,192]{1,0:T(8,128)S(1)} %add_add_fusion.refs_1_, ...), custom_call_target="tpu_custom_call" | custom-call | bytes 200000000 | tf_op jit(solution)/shard_map/opening/pallas_call | solution.py:181
  86.8 1.6 copy-done.9
  90.4 98.7 %attention.1 = (bf16[8,192,2048]{2,1,0:T(8,128)(2,1)}, f32[8,192,768]{2,1,0:T(8,128)}, f32[8,192,2]{2,1,0:T(8,128)S(1)}, f32[8,192,1]{2,1,0:T(8,128)}, bf16[8,19...) custom-call(bf16[8,192,2048]{2,1,0:T(8,128)(2,1)} %get-tuple-element, ...), custom_call_target="tpu_custom_call" | custom-call | flops 4831838208 | bytes 100000000 | tf_op jit(solution)/shard_map/attention/pallas_call | solution.py:1221
  189.2 5.9 multiply_reduce_fusion.3
  195.4 1.2 copy-done.14
  197.2 62.7 %gather_place.1 = (bf16[3,576,2048]{2,1,0:T(8,128)(2,1)}, bf16[3,576,2048]{2,1,0:T(8,128)(2,1)}, f32[8,24,192]{2,1,0:T(8,128)S(1)}) custom-call(bf16[192,2048]{1,0:T(8,128)(2,1)S(1)} %multiply_convert_fusion.refs_0_, f32[24,192]{1,0:T(8,128)S(1)} %fusion.22.refs_1_, bf16[8,216,192]{2,1,0:T(8,128)(2,1)S(1)} %fusion.3.refs_2_.refs_7_, ...), custom_call_target="tpu_custom_call" | custom-call | flops 2717908992 | bytes 150000000 | tf_op jit(solution)/shard_map/gather_place/pallas_call | solution.py:634
  260.5 1.2 reshape.140.scale_ref
  261.7 35.3 %expert.2 = (bf16[4,768,2048]{2,1,0:T(8,128)(2,1)}, bf16[1,576,2048]{2,1,0:T(8,128)(2,1)}, bf16[1,576,2048]{2,1,0:T(8,128)(2,1)}, f32[1,576,1]{2,1,0:T(8,128)}) custom-call(bf16[3,576,2048]{2,1,0:T(8,128)(2,1)} %get-tuple-element.61.x_ref, bf16[3,576,2048]{2,1,0:T(8,128)(2,1)} %get-tuple-element.62.dy_ref, f32[3,576,1]{2,1,0:T(8,128)} %reshape.140.scale_ref, ...), custom_call_target="tpu_custom_call" | custom-call | flops 21743271936 | bytes 25165824 | tf_op jit(solution)/shard_map/expert/pallas_call | solution.py:970
  297.4 65.8 %expert.3 = (bf16[4,1536,2048]{2,1,0:T(8,128)(2,1)}, bf16[2,576,2048]{2,1,0:T(8,128)(2,1)}, bf16[2,576,2048]{2,1,0:T(8,128)(2,1)}, f32[2,576,1]{2,1,0:T(8,128)}) custom-call(bf16[3,576,2048]{2,1,0:T(8,128)(2,1)} %get-tuple-element.61.x_ref, bf16[3,576,2048]{2,1,0:T(8,128)(2,1)} %get-tuple-element.62.dy_ref, f32[3,576,1]{2,1,0:T(8,128)} %reshape.140.scale_ref, ...), custom_call_target="tpu_custom_call" | custom-call | flops 43486543872 | bytes 50331648 | tf_op jit(solution)/shard_map/expert/pallas_call | solution.py:970
  364.5 1.7 copy-done.12
  367.3 83.3 %collect_reduce.1 = (bf16[192,2048]{1,0:T(8,128)(2,1)S(1)}, f32[8,3,192]{2,1,0:T(4,128)S(1)}) custom-call(bf16[8,192,72]{2,1,0:T(8,128)(2,1)S(1)} %get-tuple-element.114.refs_0_, bf16[8,192,72]{2,1,0:T(8,128)(2,1)S(1)} %get-tuple-element.115.refs_1_, bf16[8,192,72]{2,1,0:T(8,128)(2,1)S(1)} %fusion.12.refs_2_, bf16[1,8,72,2048]{3,2,1,0:T(8,128)(2,1)S(1)} %bitcast.83, ...), custom_call_target="tpu_custom_call" | custom-call | bytes 150000000 | tf_op jit(solution)/shard_map/collect_reduce/pallas_call | solution.py:709
  452.6 3.7 multiply_reduce_fusion.1
  457.8 2.5 fusion.28.grad_ref
  460.4 73.2 %attend_back.1 = (bf16[8,192,768]{2,1,0:T(8,128)(2,1)}, f32[2,256]{1,0:T(2,128)S(1)}, bf16[4,256,512]{2,1,0:T(8,128)(2,1)S(1)}) custom-call(bf16[192,2048]{1,0:T(8,128)(2,1)S(1)} %fusion.28.grad_ref, bf16[2048,2048]{1,0:T(8,128)(2,1)} %bitcast.91, bf16[8,192,768]{2,1,0:T(8,128)(2,1)} %get-tuple-element.73.refs_1_, bf16[8,192,256]{2,1,0:T(8,128)(2,1)S(1)} %copy-done.19, ...), custom_call_target="tpu_custom_call" | custom-call | bytes 150000000 | tf_op jit(solution)/shard_map/attend_back/pallas_call | solution.py:1356
  535.1 160.7 %closing.1 = (bf16[192,2048]{1,0:T(8,128)(2,1)}, bf16[192,2048]{1,0:T(8,128)(2,1)}, f32[3,512,256]{2,1,0:T(8,128)}, f32[256,512]{1,0:T(8,128)}, f32[2,256]{1,0:T...) custom-call(bf16[8,192,72]{2,1,0:T(8,128)(2,1)} %copy-done.5, bf16[8,192,72]{2,1,0:T(8,128)(2,1)} %copy-done.6, ...), custom_call_target="tpu_custom_call" | custom-call | bytes 200000000 | tf_op jit(solution)/shard_map/closing/pallas_call | solution.py:835
  695.8 1.4 fusion.27
  697.2 1.6 fusion.4
  700.5 4.2 fusion.7
  704.7 6.1 widen.2
  710.9 10.9 %widen.3 = (f32[3,512,2048]{2,1,0:T(8,128)}, f32[3,256,2048]{2,1,0:T(8,128)}) custom-call(bf16[2,768,2048]{2,1,0:T(8,128)(2,1)} %bitcast.92, f32[3,512,2048]{2,1,0:T(8,128)} %get-tuple-element.91.refs_1_, f32[3,256,2048]{2,1,0:T(8,128)} %get-tuple-element.92.refs_2_), custom_call_target="tpu_custom_call", output_to_operand_aliasing={{0}: (1, {}), {1}: (2, {})} | custom-call | flops 3145728 | bytes 18874368 | tf_op jit(solution)/shard_map/widen/pallas_call | solution.py:1046
  721.7 1.1 copy.70
  (123 shorter events, 16.8 us)
Async XLA Ops:
  7.2 697.5 %reduce-scatter.3.cloned.1.call-start = ((), (), s32[]{:S(2)}) async-start(), calls=%async_computation.2 | async-start | bytes 15728640 | tf_op jit(solution)/shard_map/reduce_scatter | solution.py:1477
  14.0 76.4 %copy-start.10 = (bf16[192,2048]{1,0:T(8,128)(2,1)S(1)}, bf16[192,2048]{1,0:T(8,128)(2,1)}, u32[]{:S(2)}) copy-start(bf16[192,2048]{1,0:T(8,128)(2,1)} %refs_8_.1) | copy-start | bytes 2359300
  14.0 76.4 %copy-start.25 = (f32[2,192,128]{2,1,0:T(8,128)S(1)}, f32[2,192,128]{2,1,0:T(8,128)}, u32[]{:S(2)}) copy-start(f32[2,192,128]{2,1,0:T(8,128)} %constant.45.clone.refs_4_.refs_6_) | copy-start | bytes 589828
  14.0 76.4 %copy-start.29 = (bf16[64,2048]{1,0:T(8,128)(2,1)S(1)}, bf16[64,2048]{1,0:T(8,128)(2,1)}, u32[]{:S(2)}) copy-start(bf16[64,2048]{1,0:T(8,128)(2,1)} %refs_7_.1) | copy-start | bytes 786436
  90.0 99.1 %copy-start.27 = (f32[1,2048]{1,0:T(1,128)}, f32[1,2048]{1,0:T(1,128)S(1)}, u32[]{:S(2)}) copy-start(f32[1,2048]{1,0:T(1,128)S(1)} %slice.47.refs_2_.refs_8_) | copy-start | bytes 24580
  90.3 98.8 %copy-start.7 = (s32[8,192,1]{2,1,0:T(8,128)}, s32[8,192,1]{2,1,0:T(8,128)S(1)}, u32[]{:S(2)}) copy-start(s32[8,192,1]{2,1,0:T(8,128)S(1)} %copy.55.refs_5_.refs_7_) | copy-start | bytes 18436
  90.4 98.8 %copy-start.1 = (bf16[192,2048]{1,0:T(8,128)(2,1)S(1)}, bf16[192,2048]{1,0:T(8,128)(2,1)}, u32[]{:S(2)}) copy-start(bf16[192,2048]{1,0:T(8,128)(2,1)} %refs_0_.1) | copy-start | bytes 2359300
  189.1 6.0 copy-start.16
  189.2 6.0 copy-start.18
  195.1 1.8 copy-start.30
  197.2 62.7 %copy-start.2 = (bf16[8,216,192]{2,1,0:T(8,128)(2,1)}, bf16[8,216,192]{2,1,0:T(8,128)(2,1)S(1)}, u32[]{:S(2)}) copy-start(bf16[8,216,192]{2,1,0:T(8,128)(2,1)S(1)} %fusion.3.refs_2_.refs_7_) | copy-start | bytes 1990660
  297.1 413.8 %reduce-scatter.5.cloned.1.call-start = ((), (), s32[]{:S(2)}) async-start(), calls=%async_computation.3 | async-start | bytes 31457280 | tf_op jit(solution)/shard_map/reduce_scatter | solution.py:1477
  363.5 87.0 %copy-start.4 = (bf16[8,192,72]{2,1,0:T(8,128)(2,1)}, bf16[8,192,72]{2,1,0:T(8,128)(2,1)S(1)}, u32[]{:S(2)}) copy-start(bf16[8,192,72]{2,1,0:T(8,128)(2,1)S(1)} %fusion.12.refs_2_) | copy-start | bytes 663556
  364.2 86.4 %copy-start.5 = (bf16[8,192,72]{2,1,0:T(8,128)(2,1)}, bf16[8,192,72]{2,1,0:T(8,128)(2,1)S(1)}, u32[]{:S(2)}) copy-start(bf16[8,192,72]{2,1,0:T(8,128)(2,1)S(1)} %get-tuple-element.114.refs_0_) | copy-start | bytes 663556
  364.2 86.4 %copy-start.6 = (bf16[8,192,72]{2,1,0:T(8,128)(2,1)}, bf16[8,192,72]{2,1,0:T(8,128)(2,1)S(1)}, u32[]{:S(2)}) copy-start(bf16[8,192,72]{2,1,0:T(8,128)(2,1)S(1)} %get-tuple-element.115.refs_1_) | copy-start | bytes 663556
  364.5 1.7 copy-start.12
  457.7 2.6 copy-start.8
  457.7 2.6 copy-start.17
  457.7 2.6 copy-start.19
  457.7 2.6 copy-start.26
  695.8 3.0 copy-start.35
  695.8 3.6 copy-start.34
  695.8 4.7 copy-start.31
  710.8 10.9 %copy-start.32 = (f32[3,512,256]{2,1,0:T(8,128)S(1)}, f32[3,512,256]{2,1,0:T(8,128)}, u32[]{:S(2)}) copy-start(f32[3,512,256]{2,1,0:T(8,128)} %get-tuple-element.84) | copy-start | bytes 4718596
  (14 other events, 16.0 us)
Sparse Core Ops, SparseCore 0:
  297.2 125.7 reduce-scatter.2
  426.1 280.5 reduce-scatter.4

commit v8 on v7

--- a/solution.py
+++ b/solution.py
@@ -682,18 +682,17 @@
     def _(turn):
         line.prepare(turn, make)
 
-    @pl.loop(0, 2 * levels)
-    def _(block):
+    def gate_block(block):
         table = table_ref[block].astype(FULL)
         capacity = table.shape[0] // local_count
         for j in range(local_count):
             part = table[j * capacity : (j + 1) * capacity] * split_at(dots, j, block)[...]
             gates[block, j : j + 1] = jnp.sum(part, axis=0, keepdims=True)
 
-    small.begin()
-
     def beside(turn):
         pl.when(turn + 4 < 2 * levels)(lambda: line.prepare(turn + 4, make))
+        pl.when(turn >= levels)(lambda: gate_block(turn - levels))
+        pl.when(turn == 3 * levels - 1)(small.begin)
 
     line.main(beside)
     small.arrive()
@@ -763,16 +762,15 @@
             weighted = grad * h_ref[block, :, columns].astype(FULL)
             gain_sum[:, columns] += jnp.sum(weighted, axis=0, keepdims=True)
 
-    def piece(k):
-        @pl.loop(0, dp_count)
-        def _(copy):
-            columns = pl.ds(pl.multiple_of(copy * high + k * 128, 128), 128)
-            rows = h_ref[:, :, columns].reshape(groups * tokens, 128)
-            grads = proj_ref[...].reshape(groups * tokens, proj_ref.shape[2])
-            qkv_parts[copy, pl.ds(k * 128, 128)] = contract_rows(rows, grads).astype(LOW)
-
-        sums.send(0, k)
-        pl.when(k == sum_cuts[0] - 1)(sums.staying(0).start)
+    def piece(turn):
+        k, copy = lax.div(turn, dp_count), lax.rem(turn, dp_count)
+        columns = pl.ds(pl.multiple_of(copy * high + k * 128, 128), 128)
+        rows = h_ref[:, :, columns].reshape(groups * tokens, 128)
+        grads = proj_ref[...].reshape(groups * tokens, proj_ref.shape[2])
+        products = contract_rows(rows, grads).astype(LOW)
+        qkv_parts[copy, pl.ds(pl.multiple_of(k * 128, 128), 128)] = products
+        pl.when(copy == dp_count - 1)(lambda: sums.send(0, k))
+        pl.when(turn == sum_cuts[0] * dp_count - 1)(lambda: sums.staying(0).start())
 
     make_mixed = functools.partial(collect_block, tables, slots)
     ahead = levels
@@ -788,7 +786,7 @@
         pl.when(turn == sum_cuts[1])(lambda: sums.send(2, 0))
         pl.when(later == 0)(gain_first.begin)
         pl.when((later >= 0) & (later < 2 * levels))(lambda: mixed.prepare(later, make_mixed))
-        pl.when((later >= 0) & (later < sum_cuts[0]))(lambda: piece(later))
+        pl.when(later >= 0)(lambda: piece(later))
 
         @pl.when(later == ahead)
         def _():
@@ -802,7 +800,7 @@
             gain_second.begin()
 
     back.main(beside)
-    mixed.main()
+    mixed.main(lambda turn: pl.when(turn < 2 * levels)(lambda: piece(2 * levels + turn)))
     second.arrive()
     shared_out[...] = sum(last[i] for i in range(dp_count))
     gain_second.arrive()
@@ -1040,7 +1038,7 @@
 def widen(first, total, high, grads, held=()):
     count, both, width = grads.shape
     low = both - high
-    rows = low // 2
+    rows = low
     steps = high // rows
     block = (1, rows, width)
     return pl.pallas_call(
@@ -1049,7 +1047,7 @@
             jax.ShapeDtypeStruct((total, high, width), FULL),
             jax.ShapeDtypeStruct((total, low, width), FULL),
         ],
-        grid=(count, steps + 2),
+        grid=(count, steps + 1),
         in_specs=[pl.BlockSpec(block, lambda e, r: (e, r, 0))] + [ANY] * len(held),
         out_specs=[
             pl.BlockSpec(block, lambda e, r: (first + e, jnp.minimum(r, steps - 1), 0)),
@@ -1105,10 +1103,10 @@
 
 def attention_kernel(size, dp_count, heads, *refs):
     x_ref, w_ref, gain_ref, gains_ref, turn_ref, column_ref, row_ref, sheet_ref, dy_ref = refs[:9]
-    h_out, rows_out, scale_ref, root_ref, kept_ref, out_ref, own_out, sheet_out, dy_out = refs[9:18]
-    x_held, h_held, rows, sums, squares, got = refs[18:24]
-    x_sem, h_sem, rows_sem, send_sem, recv_sem, stay_sem = refs[24:30]
-    square_sems, line_sems, sheet_sems = refs[30:33], refs[33:38], refs[38:]
+    h_out, rows_out, scale_ref, kept_ref, out_ref, own_out, sheet_out, dy_out = refs[9:17]
+    x_held, h_held, rows, sums, squares, got = refs[17:23]
+    x_sem, h_sem, rows_sem, send_sem, recv_sem, stay_sem = refs[23:29]
+    square_sems, line_sems, sheet_sems = refs[29:32], refs[32:37], refs[37:]
     line = LineGather(size // 2, 4, [dy_ref], [dy_out], *line_sems)
     sheets = Sheets(size, dp_count, sheet_ref, sheet_out, *sheet_sems)
     small = Exchange("expert", size, (True,), (1,), [squares], [got], *square_sems)
@@ -1138,9 +1136,7 @@
     def _(g):
         loading(g).wait()
         values = x_held[g].astype(FULL)
-        root = rms_scale(values)
-        root_ref[g] = root
-        hidden = (values * root * gain_ref[...]).astype(LOW)
+        hidden = (values * rms_scale(values) * gain_ref[...]).astype(LOW)
         h_held[g] = hidden
         projected = jnp.dot(hidden, w_ref[...], preferred_element_type=FULL)
         rows[g] = projected
@@ -1150,11 +1146,10 @@
             half = projected[:, part * width : (part + 1) * width]
             total = jnp.sum(half * half, axis=-1, keepdims=True)
             sums[...] += jnp.where(lanes == part * size + g, total, 0.0)
-        pl.when(g >= size // 2)(lambda: line.turn(g - size // 2))
-        pl.when(g == size // 2)(lambda: sheets.forward(1))
 
     squares[...] = sums[...].T[: 2 * size]
     small.begin()
+    sheets.forward(1)
     small.arrive()
     total = sum(got[i] for i in range(size))
     sums[:, : 2 * size] = lax.rsqrt(total / model_dim + NORM_EPS).T
@@ -1179,16 +1174,15 @@
             heads, g, rows, scales, gains_ref, turn_ref, column_ref[g], row_ref[g], kept_ref, out_ref
         )
         pl.when(g != place)(lambda: sending(g, place).start())
-        pl.when(i >= size // 2)(lambda: line.turn(i))
-        pl.when(i == size // 2)(lambda: sheets.forward(2))
+        pl.when(lax.rem(i, 2) == 1)(lambda: line.turn(lax.div(i, 2)))
 
     staying.start()
 
-    @pl.loop(size, 2 * size)
+    @pl.loop(size // 2, 2 * size)
     def _(i):
+        for step in range(2, size // 2):
+            pl.when(i == (step - 1) * (size // 2))(lambda: sheets.forward(step))
         line.turn(i)
-        for step in range(3, size // 2):
-            pl.when(i == size)(lambda: sheets.forward(step))
         after = i - size - size // 2
         pl.when((after >= 0) & (after < size // 2))(lambda: sheets.cross(after))
 
@@ -1224,7 +1218,6 @@
             jax.ShapeDtypeStruct(x_all.shape, LOW),
             jax.ShapeDtypeStruct(seqs + (columns,), FULL),
             jax.ShapeDtypeStruct(seqs + (2,), FULL),
-            jax.ShapeDtypeStruct(seqs + (1,), FULL),
             jax.ShapeDtypeStruct(seqs + (columns,), LOW),
             jax.ShapeDtypeStruct(seqs + (width,), LOW),
             jax.ShapeDtypeStruct((tokens, model_dim), LOW),
@@ -1232,7 +1225,7 @@
             jax.ShapeDtypeStruct((size,) + dy.shape, LOW),
         ],
         in_specs=[ANY] + [VMEM] * 6 + [ANY] * 2,
-        out_specs=[ANY] * 2 + [VMEM] * 4 + [ANY] * 3,
+        out_specs=[ANY] * 2 + [VMEM] * 3 + [ANY] * 3,
         scratch_shapes=[
             pltpu.VMEM(x_all.shape, LOW),
             pltpu.VMEM(x_all.shape, LOW),
@@ -1432,7 +1425,7 @@
     turns = rotary_tables(row_count, head_size)
     column, row = segments_all[:, :, None], segments_all[:, None, :]
     arrays = [x_all, qkv_here, gain_attn[None], both_gains, turns, column, row, w_out, out_cotangent]
-    hidden_one, projected, scales, roots, kept, attended, own_attended, out_full, dy_all = attention(
+    hidden_one, projected, scales, kept, attended, own_attended, out_full, dy_all = attention(
         line_count, dp_count, heads_here, arrays, 4
     )
     out_full = out_full.reshape(model_dim, model_dim)
@@ -1513,7 +1506,7 @@
     grad_gain_attn = lax.dynamic_slice_in_dim(gain_sum[0], here, shard)
     output = (residual + mixture.astype(FULL)).astype(LOW)
     sum_qkv = sum_qkv.transpose(1, 0, 2)
-    first_sums, output = lax.optimization_barrier((grad_sums[0], output))
+    first_sums, mixture = lax.optimization_barrier((grad_sums[0], mixture))
     wide = widen(0, local_count, gate_rows, first_sums)
     sum_gate_up, sum_down = widen(1, local_count, gate_rows, grad_sums[1], wide)
     shared = shared[:, :shard]

time: 732 us -> 740 us (1.011); the launches traced: 731 us -> 729 us
  transfers between devices with their start and end apart: 2 -> 2, of which waited for: 0 -> 0; matrix products, arithmetic and copies ran while one was open for 2% -> 2% of each run, Pallas kernels for 53% -> 54%
where the time goes in v8:
time: 740 us; the launch traced here: 729 us
  Pallas kernels  668 us (90%)
  local copies, waits for them, and re-layouts  21.9 us (3%)
  between operations  15.1 us (2%)
  other arithmetic  14.3 us (2%)
  matrix products  10.1 us (1%)
    pallas_call x1, Pallas kernels, closing(): pl.pallas_call(functools.partial(closing_kernel, size, dp_count, len(tabl...  168 us
    pallas_call x2, Pallas kernels, expert(): pl.pallas_call(functools.partial(expert_kernel, first, count, tiles), out...  101 us
    pallas_call x1, Pallas kernels, attention(): pl.pallas_call(functools.partial(attention_kernel, size, dp_count, heads)...  93.1 us
    pallas_call x1, Pallas kernels, collect_reduce(): pl.pallas_call(functools.partial(collect_reduce_kernel, levels, cuts, len...  81.8 us
    pallas_call x1, Pallas kernels, attend_back(): pl.pallas_call(functools.partial(attend_back_kernel, size // 2, 4, heads)...  73.6 us
    pallas_call x1, Pallas kernels, call(): pl.pallas_call(kernel, out_shape=outs, in_specs=[ANY] * len(arrays), out_...  72.8 us
    pallas_call x1, Pallas kernels, gather_place(): pl.pallas_call(functools.partial(gather_place_kernel, size // 2, cuts), o...  62.2 us
    unnamed x75, local copies, waits for them, and re-layouts  15.2 us
  transfers between devices with their start and end apart: 2, of which 0 were waited for; matrix products, arithmetic and copies ran while one was open for 2% of the time, Pallas kernels for 54%

profile of v8, /device:TPU:16, one launch (start us, length us, event | category | flops | bytes accessed | tf_op | source)
XLA Modules:
  0.0 729.3 jit_solution(11986116186435621358)
XLA Ops:
  7.3 1.4 fusion.8
  11.7 1.1 copy-done
  12.9 1.1 copy-done.22
  14.0 72.8 %opening.1 = (bf16[8,192,2048]{2,1,0:T(8,128)(2,1)}, s32[8,16,192]{2,1,0:T(8,128)S(1)}, bf16[4,8,64,768]{3,2,1,0:T(8,128)(2,1)S(1)}, bf16[4,8,64,24]{3,2,1,0:T(8,128)(2,1)S(1)}, bf16[4,8,4,64]{3,2,1,0:T(4,128)(2,1)S(1)}) custom-call(bf16[192,2048]{1,0:T(8,128)(2,1)S(1)} %copy-done, s32[16,192]{1,0:T(8,128)S(1)} %add_add_fusion.refs_1_, ...), custom_call_target="tpu_custom_call" | custom-call | bytes 200000000 | tf_op jit(solution)/shard_map/opening/pallas_call | solution.py:181
  86.8 1.6 copy-done.9
  90.4 93.1 %attention.1 = (bf16[8,192,2048]{2,1,0:T(8,128)(2,1)}, f32[8,192,768]{2,1,0:T(8,128)}, f32[8,192,2]{2,1,0:T(8,128)S(1)}, bf16[8,192,768]{2,1,0:T(8,128)(2,1)}, b...) custom-call(bf16[8,192,2048]{2,1,0:T(8,128)(2,1)} %get-tuple-element, ...), custom_call_target="tpu_custom_call" | custom-call | flops 4831838208 | bytes 100000000 | tf_op jit(solution)/shard_map/attention/pallas_call | solution.py:1215
  183.6 5.9 multiply_reduce_fusion.3
  189.8 1.2 copy-done.14
  191.6 62.2 %gather_place.1 = (bf16[3,576,2048]{2,1,0:T(8,128)(2,1)}, bf16[3,576,2048]{2,1,0:T(8,128)(2,1)}, f32[8,24,192]{2,1,0:T(8,128)S(1)}) custom-call(bf16[192,2048]{1,0:T(8,128)(2,1)S(1)} %multiply_convert_fusion.refs_0_, f32[24,192]{1,0:T(8,128)S(1)} %fusion.22.refs_1_, bf16[8,216,192]{2,1,0:T(8,128)(2,1)S(1)} %fusion.3.refs_2_.refs_7_, ...), custom_call_target="tpu_custom_call" | custom-call | flops 2717908992 | bytes 150000000 | tf_op jit(solution)/shard_map/gather_place/pallas_call | solution.py:634
  254.4 1.2 reshape.140.scale_ref
  255.6 35.3 %expert.2 = (bf16[4,768,2048]{2,1,0:T(8,128)(2,1)}, bf16[1,576,2048]{2,1,0:T(8,128)(2,1)}, bf16[1,576,2048]{2,1,0:T(8,128)(2,1)}, f32[1,576,1]{2,1,0:T(8,128)}) custom-call(bf16[3,576,2048]{2,1,0:T(8,128)(2,1)} %get-tuple-element.60.x_ref, bf16[3,576,2048]{2,1,0:T(8,128)(2,1)} %get-tuple-element.61.dy_ref, f32[3,576,1]{2,1,0:T(8,128)} %reshape.140.scale_ref, ...), custom_call_target="tpu_custom_call" | custom-call | flops 21743271936 | bytes 25165824 | tf_op jit(solution)/shard_map/expert/pallas_call | solution.py:968
  291.2 65.8 %expert.3 = (bf16[4,1536,2048]{2,1,0:T(8,128)(2,1)}, bf16[2,576,2048]{2,1,0:T(8,128)(2,1)}, bf16[2,576,2048]{2,1,0:T(8,128)(2,1)}, f32[2,576,1]{2,1,0:T(8,128)}) custom-call(bf16[3,576,2048]{2,1,0:T(8,128)(2,1)} %get-tuple-element.60.x_ref, bf16[3,576,2048]{2,1,0:T(8,128)(2,1)} %get-tuple-element.61.dy_ref, f32[3,576,1]{2,1,0:T(8,128)} %reshape.140.scale_ref, ...), custom_call_target="tpu_custom_call" | custom-call | flops 43486543872 | bytes 50331648 | tf_op jit(solution)/shard_map/expert/pallas_call | solution.py:968
  358.3 1.7 copy-done.12
  361.0 81.8 %collect_reduce.1 = (bf16[192,2048]{1,0:T(8,128)(2,1)S(1)}, f32[8,3,192]{2,1,0:T(4,128)S(1)}) custom-call(bf16[8,192,72]{2,1,0:T(8,128)(2,1)S(1)} %get-tuple-element.112.refs_0_, bf16[8,192,72]{2,1,0:T(8,128)(2,1)S(1)} %get-tuple-element.113.refs_1_, bf16[8,192,72]{2,1,0:T(8,128)(2,1)S(1)} %fusion.12.refs_2_, bf16[1,8,72,2048]{3,2,1,0:T(8,128)(2,1)S(1)} %bitcast.83, ...), custom_call_target="tpu_custom_call" | custom-call | bytes 150000000 | tf_op jit(solution)/shard_map/collect_reduce/pallas_call | solution.py:708
  444.9 3.4 multiply_reduce_fusion.1
  449.8 2.9 fusion.28.grad_ref
  452.7 73.6 %attend_back.1 = (bf16[8,192,768]{2,1,0:T(8,128)(2,1)}, f32[2,256]{1,0:T(2,128)S(1)}, bf16[4,256,512]{2,1,0:T(8,128)(2,1)S(1)}) custom-call(bf16[192,2048]{1,0:T(8,128)(2,1)S(1)} %fusion.28.grad_ref, bf16[2048,2048]{1,0:T(8,128)(2,1)} %bitcast.91, bf16[8,192,768]{2,1,0:T(8,128)(2,1)} %get-tuple-element.71.refs_1_, bf16[8,192,256]{2,1,0:T(8,128)(2,1)S(1)} %copy-done.19, ...), custom_call_target="tpu_custom_call" | custom-call | bytes 150000000 | tf_op jit(solution)/shard_map/attend_back/pallas_call | solution.py:1349
  527.8 168.0 %closing.1 = (bf16[192,2048]{1,0:T(8,128)(2,1)}, bf16[192,2048]{1,0:T(8,128)(2,1)}, f32[3,512,256]{2,1,0:T(8,128)}, f32[256,512]{1,0:T(8,128)}, f32[2,256]{1,0:T...) custom-call(bf16[8,192,72]{2,1,0:T(8,128)(2,1)} %copy-done.5, bf16[8,192,72]{2,1,0:T(8,128)(2,1)} %copy-done.6, ...), custom_call_target="tpu_custom_call" | custom-call | bytes 200000000 | tf_op jit(solution)/shard_map/closing/pallas_call | solution.py:833
  695.9 1.4 fusion.27
  697.3 1.6 fusion.4
  700.5 4.2 fusion.7
  704.7 5.6 widen.2
  710.3 9.5 %widen.3 = (f32[3,512,2048]{2,1,0:T(8,128)}, f32[3,256,2048]{2,1,0:T(8,128)}) custom-call(bf16[2,768,2048]{2,1,0:T(8,128)(2,1)} %bitcast.92, f32[3,512,2048]{2,1,0:T(8,128)} %get-tuple-element.89.refs_1_, f32[3,256,2048]{2,1,0:T(8,128)} %get-tuple-element.90.refs_2_), custom_call_target="tpu_custom_call", output_to_operand_aliasing={{0}: (1, {}), {1}: (2, {})} | custom-call | flops 3145728 | bytes 18874368 | tf_op jit(solution)/shard_map/widen/pallas_call | solution.py:1044
  719.9 1.1 copy.70
  (123 shorter events, 16.7 us)
Async XLA Ops:
  7.2 697.6 %reduce-scatter.5.cloned.1.call-start = ((), (), s32[]{:S(2)}) async-start(), calls=%async_computation.3 | async-start | bytes 15728640 | tf_op jit(solution)/shard_map/reduce_scatter | solution.py:1470
  14.0 76.4 %copy-start.10 = (bf16[192,2048]{1,0:T(8,128)(2,1)S(1)}, bf16[192,2048]{1,0:T(8,128)(2,1)}, u32[]{:S(2)}) copy-start(bf16[192,2048]{1,0:T(8,128)(2,1)} %refs_8_.1) | copy-start | bytes 2359300
  14.0 76.4 %copy-start.25 = (f32[2,192,128]{2,1,0:T(8,128)S(1)}, f32[2,192,128]{2,1,0:T(8,128)}, u32[]{:S(2)}) copy-start(f32[2,192,128]{2,1,0:T(8,128)} %constant.45.clone.refs_4_.refs_6_) | copy-start | bytes 589828
  14.0 76.4 %copy-start.29 = (bf16[64,2048]{1,0:T(8,128)(2,1)S(1)}, bf16[64,2048]{1,0:T(8,128)(2,1)}, u32[]{:S(2)}) copy-start(bf16[64,2048]{1,0:T(8,128)(2,1)} %refs_7_.1) | copy-start | bytes 786436
  90.0 93.5 %copy-start.27 = (f32[1,2048]{1,0:T(1,128)}, f32[1,2048]{1,0:T(1,128)S(1)}, u32[]{:S(2)}) copy-start(f32[1,2048]{1,0:T(1,128)S(1)} %slice.47.refs_2_.refs_8_) | copy-start | bytes 24580
  90.3 93.2 %copy-start.7 = (s32[8,192,1]{2,1,0:T(8,128)}, s32[8,192,1]{2,1,0:T(8,128)S(1)}, u32[]{:S(2)}) copy-start(s32[8,192,1]{2,1,0:T(8,128)S(1)} %copy.55.refs_5_.refs_7_) | copy-start | bytes 18436
  90.4 93.2 %copy-start.1 = (bf16[192,2048]{1,0:T(8,128)(2,1)S(1)}, bf16[192,2048]{1,0:T(8,128)(2,1)}, u32[]{:S(2)}) copy-start(bf16[192,2048]{1,0:T(8,128)(2,1)} %refs_0_.1) | copy-start | bytes 2359300
  183.5 6.0 copy-start.16
  183.5 6.0 copy-start.18
  189.5 1.8 copy-start.30
  191.6 62.2 %copy-start.2 = (bf16[8,216,192]{2,1,0:T(8,128)(2,1)}, bf16[8,216,192]{2,1,0:T(8,128)(2,1)S(1)}, u32[]{:S(2)}) copy-start(bf16[8,216,192]{2,1,0:T(8,128)(2,1)S(1)} %fusion.3.refs_2_.refs_7_) | copy-start | bytes 1990660
  290.9 419.4 %reduce-scatter.3.cloned.1.call-start = ((), (), s32[]{:S(2)}) async-start(), calls=%async_computation.2 | async-start | bytes 31457280 | tf_op jit(solution)/shard_map/reduce_scatter | solution.py:1470
  357.4 85.5 %copy-start.4 = (bf16[8,192,72]{2,1,0:T(8,128)(2,1)}, bf16[8,192,72]{2,1,0:T(8,128)(2,1)S(1)}, u32[]{:S(2)}) copy-start(bf16[8,192,72]{2,1,0:T(8,128)(2,1)S(1)} %fusion.12.refs_2_) | copy-start | bytes 663556
  358.0 84.9 %copy-start.5 = (bf16[8,192,72]{2,1,0:T(8,128)(2,1)}, bf16[8,192,72]{2,1,0:T(8,128)(2,1)S(1)}, u32[]{:S(2)}) copy-start(bf16[8,192,72]{2,1,0:T(8,128)(2,1)S(1)} %get-tuple-element.112.refs_0_) | copy-start | bytes 663556
  358.0 84.9 %copy-start.6 = (bf16[8,192,72]{2,1,0:T(8,128)(2,1)}, bf16[8,192,72]{2,1,0:T(8,128)(2,1)S(1)}, u32[]{:S(2)}) copy-start(bf16[8,192,72]{2,1,0:T(8,128)(2,1)S(1)} %get-tuple-element.113.refs_1_) | copy-start | bytes 663556
  358.3 1.7 copy-start.12
  449.7 2.9 copy-start.8
  449.7 3.0 copy-start.17
  449.7 3.0 copy-start.19
  449.8 3.0 copy-start.26
  695.8 3.0 copy-start.35
  695.8 3.6 copy-start.34
  695.9 4.7 copy-start.31
  710.3 9.5 %copy-start.32 = (f32[3,512,256]{2,1,0:T(8,128)S(1)}, f32[3,512,256]{2,1,0:T(8,128)}, u32[]{:S(2)}) copy-start(f32[3,512,256]{2,1,0:T(8,128)} %get-tuple-element.81) | copy-start | bytes 4718596
  (14 other events, 15.9 us)
Sparse Core Ops, SparseCore 0:
  291.1 125.1 reduce-scatter.4
  419.4 276.7 reduce-scatter.2

commit v9 on v8

--- a/solution.py
+++ b/solution.py
@@ -14,6 +14,7 @@
 MESH = pl.DeviceIdType.MESH
 ANY = pl.BlockSpec(memory_space=pl.ANY)
 LOW = jnp.bfloat16
+GATHER_CUTS, REDUCE_CUTS = 4, 3
 FULL = jnp.float32
 
 
@@ -132,9 +133,9 @@
 
     def turn(self, turn, landed=None):
         levels, cuts = self.levels, self.cuts
-        step, k = lax.div(turn, cuts) + 1, lax.rem(turn, cuts)
-
-        @pl.when(step < levels)
+        step, k = lax.div(turn, 4) + 1, lax.rem(turn, 4)
+
+        @pl.when((step < levels) & (k < cuts))
         def _():
             self.forward(step, (0, k))
 
@@ -147,7 +148,7 @@
         crossed = jnp.where(group == 0, k, crossed)
         far = jnp.where(group == 0, self.level, self.level + sign * group)
 
-        @pl.when((far >= 0) & (far < levels) & (k < 4) & ((group > 0) | (k < 2)))
+        @pl.when((far >= 0) & (far < levels) & ((group > 0) | (k < 2)))
         def _():
             block = 2 * far + self.side + crossed * (1 - 2 * self.side)
 
@@ -159,7 +160,7 @@
                 landed(block)
 
     def main(self, landed=None):
-        @pl.loop(0, self.levels * self.cuts)
+        @pl.loop(0, 4 * self.levels)
         def _(turn):
             self.turn(turn, landed)
 
@@ -287,15 +288,33 @@
         pl.when(ahead)(move(far, k).start)
 
     def main(self, beside=None):
-        @pl.loop(0, (self.levels - 1) * self.cuts)
+        levels, cuts = self.levels, self.cuts
+        lower = self.level < levels // 2
+
+        def rise(far, k):
+            self.toward(far, k, self.level < far, self.has_down, self.up, self.rising, 1)
+
+        def fall(far, k):
+            self.toward(far, k, self.level > far, self.has_up, self.down, self.falling, 0)
+
+        @pl.loop(0, 2 * cuts)
         def _(turn):
-            step, k = lax.div(turn, self.cuts), lax.rem(turn, self.cuts)
-            high, low = self.levels - 1 - step, step
+            near, k = turn < cuts, lax.rem(turn, cuts)
             if beside:
                 beside(turn)
-            self.toward(high, k, self.level < high, self.has_down, self.up, self.rising, 1)
-            self.toward(low, k, self.level > low, self.has_up, self.down, self.falling, 0)
-
+            upward = (near & lower) | jnp.logical_not(near | lower)
+            pl.when(upward)(lambda: rise(levels - 1, k))
+            pl.when(jnp.logical_not(upward))(lambda: fall(0, k))
+
+        @pl.loop(2 * cuts, levels * cuts)
+        def _(turn):
+            step, k = lax.div(turn, cuts) - 1, lax.rem(turn, cuts)
+            if beside:
+                beside(turn)
+            rise(levels - 1 - step, k)
+            fall(step, k)
+
+    def settle(self):
         @pl.loop(0, self.cuts)
         def _(k):
             self.store(self.level, k, self.pair(self.level, k))
@@ -626,7 +645,7 @@
 
 
 def gather_place(size, rows, gates, table, dy, local_count, number):
-    cuts = 4
+    cuts = GATHER_CUTS
     tokens, width = rows.shape
     capacity = table.shape[1] // local_count
     placed = jax.ShapeDtypeStruct((local_count, size * capacity, width), rows.dtype)
@@ -650,6 +669,13 @@
     )(rows, gates, table, dy)
 
 
+def several(index, turns, count, work):
+    share = -(-count // turns)
+    for i in range(share):
+        item = share * index + i
+        pl.when((index >= 0) & (item < count))(lambda item=item: work(item))
+
+
 def split_at(arrays, j, block):
     for array in arrays:
         if j < array.shape[0]:
@@ -691,17 +717,19 @@
 
     def beside(turn):
         pl.when(turn + 4 < 2 * levels)(lambda: line.prepare(turn + 4, make))
-        pl.when(turn >= levels)(lambda: gate_block(turn - levels))
-        pl.when(turn == 3 * levels - 1)(small.begin)
+        turns = levels * cuts - levels
+        several(turn - levels, turns, 2 * levels, gate_block)
+        pl.when(turn == levels * cuts - 1)(small.begin)
 
     line.main(beside)
+    line.settle()
     small.arrive()
     line.finish()
     small.finish()
 
 
 def collect_reduce(size, tables, slots, dots, table, number):
-    levels, cuts = size // 2, 4
+    levels, cuts = size // 2, REDUCE_CUTS
     block = (tables[0].shape[1], slots[0].shape[3])
     kind = slots[0].dtype
     gates = (size, len(tables), block[0])
@@ -779,16 +807,18 @@
     def _(turn):
         back.prepare(turn, make_back)
 
+    rest, count = levels * cuts - ahead, sum_cuts[0] * dp_count
+
     def beside(turn):
         later = turn - ahead
         pl.when(turn + ahead < 2 * levels)(lambda: back.prepare(turn + ahead, make_back))
         pl.when(turn < sum_cuts[1])(lambda: sums.send(1, turn))
         pl.when(turn == sum_cuts[1])(lambda: sums.send(2, 0))
         pl.when(later == 0)(gain_first.begin)
-        pl.when((later >= 0) & (later < 2 * levels))(lambda: mixed.prepare(later, make_mixed))
-        pl.when(later >= 0)(lambda: piece(later))
-
-        @pl.when(later == ahead)
+        several(later, rest, 2 * levels, lambda i: mixed.prepare(i, make_mixed))
+        several(later, 2 * rest, count, piece)
+
+        @pl.when(later == rest - 1)
         def _():
             first.arrive()
             for copy in range(dp_count):
@@ -800,7 +830,9 @@
             gain_second.begin()
 
     back.main(beside)
-    mixed.main(lambda turn: pl.when(turn < 2 * levels)(lambda: piece(2 * levels + turn)))
+    mixed.main(lambda turn: several(rest + turn, 2 * rest, count, piece))
+    back.settle()
+    mixed.settle()
     second.arrive()
     shared_out[...] = sum(last[i] for i in range(dp_count))
     gain_second.arrive()
@@ -818,7 +850,7 @@
 
 def closing(size, dp_count, tables, slots, arrays, sums, shared, number):
     proj, _, hidden, gain = arrays
-    levels, cuts = size // 2, 4
+    levels, cuts = size // 2, REDUCE_CUTS
     _, tokens, model_dim = hidden.shape
     columns, high = proj.shape[2], model_dim // dp_count
     block = (tokens, model_dim)
@@ -1107,7 +1139,7 @@
     x_held, h_held, rows, sums, squares, got = refs[17:23]
     x_sem, h_sem, rows_sem, send_sem, recv_sem, stay_sem = refs[23:29]
     square_sems, line_sems, sheet_sems = refs[29:32], refs[32:37], refs[37:]
-    line = LineGather(size // 2, 4, [dy_ref], [dy_out], *line_sems)
+    line = LineGather(size // 2, GATHER_CUTS, [dy_ref], [dy_out], *line_sems)
     sheets = Sheets(size, dp_count, sheet_ref, sheet_out, *sheet_sems)
     small = Exchange("expert", size, (True,), (1,), [squares], [got], *square_sems)
     place, model_dim = sheets.place, x_ref.shape[2]
@@ -1241,7 +1273,7 @@
             sems((1,)),
         ]
         + Exchange.scratch(size, (1,))
-        + LineGather.scratch(size, 4, 1)
+        + LineGather.scratch(size, GATHER_CUTS, 1)
         + Sheets.scratch(size, dp_count),
         compiler_params=pltpu.CompilerParams(
             collective_id=number, has_side_effects=True, vmem_limit_bytes=48 << 20
@@ -1347,7 +1379,7 @@
     tokens, model_dim = grad.shape
     small = (2 * size, tokens)
     return pl.pallas_call(
-        functools.partial(attend_back_kernel, size // 2, 4, heads),
+        functools.partial(attend_back_kernel, size // 2, GATHER_CUTS, heads),
         out_shape=[
             jax.ShapeDtypeStruct(rows.shape, LOW),
             jax.ShapeDtypeStruct((2, width), FULL),
@@ -1365,7 +1397,7 @@
             pltpu.VMEM((size,) + small, FULL),
             pltpu.SemaphoreType.DMA((1,)),
         ]
-        + LineGather.scratch(size, 4, 1)
+        + LineGather.scratch(size, GATHER_CUTS, 1)
         + Exchange.scratch(size, (1,)),
         compiler_params=pltpu.CompilerParams(
             collective_id=number, has_side_effects=True, vmem_limit_bytes=48 << 20
@@ -1409,7 +1441,7 @@
         line_count,
         dp_count,
         [layer_input, numbers],
-        4,
+        GATHER_CUTS,
         w_qkv,
         [w_router, jnp.stack([attn_gain, mlp_gain, query_gain, key_gain])],
         1,

time: 740 us -> 721 us (0.974)
  Pallas kernels: 668 us -> 616 us
  waiting for transfers between devices: 0.04 us -> 34.8 us
    pallas_call x1, Pallas kernels: 168 us -> 128 us  [closing(): pl.pallas_call(functools.partial(closing_kernel, size, dp_count, len(tabl...]
    reduce_scatter x2, waiting for transfers between devices: 0.01 us -> 34.7 us  [on_device(): grads = lax.psum_scatter(grads, 'dp', scatter_dimension=0, tiled=True)]
    pallas_call x1, Pallas kernels: 81.8 us -> 70.5 us  [collect_reduce(): pl.pallas_call(functools.partial(collect_reduce_kernel, levels, cuts, len...]
  transfers between devices with their start and end apart: 2 -> 2, of which waited for: 0 -> 1; matrix products, arithmetic and copies ran while one was open for 2% -> 2% of each run, Pallas kernels for 54% -> 48%
where the time goes in v9:
time: 721 us; the launch traced here: 712 us
  Pallas kernels  616 us (85%)
  waiting for transfers between devices  34.8 us (5%)
  local copies, waits for them, and re-layouts  21.9 us (3%)
  between operations  15.1 us (2%)
  other arithmetic  14 us (2%)
  matrix products  10.3 us (1%)
    pallas_call x1, Pallas kernels, closing(): pl.pallas_call(functools.partial(closing_kernel, size, dp_count, len(tabl...  128 us
    pallas_call x2, Pallas kernels, expert(): pl.pallas_call(functools.partial(expert_kernel, first, count, tiles), out...  101 us
    pallas_call x1, Pallas kernels, attention(): pl.pallas_call(functools.partial(attention_kernel, size, dp_count, heads)...  93.1 us
    pallas_call x1, Pallas kernels, attend_back(): pl.pallas_call(functools.partial(attend_back_kernel, size // 2, GATHER_CU...  73.2 us
    pallas_call x1, Pallas kernels, call(): pl.pallas_call(kernel, out_shape=outs, in_specs=[ANY] * len(arrays), out_...  72.8 us
    pallas_call x1, Pallas kernels, collect_reduce(): pl.pallas_call(functools.partial(collect_reduce_kernel, levels, cuts, len...  70.5 us
    pallas_call x1, Pallas kernels, gather_place(): pl.pallas_call(functools.partial(gather_place_kernel, size // 2, cuts), o...  62.2 us
    reduce_scatter x2, waiting for transfers between devices, on_device(): grads = lax.psum_scatter(grads, 'dp', scatter_dimension=0, tiled=True)  34.7 us
  transfers between devices with their start and end apart: 2, of which 1 were waited for; matrix products, arithmetic and copies ran while one was open for 2% of the time, Pallas kernels for 48%

profile of v9, /device:TPU:16, one launch (start us, length us, event | category | flops | bytes accessed | tf_op | source)
XLA Modules:
  0.0 711.9 jit_solution(2215045010872818559)
XLA Ops:
  7.3 1.4 fusion.8
  12.9 1.1 copy-done.22
  14.0 72.8 %opening.1 = (bf16[8,192,2048]{2,1,0:T(8,128)(2,1)}, s32[8,16,192]{2,1,0:T(8,128)S(1)}, bf16[4,8,64,768]{3,2,1,0:T(8,128)(2,1)S(1)}, bf16[4,8,64,24]{3,2,1,0:T(8,128)(2,1)S(1)}, bf16[4,8,4,64]{3,2,1,0:T(4,128)(2,1)S(1)}) custom-call(bf16[192,2048]{1,0:T(8,128)(2,1)S(1)} %copy-done, s32[16,192]{1,0:T(8,128)S(1)} %add_add_fusion.refs_1_, ...), custom_call_target="tpu_custom_call" | custom-call | bytes 200000000 | tf_op jit(solution)/shard_map/opening/pallas_call | solution.py:182
  86.8 1.6 copy-done.9
  90.4 93.1 %attention.1 = (bf16[8,192,2048]{2,1,0:T(8,128)(2,1)}, f32[8,192,768]{2,1,0:T(8,128)}, f32[8,192,2]{2,1,0:T(8,128)S(1)}, bf16[8,192,768]{2,1,0:T(8,128)(2,1)}, b...) custom-call(bf16[8,192,2048]{2,1,0:T(8,128)(2,1)} %get-tuple-element, ...), custom_call_target="tpu_custom_call" | custom-call | flops 4831838208 | bytes 100000000 | tf_op jit(solution)/shard_map/attention/pallas_call | solution.py:1247
  183.6 5.9 multiply_reduce_fusion.3
  189.8 1.2 copy-done.14
  191.6 62.2 %gather_place.1 = (bf16[3,576,2048]{2,1,0:T(8,128)(2,1)}, bf16[3,576,2048]{2,1,0:T(8,128)(2,1)}, f32[8,24,192]{2,1,0:T(8,128)S(1)}) custom-call(bf16[192,2048]{1,0:T(8,128)(2,1)S(1)} %multiply_convert_fusion.refs_0_, f32[24,192]{1,0:T(8,128)S(1)} %fusion.22.refs_1_, bf16[8,216,192]{2,1,0:T(8,128)(2,1)S(1)} %fusion.3.refs_2_.refs_7_, ...), custom_call_target="tpu_custom_call" | custom-call | flops 2717908992 | bytes 150000000 | tf_op jit(solution)/shard_map/gather_place/pallas_call | solution.py:653
  254.4 1.2 reshape.140.scale_ref
  255.6 35.3 %expert.2 = (bf16[4,768,2048]{2,1,0:T(8,128)(2,1)}, bf16[1,576,2048]{2,1,0:T(8,128)(2,1)}, bf16[1,576,2048]{2,1,0:T(8,128)(2,1)}, f32[1,576,1]{2,1,0:T(8,128)}) custom-call(bf16[3,576,2048]{2,1,0:T(8,128)(2,1)} %get-tuple-element.60.x_ref, bf16[3,576,2048]{2,1,0:T(8,128)(2,1)} %get-tuple-element.61.dy_ref, f32[3,576,1]{2,1,0:T(8,128)} %reshape.140.scale_ref, ...), custom_call_target="tpu_custom_call" | custom-call | flops 21743271936 | bytes 25165824 | tf_op jit(solution)/shard_map/expert/pallas_call | solution.py:1000
  291.2 65.8 %expert.3 = (bf16[4,1536,2048]{2,1,0:T(8,128)(2,1)}, bf16[2,576,2048]{2,1,0:T(8,128)(2,1)}, bf16[2,576,2048]{2,1,0:T(8,128)(2,1)}, f32[2,576,1]{2,1,0:T(8,128)}) custom-call(bf16[3,576,2048]{2,1,0:T(8,128)(2,1)} %get-tuple-element.60.x_ref, bf16[3,576,2048]{2,1,0:T(8,128)(2,1)} %get-tuple-element.61.dy_ref, f32[3,576,1]{2,1,0:T(8,128)} %reshape.140.scale_ref, ...), custom_call_target="tpu_custom_call" | custom-call | flops 43486543872 | bytes 50331648 | tf_op jit(solution)/shard_map/expert/pallas_call | solution.py:1000
  358.3 1.7 copy-done.12
  361.0 70.5 %collect_reduce.1 = (bf16[192,2048]{1,0:T(8,128)(2,1)S(1)}, f32[8,3,192]{2,1,0:T(4,128)S(1)}) custom-call(bf16[8,192,72]{2,1,0:T(8,128)(2,1)S(1)} %get-tuple-element.112.refs_0_, bf16[8,192,72]{2,1,0:T(8,128)(2,1)S(1)} %get-tuple-element.113.refs_1_, bf16[8,192,72]{2,1,0:T(8,128)(2,1)S(1)} %fusion.12.refs_2_, bf16[1,8,72,2048]{3,2,1,0:T(8,128)(2,1)S(1)} %bitcast.83, ...), custom_call_target="tpu_custom_call" | custom-call | bytes 150000000 | tf_op jit(solution)/shard_map/collect_reduce/pallas_call | solution.py:736
  433.6 3.6 multiply_reduce_fusion.1
  438.7 2.5 fusion.28.grad_ref
  441.2 73.2 %attend_back.1 = (bf16[8,192,768]{2,1,0:T(8,128)(2,1)}, f32[2,256]{1,0:T(2,128)S(1)}, bf16[4,256,512]{2,1,0:T(8,128)(2,1)S(1)}) custom-call(bf16[192,2048]{1,0:T(8,128)(2,1)S(1)} %fusion.28.grad_ref, bf16[2048,2048]{1,0:T(8,128)(2,1)} %bitcast.91, bf16[8,192,768]{2,1,0:T(8,128)(2,1)} %get-tuple-element.71.refs_1_, bf16[8,192,256]{2,1,0:T(8,128)(2,1)S(1)} %copy-done.19, ...), custom_call_target="tpu_custom_call" | custom-call | bytes 150000000 | tf_op jit(solution)/shard_map/attend_back/pallas_call | solution.py:1381
  516.0 127.5 %closing.1 = (bf16[192,2048]{1,0:T(8,128)(2,1)}, bf16[192,2048]{1,0:T(8,128)(2,1)}, f32[3,512,256]{2,1,0:T(8,128)}, f32[256,512]{1,0:T(8,128)}, f32[2,256]{1,0:T...) custom-call(bf16[8,192,72]{2,1,0:T(8,128)(2,1)} %copy-done.5, bf16[8,192,72]{2,1,0:T(8,128)(2,1)} %copy-done.6, ...), custom_call_target="tpu_custom_call" | custom-call | bytes 200000000 | tf_op jit(solution)/shard_map/closing/pallas_call | solution.py:865
  643.6 1.4 fusion.27
  644.9 1.6 fusion.4
  648.2 4.2 fusion.7
  652.4 5.7 widen.2
  658.1 34.7 %reduce-scatter.3.cloned.1.call-done = bf16[1536,2048]{1,0:T(8,128)(2,1)} async-done(((bf16[6144,2048]{1,0:T(8,128)(2,1)}), bf16[1536,2048]{1,0:T(8,128)(2,1)}) %reduce-scatter.3.cloned.1.call-update) | async-done | bytes 6291472 | tf_op jit(solution)/shard_map/reduce_scatter | solution.py:1502
  692.8 9.5 %widen.3 = (f32[3,512,2048]{2,1,0:T(8,128)}, f32[3,256,2048]{2,1,0:T(8,128)}) custom-call(bf16[2,768,2048]{2,1,0:T(8,128)(2,1)} %bitcast.92, f32[3,512,2048]{2,1,0:T(8,128)} %get-tuple-element.89.refs_1_, f32[3,256,2048]{2,1,0:T(8,128)} %get-tuple-element.90.refs_2_), custom_call_target="tpu_custom_call", output_to_operand_aliasing={{0}: (1, {}), {1}: (2, {})} | custom-call | flops 3145728 | bytes 18874368 | tf_op jit(solution)/shard_map/widen/pallas_call | solution.py:1076
  702.4 1.1 copy.70
  (123 shorter events, 17.8 us)
Async XLA Ops:
  7.2 645.2 %reduce-scatter.5.cloned.1.call-start = ((), (), s32[]{:S(2)}) async-start(), calls=%async_computation.3 | async-start | bytes 15728640 | tf_op jit(solution)/shard_map/reduce_scatter | solution.py:1502
  14.0 76.4 %copy-start.10 = (bf16[192,2048]{1,0:T(8,128)(2,1)S(1)}, bf16[192,2048]{1,0:T(8,128)(2,1)}, u32[]{:S(2)}) copy-start(bf16[192,2048]{1,0:T(8,128)(2,1)} %refs_8_.1) | copy-start | bytes 2359300
  14.0 76.4 %copy-start.25 = (f32[2,192,128]{2,1,0:T(8,128)S(1)}, f32[2,192,128]{2,1,0:T(8,128)}, u32[]{:S(2)}) copy-start(f32[2,192,128]{2,1,0:T(8,128)} %constant.45.clone.refs_4_.refs_6_) | copy-start | bytes 589828
  14.0 76.4 %copy-start.29 = (bf16[64,2048]{1,0:T(8,128)(2,1)S(1)}, bf16[64,2048]{1,0:T(8,128)(2,1)}, u32[]{:S(2)}) copy-start(bf16[64,2048]{1,0:T(8,128)(2,1)} %refs_7_.1) | copy-start | bytes 786436
  90.0 93.5 %copy-start.27 = (f32[1,2048]{1,0:T(1,128)}, f32[1,2048]{1,0:T(1,128)S(1)}, u32[]{:S(2)}) copy-start(f32[1,2048]{1,0:T(1,128)S(1)} %slice.47.refs_2_.refs_8_) | copy-start | bytes 24580
  90.3 93.2 %copy-start.7 = (s32[8,192,1]{2,1,0:T(8,128)}, s32[8,192,1]{2,1,0:T(8,128)S(1)}, u32[]{:S(2)}) copy-start(s32[8,192,1]{2,1,0:T(8,128)S(1)} %copy.55.refs_5_.refs_7_) | copy-start | bytes 18436
  90.4 93.2 %copy-start.1 = (bf16[192,2048]{1,0:T(8,128)(2,1)S(1)}, bf16[192,2048]{1,0:T(8,128)(2,1)}, u32[]{:S(2)}) copy-start(bf16[192,2048]{1,0:T(8,128)(2,1)} %refs_0_.1) | copy-start | bytes 2359300
  183.5 6.0 copy-start.16
  183.5 6.0 copy-start.18
  189.5 1.8 copy-start.30
  191.6 62.2 %copy-start.2 = (bf16[8,216,192]{2,1,0:T(8,128)(2,1)}, bf16[8,216,192]{2,1,0:T(8,128)(2,1)S(1)}, u32[]{:S(2)}) copy-start(bf16[8,216,192]{2,1,0:T(8,128)(2,1)S(1)} %fusion.3.refs_2_.refs_7_) | copy-start | bytes 1990660
  291.0 401.9 %reduce-scatter.3.cloned.1.call-start = ((), (), s32[]{:S(2)}) async-start(), calls=%async_computation.2 | async-start | bytes 31457280 | tf_op jit(solution)/shard_map/reduce_scatter | solution.py:1502
  357.4 74.2 %copy-start.4 = (bf16[8,192,72]{2,1,0:T(8,128)(2,1)}, bf16[8,192,72]{2,1,0:T(8,128)(2,1)S(1)}, u32[]{:S(2)}) copy-start(bf16[8,192,72]{2,1,0:T(8,128)(2,1)S(1)} %fusion.12.refs_2_) | copy-start | bytes 663556
  358.0 73.6 %copy-start.5 = (bf16[8,192,72]{2,1,0:T(8,128)(2,1)}, bf16[8,192,72]{2,1,0:T(8,128)(2,1)S(1)}, u32[]{:S(2)}) copy-start(bf16[8,192,72]{2,1,0:T(8,128)(2,1)S(1)} %get-tuple-element.112.refs_0_) | copy-start | bytes 663556
  358.0 73.6 %copy-start.6 = (bf16[8,192,72]{2,1,0:T(8,128)(2,1)}, bf16[8,192,72]{2,1,0:T(8,128)(2,1)S(1)}, u32[]{:S(2)}) copy-start(bf16[8,192,72]{2,1,0:T(8,128)(2,1)S(1)} %get-tuple-element.113.refs_1_) | copy-start | bytes 663556
  358.3 1.7 copy-start.12
  438.6 2.6 copy-start.8
  438.6 2.6 copy-start.17
  438.6 2.6 copy-start.19
  438.6 2.6 copy-start.26
  643.5 3.0 copy-start.35
  643.5 3.6 copy-start.34
  643.5 4.7 copy-start.31
  692.8 9.5 %copy-start.32 = (f32[3,512,256]{2,1,0:T(8,128)S(1)}, f32[3,512,256]{2,1,0:T(8,128)}, u32[]{:S(2)}) copy-start(f32[3,512,256]{2,1,0:T(8,128)} %get-tuple-element.81) | copy-start | bytes 4718596
  (14 other events, 15.9 us)
Sparse Core Ops, SparseCore 0:
  291.1 125.1 reduce-scatter.4
  419.4 273.4 reduce-scatter.2

commit v10 on v9

--- a/solution.py
+++ b/solution.py
@@ -750,6 +750,67 @@
     )(*tables, *slots, *dots, table)
 
 
+class SquareSum:
+    def __init__(self, cuts, parts, near, far, send_sem, recv_sem, last_send, last_recv):
+        self.cuts, self.parts, self.near, self.far = cuts, parts, near, far
+        self.send_sem, self.recv_sem, self.last_send, self.last_recv = send_sem, recv_sem, last_send, last_recv
+        self.mine = lax.axis_index("dp")
+        slow, fast = lax.div(self.mine, 2), lax.rem(self.mine, 2)
+        self.along = 2 * slow + 1 - fast, 2 * (1 - slow) + fast
+        self.across = 2 * (1 - slow) + 1 - fast
+        self.step = parts.shape[1] // cuts
+
+    @staticmethod
+    def scratch(cuts, shape, dtype):
+        sems = pltpu.SemaphoreType.DMA
+        buffers = [pltpu.VMEM((2,) + shape[1:], dtype), pltpu.VMEM(shape[1:], dtype)]
+        return buffers + [sems((cuts, 2)), sems((cuts, 2)), sems((cuts,)), sems((cuts,))]
+
+    def rows(self, k):
+        return pl.ds(pl.multiple_of(k * self.step, self.step), self.step)
+
+    def peer(self, k, later):
+        half = lax.div(k, self.cuts // 2)
+        return jnp.where(half == later, self.along[0], self.along[1])
+
+    def first(self, k, kind):
+        peer, rows = self.peer(k, 0), self.rows(k)
+        source = self.parts.at[self.across if kind else peer, rows]
+        sems = self.send_sem.at[k, kind], self.recv_sem.at[k, kind]
+        return remote(source, self.near.at[kind, rows], *sems, {"dp": peer})
+
+    def second(self, k):
+        peer, rows = self.peer(k, 1), self.rows(k)
+        sems = self.last_send.at[k], self.last_recv.at[k]
+        return remote(self.parts.at[peer, rows], self.far.at[rows], *sems, {"dp": peer})
+
+    def begin(self, k):
+        self.first(k, 0).start()
+        self.first(k, 1).start()
+
+    def turn(self, k):
+        self.first(k, 1).wait_recv()
+        peer, rows = self.peer(k, 1), self.rows(k)
+        total = self.parts[peer, rows].astype(FULL) + self.near[1, rows].astype(FULL)
+        self.parts[peer, rows] = total.astype(self.parts.dtype)
+        self.second(k).start()
+
+    def arrive(self):
+        for k in range(self.cuts):
+            self.first(k, 0).wait_recv()
+            self.second(k).wait_recv()
+
+    def total(self, columns):
+        own = self.parts[self.mine, :, columns].astype(FULL)
+        return own + self.near[0, :, columns].astype(FULL) + self.far[:, columns].astype(FULL)
+
+    def finish(self):
+        for k in range(self.cuts):
+            self.first(k, 0).wait_send()
+            self.first(k, 1).wait_send()
+            self.second(k).wait_send()
+
+
 def closing_kernel(size, dp_count, local_count, cuts, sum_cuts, *refs):
     refs, levels = list(refs), size // 2
 
@@ -763,10 +824,21 @@
     back_out, mixed_out, qkv_out, w_out, gains_out, gain_out, shared_out = take(7)
     back = LineReduce(levels, cuts, *take(1), back_out, *take(12))
     mixed = LineReduce(levels, cuts, *take(1), mixed_out, *take(12))
-    qkv_parts, qkv_got, out_got, gains_got = take(4)
+    square = dp_count == 4
+    if square:
+        qkv_parts, gains_got = take(2)
+        qkv_sum = SquareSum(sum_cuts[0], qkv_parts, *take(6))
+        (out_own,) = take(1)
+        out_sum = SquareSum(sum_cuts[1], out_own, *take(6))
+        out_own[...] = out_parts[...]
+    else:
+        qkv_parts, gains_got, qkv_got, out_got = take(4)
     got, half, last, gain_sum, gain_got, gain_half, gain_last = take(7)
-    parts, lands = [qkv_parts, out_parts, gain_pair], [qkv_got, out_got, gains_got]
-    sums = Exchange("dp", dp_count, (False, False, True), sum_cuts, parts, lands, *take(3))
+    parts, lands, spread, some = [gain_pair], [gains_got], (True,), (1,)
+    if not square:
+        parts, lands = parts + [qkv_parts, out_parts], lands + [qkv_got, out_got]
+        spread, some = (True, False, False), (1,) + sum_cuts
+    sums = Exchange("dp", dp_count, spread, some, parts, lands, *take(3))
     first = Exchange("expert", size, (False,), (1,), [shared_ref], [got], *take(3))
     second = Exchange("dp", dp_count, (False,), (1,), [half], [last], *take(3))
     gain_first = Exchange("expert", size, (True,), (1,), [gain_sum], [gain_got], *take(3))
@@ -775,8 +847,9 @@
     greet("dp", [(peer, None) for peer in sums.peers])
     pl.semaphore_wait(pltpu.get_barrier_semaphore(), size + dp_count - 2)
     first.begin()
-    sums.staying(1).start()
-    sums.staying(2).start()
+    sums.staying(0).start()
+    if not square:
+        sums.staying(2).start()
     gain_sum[...] = jnp.zeros_like(gain_sum)
     groups, tokens, model_dim = h_ref.shape
     tall, high = half.shape[1], model_dim // dp_count
@@ -797,8 +870,11 @@
         grads = proj_ref[...].reshape(groups * tokens, proj_ref.shape[2])
         products = contract_rows(rows, grads).astype(LOW)
         qkv_parts[copy, pl.ds(pl.multiple_of(k * 128, 128), 128)] = products
-        pl.when(copy == dp_count - 1)(lambda: sums.send(0, k))
-        pl.when(turn == sum_cuts[0] * dp_count - 1)(lambda: sums.staying(0).start())
+        if square:
+            pl.when(copy == dp_count - 1)(lambda: qkv_sum.begin(k))
+        else:
+            pl.when(copy == dp_count - 1)(lambda: sums.send(1, k))
+            pl.when(turn == count - 1)(lambda: sums.staying(1).start())
 
     make_mixed = functools.partial(collect_block, tables, slots)
     ahead = levels
@@ -812,8 +888,9 @@
     def beside(turn):
         later = turn - ahead
         pl.when(turn + ahead < 2 * levels)(lambda: back.prepare(turn + ahead, make_back))
-        pl.when(turn < sum_cuts[1])(lambda: sums.send(1, turn))
-        pl.when(turn == sum_cuts[1])(lambda: sums.send(2, 0))
+        send = out_sum.begin if square else functools.partial(sums.send, 2)
+        pl.when(turn < sum_cuts[1])(lambda: send(turn))
+        pl.when(turn == sum_cuts[1])(lambda: sums.send(0, 0))
         pl.when(later == 0)(gain_first.begin)
         several(later, rest, 2 * levels, lambda i: mixed.prepare(i, make_mixed))
         several(later, 2 * rest, count, piece)
@@ -830,7 +907,19 @@
             gain_second.begin()
 
     back.main(beside)
-    mixed.main(lambda turn: several(rest + turn, 2 * rest, count, piece))
+    wait = 2 * dp_count
+
+    def beside_mixed(turn):
+        several(rest + turn, 2 * rest, count, piece)
+        if square:
+            pl.when(turn < sum_cuts[1])(lambda: out_sum.turn(turn))
+            after = rest + turn - wait
+            here = (after >= 0) & (lax.rem(after, dp_count) == 0) & (after < count - dp_count)
+            pl.when(here)(lambda: qkv_sum.turn(lax.div(after, dp_count)))
+
+    mixed.main(beside_mixed)
+    if square:
+        qkv_sum.turn(sum_cuts[0] - 1)
     back.settle()
     mixed.settle()
     second.arrive()
@@ -839,12 +928,22 @@
     gain_out[...] = sum(gain_last[i] for i in range(dp_count)) / gain_ref[...]
     sums.arrive()
     wide = qkv_out.shape[2]
+    if square:
+        qkv_sum.arrive()
+        out_sum.arrive()
     for j in range(3):
         columns = slice(j * wide, (j + 1) * wide)
-        qkv_out[j] = sum(qkv_got[copy, :, columns].astype(FULL) for copy in range(dp_count))
-    w_out[...] = sum(out_got[copy].astype(FULL) for copy in range(dp_count))
+        if square:
+            qkv_out[j] = qkv_sum.total(columns)
+        else:
+            qkv_out[j] = sum(qkv_got[copy, :, columns].astype(FULL) for copy in range(dp_count))
+    if square:
+        w_out[...] = out_sum.total(slice(None))
+    else:
+        w_out[...] = sum(out_got[copy].astype(FULL) for copy in range(dp_count))
     gains_out[...] = sum(gains_got[copy] for copy in range(dp_count))
-    for moves in (back, mixed, first, second, sums, gain_first, gain_second):
+    moved = [back, mixed, first, second, sums, gain_first, gain_second]
+    for moves in moved + ([qkv_sum, out_sum] if square else []):
         moves.finish()
 
 
@@ -856,21 +955,27 @@
     block = (tokens, model_dim)
     tall = shared.shape[1] // dp_count
     wide = shared.shape[2]
-    sum_cuts = (high // 128, 2, 1)
+    sum_cuts = (high // 128, 2)
+    parts = (dp_count, high, columns)
     out, pair = exchange_outs(dp_count, sums, (False, True))
     shapes = [(3, high, columns // 3), out.shape[1:], pair.shape[1:], gain.shape, (tall, wide)]
     outs = [jax.ShapeDtypeStruct(block, LOW)] * 2
     outs += [jax.ShapeDtypeStruct(shape, FULL) for shape in shapes]
+    if dp_count == 4:
+        landing, some = SquareSum.scratch(sum_cuts[0], parts, LOW), (1,)
+        landing += [pltpu.VMEM(out.shape, LOW)] + SquareSum.scratch(sum_cuts[1], out.shape, LOW)
+    else:
+        landing, some = [pltpu.VMEM(parts, LOW), pltpu.VMEM(out.shape, LOW)], (1,) + sum_cuts
     line = [pltpu.VMEM((levels,) + block, LOW)] + LineReduce.scratch(size, block, LOW, cuts)
     return pl.pallas_call(
         functools.partial(closing_kernel, size, dp_count, len(tables), cuts, sum_cuts),
         out_shape=outs,
-        in_specs=[VMEM] * (len(tables) + 6) + [ANY] * 3,
+        in_specs=[VMEM] * (len(tables) + 7) + [ANY] * 2,
         out_specs=[ANY] * 2 + [VMEM] * 5,
         scratch_shapes=line
         + line
-        + [pltpu.VMEM((dp_count, high, columns), LOW)] * 2
-        + [pltpu.VMEM(a.shape, a.dtype) for a in (out, pair)]
+        + [pltpu.VMEM(parts, LOW), pltpu.VMEM(pair.shape, FULL)]
+        + landing
         + [pltpu.VMEM((size,) + shared.shape[1:], FULL)]
         + [pltpu.VMEM((dp_count, tall, wide), FULL)] * 2
         + [
@@ -879,7 +984,7 @@
             pltpu.VMEM(gain.shape, FULL),
             pltpu.VMEM((dp_count,) + gain.shape, FULL),
         ]
-        + Exchange.scratch(dp_count, sum_cuts)
+        + Exchange.scratch(dp_count, some)
         + Exchange.scratch(size, (1,))
         + Exchange.scratch(dp_count, (1,))
         + Exchange.scratch(size, (1,))

time: 721 us -> 714 us (level)
  waiting for transfers between devices: 34.8 us -> 8.69 us
  Pallas kernels: 616 us -> 636 us
    reduce_scatter x2, waiting for transfers between devices: 34.7 us -> 8.65 us  [on_device(): grads = lax.psum_scatter(grads, 'dp', scatter_dimension=0, tiled=True)]
    pallas_call x1, Pallas kernels: 128 us -> 148 us  [closing(): pl.pallas_call(functools.partial(closing_kernel, size, dp_count, len(tabl...]
  transfers between devices with their start and end apart: 2 -> 2, of which waited for: 1 -> 1; matrix products, arithmetic and copies ran while one was open for 2% -> 3% of each run, Pallas kernels for 48% -> 51%
where the time goes in v10:
time: 714 us; the launch traced here: 706 us
  Pallas kernels  636 us (89%)
  local copies, waits for them, and re-layouts  21.9 us (3%)
  between operations  15.1 us (2%)
  other arithmetic  14.2 us (2%)
  matrix products  10.3 us (1%)
  waiting for transfers between devices  8.69 us (1%)
    pallas_call x1, Pallas kernels, closing(): pl.pallas_call(functools.partial(closing_kernel, size, dp_count, len(tabl...  148 us
    pallas_call x2, Pallas kernels, expert(): pl.pallas_call(functools.partial(expert_kernel, first, count, tiles), out...  101 us
    pallas_call x1, Pallas kernels, attention(): pl.pallas_call(functools.partial(attention_kernel, size, dp_count, heads)...  93.1 us
    pallas_call x1, Pallas kernels, attend_back(): pl.pallas_call(functools.partial(attend_back_kernel, size // 2, GATHER_CU...  73.2 us
    pallas_call x1, Pallas kernels, call(): pl.pallas_call(kernel, out_shape=outs, in_specs=[ANY] * len(arrays), out_...  72.8 us
    pallas_call x1, Pallas kernels, collect_reduce(): pl.pallas_call(functools.partial(collect_reduce_kernel, levels, cuts, len...  70.5 us
    pallas_call x1, Pallas kernels, gather_place(): pl.pallas_call(functools.partial(gather_place_kernel, size // 2, cuts), o...  62.2 us
    unnamed x75, local copies, waits for them, and re-layouts  15.2 us
  transfers between devices with their start and end apart: 2, of which 1 were waited for; matrix products, arithmetic and copies ran while one was open for 3% of the time, Pallas kernels for 51%

profile of v10, /device:TPU:16, one launch (start us, length us, event | category | flops | bytes accessed | tf_op | source)
XLA Modules:
  0.0 706.4 jit_solution(17229370191446141865)
XLA Ops:
  7.3 1.4 fusion.8
  12.9 1.1 copy-done.22
  14.0 72.8 %opening.1 = (bf16[8,192,2048]{2,1,0:T(8,128)(2,1)}, s32[8,16,192]{2,1,0:T(8,128)S(1)}, bf16[4,8,64,768]{3,2,1,0:T(8,128)(2,1)S(1)}, bf16[4,8,64,24]{3,2,1,0:T(8,128)(2,1)S(1)}, bf16[4,8,4,64]{3,2,1,0:T(4,128)(2,1)S(1)}) custom-call(bf16[192,2048]{1,0:T(8,128)(2,1)S(1)} %copy-done, s32[16,192]{1,0:T(8,128)S(1)} %add_add_fusion.refs_1_, ...), custom_call_target="tpu_custom_call" | custom-call | bytes 200000000 | tf_op jit(solution)/shard_map/opening/pallas_call | solution.py:182
  86.8 1.6 copy-done.9
  90.4 93.1 %attention.1 = (bf16[8,192,2048]{2,1,0:T(8,128)(2,1)}, f32[8,192,768]{2,1,0:T(8,128)}, f32[8,192,2]{2,1,0:T(8,128)S(1)}, bf16[8,192,768]{2,1,0:T(8,128)(2,1)}, b...) custom-call(bf16[8,192,2048]{2,1,0:T(8,128)(2,1)} %get-tuple-element, ...), custom_call_target="tpu_custom_call" | custom-call | flops 4831838208 | bytes 100000000 | tf_op jit(solution)/shard_map/attention/pallas_call | solution.py:1352
  183.6 5.9 multiply_reduce_fusion.3
  189.8 1.2 copy-done.14
  191.6 62.2 %gather_place.1 = (bf16[3,576,2048]{2,1,0:T(8,128)(2,1)}, bf16[3,576,2048]{2,1,0:T(8,128)(2,1)}, f32[8,24,192]{2,1,0:T(8,128)S(1)}) custom-call(bf16[192,2048]{1,0:T(8,128)(2,1)S(1)} %multiply_convert_fusion.refs_0_, f32[24,192]{1,0:T(8,128)S(1)} %fusion.22.refs_1_, bf16[8,216,192]{2,1,0:T(8,128)(2,1)S(1)} %fusion.3.refs_2_.refs_7_, ...), custom_call_target="tpu_custom_call" | custom-call | flops 2717908992 | bytes 150000000 | tf_op jit(solution)/shard_map/gather_place/pallas_call | solution.py:653
  254.4 1.2 reshape.140.scale_ref
  255.6 35.3 %expert.2 = (bf16[4,768,2048]{2,1,0:T(8,128)(2,1)}, bf16[1,576,2048]{2,1,0:T(8,128)(2,1)}, bf16[1,576,2048]{2,1,0:T(8,128)(2,1)}, f32[1,576,1]{2,1,0:T(8,128)}) custom-call(bf16[3,576,2048]{2,1,0:T(8,128)(2,1)} %get-tuple-element.60.x_ref, bf16[3,576,2048]{2,1,0:T(8,128)(2,1)} %get-tuple-element.61.dy_ref, f32[3,576,1]{2,1,0:T(8,128)} %reshape.140.scale_ref, ...), custom_call_target="tpu_custom_call" | custom-call | flops 21743271936 | bytes 25165824 | tf_op jit(solution)/shard_map/expert/pallas_call | solution.py:1105
  291.2 65.8 %expert.3 = (bf16[4,1536,2048]{2,1,0:T(8,128)(2,1)}, bf16[2,576,2048]{2,1,0:T(8,128)(2,1)}, bf16[2,576,2048]{2,1,0:T(8,128)(2,1)}, f32[2,576,1]{2,1,0:T(8,128)}) custom-call(bf16[3,576,2048]{2,1,0:T(8,128)(2,1)} %get-tuple-element.60.x_ref, bf16[3,576,2048]{2,1,0:T(8,128)(2,1)} %get-tuple-element.61.dy_ref, f32[3,576,1]{2,1,0:T(8,128)} %reshape.140.scale_ref, ...), custom_call_target="tpu_custom_call" | custom-call | flops 43486543872 | bytes 50331648 | tf_op jit(solution)/shard_map/expert/pallas_call | solution.py:1105
  358.3 1.7 copy-done.12
  361.0 70.5 %collect_reduce.1 = (bf16[192,2048]{1,0:T(8,128)(2,1)S(1)}, f32[8,3,192]{2,1,0:T(4,128)S(1)}) custom-call(bf16[8,192,72]{2,1,0:T(8,128)(2,1)S(1)} %get-tuple-element.112.refs_0_, bf16[8,192,72]{2,1,0:T(8,128)(2,1)S(1)} %get-tuple-element.113.refs_1_, bf16[8,192,72]{2,1,0:T(8,128)(2,1)S(1)} %fusion.12.refs_2_, bf16[1,8,72,2048]{3,2,1,0:T(8,128)(2,1)S(1)} %bitcast.83, ...), custom_call_target="tpu_custom_call" | custom-call | bytes 150000000 | tf_op jit(solution)/shard_map/collect_reduce/pallas_call | solution.py:736
  433.6 3.6 multiply_reduce_fusion.1
  438.7 2.5 fusion.28.grad_ref
  441.2 73.2 %attend_back.1 = (bf16[8,192,768]{2,1,0:T(8,128)(2,1)}, f32[2,256]{1,0:T(2,128)S(1)}, bf16[4,256,512]{2,1,0:T(8,128)(2,1)S(1)}) custom-call(bf16[192,2048]{1,0:T(8,128)(2,1)S(1)} %fusion.28.grad_ref, bf16[2048,2048]{1,0:T(8,128)(2,1)} %bitcast.91, bf16[8,192,768]{2,1,0:T(8,128)(2,1)} %get-tuple-element.71.refs_1_, bf16[8,192,256]{2,1,0:T(8,128)(2,1)S(1)} %copy-done.19, ...), custom_call_target="tpu_custom_call" | custom-call | bytes 150000000 | tf_op jit(solution)/shard_map/attend_back/pallas_call | solution.py:1486
  516.0 148.0 %closing.1 = (bf16[192,2048]{1,0:T(8,128)(2,1)}, bf16[192,2048]{1,0:T(8,128)(2,1)}, f32[3,512,256]{2,1,0:T(8,128)}, f32[256,512]{1,0:T(8,128)}, f32[2,256]{1,0:T...) custom-call(bf16[8,192,72]{2,1,0:T(8,128)(2,1)} %copy-done.5, bf16[8,192,72]{2,1,0:T(8,128)(2,1)} %copy-done.6, ...), custom_call_target="tpu_custom_call" | custom-call | bytes 200000000 | tf_op jit(solution)/shard_map/closing/pallas_call | solution.py:970
  664.1 1.4 fusion.27
  665.4 1.7 fusion.4
  668.9 4.3 fusion.7
  673.1 5.6 widen.2
  678.7 8.7 %reduce-scatter.3.cloned.1.call-done = bf16[1536,2048]{1,0:T(8,128)(2,1)} async-done(((bf16[6144,2048]{1,0:T(8,128)(2,1)}), bf16[1536,2048]{1,0:T(8,128)(2,1)}) %reduce-scatter.3.cloned.1.call-update) | async-done | bytes 6291472 | tf_op jit(solution)/shard_map/reduce_scatter | solution.py:1607
  687.4 9.5 %widen.3 = (f32[3,512,2048]{2,1,0:T(8,128)}, f32[3,256,2048]{2,1,0:T(8,128)}) custom-call(bf16[2,768,2048]{2,1,0:T(8,128)(2,1)} %bitcast.92, f32[3,512,2048]{2,1,0:T(8,128)} %get-tuple-element.89.refs_1_, f32[3,256,2048]{2,1,0:T(8,128)} %get-tuple-element.90.refs_2_), custom_call_target="tpu_custom_call", output_to_operand_aliasing={{0}: (1, {}), {1}: (2, {})} | custom-call | flops 3145728 | bytes 18874368 | tf_op jit(solution)/shard_map/widen/pallas_call | solution.py:1181
  696.9 1.1 copy.70
  (123 shorter events, 17.8 us)
Async XLA Ops:
  7.2 665.9 %reduce-scatter.5.cloned.1.call-start = ((), (), s32[]{:S(2)}) async-start(), calls=%async_computation.3 | async-start | bytes 15728640 | tf_op jit(solution)/shard_map/reduce_scatter | solution.py:1607
  14.0 76.4 %copy-start.10 = (bf16[192,2048]{1,0:T(8,128)(2,1)S(1)}, bf16[192,2048]{1,0:T(8,128)(2,1)}, u32[]{:S(2)}) copy-start(bf16[192,2048]{1,0:T(8,128)(2,1)} %refs_8_.1) | copy-start | bytes 2359300
  14.0 76.4 %copy-start.25 = (f32[2,192,128]{2,1,0:T(8,128)S(1)}, f32[2,192,128]{2,1,0:T(8,128)}, u32[]{:S(2)}) copy-start(f32[2,192,128]{2,1,0:T(8,128)} %constant.45.clone.refs_4_.refs_6_) | copy-start | bytes 589828
  14.0 76.4 %copy-start.29 = (bf16[64,2048]{1,0:T(8,128)(2,1)S(1)}, bf16[64,2048]{1,0:T(8,128)(2,1)}, u32[]{:S(2)}) copy-start(bf16[64,2048]{1,0:T(8,128)(2,1)} %refs_7_.1) | copy-start | bytes 786436
  90.0 93.5 %copy-start.27 = (f32[1,2048]{1,0:T(1,128)}, f32[1,2048]{1,0:T(1,128)S(1)}, u32[]{:S(2)}) copy-start(f32[1,2048]{1,0:T(1,128)S(1)} %slice.47.refs_2_.refs_8_) | copy-start | bytes 24580
  90.3 93.2 %copy-start.7 = (s32[8,192,1]{2,1,0:T(8,128)}, s32[8,192,1]{2,1,0:T(8,128)S(1)}, u32[]{:S(2)}) copy-start(s32[8,192,1]{2,1,0:T(8,128)S(1)} %copy.55.refs_5_.refs_7_) | copy-start | bytes 18436
  90.4 93.2 %copy-start.1 = (bf16[192,2048]{1,0:T(8,128)(2,1)S(1)}, bf16[192,2048]{1,0:T(8,128)(2,1)}, u32[]{:S(2)}) copy-start(bf16[192,2048]{1,0:T(8,128)(2,1)} %refs_0_.1) | copy-start | bytes 2359300
  183.5 6.0 copy-start.16
  183.5 6.0 copy-start.18
  189.5 1.8 copy-start.30
  191.6 62.2 %copy-start.2 = (bf16[8,216,192]{2,1,0:T(8,128)(2,1)}, bf16[8,216,192]{2,1,0:T(8,128)(2,1)S(1)}, u32[]{:S(2)}) copy-start(bf16[8,216,192]{2,1,0:T(8,128)(2,1)S(1)} %fusion.3.refs_2_.refs_7_) | copy-start | bytes 1990660
  291.0 396.4 %reduce-scatter.3.cloned.1.call-start = ((), (), s32[]{:S(2)}) async-start(), calls=%async_computation.2 | async-start | bytes 31457280 | tf_op jit(solution)/shard_map/reduce_scatter | solution.py:1607
  357.4 74.2 %copy-start.4 = (bf16[8,192,72]{2,1,0:T(8,128)(2,1)}, bf16[8,192,72]{2,1,0:T(8,128)(2,1)S(1)}, u32[]{:S(2)}) copy-start(bf16[8,192,72]{2,1,0:T(8,128)(2,1)S(1)} %fusion.12.refs_2_) | copy-start | bytes 663556
  358.0 73.6 %copy-start.5 = (bf16[8,192,72]{2,1,0:T(8,128)(2,1)}, bf16[8,192,72]{2,1,0:T(8,128)(2,1)S(1)}, u32[]{:S(2)}) copy-start(bf16[8,192,72]{2,1,0:T(8,128)(2,1)S(1)} %get-tuple-element.112.refs_0_) | copy-start | bytes 663556
  358.0 73.6 %copy-start.6 = (bf16[8,192,72]{2,1,0:T(8,128)(2,1)}, bf16[8,192,72]{2,1,0:T(8,128)(2,1)S(1)}, u32[]{:S(2)}) copy-start(bf16[8,192,72]{2,1,0:T(8,128)(2,1)S(1)} %get-tuple-element.113.refs_1_) | copy-start | bytes 663556
  358.3 1.7 copy-start.12
  438.6 2.6 copy-start.8
  438.6 2.6 copy-start.17
  438.6 2.6 copy-start.19
  438.6 2.6 copy-start.26
  664.0 3.1 copy-start.35
  664.0 3.7 copy-start.34
  664.0 4.8 copy-start.31
  687.3 9.5 %copy-start.32 = (f32[3,512,256]{2,1,0:T(8,128)S(1)}, f32[3,512,256]{2,1,0:T(8,128)}, u32[]{:S(2)}) copy-start(f32[3,512,256]{2,1,0:T(8,128)} %get-tuple-element.81) | copy-start | bytes 4718596
  (14 other events, 15.9 us)
Sparse Core Ops, SparseCore 0:
  291.1 125.1 reduce-scatter.4
  419.4 267.9 reduce-scatter.2

commit v11 on v10

--- a/solution.py
+++ b/solution.py
@@ -907,19 +907,19 @@
             gain_second.begin()
 
     back.main(beside)
-    wait = 2 * dp_count
+    settled = 2
 
     def beside_mixed(turn):
         several(rest + turn, 2 * rest, count, piece)
         if square:
-            pl.when(turn < sum_cuts[1])(lambda: out_sum.turn(turn))
-            after = rest + turn - wait
-            here = (after >= 0) & (lax.rem(after, dp_count) == 0) & (after < count - dp_count)
-            pl.when(here)(lambda: qkv_sum.turn(lax.div(after, dp_count)))
+            pl.when((turn >= 4) & (turn < 4 + sum_cuts[1]))(lambda: out_sum.turn(turn - 4))
+            pl.when(turn == 7)(lambda: qkv_sum.turn(0))
+            pl.when(turn == 11)(lambda: qkv_sum.turn(1))
 
     mixed.main(beside_mixed)
     if square:
-        qkv_sum.turn(sum_cuts[0] - 1)
+        for k in range(settled, sum_cuts[0]):
+            qkv_sum.turn(k)
     back.settle()
     mixed.settle()
     second.arrive()

time: 714 us -> 721 us (level)
  transfers between devices with their start and end apart: 2 -> 2, of which waited for: 1 -> 1; matrix products, arithmetic and copies ran while one was open for 3% -> 2% of each run, Pallas kernels for 51% -> 52%
where the time goes in v11:
time: 721 us; the launch traced here: 713 us
  Pallas kernels  641 us (89%)
  local copies, waits for them, and re-layouts  21.9 us (3%)
  between operations  15.1 us (2%)
  other arithmetic  14 us (2%)
  waiting for transfers between devices  11.1 us (2%)
  matrix products  10.3 us (1%)
    pallas_call x1, Pallas kernels, closing(): pl.pallas_call(functools.partial(closing_kernel, size, dp_count, len(tabl...  153 us
    pallas_call x2, Pallas kernels, expert(): pl.pallas_call(functools.partial(expert_kernel, first, count, tiles), out...  101 us
    pallas_call x1, Pallas kernels, attention(): pl.pallas_call(functools.partial(attention_kernel, size, dp_count, heads)...  93.1 us
    pallas_call x1, Pallas kernels, attend_back(): pl.pallas_call(functools.partial(attend_back_kernel, size // 2, GATHER_CU...  73.2 us
    pallas_call x1, Pallas kernels, call(): pl.pallas_call(kernel, out_shape=outs, in_specs=[ANY] * len(arrays), out_...  72.8 us
    pallas_call x1, Pallas kernels, collect_reduce(): pl.pallas_call(functools.partial(collect_reduce_kernel, levels, cuts, len...  70.5 us
    pallas_call x1, Pallas kernels, gather_place(): pl.pallas_call(functools.partial(gather_place_kernel, size // 2, cuts), o...  62.2 us
    unnamed x75, local copies, waits for them, and re-layouts  15.2 us
  transfers between devices with their start and end apart: 2, of which 1 were waited for; matrix products, arithmetic and copies ran while one was open for 2% of the time, Pallas kernels for 52%

profile of v11, /device:TPU:16, one launch (start us, length us, event | category | flops | bytes accessed | tf_op | source)
XLA Modules:
  0.0 713.4 jit_solution(9427789004103886267)
XLA Ops:
  7.3 1.4 fusion.8
  12.9 1.1 copy-done.22
  14.0 72.8 %opening.1 = (bf16[8,192,2048]{2,1,0:T(8,128)(2,1)}, s32[8,16,192]{2,1,0:T(8,128)S(1)}, bf16[4,8,64,768]{3,2,1,0:T(8,128)(2,1)S(1)}, bf16[4,8,64,24]{3,2,1,0:T(8,128)(2,1)S(1)}, bf16[4,8,4,64]{3,2,1,0:T(4,128)(2,1)S(1)}) custom-call(bf16[192,2048]{1,0:T(8,128)(2,1)S(1)} %copy-done, s32[16,192]{1,0:T(8,128)S(1)} %add_add_fusion.refs_1_, ...), custom_call_target="tpu_custom_call" | custom-call | bytes 200000000 | tf_op jit(solution)/shard_map/opening/pallas_call | solution.py:182
  86.8 1.6 copy-done.9
  90.4 93.1 %attention.1 = (bf16[8,192,2048]{2,1,0:T(8,128)(2,1)}, f32[8,192,768]{2,1,0:T(8,128)}, f32[8,192,2]{2,1,0:T(8,128)S(1)}, bf16[8,192,768]{2,1,0:T(8,128)(2,1)}, b...) custom-call(bf16[8,192,2048]{2,1,0:T(8,128)(2,1)} %get-tuple-element, ...), custom_call_target="tpu_custom_call" | custom-call | flops 4831838208 | bytes 100000000 | tf_op jit(solution)/shard_map/attention/pallas_call | solution.py:1352
  183.6 5.9 multiply_reduce_fusion.3
  189.8 1.2 copy-done.14
  191.6 62.2 %gather_place.1 = (bf16[3,576,2048]{2,1,0:T(8,128)(2,1)}, bf16[3,576,2048]{2,1,0:T(8,128)(2,1)}, f32[8,24,192]{2,1,0:T(8,128)S(1)}) custom-call(bf16[192,2048]{1,0:T(8,128)(2,1)S(1)} %multiply_convert_fusion.refs_0_, f32[24,192]{1,0:T(8,128)S(1)} %fusion.22.refs_1_, bf16[8,216,192]{2,1,0:T(8,128)(2,1)S(1)} %fusion.3.refs_2_.refs_7_, ...), custom_call_target="tpu_custom_call" | custom-call | flops 2717908992 | bytes 150000000 | tf_op jit(solution)/shard_map/gather_place/pallas_call | solution.py:653
  254.4 1.2 reshape.140.scale_ref
  255.6 35.3 %expert.2 = (bf16[4,768,2048]{2,1,0:T(8,128)(2,1)}, bf16[1,576,2048]{2,1,0:T(8,128)(2,1)}, bf16[1,576,2048]{2,1,0:T(8,128)(2,1)}, f32[1,576,1]{2,1,0:T(8,128)}) custom-call(bf16[3,576,2048]{2,1,0:T(8,128)(2,1)} %get-tuple-element.60.x_ref, bf16[3,576,2048]{2,1,0:T(8,128)(2,1)} %get-tuple-element.61.dy_ref, f32[3,576,1]{2,1,0:T(8,128)} %reshape.140.scale_ref, ...), custom_call_target="tpu_custom_call" | custom-call | flops 21743271936 | bytes 25165824 | tf_op jit(solution)/shard_map/expert/pallas_call | solution.py:1105
  291.2 65.8 %expert.3 = (bf16[4,1536,2048]{2,1,0:T(8,128)(2,1)}, bf16[2,576,2048]{2,1,0:T(8,128)(2,1)}, bf16[2,576,2048]{2,1,0:T(8,128)(2,1)}, f32[2,576,1]{2,1,0:T(8,128)}) custom-call(bf16[3,576,2048]{2,1,0:T(8,128)(2,1)} %get-tuple-element.60.x_ref, bf16[3,576,2048]{2,1,0:T(8,128)(2,1)} %get-tuple-element.61.dy_ref, f32[3,576,1]{2,1,0:T(8,128)} %reshape.140.scale_ref, ...), custom_call_target="tpu_custom_call" | custom-call | flops 43486543872 | bytes 50331648 | tf_op jit(solution)/shard_map/expert/pallas_call | solution.py:1105
  358.3 1.7 copy-done.12
  361.0 70.5 %collect_reduce.1 = (bf16[192,2048]{1,0:T(8,128)(2,1)S(1)}, f32[8,3,192]{2,1,0:T(4,128)S(1)}) custom-call(bf16[8,192,72]{2,1,0:T(8,128)(2,1)S(1)} %get-tuple-element.112.refs_0_, bf16[8,192,72]{2,1,0:T(8,128)(2,1)S(1)} %get-tuple-element.113.refs_1_, bf16[8,192,72]{2,1,0:T(8,128)(2,1)S(1)} %fusion.12.refs_2_, bf16[1,8,72,2048]{3,2,1,0:T(8,128)(2,1)S(1)} %bitcast.83, ...), custom_call_target="tpu_custom_call" | custom-call | bytes 150000000 | tf_op jit(solution)/shard_map/collect_reduce/pallas_call | solution.py:736
  433.6 3.6 multiply_reduce_fusion.1
  438.7 2.5 fusion.28.grad_ref
  441.2 73.2 %attend_back.1 = (bf16[8,192,768]{2,1,0:T(8,128)(2,1)}, f32[2,256]{1,0:T(2,128)S(1)}, bf16[4,256,512]{2,1,0:T(8,128)(2,1)S(1)}) custom-call(bf16[192,2048]{1,0:T(8,128)(2,1)S(1)} %fusion.28.grad_ref, bf16[2048,2048]{1,0:T(8,128)(2,1)} %bitcast.91, bf16[8,192,768]{2,1,0:T(8,128)(2,1)} %get-tuple-element.71.refs_1_, bf16[8,192,256]{2,1,0:T(8,128)(2,1)S(1)} %copy-done.19, ...), custom_call_target="tpu_custom_call" | custom-call | bytes 150000000 | tf_op jit(solution)/shard_map/attend_back/pallas_call | solution.py:1486
  516.0 152.8 %closing.1 = (bf16[192,2048]{1,0:T(8,128)(2,1)}, bf16[192,2048]{1,0:T(8,128)(2,1)}, f32[3,512,256]{2,1,0:T(8,128)}, f32[256,512]{1,0:T(8,128)}, f32[2,256]{1,0:T...) custom-call(bf16[8,192,72]{2,1,0:T(8,128)(2,1)} %copy-done.5, bf16[8,192,72]{2,1,0:T(8,128)(2,1)} %copy-done.6, ...), custom_call_target="tpu_custom_call" | custom-call | bytes 200000000 | tf_op jit(solution)/shard_map/closing/pallas_call | solution.py:970
  668.8 1.4 fusion.27
  670.2 1.6 fusion.4
  673.5 4.2 fusion.7
  677.7 5.6 widen.2
  683.3 11.0 %reduce-scatter.3.cloned.1.call-done = bf16[1536,2048]{1,0:T(8,128)(2,1)} async-done(((bf16[6144,2048]{1,0:T(8,128)(2,1)}), bf16[1536,2048]{1,0:T(8,128)(2,1)}) %reduce-scatter.3.cloned.1.call-update) | async-done | bytes 6291472 | tf_op jit(solution)/shard_map/reduce_scatter | solution.py:1607
  694.4 9.5 %widen.3 = (f32[3,512,2048]{2,1,0:T(8,128)}, f32[3,256,2048]{2,1,0:T(8,128)}) custom-call(bf16[2,768,2048]{2,1,0:T(8,128)(2,1)} %bitcast.92, f32[3,512,2048]{2,1,0:T(8,128)} %get-tuple-element.89.refs_1_, f32[3,256,2048]{2,1,0:T(8,128)} %get-tuple-element.90.refs_2_), custom_call_target="tpu_custom_call", output_to_operand_aliasing={{0}: (1, {}), {1}: (2, {})} | custom-call | flops 3145728 | bytes 18874368 | tf_op jit(solution)/shard_map/widen/pallas_call | solution.py:1181
  703.9 1.1 copy.70
  (123 shorter events, 17.8 us)
Async XLA Ops:
  7.2 670.5 %reduce-scatter.5.cloned.1.call-start = ((), (), s32[]{:S(2)}) async-start(), calls=%async_computation.3 | async-start | bytes 15728640 | tf_op jit(solution)/shard_map/reduce_scatter | solution.py:1607
  14.0 76.4 %copy-start.10 = (bf16[192,2048]{1,0:T(8,128)(2,1)S(1)}, bf16[192,2048]{1,0:T(8,128)(2,1)}, u32[]{:S(2)}) copy-start(bf16[192,2048]{1,0:T(8,128)(2,1)} %refs_8_.1) | copy-start | bytes 2359300
  14.0 76.4 %copy-start.25 = (f32[2,192,128]{2,1,0:T(8,128)S(1)}, f32[2,192,128]{2,1,0:T(8,128)}, u32[]{:S(2)}) copy-start(f32[2,192,128]{2,1,0:T(8,128)} %constant.45.clone.refs_4_.refs_6_) | copy-start | bytes 589828
  14.0 76.4 %copy-start.29 = (bf16[64,2048]{1,0:T(8,128)(2,1)S(1)}, bf16[64,2048]{1,0:T(8,128)(2,1)}, u32[]{:S(2)}) copy-start(bf16[64,2048]{1,0:T(8,128)(2,1)} %refs_7_.1) | copy-start | bytes 786436
  90.0 93.5 %copy-start.27 = (f32[1,2048]{1,0:T(1,128)}, f32[1,2048]{1,0:T(1,128)S(1)}, u32[]{:S(2)}) copy-start(f32[1,2048]{1,0:T(1,128)S(1)} %slice.47.refs_2_.refs_8_) | copy-start | bytes 24580
  90.3 93.2 %copy-start.7 = (s32[8,192,1]{2,1,0:T(8,128)}, s32[8,192,1]{2,1,0:T(8,128)S(1)}, u32[]{:S(2)}) copy-start(s32[8,192,1]{2,1,0:T(8,128)S(1)} %copy.55.refs_5_.refs_7_) | copy-start | bytes 18436
  90.4 93.2 %copy-start.1 = (bf16[192,2048]{1,0:T(8,128)(2,1)S(1)}, bf16[192,2048]{1,0:T(8,128)(2,1)}, u32[]{:S(2)}) copy-start(bf16[192,2048]{1,0:T(8,128)(2,1)} %refs_0_.1) | copy-start | bytes 2359300
  183.5 6.0 copy-start.16
  183.5 6.0 copy-start.18
  189.5 1.8 copy-start.30
  191.6 62.2 %copy-start.2 = (bf16[8,216,192]{2,1,0:T(8,128)(2,1)}, bf16[8,216,192]{2,1,0:T(8,128)(2,1)S(1)}, u32[]{:S(2)}) copy-start(bf16[8,216,192]{2,1,0:T(8,128)(2,1)S(1)} %fusion.3.refs_2_.refs_7_) | copy-start | bytes 1990660
  291.0 403.4 %reduce-scatter.3.cloned.1.call-start = ((), (), s32[]{:S(2)}) async-start(), calls=%async_computation.2 | async-start | bytes 31457280 | tf_op jit(solution)/shard_map/reduce_scatter | solution.py:1607
  357.4 74.2 %copy-start.4 = (bf16[8,192,72]{2,1,0:T(8,128)(2,1)}, bf16[8,192,72]{2,1,0:T(8,128)(2,1)S(1)}, u32[]{:S(2)}) copy-start(bf16[8,192,72]{2,1,0:T(8,128)(2,1)S(1)} %fusion.12.refs_2_) | copy-start | bytes 663556
  358.0 73.6 %copy-start.5 = (bf16[8,192,72]{2,1,0:T(8,128)(2,1)}, bf16[8,192,72]{2,1,0:T(8,128)(2,1)S(1)}, u32[]{:S(2)}) copy-start(bf16[8,192,72]{2,1,0:T(8,128)(2,1)S(1)} %get-tuple-element.112.refs_0_) | copy-start | bytes 663556
  358.0 73.6 %copy-start.6 = (bf16[8,192,72]{2,1,0:T(8,128)(2,1)}, bf16[8,192,72]{2,1,0:T(8,128)(2,1)S(1)}, u32[]{:S(2)}) copy-start(bf16[8,192,72]{2,1,0:T(8,128)(2,1)S(1)} %get-tuple-element.113.refs_1_) | copy-start | bytes 663556
  358.3 1.7 copy-start.12
  438.6 2.6 copy-start.8
  438.6 2.6 copy-start.17
  438.6 2.6 copy-start.19
  438.6 2.6 copy-start.26
  668.8 3.0 copy-start.35
  668.8 3.6 copy-start.34
  668.8 4.7 copy-start.31
  694.3 9.5 %copy-start.32 = (f32[3,512,256]{2,1,0:T(8,128)S(1)}, f32[3,512,256]{2,1,0:T(8,128)}, u32[]{:S(2)}) copy-start(f32[3,512,256]{2,1,0:T(8,128)} %get-tuple-element.81) | copy-start | bytes 4718596
  (14 other events, 15.9 us)
Sparse Core Ops, SparseCore 0:
  291.1 125.1 reduce-scatter.4
  419.4 274.9 reduce-scatter.2

commit v12 on v10

--- a/solution.py
+++ b/solution.py
@@ -893,7 +893,7 @@
         pl.when(turn == sum_cuts[1])(lambda: sums.send(0, 0))
         pl.when(later == 0)(gain_first.begin)
         several(later, rest, 2 * levels, lambda i: mixed.prepare(i, make_mixed))
-        several(later, 2 * rest, count, piece)
+        several(later, rest, count, piece)
 
         @pl.when(later == rest - 1)
         def _():
@@ -907,19 +907,14 @@
             gain_second.begin()
 
     back.main(beside)
-    wait = 2 * dp_count
-
     def beside_mixed(turn):
-        several(rest + turn, 2 * rest, count, piece)
         if square:
             pl.when(turn < sum_cuts[1])(lambda: out_sum.turn(turn))
-            after = rest + turn - wait
-            here = (after >= 0) & (lax.rem(after, dp_count) == 0) & (after < count - dp_count)
-            pl.when(here)(lambda: qkv_sum.turn(lax.div(after, dp_count)))
+            after = turn - 1
+            here = (after >= 0) & (lax.rem(after, 3) == 0) & (after < 3 * sum_cuts[0])
+            pl.when(here)(lambda: qkv_sum.turn(lax.div(after, 3)))
 
     mixed.main(beside_mixed)
-    if square:
-        qkv_sum.turn(sum_cuts[0] - 1)
     back.settle()
     mixed.settle()
     second.arrive()

time: 714 us -> 704 us (0.986)
  Pallas kernels: 636 us -> 616 us
  waiting for transfers between devices: 8.69 us -> 18.6 us
    pallas_call x1, Pallas kernels: 148 us -> 128 us  [closing(): pl.pallas_call(functools.partial(closing_kernel, size, dp_count, len(tabl...]
    reduce_scatter x2, waiting for transfers between devices: 8.65 us -> 18.6 us  [on_device(): grads = lax.psum_scatter(grads, 'dp', scatter_dimension=0, tiled=True)]
  transfers between devices with their start and end apart: 2 -> 2, of which waited for: 1 -> 1; matrix products, arithmetic and copies ran while one was open for 3% -> 3% of each run, Pallas kernels for 51% -> 49%
where the time goes in v12:
time: 704 us; the launch traced here: 696 us
  Pallas kernels  616 us (88%)
  local copies, waits for them, and re-layouts  21.9 us (3%)
  waiting for transfers between devices  18.6 us (3%)
  between operations  15.1 us (2%)
  other arithmetic  14 us (2%)
  matrix products  10.3 us (1%)
    pallas_call x1, Pallas kernels, closing(): pl.pallas_call(functools.partial(closing_kernel, size, dp_count, len(tabl...  128 us
    pallas_call x2, Pallas kernels, expert(): pl.pallas_call(functools.partial(expert_kernel, first, count, tiles), out...  101 us
    pallas_call x1, Pallas kernels, attention(): pl.pallas_call(functools.partial(attention_kernel, size, dp_count, heads)...  93.1 us
    pallas_call x1, Pallas kernels, attend_back(): pl.pallas_call(functools.partial(attend_back_kernel, size // 2, GATHER_CU...  73.2 us
    pallas_call x1, Pallas kernels, call(): pl.pallas_call(kernel, out_shape=outs, in_specs=[ANY] * len(arrays), out_...  72.8 us
    pallas_call x1, Pallas kernels, collect_reduce(): pl.pallas_call(functools.partial(collect_reduce_kernel, levels, cuts, len...  70.5 us
    pallas_call x1, Pallas kernels, gather_place(): pl.pallas_call(functools.partial(gather_place_kernel, size // 2, cuts), o...  62.2 us
    reduce_scatter x2, waiting for transfers between devices, on_device(): grads = lax.psum_scatter(grads, 'dp', scatter_dimension=0, tiled=True)  18.6 us
  transfers between devices with their start and end apart: 2, of which 1 were waited for; matrix products, arithmetic and copies ran while one was open for 3% of the time, Pallas kernels for 49%

profile of v12, /device:TPU:16, one launch (start us, length us, event | category | flops | bytes accessed | tf_op | source)
XLA Modules:
  0.0 695.6 jit_solution(12926016642372700529)
XLA Ops:
  7.3 1.4 fusion.8
  12.9 1.1 copy-done.22
  14.0 72.8 %opening.1 = (bf16[8,192,2048]{2,1,0:T(8,128)(2,1)}, s32[8,16,192]{2,1,0:T(8,128)S(1)}, bf16[4,8,64,768]{3,2,1,0:T(8,128)(2,1)S(1)}, bf16[4,8,64,24]{3,2,1,0:T(8,128)(2,1)S(1)}, bf16[4,8,4,64]{3,2,1,0:T(4,128)(2,1)S(1)}) custom-call(bf16[192,2048]{1,0:T(8,128)(2,1)S(1)} %copy-done, s32[16,192]{1,0:T(8,128)S(1)} %add_add_fusion.refs_1_, ...), custom_call_target="tpu_custom_call" | custom-call | bytes 200000000 | tf_op jit(solution)/shard_map/opening/pallas_call | solution.py:182
  86.8 1.6 copy-done.9
  90.4 93.1 %attention.1 = (bf16[8,192,2048]{2,1,0:T(8,128)(2,1)}, f32[8,192,768]{2,1,0:T(8,128)}, f32[8,192,2]{2,1,0:T(8,128)S(1)}, bf16[8,192,768]{2,1,0:T(8,128)(2,1)}, b...) custom-call(bf16[8,192,2048]{2,1,0:T(8,128)(2,1)} %get-tuple-element, ...), custom_call_target="tpu_custom_call" | custom-call | flops 4831838208 | bytes 100000000 | tf_op jit(solution)/shard_map/attention/pallas_call | solution.py:1347
  183.6 5.9 multiply_reduce_fusion.3
  189.8 1.2 copy-done.14
  191.6 62.2 %gather_place.1 = (bf16[3,576,2048]{2,1,0:T(8,128)(2,1)}, bf16[3,576,2048]{2,1,0:T(8,128)(2,1)}, f32[8,24,192]{2,1,0:T(8,128)S(1)}) custom-call(bf16[192,2048]{1,0:T(8,128)(2,1)S(1)} %multiply_convert_fusion.refs_0_, f32[24,192]{1,0:T(8,128)S(1)} %fusion.22.refs_1_, bf16[8,216,192]{2,1,0:T(8,128)(2,1)S(1)} %fusion.3.refs_2_.refs_7_, ...), custom_call_target="tpu_custom_call" | custom-call | flops 2717908992 | bytes 150000000 | tf_op jit(solution)/shard_map/gather_place/pallas_call | solution.py:653
  254.4 1.2 reshape.140.scale_ref
  255.6 35.3 %expert.2 = (bf16[4,768,2048]{2,1,0:T(8,128)(2,1)}, bf16[1,576,2048]{2,1,0:T(8,128)(2,1)}, bf16[1,576,2048]{2,1,0:T(8,128)(2,1)}, f32[1,576,1]{2,1,0:T(8,128)}) custom-call(bf16[3,576,2048]{2,1,0:T(8,128)(2,1)} %get-tuple-element.60.x_ref, bf16[3,576,2048]{2,1,0:T(8,128)(2,1)} %get-tuple-element.61.dy_ref, f32[3,576,1]{2,1,0:T(8,128)} %reshape.140.scale_ref, ...), custom_call_target="tpu_custom_call" | custom-call | flops 21743271936 | bytes 25165824 | tf_op jit(solution)/shard_map/expert/pallas_call | solution.py:1100
  291.2 65.8 %expert.3 = (bf16[4,1536,2048]{2,1,0:T(8,128)(2,1)}, bf16[2,576,2048]{2,1,0:T(8,128)(2,1)}, bf16[2,576,2048]{2,1,0:T(8,128)(2,1)}, f32[2,576,1]{2,1,0:T(8,128)}) custom-call(bf16[3,576,2048]{2,1,0:T(8,128)(2,1)} %get-tuple-element.60.x_ref, bf16[3,576,2048]{2,1,0:T(8,128)(2,1)} %get-tuple-element.61.dy_ref, f32[3,576,1]{2,1,0:T(8,128)} %reshape.140.scale_ref, ...), custom_call_target="tpu_custom_call" | custom-call | flops 43486543872 | bytes 50331648 | tf_op jit(solution)/shard_map/expert/pallas_call | solution.py:1100
  358.3 1.7 copy-done.12
  361.0 70.5 %collect_reduce.1 = (bf16[192,2048]{1,0:T(8,128)(2,1)S(1)}, f32[8,3,192]{2,1,0:T(4,128)S(1)}) custom-call(bf16[8,192,72]{2,1,0:T(8,128)(2,1)S(1)} %get-tuple-element.112.refs_0_, bf16[8,192,72]{2,1,0:T(8,128)(2,1)S(1)} %get-tuple-element.113.refs_1_, bf16[8,192,72]{2,1,0:T(8,128)(2,1)S(1)} %fusion.12.refs_2_, bf16[1,8,72,2048]{3,2,1,0:T(8,128)(2,1)S(1)} %bitcast.83, ...), custom_call_target="tpu_custom_call" | custom-call | bytes 150000000 | tf_op jit(solution)/shard_map/collect_reduce/pallas_call | solution.py:736
  433.6 3.6 multiply_reduce_fusion.1
  438.7 2.5 fusion.28.grad_ref
  441.2 73.2 %attend_back.1 = (bf16[8,192,768]{2,1,0:T(8,128)(2,1)}, f32[2,256]{1,0:T(2,128)S(1)}, bf16[4,256,512]{2,1,0:T(8,128)(2,1)S(1)}) custom-call(bf16[192,2048]{1,0:T(8,128)(2,1)S(1)} %fusion.28.grad_ref, bf16[2048,2048]{1,0:T(8,128)(2,1)} %bitcast.91, bf16[8,192,768]{2,1,0:T(8,128)(2,1)} %get-tuple-element.71.refs_1_, bf16[8,192,256]{2,1,0:T(8,128)(2,1)S(1)} %copy-done.19, ...), custom_call_target="tpu_custom_call" | custom-call | bytes 150000000 | tf_op jit(solution)/shard_map/attend_back/pallas_call | solution.py:1481
  516.0 127.5 %closing.1 = (bf16[192,2048]{1,0:T(8,128)(2,1)}, bf16[192,2048]{1,0:T(8,128)(2,1)}, f32[3,512,256]{2,1,0:T(8,128)}, f32[256,512]{1,0:T(8,128)}, f32[2,256]{1,0:T...) custom-call(bf16[8,192,72]{2,1,0:T(8,128)(2,1)} %copy-done.5, bf16[8,192,72]{2,1,0:T(8,128)(2,1)} %copy-done.6, ...), custom_call_target="tpu_custom_call" | custom-call | bytes 200000000 | tf_op jit(solution)/shard_map/closing/pallas_call | solution.py:965
  643.6 1.4 fusion.27
  644.9 1.6 fusion.4
  648.2 4.2 fusion.7
  652.4 5.6 widen.2
  658.0 18.6 %reduce-scatter.3.cloned.1.call-done = bf16[1536,2048]{1,0:T(8,128)(2,1)} async-done(((bf16[6144,2048]{1,0:T(8,128)(2,1)}), bf16[1536,2048]{1,0:T(8,128)(2,1)}) %reduce-scatter.3.cloned.1.call-update) | async-done | bytes 6291472 | tf_op jit(solution)/shard_map/reduce_scatter | solution.py:1602
  676.6 9.5 %widen.3 = (f32[3,512,2048]{2,1,0:T(8,128)}, f32[3,256,2048]{2,1,0:T(8,128)}) custom-call(bf16[2,768,2048]{2,1,0:T(8,128)(2,1)} %bitcast.92, f32[3,512,2048]{2,1,0:T(8,128)} %get-tuple-element.89.refs_1_, f32[3,256,2048]{2,1,0:T(8,128)} %get-tuple-element.90.refs_2_), custom_call_target="tpu_custom_call", output_to_operand_aliasing={{0}: (1, {}), {1}: (2, {})} | custom-call | flops 3145728 | bytes 18874368 | tf_op jit(solution)/shard_map/widen/pallas_call | solution.py:1176
  686.1 1.1 copy.70
  (123 shorter events, 17.8 us)
Async XLA Ops:
  7.2 645.2 %reduce-scatter.5.cloned.1.call-start = ((), (), s32[]{:S(2)}) async-start(), calls=%async_computation.3 | async-start | bytes 15728640 | tf_op jit(solution)/shard_map/reduce_scatter | solution.py:1602
  14.0 76.4 %copy-start.10 = (bf16[192,2048]{1,0:T(8,128)(2,1)S(1)}, bf16[192,2048]{1,0:T(8,128)(2,1)}, u32[]{:S(2)}) copy-start(bf16[192,2048]{1,0:T(8,128)(2,1)} %refs_8_.1) | copy-start | bytes 2359300
  14.0 76.4 %copy-start.25 = (f32[2,192,128]{2,1,0:T(8,128)S(1)}, f32[2,192,128]{2,1,0:T(8,128)}, u32[]{:S(2)}) copy-start(f32[2,192,128]{2,1,0:T(8,128)} %constant.45.clone.refs_4_.refs_6_) | copy-start | bytes 589828
  14.0 76.4 %copy-start.29 = (bf16[64,2048]{1,0:T(8,128)(2,1)S(1)}, bf16[64,2048]{1,0:T(8,128)(2,1)}, u32[]{:S(2)}) copy-start(bf16[64,2048]{1,0:T(8,128)(2,1)} %refs_7_.1) | copy-start | bytes 786436
  90.0 93.5 %copy-start.27 = (f32[1,2048]{1,0:T(1,128)}, f32[1,2048]{1,0:T(1,128)S(1)}, u32[]{:S(2)}) copy-start(f32[1,2048]{1,0:T(1,128)S(1)} %slice.47.refs_2_.refs_8_) | copy-start | bytes 24580
  90.3 93.2 %copy-start.7 = (s32[8,192,1]{2,1,0:T(8,128)}, s32[8,192,1]{2,1,0:T(8,128)S(1)}, u32[]{:S(2)}) copy-start(s32[8,192,1]{2,1,0:T(8,128)S(1)} %copy.55.refs_5_.refs_7_) | copy-start | bytes 18436
  90.4 93.2 %copy-start.1 = (bf16[192,2048]{1,0:T(8,128)(2,1)S(1)}, bf16[192,2048]{1,0:T(8,128)(2,1)}, u32[]{:S(2)}) copy-start(bf16[192,2048]{1,0:T(8,128)(2,1)} %refs_0_.1) | copy-start | bytes 2359300
  183.5 6.0 copy-start.16
  183.5 6.0 copy-start.18
  189.5 1.8 copy-start.30
  191.6 62.2 %copy-start.2 = (bf16[8,216,192]{2,1,0:T(8,128)(2,1)}, bf16[8,216,192]{2,1,0:T(8,128)(2,1)S(1)}, u32[]{:S(2)}) copy-start(bf16[8,216,192]{2,1,0:T(8,128)(2,1)S(1)} %fusion.3.refs_2_.refs_7_) | copy-start | bytes 1990660
  290.9 385.6 %reduce-scatter.3.cloned.1.call-start = ((), (), s32[]{:S(2)}) async-start(), calls=%async_computation.2 | async-start | bytes 31457280 | tf_op jit(solution)/shard_map/reduce_scatter | solution.py:1602
  357.4 74.2 %copy-start.4 = (bf16[8,192,72]{2,1,0:T(8,128)(2,1)}, bf16[8,192,72]{2,1,0:T(8,128)(2,1)S(1)}, u32[]{:S(2)}) copy-start(bf16[8,192,72]{2,1,0:T(8,128)(2,1)S(1)} %fusion.12.refs_2_) | copy-start | bytes 663556
  358.0 73.6 %copy-start.5 = (bf16[8,192,72]{2,1,0:T(8,128)(2,1)}, bf16[8,192,72]{2,1,0:T(8,128)(2,1)S(1)}, u32[]{:S(2)}) copy-start(bf16[8,192,72]{2,1,0:T(8,128)(2,1)S(1)} %get-tuple-element.112.refs_0_) | copy-start | bytes 663556
  358.0 73.6 %copy-start.6 = (bf16[8,192,72]{2,1,0:T(8,128)(2,1)}, bf16[8,192,72]{2,1,0:T(8,128)(2,1)S(1)}, u32[]{:S(2)}) copy-start(bf16[8,192,72]{2,1,0:T(8,128)(2,1)S(1)} %get-tuple-element.113.refs_1_) | copy-start | bytes 663556
  358.3 1.7 copy-start.12
  438.6 2.6 copy-start.8
  438.6 2.6 copy-start.17
  438.6 2.6 copy-start.19
  438.6 2.6 copy-start.26
  643.5 3.0 copy-start.35
  643.5 3.6 copy-start.34
  643.5 4.7 copy-start.31
  676.6 9.5 %copy-start.32 = (f32[3,512,256]{2,1,0:T(8,128)S(1)}, f32[3,512,256]{2,1,0:T(8,128)}, u32[]{:S(2)}) copy-start(f32[3,512,256]{2,1,0:T(8,128)} %get-tuple-element.81) | copy-start | bytes 4718596
  (14 other events, 15.9 us)
Sparse Core Ops, SparseCore 0:
  291.1 125.1 reduce-scatter.4
  419.4 257.1 reduce-scatter.2
